TPU v7x, 32 devices: a whole 2x2x4 slice. The times are simulated.
32 devices in a mesh: dp: 8 (over y, x, core), tensor: 4 (over z).
Axes of the slice: x: 2, y: 2, z: 4, core: 2. Of those that a mesh axis runs over, the one named last changes fastest.
Arguments:
- hidden_in: bfloat16 [2, 8, 1024, 2048], P(None, None, ('dp', 'tensor')), may hold values from -6 to 6
- lengths: int32 [2, 8], replicated, may hold values from 1 to 1024, 6144 in all within a row
- dealing: int32 [2, 8], replicated, may hold values from 0 to 7, each once within a row
- cotangent: bfloat16 [2, 8, 1024, 2048], P(None, None, ('dp', 'tensor')), may hold values from -6 to 6
- attn_gain: bfloat16 [2048], P(('dp', 'tensor')), may hold values from 0.5 to 1.5
- attn_shift: bfloat16 [2048], P(('dp', 'tensor')), may hold values from -1.5 to 1.5
- ffn_gain: bfloat16 [2048], P(('dp', 'tensor')), may hold values from 0.5 to 1.5
- ffn_shift: bfloat16 [2048], P(('dp', 'tensor')), may hold values from -1.5 to 1.5
- qkv_weight: bfloat16 [2048, 8, 768], P('dp', 'tensor'), may hold values from -0.125 to 0.125
- qkv_bias: bfloat16 [8, 768], P('tensor', 'dp'), may hold values from -0.25 to 0.25
- dense_weight: bfloat16 [8, 256, 2048], P('tensor', 'dp'), may hold values from -1.5 to 1.5
- dense_bias: bfloat16 [2048], P(('dp', 'tensor')), may hold values from -1.5 to 1.5
- fc1_weight: bfloat16 [2048, 8192], P('dp', 'tensor'), may hold values from -0.125 to 0.125
- fc1_bias: bfloat16 [8, 1024], P('tensor', 'dp'), may hold values from -1.5 to 1.5
- fc2_weight: bfloat16 [8192, 2048], P('tensor', 'dp'), may hold values from -0.0625 to 0.0625
- fc2_bias: bfloat16 [2048], P(('dp', 'tensor')), may hold values from -1.5 to 1.5
Outputs:
- output: bfloat16 [2, 8, 1024, 2048], P(None, None, ('dp', 'tensor'))
- input_grad: bfloat16 [2, 8, 1024, 2048], P(None, None, ('dp', 'tensor'))
- attngain_grad: float32 [2048], P(('dp', 'tensor'))
- attnshift_grad: float32 [2048], P(('dp', 'tensor'))
- ffngain_grad: float32 [2048], P(('dp', 'tensor'))
- ffnshift_grad: float32 [2048], P(('dp', 'tensor'))
- qkvweight_grad: float32 [2048, 8, 768], P('dp', 'tensor')
- qkvbias_grad: float32 [8, 768], P('tensor', 'dp')
- denseweight_grad: float32 [8, 256, 2048], P('tensor', 'dp')
- densebias_grad: float32 [2048], P(('dp', 'tensor'))
- fc1weight_grad: float32 [2048, 8192], P('dp', 'tensor')
- fc1bias_grad: float32 [8, 1024], P('tensor', 'dp')
- fc2weight_grad: float32 [8192, 2048], P('tensor', 'dp')
- fc2bias_grad: float32 [2048], P(('dp', 'tensor'))
Inputs may be any that keep to these rules, and one draw needn't show every extreme that they name: lengths[m, j] belongs to the sequence in input slot dealing[m, j]; in each micro-batch the lengths sum to 6144 and the longest is 1024. Each row of dealing holds every slot number once.
All inputs are finite; a program needn't handle non-finite values.
Results may differ from a plain program's by a relative error of at most 0.013.
Values may be sent and summed in bfloat16 or wider, within the bound.
No kernel may reach another device: no remote copies, remote signals or barrier semaphores. Data moves between devices by JAX's collectives and lax.ppermute only.
A program may use at most 320 MiB of HBM per device.

v0:
```python
import math

import jax
import jax.numpy as jnp
from jax import lax
from jax.sharding import PartitionSpec as P

HD = 256
ROT = 64


EPSILON = 1e-05
ROPE_BASE = 10000.0
NEG_FILL = -1e30
SQRT_HALF = 0.7071067811865476
INV_ROOT_TWO_PI = 0.3989422804014327


def normalize(residual, gain, shift):
    centred = residual - jnp.mean(residual, axis=-1, keepdims=True)
    scaling = lax.rsqrt(jnp.mean(centred * centred, axis=-1, keepdims=True) + EPSILON)
    unit_rows = centred * scaling
    return (unit_rows * gain + shift, unit_rows, scaling)


def norm_back(grad_out, unit_rows, scaling, gain):
    grad_unit = grad_out * gain
    return scaling * (
        grad_unit
        - jnp.mean(grad_unit, axis=-1, keepdims=True)
        - unit_rows * jnp.mean(grad_unit * unit_rows, axis=-1, keepdims=True)
    )


def angles(positions):
    freqs = jnp.exp(jnp.arange(ROT // 2, dtype=jnp.float32) * (-2.0 * math.log(ROPE_BASE) / ROT))
    phases = positions.astype(jnp.float32)[:, None] * freqs[None, :]
    return (jnp.cos(phases), jnp.sin(phases))


def rotate(heads, cosines, sines):
    half_rot = ROT // 2
    lead_part = heads[..., :half_rot]
    trail_part = heads[..., half_rot:ROT]
    cos_rows = cosines[:, None, :]
    sin_rows = sines[:, None, :]
    return jnp.concatenate(
        [
            lead_part * cos_rows - trail_part * sin_rows,
            trail_part * cos_rows + lead_part * sin_rows,
            heads[..., ROT:],
        ],
        axis=-1,
    )


def take_slots(table, order):
    return jnp.take(table, order, axis=0)


def per_device(
    hidden_in,
    lengths,
    dealing,
    cotangent,
    attn_gain,
    attn_shift,
    ffn_gain,
    ffn_shift,
    qkv_weight,
    qkv_bias,
    dense_weight,
    dense_bias,
    fc1_weight,
    fc1_bias,
    fc2_weight,
    fc2_bias,
):
    n_tensor = lax.axis_size("tensor")
    n_data = lax.axis_size("dp")
    group_index = lax.axis_index("dp")
    micro_count, seq_count, piece_rows, width = hidden_in.shape
    local_rows = n_data * piece_rows
    seq_rows = n_tensor * local_rows
    block_rows = min(512, seq_rows)
    block_count = seq_rows // block_rows
    scale = 1.0 / math.sqrt(HD)
    sent_in = jax.vmap(take_slots)(hidden_in, dealing)
    sent_grad = jax.vmap(take_slots)(cotangent, dealing)
    got_in, got_grad = (
        lax.all_to_all(sent_in, "dp", split_axis=1, concat_axis=2, tiled=True),
        lax.all_to_all(sent_grad, "dp", split_axis=1, concat_axis=2, tiled=True),
    )
    small = (
        lax.all_gather(attn_gain, ("dp", "tensor"), axis=0, tiled=True),
        lax.all_gather(attn_shift, ("dp", "tensor"), axis=0, tiled=True),
        lax.all_gather(ffn_gain, ("dp", "tensor"), axis=0, tiled=True),
        lax.all_gather(ffn_shift, ("dp", "tensor"), axis=0, tiled=True),
        lax.all_gather(dense_bias, ("dp", "tensor"), axis=0, tiled=True),
        lax.all_gather(fc2_bias, ("dp", "tensor"), axis=0, tiled=True),
    )
    gain_one, shift_one, gain_two, shift_two, dense_shift, fc2_shift = [
        piece.astype(jnp.float32) for piece in small
    ]
    shard_set = (qkv_weight, qkv_bias, dense_weight, fc1_weight, fc1_bias, fc2_weight)

    def current_set():
        return (
            lax.all_gather(shard_set[0], "dp", axis=0, tiled=True),
            lax.all_gather(shard_set[1], "dp", axis=1, tiled=True),
            lax.all_gather(shard_set[2], "dp", axis=1, tiled=True),
            lax.all_gather(shard_set[3], "dp", axis=0, tiled=True),
            lax.all_gather(shard_set[4], "dp", axis=1, tiled=True),
            lax.all_gather(shard_set[5], "dp", axis=1, tiled=True),
        )

    row_ids = jnp.arange(seq_rows, dtype=jnp.int32)
    part_ids = row_ids // local_rows
    within = row_ids % local_rows
    positions = (within // piece_rows * n_tensor + part_ids) * piece_rows + within % piece_rows
    cosines, sines = angles(positions)
    my_lengths = lax.dynamic_index_in_dim(lengths, group_index, axis=1, keepdims=False)
    starts = jnp.arange(block_count, dtype=jnp.int32) * block_rows
    heads_here = qkv_weight.shape[1]
    units_here = fc1_weight.shape[1]
    weight_zero = (
        jnp.zeros((width, heads_here, 3 * HD), jnp.float32),
        jnp.zeros((heads_here, 3 * HD), jnp.float32),
        jnp.zeros((heads_here, HD, width), jnp.float32),
        jnp.zeros((width, units_here), jnp.float32),
        jnp.zeros((heads_here, units_here // heads_here), jnp.float32),
        jnp.zeros((units_here, width), jnp.float32),
    )
    small_zero = tuple((jnp.zeros((width,), jnp.float32) for index_slot in range(6)))

    def micro_step(totals, item):
        weight_totals, small_totals = totals
        rows_in, rows_grad, seq_length = item
        qkv_full, qkv_shift, dense_full, fc1_full, fc1_shift, fc2_full = current_set()
        residual = rows_in.astype(jnp.float32)
        normed_one, unit_one, scale_one = normalize(residual, gain_one, shift_one)
        normed_two = unit_one * gain_two + shift_two
        full_one, full_two = (
            lax.all_gather(normed_one.astype(jnp.bfloat16), "tensor", axis=0, tiled=True),
            lax.all_gather(normed_two.astype(jnp.bfloat16), "tensor", axis=0, tiled=True),
        )
        projected = jnp.einsum(
            "ld,dhe->lhe", full_one, qkv_full, preferred_element_type=jnp.float32
        ) + qkv_shift.astype(jnp.float32)
        queries = rotate(projected[..., :HD], cosines, sines).astype(jnp.bfloat16)
        key_rows = rotate(projected[..., HD : 2 * HD], cosines, sines).astype(jnp.bfloat16)
        value_rows = projected[..., 2 * HD :].astype(jnp.bfloat16)

        def mask_for(row_start):
            q_pos = lax.dynamic_slice_in_dim(positions, row_start, block_rows, 0)
            return (positions[None, :] <= q_pos[:, None]) & (positions[None, :] < seq_length)

        def attend(row_start):
            q_block = lax.dynamic_slice_in_dim(queries, row_start, block_rows, 0)
            scores = (
                jnp.einsum("qhe,khe->hqk", q_block, key_rows, preferred_element_type=jnp.float32)
                * scale
            )
            scores = jnp.where(mask_for(row_start)[None], scores, NEG_FILL)
            row_max = jnp.max(scores, axis=-1, keepdims=True)
            expo = jnp.exp(scores - row_max)
            row_sum = jnp.sum(expo, axis=-1, keepdims=True)
            softmax_w = (expo / row_sum).astype(jnp.bfloat16)
            mixed_block = jnp.einsum(
                "hqk,khe->qhe", softmax_w, value_rows, preferred_element_type=jnp.float32
            ).astype(jnp.bfloat16)
            return (mixed_block, (row_max + jnp.log(row_sum))[..., 0])

        mixed_blocks, lse_blocks = lax.map(attend, starts)
        mixed = mixed_blocks.reshape(seq_rows, heads_here, HD)
        attn_part = jnp.einsum("lhe,hed->ld", mixed, dense_full, preferred_element_type=jnp.float32)
        preact = jnp.dot(
            full_two, fc1_full, preferred_element_type=jnp.float32
        ) + fc1_shift.reshape(-1).astype(jnp.float32)
        activation = jax.nn.gelu(preact, approximate=False).astype(jnp.bfloat16)
        ffn_part = jnp.dot(activation, fc2_full, preferred_element_type=jnp.float32)
        branch = lax.psum_scatter(attn_part + ffn_part, "tensor", scatter_dimension=0, tiled=True)
        output_rows = (residual + branch + dense_shift + fc2_shift).astype(jnp.bfloat16)
        back_set = current_set()
        grad_full = lax.all_gather(rows_grad, "tensor", axis=0, tiled=True)
        grad_dense = jnp.einsum("lhe,ld->hed", mixed, grad_full, preferred_element_type=jnp.float32)
        grad_mixed = jnp.einsum(
            "ld,hed->lhe", grad_full, back_set[2], preferred_element_type=jnp.float32
        ).astype(jnp.bfloat16)
        grad_fc2 = jnp.einsum(
            "lf,ld->fd", activation, grad_full, preferred_element_type=jnp.float32
        )
        grad_act = jnp.einsum(
            "ld,fd->lf", grad_full, back_set[5], preferred_element_type=jnp.float32
        )
        normal_cdf = 0.5 * (1.0 + lax.erf(preact * SQRT_HALF))
        slope = normal_cdf + preact * jnp.exp(-0.5 * preact * preact) * INV_ROOT_TWO_PI
        grad_pre = (grad_act * slope).astype(jnp.bfloat16)
        grad_fc1 = jnp.einsum("ld,lf->df", full_two, grad_pre, preferred_element_type=jnp.float32)
        grad_fc1b = jnp.sum(grad_pre.astype(jnp.float32), axis=0).reshape(
            heads_here, units_here // heads_here
        )
        grad_second = jnp.einsum(
            "lf,df->ld", grad_pre, back_set[3], preferred_element_type=jnp.float32
        )

        def back_block(carry, block_item):
            key_grad, value_grad = carry
            row_start, lse_block = block_item
            q_block = lax.dynamic_slice_in_dim(queries, row_start, block_rows, 0)
            grad_block = lax.dynamic_slice_in_dim(grad_mixed, row_start, block_rows, 0)
            scores = (
                jnp.einsum("qhe,khe->hqk", q_block, key_rows, preferred_element_type=jnp.float32)
                * scale
            )
            scores = jnp.where(mask_for(row_start)[None], scores, NEG_FILL)
            softmax_f = jnp.exp(scores - lse_block[..., None])
            softmax_w = softmax_f.astype(jnp.bfloat16)
            value_grad = value_grad + jnp.einsum(
                "hqk,qhe->khe", softmax_w, grad_block, preferred_element_type=jnp.float32
            )
            grad_soft = jnp.einsum(
                "qhe,khe->hqk", grad_block, value_rows, preferred_element_type=jnp.float32
            )
            grad_scores = (
                softmax_f * (grad_soft - jnp.sum(softmax_f * grad_soft, axis=-1, keepdims=True))
            ).astype(jnp.bfloat16)
            query_part = (
                jnp.einsum(
                    "hqk,khe->qhe", grad_scores, key_rows, preferred_element_type=jnp.float32
                )
                * scale
            )
            key_grad = (
                key_grad
                + jnp.einsum(
                    "hqk,qhe->khe", grad_scores, q_block, preferred_element_type=jnp.float32
                )
                * scale
            )
            return ((key_grad, value_grad), query_part)

        zero_heads = jnp.zeros((seq_rows, heads_here, HD), jnp.float32)
        (key_grad, value_grad), query_parts = lax.scan(
            back_block, (zero_heads, zero_heads), (starts, lse_blocks)
        )
        query_grad = query_parts.reshape(seq_rows, heads_here, HD)
        grad_qkv = jnp.concatenate(
            [rotate(query_grad, cosines, -sines), rotate(key_grad, cosines, -sines), value_grad],
            axis=-1,
        ).astype(jnp.bfloat16)
        grad_qkvw = jnp.einsum(
            "ld,lhe->dhe", full_one, grad_qkv, preferred_element_type=jnp.float32
        )
        grad_qkvb = jnp.sum(grad_qkv.astype(jnp.float32), axis=0)
        grad_first = jnp.einsum(
            "lhe,dhe->ld", grad_qkv, back_set[0], preferred_element_type=jnp.float32
        )
        upstream = rows_grad.astype(jnp.float32)
        upstream_sum = jnp.sum(upstream, axis=0)
        norm_one, norm_two = (
            lax.psum_scatter(grad_first, "tensor", scatter_dimension=0, tiled=True),
            lax.psum_scatter(grad_second, "tensor", scatter_dimension=0, tiled=True),
        )
        input_rows = (
            upstream
            + norm_back(norm_one, unit_one, scale_one, gain_one)
            + norm_back(norm_two, unit_one, scale_one, gain_two)
        ).astype(jnp.bfloat16)
        small_terms = (
            jnp.sum(norm_one * unit_one, axis=0),
            jnp.sum(norm_one, axis=0),
            jnp.sum(norm_two * unit_one, axis=0),
            jnp.sum(norm_two, axis=0),
            upstream_sum,
            upstream_sum,
        )
        weight_terms = (grad_qkvw, grad_qkvb, grad_dense, grad_fc1, grad_fc1b, grad_fc2)
        new_weights = tuple((total + term for total, term in zip(weight_totals, weight_terms)))
        new_small = tuple((total + term for total, term in zip(small_totals, small_terms)))
        return ((new_weights, new_small), (output_rows, input_rows))

    (weight_totals, small_totals), (output_rows, input_rows) = lax.scan(
        micro_step, (weight_zero, small_zero), (got_in[:, 0], got_grad[:, 0], my_lengths)
    )
    weight_sums = (
        lax.psum_scatter(
            weight_totals[0].astype(jnp.bfloat16), "dp", scatter_dimension=0, tiled=True
        ).astype(jnp.float32),
        lax.psum_scatter(
            weight_totals[1].astype(jnp.bfloat16), "dp", scatter_dimension=1, tiled=True
        ).astype(jnp.float32),
        lax.psum_scatter(
            weight_totals[2].astype(jnp.bfloat16), "dp", scatter_dimension=1, tiled=True
        ).astype(jnp.float32),
        lax.psum_scatter(
            weight_totals[3].astype(jnp.bfloat16), "dp", scatter_dimension=0, tiled=True
        ).astype(jnp.float32),
        lax.psum_scatter(
            weight_totals[4].astype(jnp.bfloat16), "dp", scatter_dimension=1, tiled=True
        ).astype(jnp.float32),
        lax.psum_scatter(
            weight_totals[5].astype(jnp.bfloat16), "dp", scatter_dimension=1, tiled=True
        ).astype(jnp.float32),
    )
    small_sums = lax.psum_scatter(small_totals, ("dp", "tensor"), scatter_dimension=0, tiled=True)
    back_out, back_grad = (
        lax.all_to_all(output_rows[:, None], "dp", split_axis=2, concat_axis=1, tiled=True),
        lax.all_to_all(input_rows[:, None], "dp", split_axis=2, concat_axis=1, tiled=True),
    )
    slot_ids = jnp.arange(seq_count, dtype=jnp.int32)
    inverse = jnp.sum(
        jnp.where(dealing[:, :, None] == slot_ids[None, None, :], slot_ids[None, :, None], 0),
        axis=1,
    )
    output = jax.vmap(take_slots)(back_out, inverse)
    input_grad = jax.vmap(take_slots)(back_grad, inverse)
    return (
        output,
        input_grad,
        small_sums[0],
        small_sums[1],
        small_sums[2],
        small_sums[3],
        weight_sums[0],
        weight_sums[1],
        weight_sums[2],
        small_sums[4],
        weight_sums[3],
        weight_sums[4],
        weight_sums[5],
        small_sums[5],
    )


def solution(mesh):
    return jax.shard_map(
        per_device,
        mesh=mesh,
        in_specs=(
            P(None, None, ("dp", "tensor"), None),
            P(),
            P(),
            P(None, None, ("dp", "tensor"), None),
            P(("dp", "tensor")),
            P(("dp", "tensor")),
            P(("dp", "tensor")),
            P(("dp", "tensor")),
            P("dp", "tensor", None),
            P("tensor", "dp"),
            P("tensor", "dp", None),
            P(("dp", "tensor")),
            P("dp", "tensor"),
            P("tensor", "dp"),
            P("tensor", "dp"),
            P(("dp", "tensor")),
        ),
        out_specs=(
            P(None, None, ("dp", "tensor"), None),
            P(None, None, ("dp", "tensor"), None),
            P(("dp", "tensor")),
            P(("dp", "tensor")),
            P(("dp", "tensor")),
            P(("dp", "tensor")),
            P("dp", "tensor", None),
            P("tensor", "dp"),
            P("tensor", "dp", None),
            P(("dp", "tensor")),
            P("dp", "tensor"),
            P("tensor", "dp"),
            P("tensor", "dp"),
            P(("dp", "tensor")),
        ),
        check_vma=False,
    )
```

profile of v0, /device:TPU:0, one launch (start us, length us, event | category | flops | bytes accessed | tf_op | source)
XLA Modules:
  0.0 2300.3 jit_solution(938326112984021490)
XLA Ops:
  20.3 5.2 all-to-all-start
  28.8 23.3 %all-to-all-done = bf16[2,8,32,2048]{3,2,0,1:T(8,128)(2,1)S(1)} async-done(((bf16[2,8,32,2048]{3,2,0,1:T(8,128)(2,1)}), bf16[2,8,32,2048]{3,2,0,1:T(8,128)(2,1)S(1)}, u32[]{:S(2)}, u32[]{:S(2)}) %all-to-all-start) | async-done | bytes 2097184 | tf_op jit(solution)/shard_map/all_to_all | solution.py:91
  58.2 58.6 %all-reduce.14 = (bf16[2048]{0:T(1024)(128)(2,1)S(1)}, bf16[2048]{0:T(1024)(128)(2,1)S(1)}, bf16[2048]{0:T(1024)(128)(2,1)S(1)}, bf16[2048]{0:T(1024)(128)(2,1)S...) all-reduce(bf16[2048]{0:T(1024)(128)(2,1)S(1)} %dynamic-update-slic, ...), channel_id=1, replica_groups=mesh['dp'=8,'tensor'=4] {'dp','tensor'}, use_global_device_ids=true, to_apply=%add | all-reduce | flops 12288 | bytes 49152
  127.4 1772.7 %while.89 = (s32[]{:T(128)}, f32[2048,2,768]{2,0,1:T(8,128)}, f32[2,768]{1,0:T(2,128)}, f32[2,256,2048]{2,1,0:T(8,128)}, f32[2048,2048]{1,0:T(8,128)}, /*index=5...) while((s32[]{:T(128)}, f32[2048,2,768]{2,0,1:T(8,128)}, ...), condition=%wide.region_24.26_spmd.clone.clone.clone.clone, body=%wide.region_0.25_spmd.clone.clone.clone.clone.sunk | while | flops 81338195968 | bytes 859343296 | solution.py:283
  139.7 10.1 all-gather.10
  150.5 7.0 all-gather.24.cloned.1.call-done
  157.5 82.4 %all-gather.26.cloned.1.call-done = bf16[1,1024,2048]{2,1,0:T(8,128)(2,1)} async-done(((bf16[1,256,2048]{2,1,0:T(8,128)(2,1)}), bf16[1,1024,2048]{2,1,0:T(8,128)(2,1)}) %all-gather.26.cloned.1.call-update) | async-done | bytes 4194320 | tf_op jit(solution)/shard_map/while/body/eval_jaxpr/all_gather | solution.py:185
  239.9 6.2 fusion.249
  246.1 74.7 %all-gather.22.cloned.1.call-done = bf16[1024,2048]{1,0:T(8,128)(2,1)} async-done(((bf16[256,2048]{1,0:T(8,128)(2,1)}), bf16[1024,2048]{1,0:T(8,128)(2,1)}) %all-gather.22.cloned.1.call-update) | async-done | bytes 4194320 | tf_op jit(solution)/shard_map/while/body/eval_jaxpr/all_gather | solution.py:144
  320.8 47.0 %all-gather.20.cloned.1.call-done = bf16[2048,2,768]{0,2,1:T(8,128)(2,1)} async-done(((bf16[256,2,768]{0,2,1:T(8,128)(2,1)}), bf16[2048,2,768]{0,2,1:T(8,128)(2,1)}) %all-gather.20.cloned.1.call-update) | async-done | bytes 6291472 | tf_op jit(solution)/shard_map/while/body/eval_jaxpr/all_gather | solution.py:109
  367.8 10.1 fusion.246
  386.6 17.4 while.90
  405.0 87.3 %while.91 = (s32[]{:T(128)}, f32[1024,2,256]{0,2,1:T(8,128)}, f32[1024,2,256]{0,2,1:T(8,128)}, f32[2,512,2,256]{1,0,3,2:T(2,128)}, s32[2]{0:T(128)S(1)}, /*index...) while((s32[]{:T(128)}, f32[1024,2,256]{0,2,1:T(8,128)}, ...), condition=%wide.region_9.10_spmd.clone.clone, body=%wide.region_7.9_spmd.clone.clone.sunk | while | flops 2704015360 | bytes 111194568 | solution.py:244
  421.3 19.6 dynamic_update_slice.44
  463.7 19.6 dynamic_update_slice.44
  511.8 6.1 concatenate.44
  517.8 10.7 convolution_bitcast_fusion.2
  529.2 8.7 all_gather.105
  538.0 31.3 %fusion.250 = (bf16[1024,2048]{1,0:T(8,128)(2,1)}, f32[1024,2048]{1,0:T(8,128)}) fusion(f32[2048]{0:T(1024)S(1)} %bitcast.334, bf16[1024,2048]{1,0:T(8,128)(2,1)} %all-gather.28.cloned.1.call-done, bf16[2048,2048]{1,0:T(8,128)(2,1)} %all-gather.30.cloned.1.call-done), kind=kOutput, calls=%fused_computation.67.clone.1 | convolution fusion | flops 8728346624 | bytes 25174016 | tf_op jit(solution)/shard_map/while/body/eval_jaxpr/dot_general | solution.py:177
  569.4 17.2 convert_reduce_fusion.11
  588.6 11.3 fusion.251
  599.9 12.7 fusion.253
  612.6 5.7 bitcast_add_fusion.6
  619.5 7.2 select_add_fusion.23
  626.8 9.8 select_add_fusion.21
  636.6 15.8 select_add_fusion.24
  652.4 12.6 select_add_fusion.26
  665.1 44.9 %reduce-scatter.25.cloned.1.call-done = f32[256,2048]{1,0:T(8,128)} async-done(((f32[1024,2048]{1,0:T(8,128)}), f32[256,2048]{1,0:T(8,128)}) %reduce-scatter.25.cloned.1.call-update) | async-done | bytes 2097168 | tf_op jit(solution)/shard_map/while/body/eval_jaxpr/reduce_scatter | solution.py:262
  710.0 147.6 %reduce-scatter.23.cloned.1.call-done = f32[256,2048]{1,0:T(8,128)} async-done(((f32[1024,2048]{1,0:T(8,128)}), f32[256,2048]{1,0:T(8,128)}) %reduce-scatter.23.cloned.1.call-update) | async-done | bytes 2097168 | tf_op jit(solution)/shard_map/while/body/eval_jaxpr/reduce_scatter | solution.py:263
  861.8 143.2 %reduce-scatter.27.cloned.1.call-done = f32[256,2048]{1,0:T(8,128)} async-done(((f32[1024,2048]{1,0:T(8,128)}), f32[256,2048]{1,0:T(8,128)}) %reduce-scatter.27.cloned.1.call-update) | async-done | bytes 2097168 | tf_op jit(solution)/shard_map/while/body/eval_jaxpr/reduce_scatter | solution.py:182
  1022.2 8.9 all-gather.10
  1031.7 10.1 all-gather.24.cloned.1.call-done
  1041.8 82.2 %all-gather.26.cloned.1.call-done = bf16[1,1024,2048]{2,1,0:T(8,128)(2,1)} async-done(((bf16[1,256,2048]{2,1,0:T(8,128)(2,1)}), bf16[1,1024,2048]{2,1,0:T(8,128)(2,1)}) %all-gather.26.cloned.1.call-update) | async-done | bytes 4194320 | tf_op jit(solution)/shard_map/while/body/eval_jaxpr/all_gather | solution.py:185
  1124.0 6.2 fusion.249
  1130.2 74.7 %all-gather.22.cloned.1.call-done = bf16[1024,2048]{1,0:T(8,128)(2,1)} async-done(((bf16[256,2048]{1,0:T(8,128)(2,1)}), bf16[1024,2048]{1,0:T(8,128)(2,1)}) %all-gather.22.cloned.1.call-update) | async-done | bytes 4194320 | tf_op jit(solution)/shard_map/while/body/eval_jaxpr/all_gather | solution.py:144
  1204.9 47.0 %all-gather.20.cloned.1.call-done = bf16[2048,2,768]{0,2,1:T(8,128)(2,1)} async-done(((bf16[256,2,768]{0,2,1:T(8,128)(2,1)}), bf16[2048,2,768]{0,2,1:T(8,128)(2,1)}) %all-gather.20.cloned.1.call-update) | async-done | bytes 6291472 | tf_op jit(solution)/shard_map/while/body/eval_jaxpr/all_gather | solution.py:109
  1251.9 10.1 fusion.246
  1270.8 17.4 while.90
  1289.2 87.3 %while.91 = (s32[]{:T(128)}, f32[1024,2,256]{0,2,1:T(8,128)}, f32[1024,2,256]{0,2,1:T(8,128)}, f32[2,512,2,256]{1,0,3,2:T(2,128)}, s32[2]{0:T(128)S(1)}, /*index...) while((s32[]{:T(128)}, f32[1024,2,256]{0,2,1:T(8,128)}, ...), condition=%wide.region_9.10_spmd.clone.clone, body=%wide.region_7.9_spmd.clone.clone.sunk | while | flops 2704015360 | bytes 111194568 | solution.py:244
  1305.5 19.6 dynamic_update_slice.44
  1347.9 19.6 dynamic_update_slice.44
  1395.9 6.0 concatenate.44
  1401.9 10.7 convolution_bitcast_fusion.2
  1413.3 8.8 all_gather.105
  1422.2 31.4 %fusion.250 = (bf16[1024,2048]{1,0:T(8,128)(2,1)}, f32[1024,2048]{1,0:T(8,128)}) fusion(f32[2048]{0:T(1024)S(1)} %bitcast.334, bf16[1024,2048]{1,0:T(8,128)(2,1)} %all-gather.28.cloned.1.call-done, bf16[2048,2048]{1,0:T(8,128)(2,1)} %all-gather.30.cloned.1.call-done), kind=kOutput, calls=%fused_computation.67.clone.1 | convolution fusion | flops 8728346624 | bytes 25174016 | tf_op jit(solution)/shard_map/while/body/eval_jaxpr/dot_general | solution.py:177
  1453.5 17.2 convert_reduce_fusion.11
  1472.7 11.3 fusion.251
  1484.1 12.6 fusion.253
  1496.8 5.7 bitcast_add_fusion.6
  1503.7 8.4 select_add_fusion.23
  1512.2 12.5 select_add_fusion.21
  1524.7 18.5 select_add_fusion.24
  1543.3 16.1 select_add_fusion.26
  1559.4 34.4 %reduce-scatter.25.cloned.1.call-done = f32[256,2048]{1,0:T(8,128)} async-done(((f32[1024,2048]{1,0:T(8,128)}), f32[256,2048]{1,0:T(8,128)}) %reduce-scatter.25.cloned.1.call-update) | async-done | bytes 2097168 | tf_op jit(solution)/shard_map/while/body/eval_jaxpr/reduce_scatter | solution.py:262
  1593.8 147.6 %reduce-scatter.23.cloned.1.call-done = f32[256,2048]{1,0:T(8,128)} async-done(((f32[1024,2048]{1,0:T(8,128)}), f32[256,2048]{1,0:T(8,128)}) %reduce-scatter.23.cloned.1.call-update) | async-done | bytes 2097168 | tf_op jit(solution)/shard_map/while/body/eval_jaxpr/reduce_scatter | solution.py:263
  1745.6 143.2 %reduce-scatter.27.cloned.1.call-done = f32[256,2048]{1,0:T(8,128)} async-done(((f32[1024,2048]{1,0:T(8,128)}), f32[256,2048]{1,0:T(8,128)}) %reduce-scatter.27.cloned.1.call-update) | async-done | bytes 2097168 | tf_op jit(solution)/shard_map/while/body/eval_jaxpr/reduce_scatter | solution.py:182
  1907.4 21.9 copy.230
  1929.4 9.1 convert_element_type.189
  1938.6 9.1 convert_element_type.193
  1961.7 22.5 all-to-all-done.3
  1990.1 64.1 %all-reduce.13 = (f32[2048]{0:T(1024)S(1)}, f32[2048]{0:T(1024)S(1)}, f32[2048]{0:T(1024)S(1)}, f32[2048]{0:T(1024)S(1)}, f32[2048]{0:T(1024)S(1)}, /*index=5*/f32[2048]{0:T(1024)S(1)}) all-reduce(f32[2048]{0:T(1024)S(1)} %copy-done.33, f32[2048]{0:T(1024)S(1)} %copy-done.36, ...), channel_id=6, replica_groups=mesh['dp'=8,'tensor'=4] {'dp','tensor'}, use_global_device_ids=true, to_apply=%region_26.28.clone | all-reduce | flops 12288 | bytes 98304
  2077.5 62.7 %all-reduce.17.cloned.1.call-done = bf16[2048,2,768]{2,1,0:T(2,128)(2,1)} async-done(((bf16[2048,2,768]{2,1,0:T(2,128)(2,1)}), bf16[2048,2,768]{2,1,0:T(2,128)(2,1)}) %all-reduce.17.cloned.1.call-update) | async-done | bytes 6291472
  2143.0 72.0 %reduce-scatter.15.cloned.1.call-done = bf16[256,2048]{1,0:T(8,128)(2,1)} async-done(((bf16[2048,2048]{1,0:T(8,128)(2,1)}), bf16[256,2048]{1,0:T(8,128)(2,1)}) %reduce-scatter.15.cloned.1.call-update) | async-done | bytes 1048592 | tf_op jit(solution)/shard_map/reduce_scatter | solution.py:296
  2217.7 72.2 %reduce-scatter.17.cloned.1.call-done = bf16[2048,256]{1,0:T(8,128)(2,1)} async-done(((bf16[2048,2048]{1,0:T(8,128)(2,1)}), bf16[2048,256]{1,0:T(8,128)(2,1)}) %reduce-scatter.17.cloned.1.call-update) | async-done | bytes 1048592 | tf_op jit(solution)/shard_map/reduce_scatter | solution.py:302
  (603 shorter events, 313.4 us)
Async XLA Ops:
  20.3 31.8 %all-to-all-start = ((bf16[2,8,32,2048]{3,2,0,1:T(8,128)(2,1)}), bf16[2,8,32,2048]{3,2,0,1:T(8,128)(2,1)S(1)}, u32[]{:S(2)}, u32[]{:S(2)}) async-start(bf16[2,8,32,2048]{3,2,0,1:T(8,128)(2,1)} %copy.186), calls=%async_computation.3 | async-start | bytes 4194304 | tf_op jit(solution)/shard_map/all_to_all | solution.py:91
  25.5 94.8 %copy-start.22 = (bf16[256,2,768]{2,1,0:T(2,128)(2,1)S(1)}, bf16[256,2,768]{2,1,0:T(2,128)(2,1)}, u32[]{:S(2)}) copy-start(bf16[256,2,768]{2,1,0:T(2,128)(2,1)} %param.32) | copy-start | bytes 2359300
  25.5 96.8 %copy-start.59 = (s32[2,8]{1,0:T(2,128)S(1)}, s32[2,8]{1,0:T(2,128)}, u32[]{:S(2)}) copy-start(s32[2,8]{1,0:T(2,128)} %param.25) | copy-start | bytes 196
  52.1 70.4 %copy-start.18 = (bf16[2,8,32,2048]{3,2,0,1:T(8,128)(2,1)}, bf16[2,8,32,2048]{3,2,0,1:T(8,128)(2,1)S(1)}, u32[]{:S(2)}) copy-start(bf16[2,8,32,2048]{3,2,0,1:T(8,128)(2,1)S(1)} %all-to-all-done) | copy-start | bytes 6291460
  52.1 72.2 %all-to-all-start.1 = ((bf16[2,8,32,2048]{3,2,0,1:T(8,128)(2,1)}), bf16[2,8,32,2048]{3,2,0,1:T(8,128)(2,1)}, u32[]{:S(2)}, u32[]{:S(2)}) async-start(bf16[2,8,32,2048]{3,2,0,1:T(8,128)(2,1)} %copy.188), calls=%async_computation.4 | async-start | bytes 4194304 | tf_op jit(solution)/shard_map/all_to_all | solution.py:92
  127.8 29.7 %all-gather.24.cloned.1.call-start = ((), (), s32[]{:S(2)}) async-start(), calls=%async_computation.20 | async-start | bytes 2359296 | tf_op jit(solution)/shard_map/while/body/eval_jaxpr/all_gather | solution.py:111
  128.5 111.3 %all-gather.26.cloned.1.call-start = ((), (), s32[]{:S(2)}) async-start(), calls=%async_computation.21 | async-start | bytes 5242880 | tf_op jit(solution)/shard_map/while/body/eval_jaxpr/all_gather | solution.py:185
  131.7 189.1 %all-gather.22.cloned.1.call-start = ((), (), s32[]{:S(2)}) async-start(), calls=%async_computation.19 | async-start | bytes 5242880 | tf_op jit(solution)/shard_map/while/body/eval_jaxpr/all_gather | solution.py:144
  135.4 232.4 %all-gather.20.cloned.1.call-start = ((), (), s32[]{:S(2)}) async-start(), calls=%async_computation.18 | async-start | bytes 7077888 | tf_op jit(solution)/shard_map/while/body/eval_jaxpr/all_gather | solution.py:109
  135.9 402.0 %all-gather.28.cloned.1.call-start = ((), (), s32[]{:S(2)}) async-start(), calls=%async_computation.22 | async-start | bytes 5242880 | tf_op jit(solution)/shard_map/while/body/eval_jaxpr/all_gather | solution.py:145
  136.5 401.5 %all-gather.30.cloned.1.call-start = ((), (), s32[]{:S(2)}) async-start(), calls=%async_computation.23 | async-start | bytes 9437184 | tf_op jit(solution)/shard_map/while/body/eval_jaxpr/all_gather | solution.py:112
  137.1 432.2 %all-gather.32.cloned.1.call-start = ((), (), s32[]{:S(2)}) async-start(), calls=%async_computation.24 | async-start | bytes 9437184 | tf_op jit(solution)/shard_map/while/body/eval_jaxpr/all_gather | solution.py:114
  137.9 572.1 %reduce-scatter.25.cloned.1.call-start = ((), (), s32[]{:S(2)}) async-start(), calls=%async_computation.26 | async-start | bytes 10485760 | tf_op jit(solution)/shard_map/while/body/eval_jaxpr/reduce_scatter | solution.py:262
  528.6 329.0 %reduce-scatter.23.cloned.1.call-start = ((), (), s32[]{:S(2)}) async-start(), calls=%async_computation.25 | async-start | bytes 10485760 | tf_op jit(solution)/shard_map/while/body/eval_jaxpr/reduce_scatter | solution.py:263
  599.9 405.1 %reduce-scatter.27.cloned.1.call-start = ((), (), s32[]{:S(2)}) async-start(), calls=%async_computation.27 | async-start | bytes 10485760 | tf_op jit(solution)/shard_map/while/body/eval_jaxpr/reduce_scatter | solution.py:182
  652.4 205.1 %copy-start.12 = (bf16[2,256,2048]{2,1,0:T(8,128)(2,1)S(1)}, bf16[2,256,2048]{2,1,0:T(8,128)(2,1)}, u32[]{:S(2)}) copy-start(bf16[2,256,2048]{2,1,0:T(8,128)(2,1)} %copy-done.11) | copy-start | bytes 6291460 | tf_op jit(solution)/shard_map/while
  652.4 205.1 %copy-start.24 = (f32[256]{0:T(256)S(1)}, f32[256]{0:T(256)}, u32[]{:S(2)}) copy-start(f32[256]{0:T(256)} %copy-done.23) | copy-start | bytes 3076 | tf_op jit(solution)/shard_map/while
  652.4 205.1 %copy-start.28 = (f32[256]{0:T(256)S(1)}, f32[256]{0:T(256)}, u32[]{:S(2)}) copy-start(f32[256]{0:T(256)} %copy-done.27) | copy-start | bytes 3076 | tf_op jit(solution)/shard_map/while
  665.0 196.6 %copy-start.37 = (f32[2048]{0:T(1024)S(1)}, f32[2048]{0:T(1024)}, u32[]{:S(2)}) copy-start(f32[2048]{0:T(1024)} %get-tuple-element.2122) | copy-start | bytes 24580 | tf_op jit(solution)/shard_map/while
  665.0 196.6 %copy-start.40 = (f32[2048]{0:T(1024)S(1)}, f32[2048]{0:T(1024)}, u32[]{:S(2)}) copy-start(f32[2048]{0:T(1024)} %get-tuple-element.2123) | copy-start | bytes 24580 | tf_op jit(solution)/shard_map/while
  665.0 196.7 %copy-start.31 = (f32[2048]{0:T(1024)S(1)}, f32[2048]{0:T(1024)}, u32[]{:S(2)}) copy-start(f32[2048]{0:T(1024)} %get-tuple-element.2120) | copy-start | bytes 24580 | tf_op jit(solution)/shard_map/while
  665.0 196.7 %copy-start.34 = (f32[2048]{0:T(1024)S(1)}, f32[2048]{0:T(1024)}, u32[]{:S(2)}) copy-start(f32[2048]{0:T(1024)} %get-tuple-element.2121) | copy-start | bytes 24580 | tf_op jit(solution)/shard_map/while
  665.0 340.0 %copy-start.13 = (bf16[1,256,2048]{2,1,0:T(8,128)(2,1)S(1)}, bf16[1,256,2048]{2,1,0:T(8,128)(2,1)}, u32[]{:S(2)}) copy-start(bf16[1,256,2048]{2,1,0:T(8,128)(2,1)} %get-tuple-element.1932) | copy-start | bytes 3145732 | tf_op jit(solution)/shard_map/while
  665.0 340.0 %copy-start.49 = (f32[2048]{0:T(1024)S(1)}, f32[2048]{0:T(1024)}, u32[]{:S(2)}) copy-start(f32[2048]{0:T(1024)} %get-tuple-element.2181) | copy-start | bytes 24580 | tf_op jit(solution)/shard_map/while
  665.1 339.9 %copy-start.50 = (f32[2048]{0:T(1024)S(1)}, f32[2048]{0:T(1024)}, u32[]{:S(2)}) copy-start(f32[2048]{0:T(1024)} %get-tuple-element.2182) | copy-start | bytes 24580 | tf_op jit(solution)/shard_map/while
  861.7 148.2 %copy-start.38 = (f32[2048]{0:T(1024)}, f32[2048]{0:T(1024)S(1)}, u32[]{:S(2)}) copy-start(f32[2048]{0:T(1024)S(1)} %get-tuple-element.2162) | copy-start | bytes 24580 | tf_op jit(solution)/shard_map/while
  861.7 148.2 %copy-start.41 = (f32[2048]{0:T(1024)}, f32[2048]{0:T(1024)S(1)}, u32[]{:S(2)}) copy-start(f32[2048]{0:T(1024)S(1)} %get-tuple-element.2163) | copy-start | bytes 24580 | tf_op jit(solution)/shard_map/while
  861.7 148.1 %copy-start.32 = (f32[2048]{0:T(1024)}, f32[2048]{0:T(1024)S(1)}, u32[]{:S(2)}) copy-start(f32[2048]{0:T(1024)S(1)} %get-tuple-element.2160) | copy-start | bytes 24580 | tf_op jit(solution)/shard_map/while
  861.7 148.1 %copy-start.35 = (f32[2048]{0:T(1024)}, f32[2048]{0:T(1024)S(1)}, u32[]{:S(2)}) copy-start(f32[2048]{0:T(1024)S(1)} %get-tuple-element.2161) | copy-start | bytes 24580 | tf_op jit(solution)/shard_map/while
  1010.4 31.4 %all-gather.24.cloned.1.call-start = ((), (), s32[]{:S(2)}) async-start(), calls=%async_computation.20 | async-start | bytes 2359296 | tf_op jit(solution)/shard_map/while/body/eval_jaxpr/all_gather | solution.py:111
  1011.1 112.9 %all-gather.26.cloned.1.call-start = ((), (), s32[]{:S(2)}) async-start(), calls=%async_computation.21 | async-start | bytes 5242880 | tf_op jit(solution)/shard_map/while/body/eval_jaxpr/all_gather | solution.py:185
  1014.3 190.6 %all-gather.22.cloned.1.call-start = ((), (), s32[]{:S(2)}) async-start(), calls=%async_computation.19 | async-start | bytes 5242880 | tf_op jit(solution)/shard_map/while/body/eval_jaxpr/all_gather | solution.py:144
  1018.0 233.9 %all-gather.20.cloned.1.call-start = ((), (), s32[]{:S(2)}) async-start(), calls=%async_computation.18 | async-start | bytes 7077888 | tf_op jit(solution)/shard_map/while/body/eval_jaxpr/all_gather | solution.py:109
  1018.5 403.6 %all-gather.28.cloned.1.call-start = ((), (), s32[]{:S(2)}) async-start(), calls=%async_computation.22 | async-start | bytes 5242880 | tf_op jit(solution)/shard_map/while/body/eval_jaxpr/all_gather | solution.py:145
  1019.1 403.0 %all-gather.30.cloned.1.call-start = ((), (), s32[]{:S(2)}) async-start(), calls=%async_computation.23 | async-start | bytes 9437184 | tf_op jit(solution)/shard_map/while/body/eval_jaxpr/all_gather | solution.py:112
  1019.7 433.8 %all-gather.32.cloned.1.call-start = ((), (), s32[]{:S(2)}) async-start(), calls=%async_computation.24 | async-start | bytes 9437184 | tf_op jit(solution)/shard_map/while/body/eval_jaxpr/all_gather | solution.py:114
  1020.3 573.5 %reduce-scatter.25.cloned.1.call-start = ((), (), s32[]{:S(2)}) async-start(), calls=%async_computation.26 | async-start | bytes 10485760 | tf_op jit(solution)/shard_map/while/body/eval_jaxpr/reduce_scatter | solution.py:262
  1412.7 328.7 %reduce-scatter.23.cloned.1.call-start = ((), (), s32[]{:S(2)}) async-start(), calls=%async_computation.25 | async-start | bytes 10485760 | tf_op jit(solution)/shard_map/while/body/eval_jaxpr/reduce_scatter | solution.py:263
  1484.0 404.8 %reduce-scatter.27.cloned.1.call-start = ((), (), s32[]{:S(2)}) async-start(), calls=%async_computation.27 | async-start | bytes 10485760 | tf_op jit(solution)/shard_map/while/body/eval_jaxpr/reduce_scatter | solution.py:182
  1543.2 198.1 %copy-start.12 = (bf16[2,256,2048]{2,1,0:T(8,128)(2,1)S(1)}, bf16[2,256,2048]{2,1,0:T(8,128)(2,1)}, u32[]{:S(2)}) copy-start(bf16[2,256,2048]{2,1,0:T(8,128)(2,1)} %copy-done.11) | copy-start | bytes 6291460 | tf_op jit(solution)/shard_map/while
  1543.3 198.1 %copy-start.24 = (f32[256]{0:T(256)S(1)}, f32[256]{0:T(256)}, u32[]{:S(2)}) copy-start(f32[256]{0:T(256)} %copy-done.23) | copy-start | bytes 3076 | tf_op jit(solution)/shard_map/while
  1543.3 198.1 %copy-start.28 = (f32[256]{0:T(256)S(1)}, f32[256]{0:T(256)}, u32[]{:S(2)}) copy-start(f32[256]{0:T(256)} %copy-done.27) | copy-start | bytes 3076 | tf_op jit(solution)/shard_map/while
  1559.3 186.1 %copy-start.37 = (f32[2048]{0:T(1024)S(1)}, f32[2048]{0:T(1024)}, u32[]{:S(2)}) copy-start(f32[2048]{0:T(1024)} %get-tuple-element.2122) | copy-start | bytes 24580 | tf_op jit(solution)/shard_map/while
  1559.3 186.1 %copy-start.40 = (f32[2048]{0:T(1024)S(1)}, f32[2048]{0:T(1024)}, u32[]{:S(2)}) copy-start(f32[2048]{0:T(1024)} %get-tuple-element.2123) | copy-start | bytes 24580 | tf_op jit(solution)/shard_map/while
  1559.3 186.2 %copy-start.31 = (f32[2048]{0:T(1024)S(1)}, f32[2048]{0:T(1024)}, u32[]{:S(2)}) copy-start(f32[2048]{0:T(1024)} %get-tuple-element.2120) | copy-start | bytes 24580 | tf_op jit(solution)/shard_map/while
  1559.3 186.2 %copy-start.34 = (f32[2048]{0:T(1024)S(1)}, f32[2048]{0:T(1024)}, u32[]{:S(2)}) copy-start(f32[2048]{0:T(1024)} %get-tuple-element.2121) | copy-start | bytes 24580 | tf_op jit(solution)/shard_map/while
  1559.4 329.5 %copy-start.13 = (bf16[1,256,2048]{2,1,0:T(8,128)(2,1)S(1)}, bf16[1,256,2048]{2,1,0:T(8,128)(2,1)}, u32[]{:S(2)}) copy-start(bf16[1,256,2048]{2,1,0:T(8,128)(2,1)} %get-tuple-element.1932) | copy-start | bytes 3145732 | tf_op jit(solution)/shard_map/while
  1559.4 329.5 %copy-start.49 = (f32[2048]{0:T(1024)S(1)}, f32[2048]{0:T(1024)}, u32[]{:S(2)}) copy-start(f32[2048]{0:T(1024)} %get-tuple-element.2181) | copy-start | bytes 24580 | tf_op jit(solution)/shard_map/while
  1559.4 329.4 %copy-start.50 = (f32[2048]{0:T(1024)S(1)}, f32[2048]{0:T(1024)}, u32[]{:S(2)}) copy-start(f32[2048]{0:T(1024)} %get-tuple-element.2182) | copy-start | bytes 24580 | tf_op jit(solution)/shard_map/while
  1745.5 148.2 %copy-start.38 = (f32[2048]{0:T(1024)}, f32[2048]{0:T(1024)S(1)}, u32[]{:S(2)}) copy-start(f32[2048]{0:T(1024)S(1)} %get-tuple-element.2162) | copy-start | bytes 24580 | tf_op jit(solution)/shard_map/while
  1745.5 148.2 %copy-start.41 = (f32[2048]{0:T(1024)}, f32[2048]{0:T(1024)S(1)}, u32[]{:S(2)}) copy-start(f32[2048]{0:T(1024)S(1)} %get-tuple-element.2163) | copy-start | bytes 24580 | tf_op jit(solution)/shard_map/while
  1745.6 148.1 %copy-start.32 = (f32[2048]{0:T(1024)}, f32[2048]{0:T(1024)S(1)}, u32[]{:S(2)}) copy-start(f32[2048]{0:T(1024)S(1)} %get-tuple-element.2160) | copy-start | bytes 24580 | tf_op jit(solution)/shard_map/while
  1745.6 148.1 %copy-start.35 = (f32[2048]{0:T(1024)}, f32[2048]{0:T(1024)S(1)}, u32[]{:S(2)}) copy-start(f32[2048]{0:T(1024)S(1)} %get-tuple-element.2161) | copy-start | bytes 24580 | tf_op jit(solution)/shard_map/while
  1900.2 157.4 %reduce-scatter.19.cloned.1.call-start = ((), (), s32[]{:S(2)}) async-start(), calls=%async_computation.15 | async-start | bytes 221184
  1901.8 157.2 %reduce-scatter.21.cloned.1.call-start = ((), (), s32[]{:S(2)}) async-start(), calls=%async_computation.16 | async-start | bytes 294912
  1903.5 172.0 %reduce-scatter.13.cloned.1.call-start = ((), (), s32[]{:S(2)}) async-start(), calls=%async_computation.12 | async-start | bytes 2359296 | tf_op jit(solution)/shard_map/reduce_scatter | solution.py:293
  1907.4 232.8 %all-reduce.17.cloned.1.call-start = ((), (), s32[]{:S(2)}) async-start(), calls=%async_computation.17 | async-start | bytes 12582912
  1929.4 285.5 %reduce-scatter.15.cloned.1.call-start = ((), (), s32[]{:S(2)}) async-start(), calls=%async_computation.13 | async-start | bytes 9437184 | tf_op jit(solution)/shard_map/reduce_scatter | solution.py:296
  1938.6 351.4 %reduce-scatter.17.cloned.1.call-start = ((), (), s32[]{:S(2)}) async-start(), calls=%async_computation.14 | async-start | bytes 9437184 | tf_op jit(solution)/shard_map/reduce_scatter | solution.py:302
  1952.8 31.4 %all-to-all-start.3 = ((bf16[2,1,256,2048]{3,0,1,2:T(2,128)(2,1)}), bf16[2,1,256,2048]{3,0,1,2:T(2,128)(2,1)S(1)}, u32[]{:S(2)}, u32[]{:S(2)}) async-start(bf16[2,1,256,2048]{3,0,1,2:T(2,128)(2,1)} %bitcast.325), calls=%async_computation.6 | async-start | bytes 4194304 | tf_op jit(solution)/shard_map/all_to_all | solution.py:309
  1956.5 33.5 %copy-start.33 = (f32[2048]{0:T(1024)S(1)}, f32[2048]{0:T(1024)}, u32[]{:S(2)}) copy-start(f32[2048]{0:T(1024)} %get-tuple-element.2266) | copy-start | bytes 24580
  1956.5 33.5 %copy-start.36 = (f32[2048]{0:T(1024)S(1)}, f32[2048]{0:T(1024)}, u32[]{:S(2)}) copy-start(f32[2048]{0:T(1024)} %get-tuple-element.2267) | copy-start | bytes 24580
  1984.2 82.0 %all-to-all-start.2 = ((bf16[2,1,256,2048]{3,0,1,2:T(2,128)(2,1)}), bf16[2,1,256,2048]{3,0,1,2:T(2,128)(2,1)}, u32[]{:S(2)}, u32[]{:S(2)}) async-start(bf16[2,1,256,2048]{3,0,1,2:T(2,128)(2,1)} %bitcast.324), calls=%async_computation.5 | async-start | bytes 4194304 | tf_op jit(solution)/shard_map/all_to_all | solution.py:308
  2075.4 217.2 %copy-start.1 = (bf16[2,8,32,2048]{3,2,1,0:T(8,128)(2,1)S(1)}, bf16[2,8,32,2048]{3,2,1,0:T(8,128)(2,1)}, u32[]{:S(2)}) copy-start(bf16[2,8,32,2048]{3,2,1,0:T(8,128)(2,1)} %param.24) | copy-start | bytes 6291460
  (106 other events, 1012.0 us)
Sparse Core Ops, SparseCore 0:
  130.6 26.9 all-gather.23
  159.1 80.7 all-gather.25
  241.5 79.2 all-gather.21
  322.5 45.1 all-gather.19
  369.7 80.7 all-gather.27
  452.3 52.9 all-gather.29
  507.1 55.9 all-gather.31
  565.5 144.4 reduce-scatter.24
  712.3 145.1 reduce-scatter.22
  859.8 145.1 reduce-scatter.26
  1013.1 28.6 all-gather.23
  1043.2 80.7 all-gather.25
  1125.6 79.2 all-gather.21
  1206.7 45.1 all-gather.19
  1253.9 80.7 all-gather.27
  1336.4 52.9 all-gather.29
  1391.1 55.9 all-gather.31
  1449.3 144.4 reduce-scatter.24
  1596.2 145.1 reduce-scatter.22
  1743.6 145.1 reduce-scatter.26
Sparse Core Ops, SparseCore 1:
  1904.2 34.2 reduce-scatter.18
  1942.3 34.7 reduce-scatter.20
  1980.2 51.9 reduce-scatter.12
  2035.8 104.3 all-reduce.16
  2143.6 71.2 reduce-scatter.14
  2218.8 71.1 reduce-scatter.16
where the time goes:
time: 2310 us; the launch traced here: 2300 us
  waiting for transfers between devices  1340 us (58%)
  matrix products  387 us (17%)
  local copies, waits for them, and re-layouts  238 us (10%)
  blocking collectives  159 us (7%)
  other arithmetic  111 us (5%)
  loops' own time  25.3 us (1%)
    reduce_scatter x2, waiting for transfers between devices, micro_step(): lax.psum_scatter(grad_second, 'tensor', scatter_dimension=0, tiled=True)  295 us
    reduce_scatter x2, waiting for transfers between devices, micro_step(): lax.psum_scatter(attn_part + ffn_part, 'tensor', scatter_dimension=0, til...  286 us
    all_gather x2, waiting for transfers between devices, micro_step(): grad_full = lax.all_gather(rows_grad, 'tensor', axis=0, tiled=True)  165 us
    all_gather x2, waiting for transfers between devices, micro_step(): lax.all_gather(normed_one.astype(jnp.bfloat16), 'tensor', axis=0, tiled=T...  149 us
    unnamed x2, blocking collectives  123 us
    all_gather x2, waiting for transfers between devices, current_set(): lax.all_gather(shard_set[0], 'dp', axis=0, tiled=True)  93.9 us
    dynamic_update_slice x8, local copies, waits for them, and re-layouts, micro_step(): lax.scan(back_block, (zero_heads, zero_heads), (starts, lse_blocks))  92.7 us
    reduce_scatter x2, waiting for transfers between devices, micro_step(): lax.psum_scatter(grad_first, 'tensor', scatter_dimension=0, tiled=True)  79.3 us
  transfers between devices with their start and end apart: 30, of which 19 were waited for; matrix products, arithmetic and copies ran while one was open for 30% of the time, Pallas kernels for 0%

commit v1 on v0

v1 whole, which is shorter than its diff:
```python
import functools
import math

import jax
import jax.numpy as jnp
from jax import lax
from jax.experimental import pallas as pl
from jax.experimental.pallas import tpu as pltpu
from jax.sharding import PartitionSpec as P

HD = 256
ROT = 64
EPSILON = 1e-05
ROPE_BASE = 10000.0
NEG_FILL = -1e30
SQRT_HALF = 0.7071067811865476
INV_ROOT_TWO_PI = 0.3989422804014327
BF = jnp.bfloat16
F32 = jnp.float32
FAR = 1 << 20


def line_gather(x, axis, n):
    left, right = [None], [None]
    cur = x
    for s in range(1, n):
        cur = lax.ppermute(cur, axis, [(k, k + 1) for k in range(s - 1, n - 1)])
        left.append(cur)
    cur = x
    for s in range(1, n):
        cur = lax.ppermute(cur, axis, [(k, k - 1) for k in range(1, n - s + 1)])
        right.append(cur)
    return [x] + [left[s] + right[n - s] for s in range(1, n)]


def line_scatter(parts, axis, n):
    got_right = got_left = None
    for s in range(n - 1, 0, -1):
        val = parts[n - s] if got_right is None else parts[n - s] + got_right.astype(F32)
        got_right = lax.ppermute(val.astype(BF), axis, [(k, k + 1) for k in range(n - s)])
        val = parts[s] if got_left is None else parts[s] + got_left.astype(F32)
        got_left = lax.ppermute(val.astype(BF), axis, [(k, k - 1) for k in range(s, n)])
    return parts[0] + got_right.astype(F32) + got_left.astype(F32)


def small_gather(x, axis, n):
    me = lax.axis_index(axis)
    out = x[None]
    bit = 1
    while bit < n:
        other = lax.ppermute(out, axis, [(i, i ^ bit) for i in range(n)])
        mine_high = (me & bit) != 0
        out = jnp.concatenate(
            [jnp.where(mine_high, other, out), jnp.where(mine_high, out, other)], axis=0
        )
        bit *= 2
    return out


def small_scatter(x, axis, n):
    me = lax.axis_index(axis)
    bit = n // 2
    while bit:
        low, high = x[:bit], x[bit:]
        mine_high = (me & bit) != 0
        sent = jnp.where(mine_high, low, high)
        kept = jnp.where(mine_high, high, low)
        x = kept + lax.ppermute(sent, axis, [(i, i ^ bit) for i in range(n)])
        bit //= 2
    return x[0]


def rotated(x, cosines, sines):
    lanes = lax.broadcasted_iota(jnp.int32, x.shape, 1)
    partner = jnp.where(lanes < ROT // 2, pltpu.roll(x, 128 - ROT // 2, 1), pltpu.roll(x, ROT // 2, 1))
    return x * cosines + partner * sines


def scores_of(q, k, posq, posk):
    s = lax.dot_general(q, k, (((1,), (1,)), ((), ())), preferred_element_type=F32)
    return jnp.where(posk <= posq, s * (1.0 / math.sqrt(HD)), NEG_FILL)


def attend_kernel(n_blocks, posq_ref, posk_ref, cos_ref, sin_ref, qkv_ref, low_ref, mixed_ref):
    n_slots, rows, _ = qkv_ref.shape
    span = rows // n_blocks
    for t in range(n_slots):
        for base in (0, HD):
            lead = rotated(qkv_ref[t, :, base : base + 128], cos_ref[t], sin_ref[t])
            low_ref[t, :, base : base + 128] = lead.astype(BF)
            low_ref[t, :, base + 128 : base + HD] = qkv_ref[t, :, base + 128 : base + HD].astype(BF)
        low_ref[t, :, 2 * HD :] = qkv_ref[t, :, 2 * HD :].astype(BF)
    for b in range(n_blocks):
        own, seen = pl.ds(b * span, span), span * (b + 1)
        n_q, n_k = n_slots * span, n_slots * seen
        q = low_ref[:, own, :HD].reshape(n_q, HD)
        k = low_ref[:, :seen, HD : 2 * HD].reshape(n_k, HD)
        v = low_ref[:, :seen, 2 * HD :].reshape(n_k, HD)
        posq = posq_ref[:, own, :].reshape(n_q, 1)
        s = scores_of(q, k, posq, posk_ref[b, :, :n_k])
        e = jnp.exp(s - jnp.max(s, axis=-1, keepdims=True))
        p = e * (1.0 / jnp.sum(e, axis=-1, keepdims=True))
        mixed = jnp.dot(p.astype(BF), v, preferred_element_type=F32)
        mixed_ref[:, own, :] = mixed.astype(BF).reshape(n_slots, span, HD)


def attend_back_kernel(
    n_blocks, posq_ref, posk_ref, cos_ref, sin_ref, low_ref, dmix_ref, grad_ref, dk_ref, dv_ref
):
    n_slots, rows, _ = low_ref.shape
    span = rows // n_blocks
    scale = 1.0 / math.sqrt(HD)
    for b in reversed(range(n_blocks)):
        own, seen = pl.ds(b * span, span), span * (b + 1)
        n_q, n_k = n_slots * span, n_slots * seen
        q = low_ref[:, own, :HD].reshape(n_q, HD)
        k = low_ref[:, :seen, HD : 2 * HD].reshape(n_k, HD)
        v = low_ref[:, :seen, 2 * HD :].reshape(n_k, HD)
        dmix = dmix_ref[:, own, :].reshape(n_q, HD)
        posq = posq_ref[:, own, :].reshape(n_q, 1)
        s = scores_of(q, k, posq, posk_ref[b, :, :n_k])
        e = jnp.exp(s - jnp.max(s, axis=-1, keepdims=True))
        p = e * (1.0 / jnp.sum(e, axis=-1, keepdims=True))
        dp = lax.dot_general(dmix, v, (((1,), (1,)), ((), ())), preferred_element_type=F32)
        ds = (p * (dp - jnp.sum(p * dp, axis=-1, keepdims=True))).astype(BF)
        dq = jnp.dot(ds, k, preferred_element_type=F32) * scale
        dk = lax.dot_general(ds, q, (((0,), (0,)), ((), ())), preferred_element_type=F32)
        dv = lax.dot_general(p.astype(BF), dmix, (((0,), (0,)), ((), ())), preferred_element_type=F32)
        dk, dv = dk.reshape(n_slots, seen, HD), dv.reshape(n_slots, seen, HD)
        if b == n_blocks - 1:
            dk_ref[...] = dk
            dv_ref[...] = dv
        else:
            dk_ref[:, :seen, :] += dk
            dv_ref[:, :seen, :] += dv
        dq = dq.reshape(n_slots, span, HD)
        for t in range(n_slots):
            lead = rotated(dq[t, :, :128], cos_ref[t, own, :], -sin_ref[t, own, :])
            grad_ref[t, own, :128] = lead.astype(BF)
            grad_ref[t, own, 128:HD] = dq[t, :, 128:].astype(BF)
    for t in range(n_slots):
        lead = rotated(dk_ref[t, :, :128] * scale, cos_ref[t], -sin_ref[t])
        grad_ref[t, :, HD : HD + 128] = lead.astype(BF)
        grad_ref[t, :, HD + 128 : 2 * HD] = (dk_ref[t, :, 128:] * scale).astype(BF)
        grad_ref[t, :, 2 * HD :] = dv_ref[t].astype(BF)


def whole_spec(shape):
    return pl.BlockSpec(shape, lambda h: (0,) * len(shape))


def head_spec(n_slots, rows, width):
    return pl.BlockSpec((n_slots, rows, width), lambda h: (0, 0, h))


def attend(tables, qkv):
    posq, posk, cosines, sines = tables
    n_slots, rows, width = qkv.shape
    heads = width // (3 * HD)
    pairs = (n_slots * rows) ** 2 // 2 * heads
    return pl.pallas_call(
        functools.partial(attend_kernel, posk.shape[0]),
        grid=(heads,),
        in_specs=[whole_spec(t.shape) for t in tables] + [head_spec(n_slots, rows, 3 * HD)],
        out_specs=[head_spec(n_slots, rows, 3 * HD), head_spec(n_slots, rows, HD)],
        out_shape=[
            jax.ShapeDtypeStruct(qkv.shape, BF),
            jax.ShapeDtypeStruct((n_slots, rows, heads * HD), BF),
        ],
        cost_estimate=pl.CostEstimate(
            flops=4 * pairs * HD, bytes_accessed=qkv.size * 8, transcendentals=pairs
        ),
        compiler_params=pltpu.CompilerParams(vmem_limit_bytes=48 << 20),
        name="attend",
    )(posq, posk, cosines, sines, qkv)


def attend_back(tables, low, dmix):
    n_slots, rows, width = low.shape
    heads = width // (3 * HD)
    pairs = (n_slots * rows) ** 2 // 2 * heads
    return pl.pallas_call(
        functools.partial(attend_back_kernel, tables[1].shape[0]),
        grid=(heads,),
        in_specs=[whole_spec(t.shape) for t in tables]
        + [head_spec(n_slots, rows, 3 * HD), head_spec(n_slots, rows, HD)],
        out_specs=head_spec(n_slots, rows, 3 * HD),
        out_shape=jax.ShapeDtypeStruct(low.shape, BF),
        scratch_shapes=[pltpu.VMEM((n_slots, rows, HD), F32)] * 2,
        cost_estimate=pl.CostEstimate(
            flops=10 * pairs * HD, bytes_accessed=low.size * 5, transcendentals=pairs
        ),
        compiler_params=pltpu.CompilerParams(vmem_limit_bytes=48 << 20),
        name="attend_back",
    )(*tables, low, dmix)


def unit_of(rows):
    centred = rows - jnp.mean(rows, axis=-1, keepdims=True)
    scaling = lax.rsqrt(jnp.mean(centred * centred, axis=-1, keepdims=True) + EPSILON)
    return centred * scaling, scaling


def dot(a, b, dims, out=F32):
    return lax.dot_general(a, b, (dims, ((), ())), preferred_element_type=F32).astype(out)


def per_device(
    hidden_in,
    lengths,
    dealing,
    cotangent,
    attn_gain,
    attn_shift,
    ffn_gain,
    ffn_shift,
    qkv_weight,
    qkv_bias,
    dense_weight,
    dense_bias,
    fc1_weight,
    fc1_bias,
    fc2_weight,
    fc2_bias,
):
    n_t, n_d = lax.axis_size("tensor"), lax.axis_size("dp")
    my_t, my_d = lax.axis_index("tensor"), lax.axis_index("dp")
    micros, seqs, piece, width = hidden_in.shape
    heads = qkv_weight.shape[1]
    units = fc1_weight.shape[1]
    rows = n_d * piece
    n_blocks = 4

    def deal(x):
        return lax.all_to_all(x, "dp", split_axis=0, concat_axis=0, tiled=True).reshape(rows, width)

    def undeal(x):
        return lax.all_to_all(
            x.reshape(seqs, piece, width), "dp", split_axis=0, concat_axis=0, tiled=True
        )

    own_x = [deal(hidden_in[m]) for m in range(micros)]
    own_g = [deal(cotangent[m]) for m in range(micros)]

    eighth = width // (n_d * n_t)
    packed = jnp.concatenate(
        [attn_gain, attn_shift, ffn_gain, ffn_shift, dense_bias, fc2_bias]
        + [qkv_bias.reshape(-1), fc1_bias.reshape(-1)]
    )
    packed = small_gather(packed, "dp", n_d)
    vectors = small_gather(packed[:, : 6 * eighth], "tensor", n_t)
    vectors = vectors.reshape(n_t, n_d, 6, eighth).transpose(2, 1, 0, 3).reshape(6, width)
    vectors = vectors.astype(F32)
    gain_one, shift_one, gain_two, shift_two = vectors[0], vectors[1], vectors[2], vectors[3]
    out_shift = vectors[4] + vectors[5]
    rest = packed[:, 6 * eighth :].astype(F32)
    n_qb = qkv_bias.size
    qkv_shift = rest[:, :n_qb].reshape(n_d, heads, -1).transpose(1, 0, 2).reshape(-1)
    fc1_shift = rest[:, n_qb:].reshape(n_d, heads, -1).transpose(1, 0, 2).reshape(-1)

    w_qkv = lax.all_gather(qkv_weight.reshape(-1, heads * 3 * HD), "dp", axis=0, tiled=True)
    w_fc1 = lax.all_gather(fc1_weight, "dp", axis=0, tiled=True)
    w_dense = lax.all_gather(dense_weight, "dp", axis=1, tiled=True).reshape(heads * HD, width)
    w_fc2 = lax.all_gather(fc2_weight, "dp", axis=1, tiled=True)

    slots = jnp.arange(n_t, dtype=jnp.int32)
    part = (my_t - slots) % n_t
    local = jnp.arange(rows, dtype=jnp.int32)
    positions = ((local // piece) * n_t + part[:, None]) * piece + local % piece
    freqs = jnp.exp(
        jnp.arange(ROT // 2, dtype=F32) * (-2.0 * math.log(ROPE_BASE) / ROT)
    )
    phases = positions.astype(F32)[..., None] * freqs
    flat = jnp.zeros((n_t, rows, 128 - ROT), F32)
    cosines = jnp.concatenate([jnp.cos(phases), jnp.cos(phases), flat + 1.0], axis=-1)
    sines = jnp.concatenate([-jnp.sin(phases), jnp.sin(phases), flat], axis=-1)
    picked = dealing == my_d
    seq_lens = jnp.sum(jnp.where(picked, lengths, 0), axis=1)
    posq = positions[..., None]

    def tables(m):
        keyed = jnp.where(positions < seq_lens[m], positions, FAR)
        span = rows // n_blocks
        lists = []
        for b in range(n_blocks):
            seen = keyed[:, : span * (b + 1)].reshape(1, -1)
            lists.append(jnp.pad(seen, ((0, 0), (0, n_t * rows - seen.shape[1]))))
        return (posq, jnp.stack(lists), cosines, sines)

    all_tables = [tables(m) for m in range(micros)]
    sum_g = jnp.sum(cotangent.astype(F32), axis=(0, 1, 2))

    def gather_rows(x):
        return jnp.concatenate(line_gather(x, "tensor", n_t), axis=0)

    def scatter_rows(x):
        return line_scatter(list(x.reshape(n_t, rows, width)), "tensor", n_t)

    saved = []
    outputs = []
    for m in range(micros):
        x = gather_rows(own_x[m])
        unit, _ = unit_of(x.astype(F32))
        normed_one = (unit * gain_one + shift_one).astype(BF)
        normed_two = (unit * gain_two + shift_two).astype(BF)
        qkv = dot(normed_one, w_qkv, ((1,), (0,))) + qkv_shift
        low, mixed = attend(all_tables[m], qkv.reshape(n_t, rows, -1))
        mixed = mixed.reshape(n_t * rows, -1)
        preact = dot(normed_two, w_fc1, ((1,), (0,))) + fc1_shift
        cdf = 0.5 * (1.0 + lax.erf(preact * SQRT_HALF))
        act = (preact * cdf).astype(BF)
        slope = (cdf + preact * jnp.exp(-0.5 * preact * preact) * INV_ROOT_TWO_PI).astype(BF)
        branch = dot(mixed, w_dense, ((1,), (0,))) + dot(act, w_fc2, ((1,), (0,)))
        total = scatter_rows(branch)
        out = (own_x[m].astype(F32) + total + out_shift).astype(BF)
        outputs.append(undeal(out))
        saved.append((x, normed_one, normed_two, low, mixed, act, slope))

    backs = []
    for m in range(micros):
        x, normed_one, normed_two, low, mixed, act, slope = saved[m]
        g = gather_rows(own_g[m])
        d_mixed = dot(g, w_dense, ((1,), (1,)), BF)
        d_act = dot(g, w_fc2, ((1,), (1,)))
        d_pre = (d_act * slope.astype(F32)).astype(BF)
        d_qkv = attend_back(all_tables[m], low, d_mixed.reshape(n_t, rows, -1))
        d_qkv = d_qkv.reshape(n_t * rows, -1)
        backs.append((g, d_pre, d_qkv))

    def both(fn):
        total = fn(0)
        for m in range(1, micros):
            total = total + fn(m)
        return total

    rows_dim = ((0,), (0,))
    grad_fc2 = both(lambda m: dot(backs[m][0], saved[m][5], rows_dim)).astype(BF)
    grad_fc2 = lax.psum_scatter(grad_fc2, "dp", scatter_dimension=0, tiled=True)
    grad_fc2 = grad_fc2.astype(F32).T
    grad_dense = both(lambda m: dot(saved[m][4], backs[m][0], rows_dim)).astype(BF)
    grad_dense = lax.psum_scatter(
        grad_dense.reshape(heads, HD, width), "dp", scatter_dimension=1, tiled=True
    ).astype(F32)
    grad_fc1 = both(lambda m: dot(saved[m][2], backs[m][1], rows_dim)).astype(BF)
    grad_fc1 = lax.psum_scatter(grad_fc1, "dp", scatter_dimension=0, tiled=True).astype(F32)
    grad_qkv = both(lambda m: dot(saved[m][1], backs[m][2], rows_dim)).astype(BF)
    grad_qkv = lax.psum_scatter(grad_qkv, "dp", scatter_dimension=0, tiled=True)
    grad_qkv = grad_qkv.astype(F32).reshape(-1, heads, 3 * HD)

    grads_in = []
    norm_sums = []
    for m in range(micros):
        x = saved[m][0]
        g, d_pre, d_qkv = backs[m]
        d_one = dot(d_qkv, w_qkv, ((1,), (1,)))
        d_two = dot(d_pre, w_fc1, ((1,), (1,)))
        unit, _ = unit_of(x.astype(F32))
        norm_sums.append(
            jnp.stack(
                [
                    jnp.sum(d_one * unit, axis=0),
                    jnp.sum(d_one, axis=0),
                    jnp.sum(d_two * unit, axis=0),
                    jnp.sum(d_two, axis=0),
                ]
            )
        )
        total = scatter_rows(d_one * gain_one + d_two * gain_two)
        unit, scaling = unit_of(own_x[m].astype(F32))
        back = scaling * (
            total
            - jnp.mean(total, axis=-1, keepdims=True)
            - unit * jnp.mean(total * unit, axis=-1, keepdims=True)
        )
        grads_in.append(undeal((own_g[m].astype(F32) + back).astype(BF)))

    sums = jnp.concatenate([sum(norm_sums), sum_g[None]], axis=0)
    sums = sums.reshape(5, n_d, n_t, eighth).transpose(1, 2, 0, 3).reshape(n_d, -1)
    qkvb = both(lambda m: jnp.sum(backs[m][2].astype(F32), axis=0))
    fc1b = both(lambda m: jnp.sum(backs[m][1].astype(F32), axis=0))
    qkvb = qkvb.reshape(heads, n_d, -1).transpose(1, 0, 2).reshape(n_d, -1)
    fc1b = fc1b.reshape(heads, n_d, -1).transpose(1, 0, 2).reshape(n_d, -1)
    small = small_scatter(jnp.concatenate([sums, qkvb, fc1b], axis=1), "dp", n_d)
    n_sum = 5 * n_t * eighth
    mine = small_scatter(small[:n_sum].reshape(n_t, 5 * eighth), "tensor", n_t).reshape(5, eighth)
    qkvb = small[n_sum : n_sum + n_qb].reshape(heads, -1)
    fc1b = small[n_sum + n_qb :].reshape(heads, -1)

    return (
        jnp.stack(outputs),
        jnp.stack(grads_in),
        mine[0],
        mine[1],
        mine[2],
        mine[3],
        grad_qkv,
        qkvb,
        grad_dense,
        mine[4],
        grad_fc1,
        fc1b,
        grad_fc2,
        mine[4],
    )


def solution(mesh):
    rows = P(None, None, ("dp", "tensor"), None)
    vector = P(("dp", "tensor"))
    return jax.shard_map(
        per_device,
        mesh=mesh,
        in_specs=(
            rows,
            P(),
            P(),
            rows,
            vector,
            vector,
            vector,
            vector,
            P("dp", "tensor", None),
            P("tensor", "dp"),
            P("tensor", "dp", None),
            vector,
            P("dp", "tensor"),
            P("tensor", "dp"),
            P("tensor", "dp"),
            vector,
        ),
        out_specs=(
            rows,
            rows,
            vector,
            vector,
            vector,
            vector,
            P("dp", "tensor", None),
            P("tensor", "dp"),
            P("tensor", "dp", None),
            vector,
            P("dp", "tensor"),
            P("tensor", "dp"),
            P("tensor", "dp"),
            vector,
        ),
        check_vma=False,
    )
```

time: 2310 us -> 1120 us (0.48)
  waiting for transfers between devices: 1340 us -> 351 us
  starting transfers between devices: 18.6 us -> 222 us
  local copies, waits for them, and re-layouts: 238 us -> 38.9 us
  blocking collectives: 159 us -> 23.1 us
  matrix products: 387 us -> 305 us
  Pallas kernels: 0 us -> 34.8 us
  loops' own time: 25.3 us -> 0 us
    reduce_scatter x9 -> x4, waiting for transfers between devices: 805 us -> 0.01 us  [the longest x1 0.01 us: per_device(): grad_qkv = lax.psum_scatter(grad_qkv, 'dp', scatter_dimension=0, tiled=True)]
    all_gather x14 -> x4, waiting for transfers between devices: 425 us -> 0.08 us  [the longest x1 0.02 us: per_device(): lax.all_gather(dense_weight, 'dp', axis=1, tiled=True)]
    ppermute x0 -> x58, waiting for transfers between devices: none -> 337 us  [the longest x12 151 us: line_gather(): cur = lax.ppermute(cur, axis, [(k, k - 1) for k in range(1, n - s + 1)])]
    ppermute x0 -> x58, starting transfers between devices: none -> 194 us  [the longest x12 83 us: line_scatter(): lax.ppermute(val.astype(BF), axis, [(k, k + 1) for k in range(n - s)])]
    unnamed x2 -> x0, blocking collectives: 123 us -> none
    dynamic_update_slice x8 -> x0, local copies, waits for them, and re-layouts: 92.7 us -> none  [micro_step(): lax.scan(back_block, (zero_heads, zero_heads), (starts, lse_blocks))]
    dot_general x52 -> x24, matrix products: 387 us -> 305 us  [dot(): lax.dot_general(a, b, (dims, ((), ())), preferred_element_type=F32)]
    unnamed x9 -> x8, waiting for transfers between devices: 62.8 us -> 1.46 us
  transfers between devices with their start and end apart: 30 -> 73, of which waited for: 19 -> 26; matrix products, arithmetic and copies ran while one was open for 30% -> 40% of each run, Pallas kernels for 0% -> 3%
where the time goes in v1:
time: 1120 us; the launch traced here: 1100 us
  waiting for transfers between devices  351 us (31%)
  matrix products  305 us (27%)
  starting transfers between devices  222 us (20%)
  other arithmetic  106 us (9%)
  local copies, waits for them, and re-layouts  38.9 us (3%)
  Pallas kernels  34.8 us (3%)
  blocking collectives  23.1 us (2%)
  between operations  16.6 us (1%)
    dot_general x24, matrix products, dot(): lax.dot_general(a, b, (dims, ((), ())), preferred_element_type=F32)  305 us
    ppermute x12, waiting for transfers between devices, line_gather(): cur = lax.ppermute(cur, axis, [(k, k - 1) for k in range(1, n - s + 1)])  151 us
    ppermute x12, waiting for transfers between devices, line_scatter(): lax.ppermute(val.astype(BF), axis, [(k, k + 1) for k in range(n - s)])  104 us
    ppermute x12, starting transfers between devices, line_scatter(): lax.ppermute(val.astype(BF), axis, [(k, k + 1) for k in range(n - s)])  83 us
    ppermute x5, waiting for transfers between devices, small_gather(): other = lax.ppermute(out, axis, [(i, i ^ bit) for i in range(n)])  48.4 us
    ppermute x12, starting transfers between devices, line_gather(): cur = lax.ppermute(cur, axis, [(k, k + 1) for k in range(s - 1, n - 1)])  36.4 us
    ppermute x5, starting transfers between devices, small_scatter(): x = kept + lax.ppermute(sent, axis, [(i, i ^ bit) for i in range(n)])  34.8 us
    add x12, other arithmetic, line_gather(): return [x] + [left[s] + right[n - s] for s in range(1, n)]  31.8 us
  transfers between devices with their start and end apart: 73, of which 26 were waited for; matrix products, arithmetic and copies ran while one was open for 40% of the time, Pallas kernels for 3%

profile of v1, /device:TPU:0, one launch (start us, length us, event | category | flops | bytes accessed | tf_op | source)
XLA Modules:
  0.0 1098.2 jit_solution(1490000266136089919)
XLA Ops:
  13.7 23.1 %all_to_all.40 = bf16[8,32,2048]{2,1,0:T(8,128)(2,1)S(1)} all-to-all(bf16[8,32,2048]{2,1,0:T(8,128)(2,1)S(1)} %get-tuple-element.103), channel_id=1, replica_groups=mesh['dp'=8,'tensor'=4] {'dp'}, dimensions={0} | all-to-all | bytes 2097152 | tf_op jit(solution)/shard_map/all_to_all | solution.py:235
  45.0 12.0 %all-to-all-done = bf16[8,32,2048]{2,1,0:T(8,128)(2,1)S(1)} async-done(((bf16[8,32,2048]{2,1,0:T(8,128)(2,1)}), bf16[8,32,2048]{2,1,0:T(8,128)(2,1)S(1)}, u32[]{:S(2)}, u32[]{:S(2)}) %all-to-all-start) | async-done | bytes 1048608 | tf_op jit(solution)/shard_map/all_to_all | solution.py:235
  64.6 17.6 %collective-permute-done.7 = bf16[2,832]{1,0:T(2,128)(2,1)S(1)} collective-permute-done((bf16[2,832]{1,0:T(2,128)(2,1)S(1)}, bf16[2,832]{1,0:T(2,128)(2,1)S(1)}, u32[]{:S(2)}, u32[]{:S(2)}) %collective-permute-start.7) | collective-permute-done | bytes 3360 | tf_op jit(solution)/shard_map/ppermute | solution.py:51
  85.1 5.5 collective-permute-start.17
  92.0 5.6 collective-permute-start
  97.5 4.3 all-to-all-start.4
  104.1 30.2 %collective-permute-done.9 = bf16[1,8,384]{2,1,0:T(8,128)(2,1)S(1)} collective-permute-done((bf16[1,8,384]{2,1,0:T(8,128)(2,1)S(1)}, bf16[1,8,384]{2,1,0:T(8,128)(2,1)S(1)}, u32[]{:S(2)}, u32[]{:S(2)}) %collective-permute-start.9) | collective-permute-done | bytes 6176 | tf_op jit(solution)/shard_map/ppermute | solution.py:51
  140.7 6.1 collective-permute-start.41
  148.1 5.5 collective-permute-start.29
  158.2 10.0 collective-permute-done.42
  171.2 19.5 %collective-permute-done.30 = bf16[256,2048]{1,0:T(8,128)(2,1)} collective-permute-done((bf16[256,2048]{1,0:T(8,128)(2,1)}, bf16[256,2048]{1,0:T(8,128)(2,1)}, u32[]{:S(2)}, u32[]{:S(2)}) %collective-permute-start.30) | collective-permute-done | bytes 1048608 | tf_op jit(solution)/shard_map/ppermute | solution.py:31
  193.7 19.5 %collective-permute-done.19 = bf16[256,2048]{1,0:T(8,128)(2,1)} collective-permute-done((bf16[256,2048]{1,0:T(8,128)(2,1)}, bf16[256,2048]{1,0:T(8,128)(2,1)}, u32[]{:S(2)}, u32[]{:S(2)}) %collective-permute-start.19) | collective-permute-done | bytes 1048608 | tf_op jit(solution)/shard_map/ppermute | solution.py:31
  216.7 18.9 %collective-permute-done.2 = bf16[256,2048]{1,0:T(8,128)(2,1)} collective-permute-done((bf16[256,2048]{1,0:T(8,128)(2,1)}, bf16[256,2048]{1,0:T(8,128)(2,1)}, u32[]{:S(2)}, u32[]{:S(2)}) %collective-permute-start.2) | collective-permute-done | bytes 1048608 | tf_op jit(solution)/shard_map/ppermute | solution.py:31
  238.7 19.5 %collective-permute-done.43 = bf16[256,2048]{1,0:T(8,128)(2,1)} collective-permute-done((bf16[256,2048]{1,0:T(8,128)(2,1)}, bf16[256,2048]{1,0:T(8,128)(2,1)}, u32[]{:S(2)}, u32[]{:S(2)}) %collective-permute-start.43) | collective-permute-done | bytes 1048608 | tf_op jit(solution)/shard_map/ppermute | solution.py:31
  264.6 16.0 %collective-permute-done.31 = bf16[256,2048]{1,0:T(8,128)(2,1)} collective-permute-done((bf16[256,2048]{1,0:T(8,128)(2,1)}, bf16[256,2048]{1,0:T(8,128)(2,1)}, u32[]{:S(2)}, u32[]{:S(2)}) %collective-permute-start.31) | collective-permute-done | bytes 1048608 | tf_op jit(solution)/shard_map/ppermute | solution.py:31
  283.6 19.5 %collective-permute-done.20 = bf16[256,2048]{1,0:T(8,128)(2,1)} collective-permute-done((bf16[256,2048]{1,0:T(8,128)(2,1)}, bf16[256,2048]{1,0:T(8,128)(2,1)}, u32[]{:S(2)}, u32[]{:S(2)}) %collective-permute-start.20) | collective-permute-done | bytes 1048608 | tf_op jit(solution)/shard_map/ppermute | solution.py:31
  306.0 19.5 %collective-permute-done.3 = bf16[256,2048]{1,0:T(8,128)(2,1)} collective-permute-done((bf16[256,2048]{1,0:T(8,128)(2,1)}, bf16[256,2048]{1,0:T(8,128)(2,1)}, u32[]{:S(2)}, u32[]{:S(2)}) %collective-permute-start.3) | collective-permute-done | bytes 1048608 | tf_op jit(solution)/shard_map/ppermute | solution.py:31
  358.8 8.7 collective-permute-done.32
  382.4 6.1 convolution_convert_fusion.1
  392.2 14.5 %convolution_add_fusion.1 = f32[1024,1536]{1,0:T(8,128)} fusion(bf16[2048,1536]{1,0:T(8,128)(2,1)} %all-gather.5.cloned.1.call-done, f32[1536]{0:T(1024)S(1)} %add.458, f32[2048]{0:T(1024)S(1)} %add.455, f32[2048]{0:T(1024)S(1)} %mul.287, f32[1024]{0:T(1024)S(1)} %add_rsqrt_fusion.3, f32[1024]{0:T(1024)S(1)} %broadcast_multiply_fusion.3, ...), kind=kOutput, calls=%fused_computation.58 | convolution fusion | flops 6471286784 | bytes 16807936 | tf_op jit(solution)/shard_map/dot_general | solution.py:205
  406.7 7.8 attend.2
  414.6 16.3 %convolution_add_fusion = f32[1024,1536]{1,0:T(8,128)} fusion(bf16[2048,1536]{1,0:T(8,128)(2,1)} %all-gather.5.cloned.1.call-done, f32[1536]{0:T(1024)S(1)} %add.458, f32[1024]{0:T(1024)S(1)} %add_rsqrt_fusion.2, f32[1024]{0:T(1024)S(1)} %broadcast_multiply_fusion.2, f32[2048]{0:T(1024)S(1)} %add.455, f32[2048]{0:T(1024)S(1)} %mul.287, ...), kind=kOutput, calls=%fused_computation.57 | convolution fusion | flops 6471286784 | bytes 16807936 | tf_op jit(solution)/shard_map/dot_general | solution.py:205
  430.9 8.3 attend.3
  443.5 5.1 add_convert_fusion.3
  449.9 9.3 attend_back.2
  459.3 10.1 fusion.81
  469.4 9.3 attend_back.3
  480.6 12.6 %add_convert_fusion.2 = bf16[2048,1536]{1,0:T(8,128)(2,1)} fusion(f32[2048,1536]{1,0:T(8,128)} %fusion.81, bf16[1024,1536]{1,0:T(8,128)(2,1)S(1)} %bitcast.123, f32[1024]{0:T(1024)S(1)} %add_rsqrt_fusion.2, f32[1024]{0:T(1024)S(1)} %broadcast_multiply_fusion.2, f32[2048]{0:T(1024)S(1)} %add.455, f32[2048]{0:T(1024)S(1)} %mul.287, ...), kind=kOutput, calls=%fused_computation.2 | convolution fusion | flops 6476005376 | bytes 26238976 | tf_op jit(solution)/shard_map/dot_general | solution.py:205
  497.4 18.7 %fusion.86 = f32[1024,2048]{1,0:T(8,128)} fusion(bf16[2048,2048]{1,0:T(8,128)(2,1)} %all-gather.9.cloned.1.call-done, f32[1024]{0:T(1024)S(1)} %add_rsqrt_fusion.2, f32[1024]{0:T(1024)S(1)} %broadcast_multiply_fusion.2, f32[2048]{0:T(1024)S(1)} %add.461, f32[2048]{0:T(1024)S(1)} %mul.290, bf16[256,2048]{1,0:T(8,128)(2,1)} %copy-done.37, ...), kind=kOutput, calls=%fused_computation.234 | convolution fusion | flops 8617197568 | bytes 20996096 | tf_op jit(solution)/shard_map/dot_general | solution.py:205
  516.2 20.9 %multiply_convert_fusion.3 = (bf16[1024,2048]{1,0:T(8,128)(2,1)}, bf16[1024,2048]{1,0:T(8,128)(2,1)S(1)}, f32[1024,2048]{1,0:T(8,128)}) fusion(f32[2048]{0:T(1024)S(1)} %copy-done.78, f32[1024,2048]{1,0:T(8,128)} %fusion.86, bf16[2048,2048]{1,0:T(8,128)(2,1)S(1)} %copy-done.91, f32[2048]{0:T(1024)S(1)} %add.461, f32[2048]{0:T(1024)S(1)} %mul.290, ...), kind=kOutput, calls=%fused_computation.53 | convolution fusion | flops 8642363392 | bytes 37781504 | tf_op jit(solution)/shard_map/dot_general | solution.py:205
  537.2 15.3 %fusion.90 = f32[2048,2048]{1,0:T(8,128)} fusion(bf16[1024,2048]{1,0:T(8,128)(2,1)S(1)} %get-tuple-element.120, bf16[256,2048]{1,0:T(8,128)(2,1)S(1)} %copy-done.61, bf16[256,2048]{1,0:T(8,128)(2,1)S(1)} %copy-done.53, bf16[256,2048]{1,0:T(8,128)(2,1)S(1)} %copy-done.56, bf16[256,2048]{1,0:T(8,128)(2,1)} %bitcast.37), kind=kOutput, calls=%fused_computation.235 | convolution fusion | flops 8606711808 | bytes 25165824 | tf_op jit(solution)/shard_map/dot_general | solution.py:205
  552.4 16.4 %add_convert_fusion = bf16[2048,2048]{1,0:T(8,128)(2,1)} fusion(f32[2048,2048]{1,0:T(8,128)} %fusion.90, bf16[1024,2048]{1,0:T(8,128)(2,1)} %get-tuple-element.119, bf16[256,2048]{1,0:T(8,128)(2,1)} %add.501, bf16[256,2048]{1,0:T(8,128)(2,1)S(1)} %copy-done.49, bf16[256,2048]{1,0:T(8,128)(2,1)} %add.499, bf16[256,2048]{1,0:T(8,128)(2,1)} %bitcast.31), kind=kOutput, calls=%fused_computation | convolution fusion | flops 8615100416 | bytes 33554432 | tf_op jit(solution)/shard_map/dot_general | solution.py:205
  568.9 20.8 %convert_reduce_fusion.2 = (f32[2048]{0:T(1024)S(1)}, bf16[1024,2048]{1,0:T(8,128)(2,1)}) fusion(f32[1024,2048]{1,0:T(8,128)} %fusion.86, f32[2048]{0:T(1024)S(1)} %copy-done.78, bf16[2048,2048]{1,0:T(8,128)(2,1)} %all-gather.11.cloned.1.call-done, bf16[256,2048]{1,0:T(8,128)(2,1)} %add.514, bf16[256,2048]{1,0:T(8,128)(2,1)} %add.513, ...), kind=kOutput, calls=%fused_computation.45 | convolution fusion | flops 8638167040 | bytes 25182208 | tf_op jit(solution)/shard_map/dot_general | solution.py:205
  589.8 20.9 %convert_reduce_fusion.3 = (f32[2048]{0:T(1024)S(1)}, bf16[1024,2048]{1,0:T(8,128)(2,1)}) fusion(f32[1024,2048]{1,0:T(8,128)} %get-tuple-element.141, f32[2048]{0:T(1024)S(1)} %copy-done.78, bf16[2048,2048]{1,0:T(8,128)(2,1)} %all-gather.11.cloned.1.call-done, bf16[256,2048]{1,0:T(8,128)(2,1)S(1)} %copy-done.64, bf16[256,2048]{1,0:T(8,128)(2,1)S(1)} %copy-done.50, ...), kind=kOutput, calls=%fused_computation.46 | convolution fusion | flops 8638167040 | bytes 25182208 | tf_op jit(solution)/shard_map/dot_general | solution.py:205
  610.6 15.0 %fusion.99 = f32[1024,2048]{1,0:T(8,128)} fusion(bf16[1024,2048]{1,0:T(8,128)(2,1)} %get-tuple-element.143, bf16[2048,2048]{1,0:T(8,128)(2,1)} %all-gather.9.cloned.1.call-done), kind=kOutput, calls=%fused_computation.244 | convolution fusion | flops 8589934592 | bytes 20971520 | tf_op jit(solution)/shard_map/dot_general | solution.py:205
  625.7 14.0 %fusion.23 = (f32[2048]{0:T(1024)S(1)}, f32[2048]{0:T(1024)S(1)}, f32[2048]{0:T(1024)S(1)}, f32[2048]{0:T(1024)S(1)}, f32[1024,2048]{1,0:T(8,128)}) fusion(f32[1024]{0:T(1024)S(1)} %add_rsqrt_fusion.3, f32[1024]{0:T(1024)S(1)} %broadcast_multiply_fusion.3, bf16[256,2048]{1,0:T(8,128)(2,1)S(1)} %copy-done.45, bf16[256,2048]{1,0:T(8,128)(2,1)S(1)} %copy-done.23, ...), kind=kOutput, calls=%fused_computation.32 | convolution fusion | flops 6482288640 | bytes 30466048 | tf_op jit(solution)/shard_map/dot_general | solution.py:205
  639.7 14.7 %fusion.100 = f32[1024,2048]{1,0:T(8,128)} fusion(bf16[1024,2048]{1,0:T(8,128)(2,1)} %get-tuple-element.145, bf16[2048,2048]{1,0:T(8,128)(2,1)} %all-gather.9.cloned.1.call-done), kind=kOutput, calls=%fused_computation.245 | convolution fusion | flops 8589934592 | bytes 20971520 | tf_op jit(solution)/shard_map/dot_general | solution.py:205
  654.5 14.3 %fusion.16 = (f32[2048]{0:T(1024)S(1)}, f32[2048]{0:T(1024)S(1)}, f32[2048]{0:T(1024)S(1)}, f32[2048]{0:T(1024)S(1)}, f32[1024,2048]{1,0:T(8,128)}) fusion(f32[1024]{0:T(1024)S(1)} %copy-done.80, f32[1024]{0:T(1024)S(1)} %copy-done.71, bf16[256,2048]{1,0:T(8,128)(2,1)S(1)} %copy-done.40, bf16[256,2048]{1,0:T(8,128)(2,1)S(1)} %copy-done.27, ...), kind=kOutput, calls=%fused_computation.25 | convolution fusion | flops 6482288640 | bytes 30466048 | tf_op jit(solution)/shard_map/dot_general | solution.py:205
  669.9 12.6 %fusion.97 = f32[1024,2048]{1,0:T(8,128)S(1)} fusion(bf16[1024,2048]{1,0:T(8,128)(2,1)} %get-tuple-element.119, bf16[2048,2048]{1,0:T(8,128)(2,1)} %all-gather.11.cloned.1.call-done), kind=kOutput, calls=%fused_computation.242 | convolution fusion | flops 8589934592 | bytes 20971520 | tf_op jit(solution)/shard_map/dot_general | solution.py:205
  698.8 11.6 %fusion.98 = f32[1024,2048]{1,0:T(8,128)S(1)} fusion(bf16[1024,2048]{1,0:T(8,128)(2,1)S(1)} %copy-done.94, bf16[2048,2048]{1,0:T(8,128)(2,1)} %all-gather.11.cloned.1.call-done), kind=kOutput, calls=%fused_computation.243 | convolution fusion | flops 8589934592 | bytes 20971520 | tf_op jit(solution)/shard_map/dot_general | solution.py:205
  710.5 5.6 convolution_add_fusion.2
  716.1 12.7 %fusion.84 = f32[2048,2048]{1,0:T(8,128)} fusion(bf16[1024,2048]{1,0:T(8,128)(2,1)S(1)} %copy-done.95, f32[1024]{0:T(1024)S(1)} %copy-done.80, f32[1024]{0:T(1024)S(1)} %copy-done.71, f32[2048]{0:T(1024)S(1)} %copy-done.77, f32[2048]{0:T(1024)S(1)} %mul.290, bf16[256,2048]{1,0:T(8,128)(2,1)S(1)} %copy-done.41, bf16[256,2048]{1,0:T(8,128)(2,1)S(1)} %copy-done.28, ...), kind=kOutput, calls=%fused_computation.233 | convolution fusion | flops 8617197568 | bytes 25190400 | tf_op jit(solution)/shard_map/dot_general | solution.py:205
  728.8 17.0 %add_convert_fusion.1 = bf16[2048,2048]{1,0:T(8,128)(2,1)} fusion(f32[2048,2048]{1,0:T(8,128)} %fusion.84, bf16[1024,2048]{1,0:T(8,128)(2,1)} %get-tuple-element.143, f32[2048]{0:T(1024)S(1)} %copy-done.77, f32[2048]{0:T(1024)S(1)} %mul.290, f32[1024]{0:T(1024)S(1)} %add_rsqrt_fusion.3, f32[1024]{0:T(1024)S(1)} %broadcast_multiply_fusion.3, ...), kind=kOutput, calls=%fused_computation.1 | convolution fusion | flops 8625586176 | bytes 33579008 | tf_op jit(solution)/shard_map/dot_general | solution.py:205
  760.6 15.8 %collective-permute-done.23 = bf16[256,2048]{1,0:T(8,128)(2,1)S(1)} collective-permute-done((bf16[256,2048]{1,0:T(8,128)(2,1)S(1)}, bf16[256,2048]{1,0:T(8,128)(2,1)S(1)}, u32[]{:S(2)}, u32[]{:S(2)}) %collective-permute-start.23) | collective-permute-done | bytes 1048608 | tf_op jit(solution)/shard_map/ppermute | solution.py:40
  776.4 4.4 collective-permute-start.12
  781.2 17.7 %collective-permute-done.47 = bf16[256,2048]{1,0:T(8,128)(2,1)S(1)} collective-permute-done((bf16[256,2048]{1,0:T(8,128)(2,1)S(1)}, bf16[256,2048]{1,0:T(8,128)(2,1)S(1)}, u32[]{:S(2)}, u32[]{:S(2)}) %collective-permute-start.47) | collective-permute-done | bytes 1048608 | tf_op jit(solution)/shard_map/ppermute | solution.py:40
  798.8 5.4 collective-permute-start.36
  808.0 13.3 %collective-permute-done.12 = bf16[256,2048]{1,0:T(8,128)(2,1)S(1)} collective-permute-done((bf16[256,2048]{1,0:T(8,128)(2,1)S(1)}, bf16[256,2048]{1,0:T(8,128)(2,1)S(1)}, u32[]{:S(2)}, u32[]{:S(2)}) %collective-permute-start.12) | collective-permute-done | bytes 1048608 | tf_op jit(solution)/shard_map/ppermute | solution.py:40
  821.3 4.4 collective-permute-start.24
  830.8 12.9 %collective-permute-done.36 = bf16[256,2048]{1,0:T(8,128)(2,1)} collective-permute-done((bf16[256,2048]{1,0:T(8,128)(2,1)S(1)}, bf16[256,2048]{1,0:T(8,128)(2,1)}, u32[]{:S(2)}, u32[]{:S(2)}) %collective-permute-start.36) | collective-permute-done | bytes 1048608 | tf_op jit(solution)/shard_map/ppermute | solution.py:40
  843.8 5.4 collective-permute-start.48
  854.5 11.8 %collective-permute-done.24 = bf16[256,2048]{1,0:T(8,128)(2,1)S(1)} collective-permute-done((bf16[256,2048]{1,0:T(8,128)(2,1)S(1)}, bf16[256,2048]{1,0:T(8,128)(2,1)S(1)}, u32[]{:S(2)}, u32[]{:S(2)}) %collective-permute-start.24) | collective-permute-done | bytes 1048608 | tf_op jit(solution)/shard_map/ppermute | solution.py:40
  867.2 5.7 collective-permute-start.13
  878.1 10.6 collective-permute-done.48
  888.7 4.7 collective-permute-start.37
  907.0 21.6 %collective-permute-done.37 = bf16[256,2048]{1,0:T(8,128)(2,1)S(1)} collective-permute-done((bf16[256,2048]{1,0:T(8,128)(2,1)}, bf16[256,2048]{1,0:T(8,128)(2,1)S(1)}, u32[]{:S(2)}, u32[]{:S(2)}) %collective-permute-start.37) | collective-permute-done | bytes 1048608 | tf_op jit(solution)/shard_map/ppermute | solution.py:40
  928.6 24.0 %collective-permute-start.49 = (bf16[256,2048]{1,0:T(8,128)(2,1)}, bf16[256,2048]{1,0:T(8,128)(2,1)S(1)}, u32[]{:S(2)}, u32[]{:S(2)}) collective-permute-start(bf16[256,2048]{1,0:T(8,128)(2,1)} %get-tuple-element.88), channel_id=1, source_target_pairs={{0,1},{1,2},{2,3},{4,5},{5,6},{6,7},{8,9},{9,10},{10,11},{12,13},{... | collective-permute-start | bytes 3145736 | tf_op jit(solution)/shard_map/ppermute | solution.py:40
  954.8 20.8 %collective-permute-start.25 = (bf16[256,2048]{1,0:T(8,128)(2,1)}, bf16[256,2048]{1,0:T(8,128)(2,1)}, u32[]{:S(2)}, u32[]{:S(2)}) collective-permute-start(bf16[256,2048]{1,0:T(8,128)(2,1)} %get-tuple-element.96), channel_id=1, source_target_pairs={{0,1},{1,2},{2,3},{4,5},{5,6},{6,7},{8,9},{9,10},{10,11},{12,13},{... | collective-permute-start | bytes 3145736 | tf_op jit(solution)/shard_map/ppermute | solution.py:40
  984.7 9.6 collective-permute-done.52
  997.0 10.4 collective-permute-done.28
  1007.4 5.3 fusion.55
  1018.3 12.7 %collective-permute-done.54 = f32[2,1728]{1,0:T(2,128)S(1)} collective-permute-done((f32[2,1728]{1,0:T(2,128)S(1)}, f32[2,1728]{1,0:T(2,128)S(1)}, u32[]{:S(2)}, u32[]{:S(2)}) %collective-permute-start.54) | collective-permute-done | bytes 13856 | tf_op jit(solution)/shard_map/ppermute | solution.py:68
  1036.7 19.1 %collective-permute-start.56 = (f32[2,320]{1,0:T(2,128)S(1)}, f32[2,320]{1,0:T(2,128)S(1)}, u32[]{:S(2)}, u32[]{:S(2)}) collective-permute-start(f32[2,320]{1,0:T(2,128)S(1)} %select_n.226), channel_id=1, source_target_pairs={{0,2},{1,3},{2,0},{3,1},{4,6},{5,7},{6,4},{7,5},{8,10},{9,11},{10,... | collective-permute-start | bytes 7688 | tf_op jit(solution)/shard_map/ppermute | solution.py:68
  1062.0 13.1 %collective-permute-start.57 = (f32[1,320]{1,0:T(1,128)S(1)}, f32[1,320]{1,0:T(1,128)S(1)}, u32[]{:S(2)}, u32[]{:S(2)}) collective-permute-start(f32[1,320]{1,0:T(1,128)S(1)} %broadcast_select_fusion.15), channel_id=1, source_target_pairs={{0,1},{1,0},{2,3},{3,2},{4,5},{5,4},{6,7},{7,6},{8,9},{9,8},{10,11... | collective-permute-start | bytes 3848 | tf_op jit(solution)/shard_map/ppermute | solution.py:68
  (498 shorter events, 241.7 us)
Async XLA Ops:
  7.3 375.1 %all-gather.7.cloned.1.call-start = ((), (), s32[]{:S(2)}) async-start(), calls=%async_computation.13 | async-start | bytes 2359296 | tf_op jit(solution)/shard_map/all_gather | solution.py:263
  8.0 384.1 %all-gather.5.cloned.1.call-start = ((), (), s32[]{:S(2)}) async-start(), calls=%async_computation.12 | async-start | bytes 7077888 | tf_op jit(solution)/shard_map/all_gather | solution.py:261
  10.3 487.1 %all-gather.9.cloned.1.call-start = ((), (), s32[]{:S(2)}) async-start(), calls=%async_computation.14 | async-start | bytes 9437184 | tf_op jit(solution)/shard_map/all_gather | solution.py:262
  40.4 528.5 %all-gather.11.cloned.1.call-start = ((), (), s32[]{:S(2)}) async-start(), calls=%async_computation.15 | async-start | bytes 9437184 | tf_op jit(solution)/shard_map/all_gather | solution.py:264
  56.9 40.6 %all-to-all-start.6 = ((bf16[8,32,2048]{2,1,0:T(8,128)(2,1)}), bf16[8,32,2048]{2,1,0:T(8,128)(2,1)}, u32[]{:S(2)}, u32[]{:S(2)}) async-start(bf16[8,32,2048]{2,1,0:T(8,128)(2,1)} %get-tuple-element.101), calls=%async_computation.6 | async-start | bytes 2097152 | tf_op jit(solution)/shard_map/all_to_all | solution.py:235
  61.3 21.0 %collective-permute-start.7 = (bf16[2,832]{1,0:T(2,128)(2,1)S(1)}, bf16[2,832]{1,0:T(2,128)(2,1)S(1)}, u32[]{:S(2)}, u32[]{:S(2)}) collective-permute-start(bf16[2,832]{1,0:T(2,128)(2,1)S(1)} %pad_maximum_fusion.9), channel_id=1, source_target_pairs={{0,8},{4,12},{8,0},{12,4},{16,24},{20,28},{24,16},{28,20},{1,9},{5... | collective-permute-start | bytes 9992 | tf_op jit(solution)/shard_map/ppermute | solution.py:51
  82.3 21.6 %collective-permute-start.8 = (bf16[4,832]{1,0:T(4,128)(2,1)S(1)}, bf16[4,832]{1,0:T(4,128)(2,1)S(1)}, u32[]{:S(2)}, u32[]{:S(2)}) collective-permute-start(bf16[4,832]{1,0:T(4,128)(2,1)S(1)} %pad_maximum_fusion.8), channel_id=1, source_target_pairs={{0,16},{4,20},{8,24},{12,28},{16,0},{20,4},{24,8},{28,12},{1,17},{... | collective-permute-start | bytes 19976 | tf_op jit(solution)/shard_map/ppermute | solution.py:51
  83.8 56.9 %collective-permute-start.18 = (bf16[256,2048]{1,0:T(8,128)(2,1)S(1)}, bf16[256,2048]{1,0:T(8,128)(2,1)}, u32[]{:S(2)}, u32[]{:S(2)}) collective-permute-start(bf16[256,2048]{1,0:T(8,128)(2,1)S(1)} %bitcast.137), channel_id=1, source_target_pairs={{1,0},{2,1},{3,2},{5,4},{6,5},{7,6},{9,8},{10,9},{11,10},{13,12},{... | collective-permute-start | bytes 3145736 | tf_op jit(solution)/shard_map/ppermute | solution.py:31
  85.1 61.7 %collective-permute-start.17 = (bf16[256,2048]{1,0:T(8,128)(2,1)S(1)}, bf16[256,2048]{1,0:T(8,128)(2,1)}, u32[]{:S(2)}, u32[]{:S(2)}) collective-permute-start(bf16[256,2048]{1,0:T(8,128)(2,1)S(1)} %bitcast.138), channel_id=1, source_target_pairs={{0,1},{1,2},{2,3},{4,5},{5,6},{6,7},{8,9},{9,10},{10,11},{12,13},{... | collective-permute-start | bytes 3145736 | tf_op jit(solution)/shard_map/ppermute | solution.py:27
  90.7 57.5 %collective-permute-start.1 = (bf16[256,2048]{1,0:T(8,128)(2,1)S(1)}, bf16[256,2048]{1,0:T(8,128)(2,1)}, u32[]{:S(2)}, u32[]{:S(2)}) collective-permute-start(bf16[256,2048]{1,0:T(8,128)(2,1)S(1)} %bitcast.146), channel_id=1, source_target_pairs={{1,0},{2,1},{3,2},{5,4},{6,5},{7,6},{9,8},{10,9},{11,10},{13,12},{... | collective-permute-start | bytes 3145736 | tf_op jit(solution)/shard_map/ppermute | solution.py:31
  92.0 61.7 %collective-permute-start = (bf16[256,2048]{1,0:T(8,128)(2,1)S(1)}, bf16[256,2048]{1,0:T(8,128)(2,1)}, u32[]{:S(2)}, u32[]{:S(2)}) collective-permute-start(bf16[256,2048]{1,0:T(8,128)(2,1)S(1)} %bitcast.147), channel_id=1, source_target_pairs={{0,1},{1,2},{2,3},{4,5},{5,6},{6,7},{8,9},{9,10},{10,11},{12,13},{... | collective-permute-start | bytes 3145736 | tf_op jit(solution)/shard_map/ppermute | solution.py:27
  97.5 49.3 %all-to-all-start.4 = ((bf16[8,32,2048]{2,1,0:T(8,128)(2,1)}), bf16[8,32,2048]{2,1,0:T(8,128)(2,1)}, u32[]{:S(2)}, u32[]{:S(2)}) async-start(bf16[8,32,2048]{2,1,0:T(8,128)(2,1)} %get-tuple-element.100), calls=%async_computation.4 | async-start | bytes 2097152 | tf_op jit(solution)/shard_map/all_to_all | solution.py:235
  101.8 954.1 %reduce-scatter.7.cloned.1.call-start = ((), (), s32[]{:S(2)}) async-start(), calls=%async_computation.17 | async-start | bytes 2359296 | tf_op jit(solution)/shard_map/reduce_scatter | solution.py:341
  103.9 30.4 %collective-permute-start.9 = (bf16[1,8,384]{2,1,0:T(8,128)(2,1)S(1)}, bf16[1,8,384]{2,1,0:T(8,128)(2,1)S(1)}, u32[]{:S(2)}, u32[]{:S(2)}) collective-permute-start(bf16[1,8,384]{2,1,0:T(8,128)(2,1)S(1)} %maximum_bitcast_fusion.1), channel_id=1, source_target_pairs={{0,1},{1,0},{2,3},{3,2},{4,5},{5,4},{6,7},{7,6},{8,9},{9,8},{10,11... | collective-permute-start | bytes 18440 | tf_op jit(solution)/shard_map/ppermute | solution.py:51
  139.4 28.8 %collective-permute-start.42 = (bf16[256,2048]{1,0:T(8,128)(2,1)}, bf16[256,2048]{1,0:T(8,128)(2,1)}, u32[]{:S(2)}, u32[]{:S(2)}) collective-permute-start(bf16[256,2048]{1,0:T(8,128)(2,1)} %bitcast.37), channel_id=1, source_target_pairs={{1,0},{2,1},{3,2},{5,4},{6,5},{7,6},{9,8},{10,9},{11,10},{13,12},{... | collective-permute-start | bytes 3145736 | tf_op jit(solution)/shard_map/ppermute | solution.py:31
  140.7 29.2 %collective-permute-start.41 = (bf16[256,2048]{1,0:T(8,128)(2,1)}, bf16[256,2048]{1,0:T(8,128)(2,1)}, u32[]{:S(2)}, u32[]{:S(2)}) collective-permute-start(bf16[256,2048]{1,0:T(8,128)(2,1)} %bitcast.37), channel_id=1, source_target_pairs={{0,1},{1,2},{2,3},{4,5},{5,6},{6,7},{8,9},{9,10},{10,11},{12,13},{... | collective-permute-start | bytes 3145736 | tf_op jit(solution)/shard_map/ppermute | solution.py:27
  146.8 43.9 %collective-permute-start.30 = (bf16[256,2048]{1,0:T(8,128)(2,1)}, bf16[256,2048]{1,0:T(8,128)(2,1)}, u32[]{:S(2)}, u32[]{:S(2)}) collective-permute-start(bf16[256,2048]{1,0:T(8,128)(2,1)} %bitcast.31), channel_id=1, source_target_pairs={{1,0},{2,1},{3,2},{5,4},{6,5},{7,6},{9,8},{10,9},{11,10},{13,12},{... | collective-permute-start | bytes 3145736 | tf_op jit(solution)/shard_map/ppermute | solution.py:31
  148.1 44.2 %collective-permute-start.29 = (bf16[256,2048]{1,0:T(8,128)(2,1)}, bf16[256,2048]{1,0:T(8,128)(2,1)}, u32[]{:S(2)}, u32[]{:S(2)}) collective-permute-start(bf16[256,2048]{1,0:T(8,128)(2,1)} %bitcast.31), channel_id=1, source_target_pairs={{0,1},{1,2},{2,3},{4,5},{5,6},{6,7},{8,9},{9,10},{10,11},{12,13},{... | collective-permute-start | bytes 3145736 | tf_op jit(solution)/shard_map/ppermute | solution.py:27
  153.7 59.5 %collective-permute-start.19 = (bf16[256,2048]{1,0:T(8,128)(2,1)}, bf16[256,2048]{1,0:T(8,128)(2,1)}, u32[]{:S(2)}, u32[]{:S(2)}) collective-permute-start(bf16[256,2048]{1,0:T(8,128)(2,1)} %collective-permute-done.18), channel_id=1, source_target_pairs={{1,0},{2,1},{5,4},{6,5},{9,8},{10,9},{13,12},{14,13},{17,16},{18,1... | collective-permute-start | bytes 3145736 | tf_op jit(solution)/shard_map/ppermute | solution.py:31
  168.3 47.2 %collective-permute-start.21 = (bf16[256,2048]{1,0:T(8,128)(2,1)}, bf16[256,2048]{1,0:T(8,128)(2,1)}, u32[]{:S(2)}, u32[]{:S(2)}) collective-permute-start(bf16[256,2048]{1,0:T(8,128)(2,1)} %collective-permute-done.17), channel_id=1, source_target_pairs={{1,2},{2,3},{5,6},{6,7},{9,10},{10,11},{13,14},{14,15},{17,18},{18... | collective-permute-start | bytes 3145736 | tf_op jit(solution)/shard_map/ppermute | solution.py:27
  169.9 65.7 %collective-permute-start.2 = (bf16[256,2048]{1,0:T(8,128)(2,1)}, bf16[256,2048]{1,0:T(8,128)(2,1)}, u32[]{:S(2)}, u32[]{:S(2)}) collective-permute-start(bf16[256,2048]{1,0:T(8,128)(2,1)} %collective-permute-done.1), channel_id=1, source_target_pairs={{1,0},{2,1},{5,4},{6,5},{9,8},{10,9},{13,12},{14,13},{17,16},{18,1... | collective-permute-start | bytes 3145736 | tf_op jit(solution)/shard_map/ppermute | solution.py:31
  190.7 46.7 %collective-permute-start.4 = (bf16[256,2048]{1,0:T(8,128)(2,1)}, bf16[256,2048]{1,0:T(8,128)(2,1)}, u32[]{:S(2)}, u32[]{:S(2)}) collective-permute-start(bf16[256,2048]{1,0:T(8,128)(2,1)} %collective-permute-done), channel_id=1, source_target_pairs={{1,2},{2,3},{5,6},{6,7},{9,10},{10,11},{13,14},{14,15},{17,18},{18... | collective-permute-start | bytes 3145736 | tf_op jit(solution)/shard_map/ppermute | solution.py:27
  192.4 65.8 %collective-permute-start.43 = (bf16[256,2048]{1,0:T(8,128)(2,1)}, bf16[256,2048]{1,0:T(8,128)(2,1)}, u32[]{:S(2)}, u32[]{:S(2)}) collective-permute-start(bf16[256,2048]{1,0:T(8,128)(2,1)} %collective-permute-done.42), channel_id=1, source_target_pairs={{1,0},{2,1},{5,4},{6,5},{9,8},{10,9},{13,12},{14,13},{17,16},{18,1... | collective-permute-start | bytes 3145736 | tf_op jit(solution)/shard_map/ppermute | solution.py:31
  213.2 46.6 %collective-permute-start.45 = (bf16[256,2048]{1,0:T(8,128)(2,1)}, bf16[256,2048]{1,0:T(8,128)(2,1)}, u32[]{:S(2)}, u32[]{:S(2)}) collective-permute-start(bf16[256,2048]{1,0:T(8,128)(2,1)} %collective-permute-done.41), channel_id=1, source_target_pairs={{1,2},{2,3},{5,6},{6,7},{9,10},{10,11},{13,14},{14,15},{17,18},{18... | collective-permute-start | bytes 3145736 | tf_op jit(solution)/shard_map/ppermute | solution.py:27
  215.4 65.2 %collective-permute-start.31 = (bf16[256,2048]{1,0:T(8,128)(2,1)}, bf16[256,2048]{1,0:T(8,128)(2,1)}, u32[]{:S(2)}, u32[]{:S(2)}) collective-permute-start(bf16[256,2048]{1,0:T(8,128)(2,1)} %collective-permute-done.30), channel_id=1, source_target_pairs={{1,0},{2,1},{5,4},{6,5},{9,8},{10,9},{13,12},{14,13},{17,16},{18,1... | collective-permute-start | bytes 3145736 | tf_op jit(solution)/shard_map/ppermute | solution.py:31
  235.7 46.6 %collective-permute-start.33 = (bf16[256,2048]{1,0:T(8,128)(2,1)}, bf16[256,2048]{1,0:T(8,128)(2,1)}, u32[]{:S(2)}, u32[]{:S(2)}) collective-permute-start(bf16[256,2048]{1,0:T(8,128)(2,1)} %collective-permute-done.29), channel_id=1, source_target_pairs={{1,2},{2,3},{5,6},{6,7},{9,10},{10,11},{13,14},{14,15},{17,18},{18... | collective-permute-start | bytes 3145736 | tf_op jit(solution)/shard_map/ppermute | solution.py:27
  237.4 65.7 %collective-permute-start.20 = (bf16[256,2048]{1,0:T(8,128)(2,1)}, bf16[256,2048]{1,0:T(8,128)(2,1)}, u32[]{:S(2)}, u32[]{:S(2)}) collective-permute-start(bf16[256,2048]{1,0:T(8,128)(2,1)} %collective-permute-done.19), channel_id=1, source_target_pairs={{1,0},{5,4},{9,8},{13,12},{17,16},{21,20},{25,24},{29,28}} | collective-permute-start | bytes 3145736 | tf_op jit(solution)/shard_map/ppermute | solution.py:31
  258.1 46.6 %collective-permute-start.22 = (bf16[256,2048]{1,0:T(8,128)(2,1)}, bf16[256,2048]{1,0:T(8,128)(2,1)}, u32[]{:S(2)}, u32[]{:S(2)}) collective-permute-start(bf16[256,2048]{1,0:T(8,128)(2,1)} %collective-permute-done.21), channel_id=1, source_target_pairs={{2,3},{6,7},{10,11},{14,15},{18,19},{22,23},{26,27},{30,31}} | collective-permute-start | bytes 3145736 | tf_op jit(solution)/shard_map/ppermute | solution.py:27
  259.8 65.8 %collective-permute-start.3 = (bf16[256,2048]{1,0:T(8,128)(2,1)}, bf16[256,2048]{1,0:T(8,128)(2,1)}, u32[]{:S(2)}, u32[]{:S(2)}) collective-permute-start(bf16[256,2048]{1,0:T(8,128)(2,1)} %collective-permute-done.2), channel_id=1, source_target_pairs={{1,0},{5,4},{9,8},{13,12},{17,16},{21,20},{25,24},{29,28}} | collective-permute-start | bytes 3145736 | tf_op jit(solution)/shard_map/ppermute | solution.py:31
  280.6 69.4 %collective-permute-start.5 = (bf16[256,2048]{1,0:T(8,128)(2,1)}, bf16[256,2048]{1,0:T(8,128)(2,1)}, u32[]{:S(2)}, u32[]{:S(2)}) collective-permute-start(bf16[256,2048]{1,0:T(8,128)(2,1)} %collective-permute-done.4), channel_id=1, source_target_pairs={{2,3},{6,7},{10,11},{14,15},{18,19},{22,23},{26,27},{30,31}} | collective-permute-start | bytes 3145736 | tf_op jit(solution)/shard_map/ppermute | solution.py:27
  282.3 70.2 %collective-permute-start.44 = (bf16[256,2048]{1,0:T(8,128)(2,1)}, bf16[256,2048]{1,0:T(8,128)(2,1)}, u32[]{:S(2)}, u32[]{:S(2)}) collective-permute-start(bf16[256,2048]{1,0:T(8,128)(2,1)} %collective-permute-done.43), channel_id=1, source_target_pairs={{1,0},{5,4},{9,8},{13,12},{17,16},{21,20},{25,24},{29,28}} | collective-permute-start | bytes 3145736 | tf_op jit(solution)/shard_map/ppermute | solution.py:31
  303.1 52.7 %collective-permute-start.46 = (bf16[256,2048]{1,0:T(8,128)(2,1)}, bf16[256,2048]{1,0:T(8,128)(2,1)}, u32[]{:S(2)}, u32[]{:S(2)}) collective-permute-start(bf16[256,2048]{1,0:T(8,128)(2,1)} %collective-permute-done.45), channel_id=1, source_target_pairs={{2,3},{6,7},{10,11},{14,15},{18,19},{22,23},{26,27},{30,31}} | collective-permute-start | bytes 3145736 | tf_op jit(solution)/shard_map/ppermute | solution.py:27
  304.7 62.8 %collective-permute-start.32 = (bf16[256,2048]{1,0:T(8,128)(2,1)}, bf16[256,2048]{1,0:T(8,128)(2,1)}, u32[]{:S(2)}, u32[]{:S(2)}) collective-permute-start(bf16[256,2048]{1,0:T(8,128)(2,1)} %collective-permute-done.31), channel_id=1, source_target_pairs={{1,0},{5,4},{9,8},{13,12},{17,16},{21,20},{25,24},{29,28}} | collective-permute-start | bytes 3145736 | tf_op jit(solution)/shard_map/ppermute | solution.py:31
  325.5 44.9 %collective-permute-start.34 = (bf16[256,2048]{1,0:T(8,128)(2,1)}, bf16[256,2048]{1,0:T(8,128)(2,1)}, u32[]{:S(2)}, u32[]{:S(2)}) collective-permute-start(bf16[256,2048]{1,0:T(8,128)(2,1)} %collective-permute-done.33), channel_id=1, source_target_pairs={{2,3},{6,7},{10,11},{14,15},{18,19},{22,23},{26,27},{30,31}} | collective-permute-start | bytes 3145736 | tf_op jit(solution)/shard_map/ppermute | solution.py:27
  448.6 632.9 %reduce-scatter.5.cloned.1.call-start = ((), (), s32[]{:S(2)}) async-start(), calls=%async_computation.16 | async-start | bytes 7077888 | tf_op jit(solution)/shard_map/reduce_scatter | solution.py:347
  493.3 591.3 %reduce-scatter.11.cloned.1.call-start = ((), (), s32[]{:S(2)}) async-start(), calls=%async_computation.19 | async-start | bytes 9437184 | tf_op jit(solution)/shard_map/reduce_scatter | solution.py:338
  568.8 519.0 %reduce-scatter.9.cloned.1.call-start = ((), (), s32[]{:S(2)}) async-start(), calls=%async_computation.18 | async-start | bytes 9437184 | tf_op jit(solution)/shard_map/reduce_scatter | solution.py:345
  669.9 346.4 %collective-permute-start.53 = (f32[4,1728]{1,0:T(4,128)S(1)}, f32[4,1728]{1,0:T(4,128)S(1)}, u32[]{:S(2)}, u32[]{:S(2)}) collective-permute-start(f32[4,1728]{1,0:T(4,128)S(1)} %slice_select_fusion), channel_id=1, source_target_pairs={{0,16},{4,20},{8,24},{12,28},{16,0},{20,4},{24,8},{28,12},{1,17},{... | collective-permute-start | bytes 82952 | tf_op jit(solution)/shard_map/ppermute | solution.py:68
  686.6 64.6 %collective-permute-start.11 = (bf16[256,2048]{1,0:T(8,128)(2,1)}, bf16[256,2048]{1,0:T(8,128)(2,1)}, u32[]{:S(2)}, u32[]{:S(2)}) collective-permute-start(bf16[256,2048]{1,0:T(8,128)(2,1)} %get-tuple-element.94), channel_id=1, source_target_pairs={{0,1},{4,5},{8,9},{12,13},{16,17},{20,21},{24,25},{28,29}} | collective-permute-start | bytes 3145736 | tf_op jit(solution)/shard_map/ppermute | solution.py:40
  689.0 117.1 %collective-permute-start.14 = (bf16[256,2048]{1,0:T(8,128)(2,1)}, bf16[256,2048]{1,0:T(8,128)(2,1)}, u32[]{:S(2)}, u32[]{:S(2)}) collective-permute-start(bf16[256,2048]{1,0:T(8,128)(2,1)} %get-tuple-element.95), channel_id=1, source_target_pairs={{3,2},{7,6},{11,10},{15,14},{19,18},{23,22},{27,26},{31,30}} | collective-permute-start | bytes 3145736 | tf_op jit(solution)/shard_map/ppermute | solution.py:42
  694.7 61.0 %collective-permute-start.35 = (bf16[256,2048]{1,0:T(8,128)(2,1)}, bf16[256,2048]{1,0:T(8,128)(2,1)}, u32[]{:S(2)}, u32[]{:S(2)}) collective-permute-start(bf16[256,2048]{1,0:T(8,128)(2,1)} %get-tuple-element.86), channel_id=1, source_target_pairs={{0,1},{4,5},{8,9},{12,13},{16,17},{20,21},{24,25},{28,29}} | collective-permute-start | bytes 3145736 | tf_op jit(solution)/shard_map/ppermute | solution.py:40
  697.0 132.1 %collective-permute-start.38 = (bf16[256,2048]{1,0:T(8,128)(2,1)}, bf16[256,2048]{1,0:T(8,128)(2,1)}, u32[]{:S(2)}, u32[]{:S(2)}) collective-permute-start(bf16[256,2048]{1,0:T(8,128)(2,1)} %get-tuple-element.87), channel_id=1, source_target_pairs={{3,2},{7,6},{11,10},{15,14},{19,18},{23,22},{27,26},{31,30}} | collective-permute-start | bytes 3145736 | tf_op jit(solution)/shard_map/ppermute | solution.py:42
  751.2 25.2 %collective-permute-start.23 = (bf16[256,2048]{1,0:T(8,128)(2,1)S(1)}, bf16[256,2048]{1,0:T(8,128)(2,1)S(1)}, u32[]{:S(2)}, u32[]{:S(2)}) collective-permute-start(bf16[256,2048]{1,0:T(8,128)(2,1)S(1)} %get-tuple-element.98), channel_id=1, source_target_pairs={{0,1},{4,5},{8,9},{12,13},{16,17},{20,21},{24,25},{28,29}} | collective-permute-start | bytes 3145736 | tf_op jit(solution)/shard_map/ppermute | solution.py:40
  755.7 43.1 %collective-permute-start.47 = (bf16[256,2048]{1,0:T(8,128)(2,1)S(1)}, bf16[256,2048]{1,0:T(8,128)(2,1)S(1)}, u32[]{:S(2)}, u32[]{:S(2)}) collective-permute-start(bf16[256,2048]{1,0:T(8,128)(2,1)S(1)} %get-tuple-element.90), channel_id=1, source_target_pairs={{0,1},{4,5},{8,9},{12,13},{16,17},{20,21},{24,25},{28,29}} | collective-permute-start | bytes 3145736 | tf_op jit(solution)/shard_map/ppermute | solution.py:40
  776.4 44.9 %collective-permute-start.12 = (bf16[256,2048]{1,0:T(8,128)(2,1)S(1)}, bf16[256,2048]{1,0:T(8,128)(2,1)S(1)}, u32[]{:S(2)}, u32[]{:S(2)}) collective-permute-start(bf16[256,2048]{1,0:T(8,128)(2,1)S(1)} %add_convert_fusion.19), channel_id=1, source_target_pairs={{0,1},{1,2},{4,5},{5,6},{8,9},{9,10},{12,13},{13,14},{16,17},{17,1... | collective-permute-start | bytes 3145736 | tf_op jit(solution)/shard_map/ppermute | solution.py:40
  798.8 44.9 %collective-permute-start.36 = (bf16[256,2048]{1,0:T(8,128)(2,1)S(1)}, bf16[256,2048]{1,0:T(8,128)(2,1)}, u32[]{:S(2)}, u32[]{:S(2)}) collective-permute-start(bf16[256,2048]{1,0:T(8,128)(2,1)S(1)} %add_convert_fusion.11), channel_id=1, source_target_pairs={{0,1},{1,2},{4,5},{5,6},{8,9},{9,10},{12,13},{13,14},{16,17},{17,1... | collective-permute-start | bytes 3145736 | tf_op jit(solution)/shard_map/ppermute | solution.py:40
  806.2 46.6 %collective-permute-start.26 = (bf16[256,2048]{1,0:T(8,128)(2,1)S(1)}, bf16[256,2048]{1,0:T(8,128)(2,1)}, u32[]{:S(2)}, u32[]{:S(2)}) collective-permute-start(bf16[256,2048]{1,0:T(8,128)(2,1)S(1)} %get-tuple-element.99), channel_id=1, source_target_pairs={{3,2},{7,6},{11,10},{15,14},{19,18},{23,22},{27,26},{31,30}} | collective-permute-start | bytes 3145736 | tf_op jit(solution)/shard_map/ppermute | solution.py:42
  821.3 44.9 %collective-permute-start.24 = (bf16[256,2048]{1,0:T(8,128)(2,1)S(1)}, bf16[256,2048]{1,0:T(8,128)(2,1)S(1)}, u32[]{:S(2)}, u32[]{:S(2)}) collective-permute-start(bf16[256,2048]{1,0:T(8,128)(2,1)S(1)} %add_convert_fusion.15), channel_id=1, source_target_pairs={{0,1},{1,2},{4,5},{5,6},{8,9},{9,10},{12,13},{13,14},{16,17},{17,1... | collective-permute-start | bytes 3145736 | tf_op jit(solution)/shard_map/ppermute | solution.py:40
  829.1 47.4 %collective-permute-start.50 = (bf16[256,2048]{1,0:T(8,128)(2,1)S(1)}, bf16[256,2048]{1,0:T(8,128)(2,1)}, u32[]{:S(2)}, u32[]{:S(2)}) collective-permute-start(bf16[256,2048]{1,0:T(8,128)(2,1)S(1)} %get-tuple-element.91), channel_id=1, source_target_pairs={{3,2},{7,6},{11,10},{15,14},{19,18},{23,22},{27,26},{31,30}} | collective-permute-start | bytes 3145736 | tf_op jit(solution)/shard_map/ppermute | solution.py:42
  843.8 44.9 %collective-permute-start.48 = (bf16[256,2048]{1,0:T(8,128)(2,1)S(1)}, bf16[256,2048]{1,0:T(8,128)(2,1)}, u32[]{:S(2)}, u32[]{:S(2)}) collective-permute-start(bf16[256,2048]{1,0:T(8,128)(2,1)S(1)} %add_convert_fusion.7), channel_id=1, source_target_pairs={{0,1},{1,2},{4,5},{5,6},{8,9},{9,10},{12,13},{13,14},{16,17},{17,1... | collective-permute-start | bytes 3145736 | tf_op jit(solution)/shard_map/ppermute | solution.py:40
  852.8 44.2 %collective-permute-start.15 = (bf16[256,2048]{1,0:T(8,128)(2,1)}, bf16[256,2048]{1,0:T(8,128)(2,1)}, u32[]{:S(2)}, u32[]{:S(2)}) collective-permute-start(bf16[256,2048]{1,0:T(8,128)(2,1)} %get-tuple-element.93), channel_id=1, source_target_pairs={{2,1},{3,2},{6,5},{7,6},{10,9},{11,10},{14,13},{15,14},{18,17},{19... | collective-permute-start | bytes 3145736 | tf_op jit(solution)/shard_map/ppermute | solution.py:42
  867.2 87.6 %collective-permute-start.13 = (bf16[256,2048]{1,0:T(8,128)(2,1)}, bf16[256,2048]{1,0:T(8,128)(2,1)}, u32[]{:S(2)}, u32[]{:S(2)}) collective-permute-start(bf16[256,2048]{1,0:T(8,128)(2,1)} %get-tuple-element.92), channel_id=1, source_target_pairs={{0,1},{1,2},{2,3},{4,5},{5,6},{6,7},{8,9},{9,10},{10,11},{12,13},{... | collective-permute-start | bytes 3145736 | tf_op jit(solution)/shard_map/ppermute | solution.py:40
  876.5 22.8 %collective-permute-start.39 = (bf16[256,2048]{1,0:T(8,128)(2,1)}, bf16[256,2048]{1,0:T(8,128)(2,1)}, u32[]{:S(2)}, u32[]{:S(2)}) collective-permute-start(bf16[256,2048]{1,0:T(8,128)(2,1)} %get-tuple-element.85), channel_id=1, source_target_pairs={{2,1},{3,2},{6,5},{7,6},{10,9},{11,10},{14,13},{15,14},{18,17},{19... | collective-permute-start | bytes 3145736 | tf_op jit(solution)/shard_map/ppermute | solution.py:42
  888.7 39.8 %collective-permute-start.37 = (bf16[256,2048]{1,0:T(8,128)(2,1)}, bf16[256,2048]{1,0:T(8,128)(2,1)S(1)}, u32[]{:S(2)}, u32[]{:S(2)}) collective-permute-start(bf16[256,2048]{1,0:T(8,128)(2,1)} %get-tuple-element.84), channel_id=1, source_target_pairs={{0,1},{1,2},{2,3},{4,5},{5,6},{6,7},{8,9},{9,10},{10,11},{12,13},{... | collective-permute-start | bytes 3145736 | tf_op jit(solution)/shard_map/ppermute | solution.py:40
  901.6 51.1 %collective-permute-start.40 = (bf16[256,2048]{1,0:T(8,128)(2,1)S(1)}, bf16[256,2048]{1,0:T(8,128)(2,1)S(1)}, u32[]{:S(2)}, u32[]{:S(2)}) collective-permute-start(bf16[256,2048]{1,0:T(8,128)(2,1)S(1)} %add_convert_fusion.8), channel_id=1, source_target_pairs={{1,0},{2,1},{3,2},{5,4},{6,5},{7,6},{9,8},{10,9},{11,10},{13,12},{... | collective-permute-start | bytes 3145736 | tf_op jit(solution)/shard_map/ppermute | solution.py:42
  904.4 71.3 %collective-permute-start.16 = (bf16[256,2048]{1,0:T(8,128)(2,1)S(1)}, bf16[256,2048]{1,0:T(8,128)(2,1)S(1)}, u32[]{:S(2)}, u32[]{:S(2)}) collective-permute-start(bf16[256,2048]{1,0:T(8,128)(2,1)S(1)} %add_convert_fusion.16), channel_id=1, source_target_pairs={{1,0},{2,1},{3,2},{5,4},{6,5},{7,6},{9,8},{10,9},{11,10},{13,12},{... | collective-permute-start | bytes 3145736 | tf_op jit(solution)/shard_map/ppermute | solution.py:42
  928.6 56.1 %collective-permute-start.49 = (bf16[256,2048]{1,0:T(8,128)(2,1)}, bf16[256,2048]{1,0:T(8,128)(2,1)S(1)}, u32[]{:S(2)}, u32[]{:S(2)}) collective-permute-start(bf16[256,2048]{1,0:T(8,128)(2,1)} %get-tuple-element.88), channel_id=1, source_target_pairs={{0,1},{1,2},{2,3},{4,5},{5,6},{6,7},{8,9},{9,10},{10,11},{12,13},{... | collective-permute-start | bytes 3145736 | tf_op jit(solution)/shard_map/ppermute | solution.py:40
  952.6 41.6 %collective-permute-start.52 = (bf16[256,2048]{1,0:T(8,128)(2,1)}, bf16[256,2048]{1,0:T(8,128)(2,1)}, u32[]{:S(2)}, u32[]{:S(2)}) collective-permute-start(bf16[256,2048]{1,0:T(8,128)(2,1)} %add_convert_fusion.4), channel_id=1, source_target_pairs={{1,0},{2,1},{3,2},{5,4},{6,5},{7,6},{9,8},{10,9},{11,10},{13,12},{... | collective-permute-start | bytes 3145736 | tf_op jit(solution)/shard_map/ppermute | solution.py:42
  954.8 42.2 %collective-permute-start.25 = (bf16[256,2048]{1,0:T(8,128)(2,1)}, bf16[256,2048]{1,0:T(8,128)(2,1)}, u32[]{:S(2)}, u32[]{:S(2)}) collective-permute-start(bf16[256,2048]{1,0:T(8,128)(2,1)} %get-tuple-element.96), channel_id=1, source_target_pairs={{0,1},{1,2},{2,3},{4,5},{5,6},{6,7},{8,9},{9,10},{10,11},{12,13},{... | collective-permute-start | bytes 3145736 | tf_op jit(solution)/shard_map/ppermute | solution.py:40
  975.6 31.7 %collective-permute-start.28 = (bf16[256,2048]{1,0:T(8,128)(2,1)}, bf16[256,2048]{1,0:T(8,128)(2,1)}, u32[]{:S(2)}, u32[]{:S(2)}) collective-permute-start(bf16[256,2048]{1,0:T(8,128)(2,1)} %add_convert_fusion.12), channel_id=1, source_target_pairs={{1,0},{2,1},{3,2},{5,4},{6,5},{7,6},{9,8},{10,9},{11,10},{13,12},{... | collective-permute-start | bytes 3145736 | tf_op jit(solution)/shard_map/ppermute | solution.py:42
  981.1 31.5 %all-to-all-start.5 = ((bf16[8,32,2048]{2,1,0:T(8,128)(2,1)}), bf16[8,32,2048]{2,1,0:T(8,128)(2,1)S(1)}, u32[]{:S(2)}, u32[]{:S(2)}) async-start(bf16[8,32,2048]{2,1,0:T(8,128)(2,1)} %bitcast.34), calls=%async_computation.5 | async-start | bytes 2097152 | tf_op jit(solution)/shard_map/all_to_all | solution.py:238
  1031.7 26.0 %all-to-all-start.1 = ((bf16[8,32,2048]{2,1,0:T(8,128)(2,1)}), bf16[8,32,2048]{2,1,0:T(8,128)(2,1)S(1)}, u32[]{:S(2)}, u32[]{:S(2)}) async-start(bf16[8,32,2048]{2,1,0:T(8,128)(2,1)} %bitcast.17), calls=%async_computation.1 | async-start | bytes 2097152 | tf_op jit(solution)/shard_map/all_to_all | solution.py:238
  1036.7 21.0 %collective-permute-start.56 = (f32[2,320]{1,0:T(2,128)S(1)}, f32[2,320]{1,0:T(2,128)S(1)}, u32[]{:S(2)}, u32[]{:S(2)}) collective-permute-start(f32[2,320]{1,0:T(2,128)S(1)} %select_n.226), channel_id=1, source_target_pairs={{0,2},{1,3},{2,0},{3,1},{4,6},{5,7},{6,4},{7,5},{8,10},{9,11},{10,... | collective-permute-start | bytes 7688 | tf_op jit(solution)/shard_map/ppermute | solution.py:68
  1057.7 21.0 %all-to-all-start.3 = ((bf16[8,32,2048]{2,1,0:T(8,128)(2,1)}), bf16[8,32,2048]{2,1,0:T(8,128)(2,1)}, u32[]{:S(2)}, u32[]{:S(2)}) async-start(bf16[8,32,2048]{2,1,0:T(8,128)(2,1)} %bitcast.28), calls=%async_computation.3 | async-start | bytes 2097152 | tf_op jit(solution)/shard_map/all_to_all | solution.py:238
  (113 other events, 3209.7 us)
Sparse Core Ops, SparseCore 0:
  10.0 37.5 all-gather.6
  49.5 61.6 all-gather.4
  113.1 62.3 all-gather.8
  177.2 55.9 all-gather.10
  448.7 40.2 reduce-scatter.6
  493.4 60.9 reduce-scatter.4
  568.9 70.4 reduce-scatter.10
  745.9 71.4 reduce-scatter.8

commit v2 on v1

v2 whole, which is shorter than its diff:
```python
import functools
import math

import jax
import jax.numpy as jnp
from jax import lax
from jax.experimental import pallas as pl
from jax.experimental.pallas import tpu as pltpu
from jax.sharding import PartitionSpec as P

HD = 256
ROT = 64
EPSILON = 1e-05
ROPE_BASE = 10000.0
NEG_FILL = -1e30
SQRT_HALF = 0.7071067811865476
INV_ROOT_TWO_PI = 0.3989422804014327
BF = jnp.bfloat16
F32 = jnp.float32
FAR = 1 << 20


class GatherChain:
    def __init__(self, x, axis, n):
        self.x, self.axis, self.n, self.step_no = x, axis, n, 0
        self.me = lax.axis_index(axis)
        self.left, self.right = [], []

    def steps(self):
        return self.n - 1

    def step(self):
        n = self.n
        s = self.step_no = self.step_no + 1
        to_right = self.left[-1] if self.left else self.x
        to_left = self.right[-1] if self.right else self.x
        pairs = [(k, k + 1) for k in range(s - 1, n - 1)]
        self.left.append(lax.ppermute(to_right, self.axis, pairs))
        pairs = [(k, k - 1) for k in range(1, n - s + 1)]
        self.right.append(lax.ppermute(to_left, self.axis, pairs))

    def live(self):
        return [self.left[-1], self.right[-1]]

    def set_live(self, values):
        self.left[-1], self.right[-1] = values


class SmallGather:
    def __init__(self, x, axis, n):
        self.out, self.axis, self.n, self.bit = x[None], axis, n, 1
        self.me = lax.axis_index(axis)

    def steps(self):
        return self.n.bit_length() - 1

    def step(self):
        bit, out = self.bit, self.out
        other = lax.ppermute(out, self.axis, [(i, i ^ bit) for i in range(self.n)])
        high = (self.me & bit) != 0
        self.out = jnp.concatenate(
            [jnp.where(high, other, out), jnp.where(high, out, other)], axis=0
        )
        self.bit *= 2

    def live(self):
        return [self.out]

    def set_live(self, values):
        self.out = values[0]


class SmallScatter:
    def __init__(self, x, axis, n):
        self.out, self.axis, self.n, self.bit = x, axis, n, n // 2
        self.me = lax.axis_index(axis)

    def steps(self):
        return self.n.bit_length() - 1

    def step(self):
        bit, x = self.bit, self.out
        low, high = x[:bit], x[bit:]
        mine_high = (self.me & bit) != 0
        sent = jnp.where(mine_high, low, high)
        kept = jnp.where(mine_high, high, low)
        self.out = kept + lax.ppermute(sent, self.axis, [(i, i ^ bit) for i in range(self.n)])
        self.bit //= 2

    def live(self):
        return [self.out]

    def set_live(self, values):
        self.out = values[0]


def shifts(n):
    return [[(k, (k + s) % n) for k in range(n)] for s in range(1, n)]


def direct_gather(x, axis, n):
    me = lax.axis_index(axis)
    got = jnp.stack([x] + [lax.ppermute(x, axis, pairs) for pairs in shifts(n)])
    order = (me - jnp.arange(n)) % n
    chosen = order[None, :] == jnp.arange(n)[:, None]
    return jnp.sum(jnp.where(chosen[:, :, None], got[None], 0), axis=1).astype(x.dtype)


def direct_scatter(x, axis, n):
    me = lax.axis_index(axis)
    total = lax.dynamic_index_in_dim(x, me, 0, keepdims=False)
    for s, pairs in enumerate(shifts(n), 1):
        sent = lax.dynamic_index_in_dim(x, (me + s) % n, 0, keepdims=False)
        total = total + lax.ppermute(sent, axis, pairs)
    return total


def rotated(x, cosines, sines):
    lanes = lax.broadcasted_iota(jnp.int32, x.shape, 1)
    partner = jnp.where(lanes < ROT // 2, pltpu.roll(x, 128 - ROT // 2, 1), pltpu.roll(x, ROT // 2, 1))
    return x * cosines + partner * sines


def scores_of(q, k, posq, posk):
    s = lax.dot_general(q, k, (((1,), (1,)), ((), ())), preferred_element_type=F32)
    return jnp.where(posk <= posq, s * (1.0 / math.sqrt(HD)), NEG_FILL)


def attend_kernel(n_blocks, posq_ref, posk_ref, cos_ref, sin_ref, qkv_ref, low_ref, mixed_ref):
    n_slots, rows, _ = qkv_ref.shape
    span = rows // n_blocks
    for t in range(n_slots):
        for base in (0, HD):
            lead = rotated(qkv_ref[t, :, base : base + 128], cos_ref[t], sin_ref[t])
            low_ref[t, :, base : base + 128] = lead.astype(BF)
            low_ref[t, :, base + 128 : base + HD] = qkv_ref[t, :, base + 128 : base + HD].astype(BF)
        low_ref[t, :, 2 * HD :] = qkv_ref[t, :, 2 * HD :].astype(BF)
    for b in range(n_blocks):
        own, seen = pl.ds(b * span, span), span * (b + 1)
        n_q, n_k = n_slots * span, n_slots * seen
        q = low_ref[:, own, :HD].reshape(n_q, HD)
        k = low_ref[:, :seen, HD : 2 * HD].reshape(n_k, HD)
        v = low_ref[:, :seen, 2 * HD :].reshape(n_k, HD)
        posq = posq_ref[:, own, :].reshape(n_q, 1)
        s = scores_of(q, k, posq, posk_ref[b, :, :n_k])
        e = jnp.exp(s - jnp.max(s, axis=-1, keepdims=True))
        p = e * (1.0 / jnp.sum(e, axis=-1, keepdims=True))
        mixed = jnp.dot(p.astype(BF), v, preferred_element_type=F32)
        mixed_ref[:, own, :] = mixed.astype(BF).reshape(n_slots, span, HD)


def attend_back_kernel(
    n_blocks,
    posq_ref,
    posk_ref,
    cos_ref,
    sin_ref,
    low_ref,
    dmix_ref,
    grad_ref,
    bias_ref,
    dk_ref,
    dv_ref,
):
    n_slots, rows, _ = low_ref.shape
    span = rows // n_blocks
    scale = 1.0 / math.sqrt(HD)
    for b in reversed(range(n_blocks)):
        own, seen = pl.ds(b * span, span), span * (b + 1)
        n_q, n_k = n_slots * span, n_slots * seen
        q = low_ref[:, own, :HD].reshape(n_q, HD)
        k = low_ref[:, :seen, HD : 2 * HD].reshape(n_k, HD)
        v = low_ref[:, :seen, 2 * HD :].reshape(n_k, HD)
        dmix = dmix_ref[:, own, :].reshape(n_q, HD)
        posq = posq_ref[:, own, :].reshape(n_q, 1)
        s = scores_of(q, k, posq, posk_ref[b, :, :n_k])
        e = jnp.exp(s - jnp.max(s, axis=-1, keepdims=True))
        p = e * (1.0 / jnp.sum(e, axis=-1, keepdims=True))
        dp = lax.dot_general(dmix, v, (((1,), (1,)), ((), ())), preferred_element_type=F32)
        ds = (p * (dp - jnp.sum(p * dp, axis=-1, keepdims=True))).astype(BF)
        dq = jnp.dot(ds, k, preferred_element_type=F32) * scale
        dk = lax.dot_general(ds, q, (((0,), (0,)), ((), ())), preferred_element_type=F32)
        dv = lax.dot_general(p.astype(BF), dmix, (((0,), (0,)), ((), ())), preferred_element_type=F32)
        dk, dv = dk.reshape(n_slots, seen, HD), dv.reshape(n_slots, seen, HD)
        if b == n_blocks - 1:
            dk_ref[...] = dk
            dv_ref[...] = dv
        else:
            dk_ref[:, :seen, :] += dk
            dv_ref[:, :seen, :] += dv
        dq = dq.reshape(n_slots, span, HD)
        for t in range(n_slots):
            lead = rotated(dq[t, :, :128], cos_ref[t, own, :], -sin_ref[t, own, :])
            grad_ref[t, own, :128] = lead.astype(BF)
            grad_ref[t, own, 128:HD] = dq[t, :, 128:].astype(BF)
    for t in range(n_slots):
        lead = rotated(dk_ref[t, :, :128] * scale, cos_ref[t], -sin_ref[t])
        grad_ref[t, :, HD : HD + 128] = lead.astype(BF)
        grad_ref[t, :, HD + 128 : 2 * HD] = (dk_ref[t, :, 128:] * scale).astype(BF)
        grad_ref[t, :, 2 * HD :] = dv_ref[t].astype(BF)
        summed = jnp.sum(grad_ref[t].astype(F32), axis=0, keepdims=True)
        bias_ref[0] = summed if t == 0 else bias_ref[0] + summed


def whole_spec(shape):
    return pl.BlockSpec(shape, lambda h: (0,) * len(shape))


def head_spec(n_slots, rows, width):
    return pl.BlockSpec((n_slots, rows, width), lambda h: (0, 0, h))


def attend(tables, qkv):
    posq, posk, cosines, sines = tables
    n_slots, rows, width = qkv.shape
    heads = width // (3 * HD)
    pairs = (n_slots * rows) ** 2 // 2 * heads
    return pl.pallas_call(
        functools.partial(attend_kernel, posk.shape[0]),
        grid=(heads,),
        in_specs=[whole_spec(t.shape) for t in tables] + [head_spec(n_slots, rows, 3 * HD)],
        out_specs=[head_spec(n_slots, rows, 3 * HD), head_spec(n_slots, rows, HD)],
        out_shape=[
            jax.ShapeDtypeStruct(qkv.shape, BF),
            jax.ShapeDtypeStruct((n_slots, rows, heads * HD), BF),
        ],
        cost_estimate=pl.CostEstimate(
            flops=4 * pairs * HD, bytes_accessed=qkv.size * 8, transcendentals=pairs
        ),
        compiler_params=pltpu.CompilerParams(vmem_limit_bytes=48 << 20),
        name="attend",
    )(posq, posk, cosines, sines, qkv)


def attend_back(tables, low, dmix):
    n_slots, rows, width = low.shape
    heads = width // (3 * HD)
    pairs = (n_slots * rows) ** 2 // 2 * heads
    return pl.pallas_call(
        functools.partial(attend_back_kernel, tables[1].shape[0]),
        grid=(heads,),
        in_specs=[whole_spec(t.shape) for t in tables]
        + [head_spec(n_slots, rows, 3 * HD), head_spec(n_slots, rows, HD)],
        out_specs=[
            head_spec(n_slots, rows, 3 * HD),
            pl.BlockSpec((1, 1, 3 * HD), lambda h: (h, 0, 0)),
        ],
        out_shape=[
            jax.ShapeDtypeStruct(low.shape, BF),
            jax.ShapeDtypeStruct((heads, 1, 3 * HD), F32),
        ],
        scratch_shapes=[pltpu.VMEM((n_slots, rows, HD), F32)] * 2,
        cost_estimate=pl.CostEstimate(
            flops=10 * pairs * HD, bytes_accessed=low.size * 5, transcendentals=pairs
        ),
        compiler_params=pltpu.CompilerParams(vmem_limit_bytes=48 << 20),
        name="attend_back",
    )(*tables, low, dmix)


def slot_rows(blocks, s):
    n = (len(blocks) + 1) // 2
    if s == 0:
        return blocks[0][...].astype(F32)
    return blocks[s][...].astype(F32) + blocks[2 * n - 1 - s][...].astype(F32)


def part_of(me_ref, s):
    return lax.rem(me_ref[0] - s + me_ref[1], me_ref[1])


def cdf_and_slope(x):
    size = jnp.abs(x)
    bell = jnp.exp(-0.5 * x * x)
    t = 1.0 / (1.0 + (0.3275911 * SQRT_HALF) * size)
    poly = ((((1.061405429 * t - 1.453152027) * t) + 1.421413741) * t - 0.284496736) * t + 0.254829592
    tail = 0.5 * poly * t * bell
    cdf = jnp.where(x >= 0, 1.0 - tail, tail)
    return cdf, cdf + x * bell * INV_ROOT_TWO_PI


def norm_qkv_kernel(n_blocks, me_ref, vectors_ref, bias_ref, *refs):
    blocks, w_hbm = refs[:n_blocks], refs[n_blocks]
    one_ref, two_ref, unit_ref, qkv_ref, w_ref, sem = refs[n_blocks + 1 :]
    n_slots, block, width = one_ref.shape
    n_qkv = w_ref.shape[1]
    first = pl.program_id(0) == 0
    copy = pltpu.make_async_copy(w_hbm.at[:, pl.ds(0, n_qkv)], w_ref, sem)

    @pl.when(first)
    def _():
        copy.start()

    for s in range(n_slots):
        rows = slot_rows(blocks, s)
        centred = rows - jnp.mean(rows, axis=-1, keepdims=True)
        unit = centred * lax.rsqrt(jnp.mean(centred * centred, axis=-1, keepdims=True) + EPSILON)
        part = part_of(me_ref, s)
        one_ref[part] = (unit * vectors_ref[0:1] + vectors_ref[1:2]).astype(BF)
        two_ref[part] = (unit * vectors_ref[2:3] + vectors_ref[3:4]).astype(BF)
        unit_ref[part] = unit.astype(BF)

    @pl.when(first)
    def _():
        copy.wait()

    one = one_ref[...].reshape(n_slots * block, width)
    tile = 768
    for c in range(0, n_qkv, tile):
        out = jnp.dot(one, w_ref[:, c : c + tile], preferred_element_type=F32)
        out = out + bias_ref[:, c : c + tile]
        qkv_ref[:, :, c : c + tile] = out.reshape(n_slots, block, tile)


def hidden_kernel(two_ref, w_ref, bias_ref, act_ref, slope_ref):
    pre = jnp.dot(two_ref[...], w_ref[...], preferred_element_type=F32) + bias_ref[...]
    cdf, slope = cdf_and_slope(pre)
    act_ref[...] = (pre * cdf).astype(BF)
    slope_ref[...] = slope.astype(BF)


def big(limit=56):
    return pltpu.CompilerParams(vmem_limit_bytes=limit << 20)


def cost(flops, moved, special=0):
    return pl.CostEstimate(flops=int(flops) // 16, bytes_accessed=int(moved) // 16, transcendentals=int(special) // 16)


def norm_qkv(chain, vectors, bias, w, n_qkv):
    n = chain.n
    rows, width = chain.x.shape
    block = 64
    me = jnp.stack([chain.me, jnp.int32(n)])
    blocks = [chain.x] + chain.left + chain.right

    def out(cols, dtype):
        return (
            jax.ShapeDtypeStruct((n, rows, cols), dtype),
            pl.BlockSpec((n, block, cols), lambda i, me: (0, i, 0)),
        )

    shapes, specs = zip(out(width, BF), out(width, BF), out(width, BF), out(n_qkv, F32))
    total = n * rows
    return pl.pallas_call(
        functools.partial(norm_qkv_kernel, len(blocks)),
        grid_spec=pltpu.PrefetchScalarGridSpec(
            num_scalar_prefetch=1,
            grid=(rows // block,),
            in_specs=[
                pl.BlockSpec(vectors.shape, lambda i, me: (0, 0)),
                pl.BlockSpec(bias.shape, lambda i, me: (0, 0)),
            ]
            + [pl.BlockSpec((block, width), lambda i, me: (i, 0))] * len(blocks)
            + [pl.BlockSpec(memory_space=pl.ANY)],
            out_specs=list(specs),
            scratch_shapes=[pltpu.VMEM((width, n_qkv), BF), pltpu.SemaphoreType.DMA],
        ),
        out_shape=list(shapes),
        cost_estimate=cost(2 * total * width * n_qkv, 10 * total * width + width * n_qkv * 2),
        compiler_params=big(),
        name="norm_qkv",
    )(me, vectors, bias, *blocks, w)


def hidden_of(two, w, bias, n_qkv):
    total, width = two.shape
    n_ff, tile = w.shape[1] - n_qkv, 256
    skip = n_qkv // tile
    columns = pl.BlockSpec((total, tile), lambda j: (0, j))
    return pl.pallas_call(
        hidden_kernel,
        grid=(n_ff // tile,),
        in_specs=[
            resident(two.shape),
            pl.BlockSpec((width, tile), lambda j: (0, j + skip)),
            pl.BlockSpec((1, tile), lambda j: (0, j + skip)),
        ],
        out_specs=[columns, columns],
        out_shape=[jax.ShapeDtypeStruct((total, n_ff), BF)] * 2,
        cost_estimate=cost(2 * total * width * n_ff, 2 * width * n_ff + 8 * total * n_ff, total * n_ff),
        compiler_params=big(),
        name="hidden",
    )(two, w, bias)


def arrange_kernel(me_ref, *refs):
    blocks, out_ref = refs[:-1], refs[-1]
    n = (len(blocks) + 1) // 2
    for s in range(n):
        part = part_of(me_ref, s)
        if s == 0:
            out_ref[part] = blocks[0][...]
        else:
            out_ref[part] = blocks[s][...] + blocks[2 * n - 1 - s][...]


def arrange(chain):
    n = chain.n
    rows, width = chain.x.shape
    block = 64
    me = jnp.stack([chain.me, jnp.int32(n)])
    blocks = [chain.x] + chain.left + chain.right
    return pl.pallas_call(
        arrange_kernel,
        grid_spec=pltpu.PrefetchScalarGridSpec(
            num_scalar_prefetch=1,
            grid=(rows // block,),
            in_specs=[pl.BlockSpec((block, width), lambda i, me: (i, 0))] * len(blocks),
            out_specs=pl.BlockSpec((n, block, width), lambda i, me: (0, i, 0)),
        ),
        out_shape=jax.ShapeDtypeStruct((n, rows, width), BF),
        cost_estimate=cost(0, 6 * n * rows * width),
        compiler_params=big(),
        name="arrange",
    )(me, *blocks)


def nt(a, b):
    return lax.dot_general(a, b, (((1,), (1,)), ((), ())), preferred_element_type=F32)


def tn(a, b):
    return lax.dot_general(a, b, (((0,), (0,)), ((), ())), preferred_element_type=F32)


def resident(shape):
    return pl.BlockSpec(shape, lambda j: (0,) * len(shape), pipeline_mode=pl.Buffered(1))


def head_rows(dense_ref, h):
    n, _, e, cols = dense_ref.shape
    return dense_ref[:, h].reshape(n * e, cols)


def branch_kernel(mixed_ref, act_ref, dense_ref, w_ref, out_ref):
    total = nt(act_ref[...], w_ref[...])
    for h in range(dense_ref.shape[1]):
        total += jnp.dot(
            mixed_ref[:, h * HD : (h + 1) * HD],
            head_rows(dense_ref, h),
            preferred_element_type=F32,
        )
    out_ref[...] = total.astype(BF)


def branch_of(mixed, act, dense, w_fc2):
    total, width, tile = act.shape[0], w_fc2.shape[0], 512
    return pl.pallas_call(
        branch_kernel,
        grid=(width // tile,),
        in_specs=[
            resident(mixed.shape),
            resident(act.shape),
            pl.BlockSpec(dense.shape[:3] + (tile,), lambda j: (0, 0, 0, j)),
            pl.BlockSpec((tile, w_fc2.shape[1]), lambda j: (j, 0)),
        ],
        out_specs=pl.BlockSpec((total, tile), lambda j: (0, j)),
        out_shape=jax.ShapeDtypeStruct((total, width), BF),
        cost_estimate=cost(2 * total * (dense.size + w_fc2.size), 2 * (act.size * 3 + w_fc2.size)),
        compiler_params=big(),
        name="branch",
    )(mixed, act, dense, w_fc2)


def back_in_kernel(g_ref, dense_ref, w_ref, slope_ref, dmix_ref, pre_ref, bias_ref):
    @pl.when(pl.program_id(0) == 0)
    def _():
        for h in range(dense_ref.shape[1]):
            dmix_ref[:, h * HD : (h + 1) * HD] = nt(g_ref[...], head_rows(dense_ref, h)).astype(BF)

    d_act = jnp.dot(g_ref[...], w_ref[...], preferred_element_type=F32)
    d_pre = (d_act * slope_ref[...].astype(F32)).astype(BF)
    pre_ref[...] = d_pre
    bias_ref[...] = jnp.sum(d_pre.astype(F32), axis=0, keepdims=True)


def back_in_of(g, dense, w_fc2, slope):
    total, width = g.shape
    n_ff, tile = w_fc2.shape[1], 512
    heads = dense.shape[1]
    columns = pl.BlockSpec((total, tile), lambda j: (0, j))
    return pl.pallas_call(
        back_in_kernel,
        grid=(n_ff // tile,),
        in_specs=[
            resident(g.shape),
            resident(dense.shape),
            pl.BlockSpec((width, tile), lambda j: (0, j)),
            columns,
        ],
        out_specs=[
            pl.BlockSpec((total, heads * HD), lambda j: (0, 0)),
            columns,
            pl.BlockSpec((1, tile), lambda j: (0, j)),
        ],
        out_shape=[
            jax.ShapeDtypeStruct((total, heads * HD), BF),
            jax.ShapeDtypeStruct((total, n_ff), BF),
            jax.ShapeDtypeStruct((1, n_ff), F32),
        ],
        cost_estimate=cost(2 * total * (dense.size + w_fc2.size), 2 * (g.size * 3 + w_fc2.size)),
        compiler_params=big(),
        name="back_in",
    )(g, dense, w_fc2, slope)


def back_out_kernel(vectors_ref, dqkv_ref, pre_ref, w_ref, unit_ref, e_ref, sums_ref):
    n_qkv = dqkv_ref.shape[1]
    one = nt(dqkv_ref[...], w_ref[:, :n_qkv])
    two = nt(pre_ref[...], w_ref[:, n_qkv:])
    unit = unit_ref[...].astype(F32)
    e_ref[...] = (one * vectors_ref[0:1] + two * vectors_ref[2:3]).astype(BF)
    sums_ref[0:1] = jnp.sum(one * unit, axis=0, keepdims=True)
    sums_ref[1:2] = jnp.sum(one, axis=0, keepdims=True)
    sums_ref[2:3] = jnp.sum(two * unit, axis=0, keepdims=True)
    sums_ref[3:4] = jnp.sum(two, axis=0, keepdims=True)


def back_out_of(vectors, dqkv, pre, w, unit):
    total, width = unit.shape
    tile = 256
    columns = pl.BlockSpec((total, tile), lambda j: (0, j))
    return pl.pallas_call(
        back_out_kernel,
        grid=(width // tile,),
        in_specs=[
            pl.BlockSpec((vectors.shape[0], tile), lambda j: (0, j)),
            resident(dqkv.shape),
            resident(pre.shape),
            pl.BlockSpec((tile, w.shape[1]), lambda j: (j, 0)),
            columns,
        ],
        out_specs=[columns, pl.BlockSpec((4, tile), lambda j: (0, j))],
        out_shape=[
            jax.ShapeDtypeStruct((total, width), BF),
            jax.ShapeDtypeStruct((4, width), F32),
        ],
        cost_estimate=cost(2 * total * w.size, 2 * (unit.size * 4 + w.size)),
        compiler_params=big(),
        name="back_out",
    )(vectors, dqkv, pre, w, unit)


def grad_kernel(count, me_ref, *refs):
    lhs, rhs, (sent_ref, kept_ref) = refs[:count], refs[count : 2 * count], refs[-2:]
    total = tn(lhs[0][...], rhs[0][...])
    for a, b in zip(lhs[1:], rhs[1:]):
        total += tn(a[...], b[...])
    step, half = pl.program_id(0), pl.num_programs(0) // 2

    @pl.when(step < half)
    def _():
        sent_ref[0] = total.astype(BF)

    @pl.when(step >= half)
    def _():
        kept_ref[0] = total.astype(BF)


def grad_of(parity, lhs, rhs, cuts, name):
    total, m = lhs[0].shape
    n, tile, half = rhs[0].shape[1], m // cuts, cuts // 2
    shape = jax.ShapeDtypeStruct((half, tile, n), BF)

    def left(j, me):
        return (0, jnp.where(j < half, 2 * j + 1 - me[0], 2 * (j - half) + me[0]))

    return pl.pallas_call(
        functools.partial(grad_kernel, len(lhs)),
        grid_spec=pltpu.PrefetchScalarGridSpec(
            num_scalar_prefetch=1,
            grid=(cuts,),
            in_specs=[pl.BlockSpec((total, tile), left)] * len(lhs)
            + [
                pl.BlockSpec(r.shape, lambda j, me: (0, 0), pipeline_mode=pl.Buffered(1))
                for r in rhs
            ],
            out_specs=[
                pl.BlockSpec((1, tile, n), lambda j, me: (jnp.minimum(j, half - 1), 0, 0)),
                pl.BlockSpec((1, tile, n), lambda j, me: (jnp.maximum(j - half, 0), 0, 0)),
            ],
        ),
        out_shape=[shape, shape],
        cost_estimate=cost(2 * len(lhs) * total * m * n, 4 * total * (m + n) + 2 * m * n),
        compiler_params=big(),
        name=name,
    )(parity, *lhs, *rhs)


def head_grad_kernel(count, me_ref, *refs):
    lhs, rhs, (sent_ref, kept_ref) = refs[:count], refs[count : 2 * count], refs[-2:]
    total = tn(lhs[0][...], rhs[0][...])
    for a, b in zip(lhs[1:], rhs[1:]):
        total += tn(a[...], b[...])
    half, _, e, n = sent_ref.shape
    total = total.astype(BF).reshape(half, 2, e, n)
    even = me_ref[0] == 0
    kept_ref[:, 0] = jnp.where(even, total[:, 0], total[:, 1])
    sent_ref[:, 0] = jnp.where(even, total[:, 1], total[:, 0])


def head_grad_of(parity, lhs, rhs, cuts, name):
    total, m = lhs[0].shape
    n, e = rhs[0].shape[1], HD // cuts
    shape = jax.ShapeDtypeStruct((cuts // 2, m // HD, e, n), BF)
    return pl.pallas_call(
        functools.partial(head_grad_kernel, len(lhs)),
        grid_spec=pltpu.PrefetchScalarGridSpec(
            num_scalar_prefetch=1,
            grid=(m // HD,),
            in_specs=[pl.BlockSpec((total, HD), lambda j, me: (0, j))] * len(lhs)
            + [
                pl.BlockSpec(r.shape, lambda j, me: (0, 0), pipeline_mode=pl.Buffered(1))
                for r in rhs
            ],
            out_specs=[pl.BlockSpec((cuts // 2, 1, e, n), lambda j, me: (0, j, 0, 0))] * 2,
        ),
        out_shape=[shape, shape],
        cost_estimate=cost(2 * len(lhs) * total * m * n, 4 * total * (m + n) + 2 * m * n),
        compiler_params=big(),
        name=name,
    )(parity, *lhs, *rhs)


def unit_of(rows):
    centred = rows - jnp.mean(rows, axis=-1, keepdims=True)
    scaling = lax.rsqrt(jnp.mean(centred * centred, axis=-1, keepdims=True) + EPSILON)
    return centred * scaling, scaling


def per_device(
    hidden_in,
    lengths,
    dealing,
    cotangent,
    attn_gain,
    attn_shift,
    ffn_gain,
    ffn_shift,
    qkv_weight,
    qkv_bias,
    dense_weight,
    dense_bias,
    fc1_weight,
    fc1_bias,
    fc2_weight,
    fc2_bias,
):
    n_t, n_d = lax.axis_size("tensor"), lax.axis_size("dp")
    my_t, my_d = lax.axis_index("tensor"), lax.axis_index("dp")
    micros, seqs, piece, width = hidden_in.shape
    heads = qkv_weight.shape[1]
    rows = n_d * piece
    n_blocks = 4

    def deal(x):
        return lax.all_to_all(x, "dp", split_axis=0, concat_axis=0, tiled=True).reshape(rows, width)

    def undeal(x):
        return lax.all_to_all(
            x.reshape(seqs, piece, width), "dp", split_axis=0, concat_axis=0, tiled=True
        )

    env = {}

    def stage(chains, computes=()):
        for chain in chains:
            chain.step()
        for fn in computes:
            fn()
        keys = list(env)
        values = [env[k] for k in keys]
        for chain in chains:
            values += chain.live()
        out = list(lax.optimization_barrier(tuple(values)))
        env.update(zip(keys, out))
        at = len(keys)
        for chain in chains:
            count = len(chain.live())
            chain.set_live(out[at : at + count])
            at += count

    def after(x):
        return lax.optimization_barrier((x, env["mark"]))[0]

    eighth = width // (n_d * n_t)
    n_six = 6 * n_t * eighth
    env["x0"] = deal(hidden_in[0])
    env["mark"] = jnp.concatenate(
        [attn_gain, attn_shift, ffn_gain, ffn_shift, dense_bias, fc2_bias]
    )
    stage([])

    n_qkv = heads * 3 * HD
    near = jnp.concatenate([after(qkv_weight).reshape(-1, n_qkv), after(fc1_weight)], axis=1)
    w_near = lax.all_gather(near, "dp", axis=0, tiled=True)

    parts = jnp.arange(n_t, dtype=jnp.int32)
    local = jnp.arange(rows, dtype=jnp.int32)
    positions = ((local // piece) * n_t + parts[:, None]) * piece + local % piece
    freqs = jnp.exp(jnp.arange(ROT // 2, dtype=F32) * (-2.0 * math.log(ROPE_BASE) / ROT))
    phases = positions.astype(F32)[..., None] * freqs
    flat = jnp.zeros((n_t, rows, 128 - ROT), F32)
    cosines = jnp.concatenate([jnp.cos(phases), jnp.cos(phases), flat + 1.0], axis=-1)
    sines = jnp.concatenate([-jnp.sin(phases), jnp.sin(phases), flat], axis=-1)
    picked = dealing == my_d
    seq_lens = jnp.sum(jnp.where(picked, lengths, 0), axis=1)
    posq = positions[..., None]

    def tables(m):
        keyed = jnp.where(positions < seq_lens[m], positions, FAR)
        span = rows // n_blocks
        lists = []
        for b in range(n_blocks):
            seen = keyed[:, : span * (b + 1)].reshape(1, -1)
            lists.append(jnp.pad(seen, ((0, 0), (0, n_t * rows - seen.shape[1]))))
        return (posq, jnp.stack(lists), cosines, sines)

    all_tables = [tables(m) for m in range(micros)]
    sum_g = jnp.sum(cotangent.astype(F32), axis=(0, 1, 2))

    chains = {"x0": GatherChain(env["x0"], "tensor", n_t)}
    pending = {}

    def join(*keys):
        def fn():
            for key in keys:
                env[key] = pending.pop(key)

        return fn

    def vectors_over_tensor():
        vectors = direct_gather(env["mark"], "tensor", n_t)
        env["six"] = jnp.concatenate(
            [vectors.reshape(-1), qkv_bias.reshape(-1), fc1_bias.reshape(-1)]
        )

    def vectors_over_dp():
        env["six"] = direct_gather(env["six"], "dp", n_d)

    def deal_x1():
        pending["x1"] = deal(after(hidden_in[1]))

    last = n_t - 2

    def at(i, *plan):
        if i < last:
            return list(plan[i]) if i < len(plan) else []
        return [fn for entry in plan[i:] for fn in entry]

    for i in range(n_t - 1):
        stage(
            [chains["x0"]],
            at(i, [vectors_over_tensor, deal_x1], [vectors_over_dp, join("x1")]),
        )
    w_fc2 = lax.all_gather(after(fc2_weight.T), "dp", axis=0, tiled=True)
    w_dense = lax.all_gather(after(dense_weight), "dp", axis=0, tiled=False)
    own_x = [env.pop("x0"), env.pop("x1")]
    six = env.pop("six")
    vectors = six[:, :n_six].reshape(n_d, n_t, 6, eighth).transpose(2, 0, 1, 3)
    vectors = vectors.reshape(6, width).astype(F32)
    out_shift = vectors[4] + vectors[5]
    rest = six[:, n_six:].astype(F32)
    n_qb = qkv_bias.size
    bias = jnp.concatenate(
        [
            rest[:, :n_qb].reshape(n_d, heads, -1).transpose(1, 0, 2).reshape(1, -1),
            rest[:, n_qb:].reshape(n_d, heads, -1).transpose(1, 0, 2).reshape(1, -1),
        ],
        axis=1,
    )
    env["mark"], env["bias"] = vectors, bias

    def norm_qkv_of(m):
        def fn():
            outs = norm_qkv(chains[f"x{m}"], env["mark"], env["bias"], w_near, n_qkv)
            for key, value in zip(("one", "two", "unit", "qkv"), outs):
                env[f"{key}{m}"] = value if key == "qkv" else value.reshape(n_t * rows, -1)

        return fn

    def hidden(m):
        def fn():
            env[f"act{m}"], env[f"slope{m}"] = hidden_of(
                env[f"two{m}"], w_near, env["bias"], n_qkv
            )

        return fn

    def attend_of(m):
        def fn():
            low, mixed = attend(all_tables[m], env.pop(f"qkv{m}"))
            env[f"low{m}"], env[f"mixed{m}"] = low, mixed.reshape(n_t * rows, -1)

        return fn

    def branch(m):
        def fn():
            parts = branch_of(env[f"mixed{m}"], env[f"act{m}"], w_dense, w_fc2)
            env[f"branch{m}"] = parts

        return fn

    def scattered_rows(name):
        return lax.psum_scatter(env.pop(name), "tensor", scatter_dimension=0, tiled=True)

    def output_of(m):
        def fn():
            total = env.pop(f"so{m}").astype(F32)
            out = (own_x[m].astype(F32) + total + out_shift).astype(BF)
            env[f"output{m}"] = undeal(out)

        return fn

    def arrange_g(m):
        def fn():
            env[f"g{m}"] = arrange(chains[f"g{m}"]).reshape(n_t * rows, width)

        return fn

    def back_in(m):
        def fn():
            if f"g{m}" not in env:
                arrange_g(m)()
            dmix, env[f"pre{m}"], env[f"b1{m}"] = back_in_of(
                env[f"g{m}"], w_dense, w_fc2, env.pop(f"slope{m}")
            )
            env[f"dmix{m}"] = dmix.reshape(n_t, rows, -1)

        return fn

    def back_attend(m):
        def fn():
            d_qkv, env[f"bq{m}"] = attend_back(
                all_tables[m], env.pop(f"low{m}"), env.pop(f"dmix{m}")
            )
            env[f"dqkv{m}"] = d_qkv.reshape(n_t * rows, -1)

        return fn

    def back_out(m):
        def fn():
            env[f"e{m}"], env[f"sums{m}"] = back_out_of(
                env["mark"], env[f"dqkv{m}"], env[f"pre{m}"], w_near, env.pop(f"unit{m}")
            )

        return fn

    def input_of(m):
        def fn():
            total = env.pop(f"si{m}").astype(F32)
            unit, scaling = unit_of(own_x[m].astype(F32))
            back = scaling * (
                total
                - jnp.mean(total, axis=-1, keepdims=True)
                - unit * jnp.mean(total * unit, axis=-1, keepdims=True)
            )
            env[f"input{m}"] = undeal((own_g[m].astype(F32) + back).astype(BF))

        return fn

    def pair(key):
        return [env[f"{key}{m}"] for m in range(micros)]

    parity = (my_d % 2)[None]
    swap = [(i, i ^ 1) for i in range(n_d)]
    same_parity = [list(range(p, n_d, 2)) for p in range(2)]

    def fc2_grads():
        env["w2_sent"], env["w2_kept"] = grad_of(parity, pair("g"), pair("act"), n_d, "grad_fc2")

    def dense_grads():
        halves = head_grad_of(parity, pair("mixed"), pair("g"), n_d, "grad_dense")
        env["wd_sent"], env["wd_kept"] = (h.reshape(n_d // 2, -1, width) for h in halves)

    def fc1_grads():
        env["w1_sent"], env["w1_kept"] = grad_of(parity, pair("two"), pair("pre"), n_d, "grad_fc1")

    def qkv_grads():
        env["wq_sent"], env["wq_kept"] = grad_of(parity, pair("one"), pair("dqkv"), n_d, "grad_qkv")

    def swapped(key):
        def fn():
            env[f"{key}_got"] = lax.ppermute(env.pop(f"{key}_sent"), "dp", swap)

        return fn

    def spread(key):
        both_cores = env.pop(f"{key}_kept").astype(F32) + env.pop(f"{key}_got").astype(F32)
        return lax.all_to_all(
            both_cores.astype(BF),
            "dp",
            split_axis=0,
            concat_axis=0,
            axis_index_groups=same_parity,
            tiled=True,
        )

    def both(*fns):
        def fn():
            for each in fns:
                each()

        return fn

    def summed(key):
        return jnp.sum(env.pop(key).astype(F32), axis=0)

    def fc2_final():
        env["grad_fc2"] = summed("w2").T

    def fc1_final():
        env["grad_fc1"] = summed("w1")

    def qkv_final():
        env["grad_qkv"] = summed("wq").reshape(-1, heads, 3 * HD)

    def dense_final():
        env["grad_dense"] = summed("wd").reshape(heads, -1, width)

    def gather_chain(name, x):
        chains[name] = GatherChain(after(x), "tensor", n_t)
        return chains[name]

    def deal_g():
        pending["g"] = lax.all_to_all(after(cotangent), "dp", split_axis=1, concat_axis=1, tiled=True)

    def spread_later(*keys):
        for key in keys:
            pending[key] = spread(key)

    def steps_of(chain, *plan):
        for i in range(chain.steps()):
            stage([chain], at(i, *plan))

    steps_of(
        gather_chain("x1", own_x[1]), [norm_qkv_of(0)], [attend_of(0), hidden(0), deal_g], [join("g")]
    )
    own_g = list(env.pop("g").reshape(micros, rows, width))
    steps_of(
        gather_chain("g0", own_g[0]), [branch(0)], [norm_qkv_of(1)], [attend_of(1), hidden(1)]
    )
    pending["so0"] = scattered_rows("branch0")
    steps_of(
        gather_chain("g1", own_g[1]),
        [branch(1), arrange_g(0)],
        [back_in(0), back_attend(0)],
        [back_out(0), join("so0")],
    )
    pending["so1"] = scattered_rows("branch1")
    pending["si0"] = scattered_rows("e0")
    stage([], [arrange_g(1), fc2_grads, swapped("w2"), back_in(1), output_of(0)])
    spread_later("w2")
    stage([], [fc1_grads, swapped("w1"), back_attend(1), back_out(1), join("w2", "so1")])
    pending["si1"] = scattered_rows("e1")
    spread_later("w1")
    sums = jnp.concatenate([env["sums0"] + env["sums1"], sum_g[None]], axis=0)
    sums = sums.reshape(5, n_d, n_t, eighth).transpose(1, 2, 0, 3).reshape(n_d, -1)
    qkvb = (env["bq0"] + env["bq1"]).reshape(heads, n_d, -1).transpose(1, 0, 2).reshape(n_d, -1)
    fc1b = (env["b10"] + env["b11"]).reshape(heads, n_d, -1).transpose(1, 0, 2).reshape(n_d, -1)
    small = SmallScatter(jnp.concatenate([sums, qkvb, fc1b], axis=1), "dp", n_d)
    stage([small], [qkv_grads, swapped("wq"), dense_grads, swapped("wd"), fc2_final, join("w1")])
    spread_later("wq")
    stage([small], [output_of(1), fc1_final, join("wq")])
    spread_later("wd")
    stage([small], [qkv_final, join("wd", "si0")])
    while small.bit:
        stage([small])
    small_out = small.out[0]
    n_sum = 5 * n_t * eighth
    env["mine"] = direct_scatter(small_out[:n_sum].reshape(n_t, 5 * eighth), "tensor", n_t)
    stage([], [input_of(0), dense_final, join("si1")])
    input_of(1)()

    outputs = pair("output")
    grads_in = pair("input")

    small = small_out
    mine = env["mine"].reshape(5, eighth)
    qkvb = small[n_sum : n_sum + n_qb].reshape(heads, -1)
    fc1b = small[n_sum + n_qb :].reshape(heads, -1)

    return (
        jnp.stack(outputs),
        jnp.stack(grads_in),
        mine[0],
        mine[1],
        mine[2],
        mine[3],
        env["grad_qkv"],
        qkvb,
        env["grad_dense"],
        mine[4],
        env["grad_fc1"],
        fc1b,
        env["grad_fc2"],
        mine[4],
    )


def solution(mesh):
    rows = P(None, None, ("dp", "tensor"), None)
    vector = P(("dp", "tensor"))
    return jax.shard_map(
        per_device,
        mesh=mesh,
        in_specs=(
            rows,
            P(),
            P(),
            rows,
            vector,
            vector,
            vector,
            vector,
            P("dp", "tensor", None),
            P("tensor", "dp"),
            P("tensor", "dp", None),
            vector,
            P("dp", "tensor"),
            P("tensor", "dp"),
            P("tensor", "dp"),
            vector,
        ),
        out_specs=(
            rows,
            rows,
            vector,
            vector,
            vector,
            vector,
            P("dp", "tensor", None),
            P("tensor", "dp"),
            P("tensor", "dp", None),
            vector,
            P("dp", "tensor"),
            P("tensor", "dp"),
            P("tensor", "dp"),
            vector,
        ),
        check_vma=False,
    )
```

time: 1120 us -> 825 us (0.74)
  matrix products: 305 us -> 0 us
  Pallas kernels: 34.8 us -> 317 us
  waiting for transfers between devices: 351 us -> 254 us
  starting transfers between devices: 222 us -> 127 us
  other arithmetic: 106 us -> 66.1 us
  blocking collectives: 23.1 us -> 0 us
    dot_general x24 -> x0, matrix products: 305 us -> none  [dot(): lax.dot_general(a, b, (dims, ((), ())), preferred_element_type=F32)]
    pallas_call x0 -> x16, Pallas kernels: none -> 282 us  [the longest x3 71.3 us: grad_of(): pl.pallas_call(functools.partial(grad_kernel, len(lhs)), grid_spec=pltpu....]
    ppermute x58 -> x44, waiting for transfers between devices: 337 us -> 196 us  [the longest x12 120 us: step(): self.right.append(lax.ppermute(to_left, self.axis, pairs))]
    ppermute x58 -> x44, starting transfers between devices: 194 us -> 77 us  [the longest x12 34.4 us: step(): self.left.append(lax.ppermute(to_right, self.axis, pairs))]
    add x20 -> x8, other arithmetic: 32.2 us -> 0.24 us  [the longest x1 0.13 us: per_device(): positions = (local // piece * n_t + parts[:, None]) * piece + local % piece]
    all_to_all x0 -> x5, starting transfers between devices: none -> 23.6 us  [the longest x4 19.2 us: spread(): lax.all_to_all(both_cores.astype(BF), 'dp', split_axis=0, concat_axis=0,...]
    all_to_all x1 -> x0, blocking collectives: 23.1 us -> none  [deal(): lax.all_to_all(x, 'dp', split_axis=0, concat_axis=0, tiled=True)]
    all_to_all x4, waiting for transfers between devices: 0.76 us -> 23.1 us  [undeal(): lax.all_to_all(x.reshape(seqs, piece, width), 'dp', split_axis=0, concat_...]
  transfers between devices with their start and end apart: 73 -> 62, of which waited for: 26 -> 22; matrix products, arithmetic and copies ran while one was open for 40% -> 9% of each run, Pallas kernels for 3% -> 39%
where the time goes in v2:
time: 825 us; the launch traced here: 814 us
  Pallas kernels  317 us (38%)
  waiting for transfers between devices  254 us (31%)
  starting transfers between devices  127 us (15%)
  other arithmetic  66.1 us (8%)
  local copies, waits for them, and re-layouts  33.3 us (4%)
  between operations  15.5 us (2%)
    ppermute x12, waiting for transfers between devices, step(): self.right.append(lax.ppermute(to_left, self.axis, pairs))  120 us
    pallas_call x3, Pallas kernels, grad_of(): pl.pallas_call(functools.partial(grad_kernel, len(lhs)), grid_spec=pltpu....  71.3 us
    pallas_call x2, Pallas kernels, back_out_of(): pl.pallas_call(back_out_kernel, grid=(width // tile,), in_specs=[pl.Block...  45 us
    pallas_call x2, Pallas kernels, hidden_of(): pl.pallas_call(hidden_kernel, grid=(n_ff // tile,), in_specs=[resident(tw...  39.6 us
    pallas_call x2, Pallas kernels, norm_qkv(): pl.pallas_call(functools.partial(norm_qkv_kernel, len(blocks)), grid_spec...  38.5 us
    ppermute x10, waiting for transfers between devices, direct_gather(): got = jnp.stack([x] + [lax.ppermute(x, axis, pairs) for pairs in shifts(n)])  38.2 us
    ppermute x3, waiting for transfers between devices, step(): lax.ppermute(sent, self.axis, [(i, i ^ bit) for i in range(self.n)])  36.6 us
    ppermute x12, starting transfers between devices, step(): self.left.append(lax.ppermute(to_right, self.axis, pairs))  34.4 us
  transfers between devices with their start and end apart: 62, of which 22 were waited for; matrix products, arithmetic and copies ran while one was open for 9% of the time, Pallas kernels for 39%

profile of v2, /device:TPU:0, one launch (start us, length us, event | category | flops | bytes accessed | tf_op | source)
XLA Modules:
  0.0 813.9 jit_solution(7867369431822848108)
XLA Ops:
  7.2 3.1 slice_bitcast_fusion
  10.3 5.3 all-to-all-start
  15.9 15.2 %all-to-all-done = bf16[8,32,2048]{2,1,0:T(8,128)(2,1)S(1)} async-done(((bf16[8,32,2048]{2,1,0:T(8,128)(2,1)}), bf16[8,32,2048]{2,1,0:T(8,128)(2,1)S(1)}, u32[]{:S(2)}, u32[]{:S(2)}) %all-to-all-start) | async-done | bytes 1048608 | tf_op jit(solution)/shard_map/all_to_all | solution.py:658
  34.1 5.6 collective-permute-start.3
  44.4 13.7 %collective-permute-done.2 = bf16[384]{0:T(512)(128)(2,1)S(1)} collective-permute-done((bf16[384]{0:T(512)(128)(2,1)S(1)}, bf16[384]{0:T(512)(128)(2,1)S(1)}, u32[]{:S(2)}, u32[]{:S(2)}) %collective-permute-start.2) | collective-permute-done | bytes 800 | tf_op jit(solution)/shard_map/ppermute | solution.py:103
  62.0 4.8 all-to-all-start.1
  70.5 18.9 %collective-permute-done.11 = bf16[1984]{0:T(1024)(128)(2,1)S(1)} collective-permute-done((bf16[1984]{0:T(1024)(128)(2,1)S(1)}, bf16[1984]{0:T(1024)(128)(2,1)S(1)}, u32[]{:S(2)}, u32[]{:S(2)}) %collective-permute-start.11) | collective-permute-done | bytes 4000 | tf_op jit(solution)/shard_map/ppermute | solution.py:103
  102.6 28.2 %collective-permute-done.15.refs_6_ = bf16[256,2048]{1,0:T(8,128)(2,1)} collective-permute-done((bf16[256,2048]{1,0:T(8,128)(2,1)}, bf16[256,2048]{1,0:T(8,128)(2,1)}, u32[]{:S(2)}, u32[]{:S(2)}) %collective-permute-start.15) | collective-permute-done | bytes 1048608 | tf_op jit(solution)/shard_map/ppermute | solution.py:40
  138.7 5.6 collective-permute-start.16
  146.0 19.3 %norm_qkv.2 = (bf16[4,256,2048]{2,1,0:T(8,128)(2,1)}, bf16[4,256,2048]{2,1,0:T(8,128)(2,1)}, bf16[4,256,2048]{2,1,0:T(8,128)(2,1)}, f32[4,256,1536]{2,1,0:T(8,128)}) custom-call(s32[2]{0:T(128)} %pad_add_fusion.2.me_ref, f32[6,2048]{1,0:T(8,128)} %convert_element_type.125.vectors_ref, f32[1,3584]{1,0:T(1,128)} %pad_maximum_fusion.3.bias_ref, ...), custom_call_target="tpu_custom_call" | custom-call | flops 402653184 | bytes 1703936 | tf_op jit(solution)/shard_map/norm_qkv/pallas_call | solution.py:345
  171.2 4.4 all-to-all-start.2
  176.6 19.8 %hidden.2 = (bf16[1024,2048]{1,0:T(8,128)(2,1)}, bf16[1024,2048]{1,0:T(8,128)(2,1)}) custom-call(bf16[1024,2048]{1,0:T(8,128)(2,1)} %bitcast.113, bf16[2048,3584]{1,0:T(8,128)(2,1)} %all-gather.5.cloned.1.call-done.refs_7_.w_ref, f32[1,3584]{1,0:T(1,128)} %pad_maximum_fusion.3.bias_ref), custom_call_target="tpu_custom_call" | custom-call | flops 536870912 | bytes 1572864 | tf_op jit(solution)/shard_map/hidden/pallas_call | solution.py:371
  196.4 7.9 attend.2
  210.2 25.6 %collective-permute-done.21.refs_6_ = bf16[256,2048]{1,0:T(8,128)(2,1)} collective-permute-done((bf16[256,2048]{1,0:T(8,128)(2,1)}, bf16[256,2048]{1,0:T(8,128)(2,1)}, u32[]{:S(2)}, u32[]{:S(2)}) %collective-permute-start.21) | collective-permute-done | bytes 1048608 | tf_op jit(solution)/shard_map/ppermute | solution.py:40
  239.8 5.6 collective-permute-start.22
  245.3 16.1 %branch.2 = bf16[1024,2048]{1,0:T(8,128)(2,1)} custom-call(bf16[1024,512]{1,0:T(8,128)(2,1)} %bitcast.83, bf16[1024,2048]{1,0:T(8,128)(2,1)} %get-tuple-element.467.act_ref.refs_2_, bf16[8,2,32,2048]{3,2,1,0:T(8,128)(2,1)} %bitcast.109, bf16[2048,2048]{1,0:T(8,128)(2,1)} %all-gather.7.cloned.1.call-done.w_ref), custom_call_target="tpu_custom_call" | custom-call | flops 671088640 | bytes 1310720 | tf_op jit(solution)/shard_map/branch/pallas_call | solution.py:449
  261.4 4.2 collective-permute-done.23.refs_4_
  269.8 19.2 %norm_qkv.3 = (bf16[4,256,2048]{2,1,0:T(8,128)(2,1)}, bf16[4,256,2048]{2,1,0:T(8,128)(2,1)}, bf16[4,256,2048]{2,1,0:T(8,128)(2,1)}, f32[4,256,1536]{2,1,0:T(8,128)}) custom-call(s32[2]{0:T(128)} %pad_add_fusion.2.me_ref, f32[6,2048]{1,0:T(8,128)} %convert_element_type.125.vectors_ref, f32[1,3584]{1,0:T(1,128)} %pad_maximum_fusion.3.bias_ref, ...), custom_call_target="tpu_custom_call" | custom-call | flops 402653184 | bytes 1703936 | tf_op jit(solution)/shard_map/norm_qkv/pallas_call | solution.py:345
  289.0 8.5 %collective-permute-done.25.refs_5_ = bf16[256,2048]{1,0:T(8,128)(2,1)} collective-permute-done((bf16[256,2048]{1,0:T(8,128)(2,1)}, bf16[256,2048]{1,0:T(8,128)(2,1)}, u32[]{:S(2)}, u32[]{:S(2)}) %collective-permute-start.25) | collective-permute-done | bytes 1048608 | tf_op jit(solution)/shard_map/ppermute | solution.py:40
  300.6 19.8 %hidden.3 = (bf16[1024,2048]{1,0:T(8,128)(2,1)}, bf16[1024,2048]{1,0:T(8,128)(2,1)}) custom-call(bf16[1024,2048]{1,0:T(8,128)(2,1)} %bitcast.115, bf16[2048,3584]{1,0:T(8,128)(2,1)} %all-gather.5.cloned.1.call-done.refs_7_.w_ref, f32[1,3584]{1,0:T(1,128)} %pad_maximum_fusion.3.bias_ref), custom_call_target="tpu_custom_call" | custom-call | flops 536870912 | bytes 1572864 | tf_op jit(solution)/shard_map/hidden/pallas_call | solution.py:371
  320.4 7.8 attend.3
  332.4 7.2 collective-permute-start.28
  339.6 6.1 arrange.2
  345.7 16.1 %branch.3 = bf16[1024,2048]{1,0:T(8,128)(2,1)} custom-call(bf16[1024,512]{1,0:T(8,128)(2,1)} %bitcast.85, bf16[1024,2048]{1,0:T(8,128)(2,1)} %get-tuple-element.473.act_ref.refs_3_, bf16[8,2,32,2048]{3,2,1,0:T(8,128)(2,1)} %bitcast.110, bf16[2048,2048]{1,0:T(8,128)(2,1)} %all-gather.7.cloned.1.call-done.w_ref), custom_call_target="tpu_custom_call" | custom-call | flops 671088640 | bytes 1310720 | tf_op jit(solution)/shard_map/branch/pallas_call | solution.py:449
  361.8 38.8 %collective-permute-done.29.refs_4_ = bf16[256,2048]{1,0:T(8,128)(2,1)} collective-permute-done((bf16[256,2048]{1,0:T(8,128)(2,1)S(1)}, bf16[256,2048]{1,0:T(8,128)(2,1)}, u32[]{:S(2)}, u32[]{:S(2)}) %collective-permute-start.29) | collective-permute-done | bytes 1048608 | tf_op jit(solution)/shard_map/ppermute | solution.py:40
  402.8 17.1 %back_in.2 = (bf16[1024,512]{1,0:T(8,128)(2,1)}, bf16[1024,2048]{1,0:T(8,128)(2,1)}, f32[1,2048]{1,0:T(1,128)}) custom-call(bf16[1024,2048]{1,0:T(8,128)(2,1)} %bitcast.89, bf16[8,2,32,2048]{3,2,1,0:T(8,128)(2,1)} %bitcast.111, bf16[2048,2048]{1,0:T(8,128)(2,1)} %all-gather.7.cloned.1.call-done.w_ref, bf16[1024,2048]{1,0:T(8,128)(2,1)} %get-tuple-element.430.slope_ref), custom_call_target="tpu_custom_call" | custom-call | flops 671088640 | bytes 1310720 | tf_op jit(solution)/shard_map/back_in/pallas_call | solution.py:483
  421.1 9.7 %attend_back.2 = (bf16[4,256,1536]{2,1,0:T(8,128)(2,1)S(1)}, f32[2,1,768]{2,1,0:T(1,128)S(1)}) custom-call(s32[4,256,1]{2,1,0:T(8,128)S(1)} %multiply_add_fusion.posq_ref, s32[4,1,1024]{2,1,0:T(1,128)S(1)} %pad_add_fusion.posk_ref, f32[4,256,128]{2,1,0:T(8,128)S(1)} %maximum_maximum_fusion.cos_ref, f32[4,256,128]{2,1,0:T(8,128)S(1)} %maximum_maximum_fusion.1.sin_ref, ...), custom_call_target="tpu_custom_call" | custom-call | flops 2684354560 | bytes 7864320 | tf_op jit(solution)/shard_map/attend_back/pallas_call | solution.py:239
  432.4 14.9 %collective-permute-done.31.refs_5_ = bf16[256,2048]{1,0:T(8,128)(2,1)S(1)} collective-permute-done((bf16[256,2048]{1,0:T(8,128)(2,1)}, bf16[256,2048]{1,0:T(8,128)(2,1)S(1)}, u32[]{:S(2)}, u32[]{:S(2)}) %collective-permute-start.31) | collective-permute-done | bytes 1048608 | tf_op jit(solution)/shard_map/ppermute | solution.py:40
  449.4 22.5 %back_out.2 = (bf16[1024,2048]{1,0:T(8,128)(2,1)}, f32[4,2048]{1,0:T(4,128)}) custom-call(f32[6,2048]{1,0:T(8,128)} %convert_element_type.125.vectors_ref, bf16[1024,1536]{1,0:T(8,128)(2,1)} %bitcast.79, bf16[1024,2048]{1,0:T(8,128)(2,1)} %get-tuple-element.498.pre_ref.refs_2_, bf16[2048,3584]{1,0:T(8,128)(2,1)} %all-gather.5.cloned.1.call-done.refs_7_.w_ref, ...), custom_call_target="tpu_custom_call" | custom-call | flops 939524096 | bytes 1966080 | tf_op jit(solution)/shard_map/back_out/pallas_call | solution.py:524
  473.3 6.1 arrange.3
  479.4 25.5 %grad_fc2.1 = (bf16[4,256,2048]{2,1,0:T(8,128)(2,1)}, bf16[4,256,2048]{2,1,0:T(8,128)(2,1)}) custom-call(s32[1]{0:T(128)} %bitcast.37.me_ref, bf16[1024,2048]{1,0:T(8,128)(2,1)} %bitcast.90, bf16[1024,2048]{1,0:T(8,128)(2,1)} %bitcast.92, bf16[1024,2048]{1,0:T(8,128)(2,1)} %get-tuple-element.467.act_ref.refs_2_, ...), custom_call_target="tpu_custom_call" | custom-call | flops 1073741824 | bytes 1572864 | tf_op jit(solution)/shard_map/grad_fc2/pallas_call | solution.py:569
  505.4 2.7 fusion.15
  508.1 3.8 all-to-all-start.3
  511.9 17.0 %back_in.3 = (bf16[1024,512]{1,0:T(8,128)(2,1)}, bf16[1024,2048]{1,0:T(8,128)(2,1)}, f32[1,2048]{1,0:T(1,128)}) custom-call(bf16[1024,2048]{1,0:T(8,128)(2,1)} %bitcast.93, bf16[8,2,32,2048]{3,2,1,0:T(8,128)(2,1)} %bitcast.112, bf16[2048,2048]{1,0:T(8,128)(2,1)} %all-gather.7.cloned.1.call-done.w_ref, bf16[1024,2048]{1,0:T(8,128)(2,1)} %get-tuple-element.484.slope_ref), custom_call_target="tpu_custom_call" | custom-call | flops 671088640 | bytes 1310720 | tf_op jit(solution)/shard_map/back_in/pallas_call | solution.py:483
  529.0 25.7 %grad_fc1.1 = (bf16[4,256,2048]{2,1,0:T(8,128)(2,1)}, bf16[4,256,2048]{2,1,0:T(8,128)(2,1)}) custom-call(s32[1]{0:T(128)} %bitcast.37.me_ref, bf16[1024,2048]{1,0:T(8,128)(2,1)} %bitcast.114, bf16[1024,2048]{1,0:T(8,128)(2,1)} %bitcast.116, bf16[1024,2048]{1,0:T(8,128)(2,1)} %get-tuple-element.498.pre_ref.refs_2_, ...), custom_call_target="tpu_custom_call" | custom-call | flops 1073741824 | bytes 1572864 | tf_op jit(solution)/shard_map/grad_fc1/pallas_call | solution.py:569
  555.2 6.4 add_convert_fusion.1
  561.6 5.3 all-to-all-start.4
  566.9 9.7 %attend_back.3 = (bf16[4,256,1536]{2,1,0:T(8,128)(2,1)S(1)}, f32[2,1,768]{2,1,0:T(1,128)S(1)}) custom-call(s32[4,256,1]{2,1,0:T(8,128)S(1)} %multiply_add_fusion.posq_ref, s32[4,1,1024]{2,1,0:T(1,128)S(1)} %pad_add_fusion.1.posk_ref, f32[4,256,128]{2,1,0:T(8,128)S(1)} %maximum_maximum_fusion.cos_ref, f32[4,256,128]{2,1,0:T(8,128)S(1)} %maximum_maximum_fusion.1.sin_ref, ...), custom_call_target="tpu_custom_call" | custom-call | flops 2684354560 | bytes 7864320 | tf_op jit(solution)/shard_map/attend_back/pallas_call | solution.py:239
  578.2 22.5 %back_out.3 = (bf16[1024,2048]{1,0:T(8,128)(2,1)}, f32[4,2048]{1,0:T(4,128)}) custom-call(f32[6,2048]{1,0:T(8,128)} %convert_element_type.125.vectors_ref, bf16[1024,1536]{1,0:T(8,128)(2,1)} %bitcast.81, bf16[1024,2048]{1,0:T(8,128)(2,1)} %get-tuple-element.504.refs_3_.pre_ref, bf16[2048,3584]{1,0:T(8,128)(2,1)} %all-gather.5.cloned.1.call-done.refs_7_.w_ref, ...), custom_call_target="tpu_custom_call" | custom-call | flops 939524096 | bytes 1966080 | tf_op jit(solution)/shard_map/back_out/pallas_call | solution.py:524
  600.7 14.2 %all-to-all-done.4 = bf16[4,256,2048]{2,1,0:T(8,128)(2,1)} async-done(((bf16[4,256,2048]{2,1,0:T(8,128)(2,1)}), bf16[4,256,2048]{2,1,0:T(8,128)(2,1)}, u32[]{:S(2)}, u32[]{:S(2)}) %all-to-all-start.4) | async-done | bytes 4194336 | tf_op jit(solution)/shard_map/all_to_all | solution.py:891
  614.9 8.0 add_convert_fusion
  622.9 4.9 all-to-all-start.5
  628.3 20.0 %grad_qkv.1 = (bf16[4,256,1536]{2,1,0:T(8,128)(2,1)}, bf16[4,256,1536]{2,1,0:T(8,128)(2,1)}) custom-call(s32[1]{0:T(128)} %bitcast.37.me_ref, bf16[1024,2048]{1,0:T(8,128)(2,1)} %bitcast.121, bf16[1024,2048]{1,0:T(8,128)(2,1)} %bitcast.122, bf16[1024,1536]{1,0:T(8,128)(2,1)} %bitcast.80, bf16[1024,1536]{1,0:T(8,128)(2,1)} %bitcast.82), custom_call_target="tpu_custom_call" | custom-call | flops 805306368 | bytes 1310720 | tf_op jit(solution)/shard_map/grad_qkv/pallas_call | solution.py:569
  651.3 9.5 %grad_dense.1 = (bf16[4,2,32,2048]{3,2,1,0:T(8,128)(2,1)}, bf16[4,2,32,2048]{3,2,1,0:T(8,128)(2,1)}) custom-call(s32[1]{0:T(128)} %bitcast.37.me_ref, bf16[1024,512]{1,0:T(8,128)(2,1)} %bitcast.84, bf16[1024,512]{1,0:T(8,128)(2,1)} %bitcast.86, bf16[1024,2048]{1,0:T(8,128)(2,1)} %bitcast.91, bf16[1024,2048]{1,0:T(8,128)(2,1)} %bitcast.94), custom_call_target="tpu_custom_call" | custom-call | flops 268435456 | bytes 786432 | tf_op jit(solution)/shard_map/grad_dense/pallas_call | solution.py:607
  663.6 4.5 convert_reduce_fusion.1
  668.1 7.4 collective-permute-done.38
  677.1 3.6 all-to-all-start.6
  680.7 5.5 add_convert_fusion.2
  686.1 9.9 %all-to-all-done.6 = bf16[8,32,2048]{2,1,0:T(8,128)(2,1)S(1)} async-done(((bf16[8,32,2048]{2,1,0:T(8,128)(2,1)}), bf16[8,32,2048]{2,1,0:T(8,128)(2,1)S(1)}, u32[]{:S(2)}, u32[]{:S(2)}) %all-to-all-start.6) | async-done | bytes 1048608 | tf_op jit(solution)/shard_map/all_to_all | solution.py:661
  697.1 4.6 all-to-all-start.7
  703.8 4.5 convert_reduce_fusion
  708.3 29.2 %collective-permute-done.39 = f32[2,1728]{1,0:T(2,128)S(1)} collective-permute-done((f32[2,1728]{1,0:T(2,128)S(1)}, f32[2,1728]{1,0:T(2,128)S(1)}, u32[]{:S(2)}, u32[]{:S(2)}) %collective-permute-start.39) | collective-permute-done | bytes 13856 | tf_op jit(solution)/shard_map/ppermute | solution.py:87
  738.9 4.4 all-to-all-start.8
  743.4 3.6 convert_reduce_fusion.2
  747.0 3.2 reshape.536
  750.3 5.3 all-to-all-done.8
  757.5 3.1 fusion.9
  760.6 3.6 all-to-all-start.9
  764.4 4.4 collective-permute-start.41
  775.2 4.3 all-to-all-done.9
  783.8 4.4 all-to-all-start.10
  791.9 2.8 pad_maximum_fusion
  794.7 8.9 %all-to-all-done.10 = bf16[8,32,2048]{2,1,0:T(8,128)(2,1)} async-done(((bf16[8,32,2048]{2,1,0:T(8,128)(2,1)}), bf16[8,32,2048]{2,1,0:T(8,128)(2,1)}, u32[]{:S(2)}, u32[]{:S(2)}) %all-to-all-start.10) | async-done | bytes 1048608 | tf_op jit(solution)/shard_map/all_to_all | solution.py:661
  803.6 2.7 pad_maximum_fusion.1
  (316 shorter events, 106.3 us)
Async XLA Ops:
  10.3 20.7 %all-to-all-start = ((bf16[8,32,2048]{2,1,0:T(8,128)(2,1)}), bf16[8,32,2048]{2,1,0:T(8,128)(2,1)S(1)}, u32[]{:S(2)}, u32[]{:S(2)}) async-start(bf16[8,32,2048]{2,1,0:T(8,128)(2,1)} %get-tuple-element.617), calls=%async_computation | async-start | bytes 2097152 | tf_op jit(solution)/shard_map/all_to_all | solution.py:658
  15.7 130.4 %all-gather.5.cloned.1.call-start = ((), (), s32[]{:S(2)}) async-start(), calls=%async_computation.15 | async-start | bytes 16515072 | tf_op jit(solution)/shard_map/all_gather | solution.py:697
  32.6 98.2 %copy-start.30 = (bf16[2048,256]{1,0:T(8,128)(2,1)S(1)}, bf16[2048,256]{1,0:T(8,128)(2,1)}, u32[]{:S(2)}) copy-start(bf16[2048,256]{1,0:T(8,128)(2,1)} %param.30) | copy-start | bytes 3145732
  32.7 26.5 %collective-permute-start.4 = (bf16[256,2048]{1,0:T(8,128)(2,1)S(1)}, bf16[256,2048]{1,0:T(8,128)(2,1)}, u32[]{:S(2)}, u32[]{:S(2)}) collective-permute-start(bf16[256,2048]{1,0:T(8,128)(2,1)S(1)} %bitcast.102), channel_id=1, source_target_pairs={{1,0},{2,1},{3,2},{5,4},{6,5},{7,6},{9,8},{10,9},{11,10},{13,12},{... | collective-permute-start | bytes 3145736 | tf_op jit(solution)/shard_map/ppermute | solution.py:40
  34.1 25.0 %collective-permute-start.3 = (bf16[256,2048]{1,0:T(8,128)(2,1)S(1)}, bf16[256,2048]{1,0:T(8,128)(2,1)}, u32[]{:S(2)}, u32[]{:S(2)}) collective-permute-start(bf16[256,2048]{1,0:T(8,128)(2,1)S(1)} %bitcast.103), channel_id=1, source_target_pairs={{0,1},{1,2},{2,3},{4,5},{5,6},{6,7},{8,9},{9,10},{10,11},{12,13},{... | collective-permute-start | bytes 3145736 | tf_op jit(solution)/shard_map/ppermute | solution.py:38
  39.7 18.4 %collective-permute-start.2 = (bf16[384]{0:T(512)(128)(2,1)S(1)}, bf16[384]{0:T(512)(128)(2,1)S(1)}, u32[]{:S(2)}, u32[]{:S(2)}) collective-permute-start(bf16[384]{0:T(512)(128)(2,1)S(1)} %concatenate.29), channel_id=1, source_target_pairs={{0,3},{1,0},{2,1},{3,2},{4,7},{5,4},{6,5},{7,6},{8,11},{9,8},{10,9... | collective-permute-start | bytes 2312 | tf_op jit(solution)/shard_map/ppermute | solution.py:103
  41.1 17.0 %collective-permute-start.1 = (bf16[384]{0:T(512)(128)(2,1)S(1)}, bf16[384]{0:T(512)(128)(2,1)S(1)}, u32[]{:S(2)}, u32[]{:S(2)}) collective-permute-start(bf16[384]{0:T(512)(128)(2,1)S(1)} %concatenate.29), channel_id=1, source_target_pairs={{0,2},{1,3},{2,0},{3,1},{4,6},{5,7},{6,4},{7,5},{8,10},{9,11},{10,... | collective-permute-start | bytes 2312 | tf_op jit(solution)/shard_map/ppermute | solution.py:103
  42.4 16.5 %collective-permute-start = (bf16[384]{0:T(512)(128)(2,1)S(1)}, bf16[384]{0:T(512)(128)(2,1)S(1)}, u32[]{:S(2)}, u32[]{:S(2)}) collective-permute-start(bf16[384]{0:T(512)(128)(2,1)S(1)} %concatenate.29), channel_id=1, source_target_pairs={{0,1},{1,2},{2,3},{3,0},{4,5},{5,6},{6,7},{7,4},{8,9},{9,10},{10,1... | collective-permute-start | bytes 2312 | tf_op jit(solution)/shard_map/ppermute | solution.py:103
  59.1 40.5 %collective-permute-start.12 = (bf16[256,2048]{1,0:T(8,128)(2,1)}, bf16[256,2048]{1,0:T(8,128)(2,1)}, u32[]{:S(2)}, u32[]{:S(2)}) collective-permute-start(bf16[256,2048]{1,0:T(8,128)(2,1)} %collective-permute-done.3.refs_1_), channel_id=1, source_target_pairs={{1,2},{2,3},{5,6},{6,7},{9,10},{10,11},{13,14},{14,15},{17,18},{18... | collective-permute-start | bytes 3145736 | tf_op jit(solution)/shard_map/ppermute | solution.py:38
  60.8 38.9 %collective-permute-start.13 = (bf16[256,2048]{1,0:T(8,128)(2,1)}, bf16[256,2048]{1,0:T(8,128)(2,1)}, u32[]{:S(2)}, u32[]{:S(2)}) collective-permute-start(bf16[256,2048]{1,0:T(8,128)(2,1)} %collective-permute-done.4.refs_4_), channel_id=1, source_target_pairs={{1,0},{2,1},{5,4},{6,5},{9,8},{10,9},{13,12},{14,13},{17,16},{18,1... | collective-permute-start | bytes 3145736 | tf_op jit(solution)/shard_map/ppermute | solution.py:40
  62.0 37.6 %all-to-all-start.1 = ((bf16[8,32,2048]{2,1,0:T(8,128)(2,1)}), bf16[8,32,2048]{2,1,0:T(8,128)(2,1)S(1)}, u32[]{:S(2)}, u32[]{:S(2)}) async-start(bf16[8,32,2048]{2,1,0:T(8,128)(2,1)} %get-tuple-element.301), calls=%async_computation.1 | async-start | bytes 2097152 | tf_op jit(solution)/shard_map/all_to_all | solution.py:658
  66.9 178.4 %all-gather.9.cloned.1.call-start = ((), (), s32[]{:S(2)}) async-start(), calls=%async_computation.21 | async-start | bytes 2359296 | tf_op jit(solution)/shard_map/all_gather | solution.py:758
  66.9 22.5 %collective-permute-start.11 = (bf16[1984]{0:T(1024)(128)(2,1)S(1)}, bf16[1984]{0:T(1024)(128)(2,1)S(1)}, u32[]{:S(2)}, u32[]{:S(2)}) collective-permute-start(bf16[1984]{0:T(1024)(128)(2,1)S(1)} %concatenate.30), channel_id=1, source_target_pairs={{0,28},{4,0},{8,4},{12,8},{16,12},{20,16},{24,20},{28,24},{1,29},{... | collective-permute-start | bytes 11912 | tf_op jit(solution)/shard_map/ppermute | solution.py:103
  69.6 22.6 %collective-permute-start.10 = (bf16[1984]{0:T(1024)(128)(2,1)S(1)}, bf16[1984]{0:T(1024)(128)(2,1)S(1)}, u32[]{:S(2)}, u32[]{:S(2)}) collective-permute-start(bf16[1984]{0:T(1024)(128)(2,1)S(1)} %concatenate.30), channel_id=1, source_target_pairs={{0,24},{4,28},{8,0},{12,4},{16,8},{20,12},{24,16},{28,20},{1,25},{... | collective-permute-start | bytes 11912 | tf_op jit(solution)/shard_map/ppermute | solution.py:103
  70.2 22.7 %collective-permute-start.9 = (bf16[1984]{0:T(1024)(128)(2,1)S(1)}, bf16[1984]{0:T(1024)(128)(2,1)S(1)}, u32[]{:S(2)}, u32[]{:S(2)}) collective-permute-start(bf16[1984]{0:T(1024)(128)(2,1)S(1)} %concatenate.30), channel_id=1, source_target_pairs={{0,20},{4,24},{8,28},{12,0},{16,4},{20,8},{24,12},{28,16},{1,21},{... | collective-permute-start | bytes 11912 | tf_op jit(solution)/shard_map/ppermute | solution.py:103
  89.5 5.8 collective-permute-start.8
  92.3 3.1 collective-permute-start.7
  92.9 4.8 collective-permute-start.6
  95.3 4.0 collective-permute-start.5
  99.6 2.9 collective-permute-start.14
  101.3 29.5 %collective-permute-start.15 = (bf16[256,2048]{1,0:T(8,128)(2,1)}, bf16[256,2048]{1,0:T(8,128)(2,1)}, u32[]{:S(2)}, u32[]{:S(2)}) collective-permute-start(bf16[256,2048]{1,0:T(8,128)(2,1)} %collective-permute-done.13.refs_5_), channel_id=1, source_target_pairs={{1,0},{5,4},{9,8},{13,12},{17,16},{21,20},{25,24},{29,28}} | collective-permute-start | bytes 3145736 | tf_op jit(solution)/shard_map/ppermute | solution.py:40
  130.8 114.5 %all-gather.7.cloned.1.call-start = ((), (), s32[]{:S(2)}) async-start(), calls=%async_computation.16 | async-start | bytes 9437184 | tf_op jit(solution)/shard_map/all_gather | solution.py:757
  137.4 27.9 %collective-permute-start.17 = (bf16[256,2048]{1,0:T(8,128)(2,1)S(1)}, bf16[256,2048]{1,0:T(8,128)(2,1)}, u32[]{:S(2)}, u32[]{:S(2)}) collective-permute-start(bf16[256,2048]{1,0:T(8,128)(2,1)S(1)} %bitcast.95), channel_id=1, source_target_pairs={{1,0},{2,1},{3,2},{5,4},{6,5},{7,6},{9,8},{10,9},{11,10},{13,12},{... | collective-permute-start | bytes 3145736 | tf_op jit(solution)/shard_map/ppermute | solution.py:40
  138.7 26.7 %collective-permute-start.16 = (bf16[256,2048]{1,0:T(8,128)(2,1)S(1)}, bf16[256,2048]{1,0:T(8,128)(2,1)}, u32[]{:S(2)}, u32[]{:S(2)}) collective-permute-start(bf16[256,2048]{1,0:T(8,128)(2,1)S(1)} %bitcast.96), channel_id=1, source_target_pairs={{0,1},{1,2},{2,3},{4,5},{5,6},{6,7},{8,9},{9,10},{10,11},{12,13},{... | collective-permute-start | bytes 3145736 | tf_op jit(solution)/shard_map/ppermute | solution.py:38
  165.4 41.7 %collective-permute-start.18 = (bf16[256,2048]{1,0:T(8,128)(2,1)}, bf16[256,2048]{1,0:T(8,128)(2,1)}, u32[]{:S(2)}, u32[]{:S(2)}) collective-permute-start(bf16[256,2048]{1,0:T(8,128)(2,1)} %collective-permute-done.16.refs_1_), channel_id=1, source_target_pairs={{1,2},{2,3},{5,6},{6,7},{9,10},{10,11},{13,14},{14,15},{17,18},{18... | collective-permute-start | bytes 3145736 | tf_op jit(solution)/shard_map/ppermute | solution.py:38
  167.1 40.1 %collective-permute-start.19 = (bf16[256,2048]{1,0:T(8,128)(2,1)}, bf16[256,2048]{1,0:T(8,128)(2,1)}, u32[]{:S(2)}, u32[]{:S(2)}) collective-permute-start(bf16[256,2048]{1,0:T(8,128)(2,1)} %collective-permute-done.17.refs_4_), channel_id=1, source_target_pairs={{1,0},{2,1},{5,4},{6,5},{9,8},{10,9},{13,12},{14,13},{17,16},{18,1... | collective-permute-start | bytes 3145736 | tf_op jit(solution)/shard_map/ppermute | solution.py:40
  171.2 37.9 %all-to-all-start.2 = ((bf16[2,8,32,2048]{3,2,0,1:T(8,128)(2,1)}), bf16[2,8,32,2048]{3,2,0,1:T(8,128)(2,1)}, u32[]{:S(2)}, u32[]{:S(2)}) async-start(bf16[2,8,32,2048]{3,2,0,1:T(8,128)(2,1)} %copy.45), calls=%async_computation.2 | async-start | bytes 4194304 | tf_op jit(solution)/shard_map/all_to_all | solution.py:927
  175.6 297.6 %reduce-scatter.5.cloned.1.call-start = ((), (), s32[]{:S(2)}) async-start(), calls=%async_computation.17 | async-start | bytes 5242880 | tf_op jit(solution)/shard_map/reduce_scatter | solution.py:806
  207.2 2.0 collective-permute-start.20
  207.9 27.9 %collective-permute-start.21 = (bf16[256,2048]{1,0:T(8,128)(2,1)}, bf16[256,2048]{1,0:T(8,128)(2,1)}, u32[]{:S(2)}, u32[]{:S(2)}) collective-permute-start(bf16[256,2048]{1,0:T(8,128)(2,1)} %collective-permute-done.19.refs_5_), channel_id=1, source_target_pairs={{1,0},{5,4},{9,8},{13,12},{17,16},{21,20},{25,24},{29,28}} | collective-permute-start | bytes 3145736 | tf_op jit(solution)/shard_map/ppermute | solution.py:40
  238.5 93.9 %copy-start.13 = (bf16[1,8,32,2048]{3,2,0,1:T(8,128)(2,1)}, bf16[1,8,32,2048]{3,2,0,1:T(8,128)(2,1)S(1)}, u32[]{:S(2)}) copy-start(bf16[1,8,32,2048]{3,2,0,1:T(8,128)(2,1)S(1)} %get-tuple-element.614) | copy-start | bytes 3145732
  238.5 27.1 %collective-permute-start.23 = (bf16[256,2048]{1,0:T(8,128)(2,1)}, bf16[256,2048]{1,0:T(8,128)(2,1)}, u32[]{:S(2)}, u32[]{:S(2)}) collective-permute-start(bf16[256,2048]{1,0:T(8,128)(2,1)} %bitcast.22.refs_0_), channel_id=1, source_target_pairs={{1,0},{2,1},{3,2},{5,4},{6,5},{7,6},{9,8},{10,9},{11,10},{13,12},{... | collective-permute-start | bytes 3145736 | tf_op jit(solution)/shard_map/ppermute | solution.py:40
  239.8 27.0 %collective-permute-start.22 = (bf16[256,2048]{1,0:T(8,128)(2,1)}, bf16[256,2048]{1,0:T(8,128)(2,1)}, u32[]{:S(2)}, u32[]{:S(2)}) collective-permute-start(bf16[256,2048]{1,0:T(8,128)(2,1)} %bitcast.22.refs_0_), channel_id=1, source_target_pairs={{0,1},{1,2},{2,3},{4,5},{5,6},{6,7},{8,9},{9,10},{10,11},{12,13},{... | collective-permute-start | bytes 3145736 | tf_op jit(solution)/shard_map/ppermute | solution.py:38
  266.8 22.2 %collective-permute-start.24 = (bf16[256,2048]{1,0:T(8,128)(2,1)}, bf16[256,2048]{1,0:T(8,128)(2,1)}, u32[]{:S(2)}, u32[]{:S(2)}) collective-permute-start(bf16[256,2048]{1,0:T(8,128)(2,1)} %collective-permute-done.22.refs_1_), channel_id=1, source_target_pairs={{1,2},{2,3},{5,6},{6,7},{9,10},{10,11},{13,14},{14,15},{17,18},{18... | collective-permute-start | bytes 3145736 | tf_op jit(solution)/shard_map/ppermute | solution.py:38
  268.5 29.0 %collective-permute-start.25 = (bf16[256,2048]{1,0:T(8,128)(2,1)}, bf16[256,2048]{1,0:T(8,128)(2,1)}, u32[]{:S(2)}, u32[]{:S(2)}) collective-permute-start(bf16[256,2048]{1,0:T(8,128)(2,1)} %collective-permute-done.23.refs_4_), channel_id=1, source_target_pairs={{1,0},{2,1},{5,4},{6,5},{9,8},{10,9},{13,12},{14,13},{17,16},{18,1... | collective-permute-start | bytes 3145736 | tf_op jit(solution)/shard_map/ppermute | solution.py:40
  297.5 33.5 %collective-permute-start.26 = (bf16[256,2048]{1,0:T(8,128)(2,1)}, bf16[256,2048]{1,0:T(8,128)(2,1)}, u32[]{:S(2)}, u32[]{:S(2)}) collective-permute-start(bf16[256,2048]{1,0:T(8,128)(2,1)} %collective-permute-done.24.refs_2_), channel_id=1, source_target_pairs={{2,3},{6,7},{10,11},{14,15},{18,19},{22,23},{26,27},{30,31}} | collective-permute-start | bytes 3145736 | tf_op jit(solution)/shard_map/ppermute | solution.py:38
  299.1 31.9 %collective-permute-start.27 = (bf16[256,2048]{1,0:T(8,128)(2,1)}, bf16[256,2048]{1,0:T(8,128)(2,1)}, u32[]{:S(2)}, u32[]{:S(2)}) collective-permute-start(bf16[256,2048]{1,0:T(8,128)(2,1)} %collective-permute-done.25.refs_5_), channel_id=1, source_target_pairs={{1,0},{5,4},{9,8},{13,12},{17,16},{21,20},{25,24},{29,28}} | collective-permute-start | bytes 3145736 | tf_op jit(solution)/shard_map/ppermute | solution.py:40
  331.0 283.9 %reduce-scatter.7.cloned.1.call-start = ((), (), s32[]{:S(2)}) async-start(), calls=%async_computation.18 | async-start | bytes 5242880 | tf_op jit(solution)/shard_map/reduce_scatter | solution.py:806
  331.1 69.5 %collective-permute-start.29 = (bf16[256,2048]{1,0:T(8,128)(2,1)S(1)}, bf16[256,2048]{1,0:T(8,128)(2,1)}, u32[]{:S(2)}, u32[]{:S(2)}) collective-permute-start(bf16[256,2048]{1,0:T(8,128)(2,1)S(1)} %bitcast.117), channel_id=1, source_target_pairs={{1,0},{2,1},{3,2},{5,4},{6,5},{7,6},{9,8},{10,9},{11,10},{13,12},{... | collective-permute-start | bytes 3145736 | tf_op jit(solution)/shard_map/ppermute | solution.py:40
  332.4 68.2 %collective-permute-start.28 = (bf16[256,2048]{1,0:T(8,128)(2,1)S(1)}, bf16[256,2048]{1,0:T(8,128)(2,1)}, u32[]{:S(2)}, u32[]{:S(2)}) collective-permute-start(bf16[256,2048]{1,0:T(8,128)(2,1)S(1)} %bitcast.118), channel_id=1, source_target_pairs={{0,1},{1,2},{2,3},{4,5},{5,6},{6,7},{8,9},{9,10},{10,11},{12,13},{... | collective-permute-start | bytes 3145736 | tf_op jit(solution)/shard_map/ppermute | solution.py:38
  400.6 31.9 %collective-permute-start.30 = (bf16[256,2048]{1,0:T(8,128)(2,1)}, bf16[256,2048]{1,0:T(8,128)(2,1)S(1)}, u32[]{:S(2)}, u32[]{:S(2)}) collective-permute-start(bf16[256,2048]{1,0:T(8,128)(2,1)} %collective-permute-done.28.refs_1_), channel_id=1, source_target_pairs={{1,2},{2,3},{5,6},{6,7},{9,10},{10,11},{13,14},{14,15},{17,18},{18... | collective-permute-start | bytes 3145736 | tf_op jit(solution)/shard_map/ppermute | solution.py:38
  401.3 46.1 %collective-permute-start.31 = (bf16[256,2048]{1,0:T(8,128)(2,1)}, bf16[256,2048]{1,0:T(8,128)(2,1)S(1)}, u32[]{:S(2)}, u32[]{:S(2)}) collective-permute-start(bf16[256,2048]{1,0:T(8,128)(2,1)} %collective-permute-done.29.refs_4_), channel_id=1, source_target_pairs={{1,0},{2,1},{5,4},{6,5},{9,8},{10,9},{13,12},{14,13},{17,16},{18,1... | collective-permute-start | bytes 3145736 | tf_op jit(solution)/shard_map/ppermute | solution.py:40
  447.4 24.5 %collective-permute-start.32 = (bf16[256,2048]{1,0:T(8,128)(2,1)S(1)}, bf16[256,2048]{1,0:T(8,128)(2,1)S(1)}, u32[]{:S(2)}, u32[]{:S(2)}) collective-permute-start(bf16[256,2048]{1,0:T(8,128)(2,1)S(1)} %collective-permute-done.30.refs_2_), channel_id=1, source_target_pairs={{2,3},{6,7},{10,11},{14,15},{18,19},{22,23},{26,27},{30,31}} | collective-permute-start | bytes 3145736 | tf_op jit(solution)/shard_map/ppermute | solution.py:38
  448.1 25.1 %collective-permute-start.33 = (bf16[256,2048]{1,0:T(8,128)(2,1)S(1)}, bf16[256,2048]{1,0:T(8,128)(2,1)}, u32[]{:S(2)}, u32[]{:S(2)}) collective-permute-start(bf16[256,2048]{1,0:T(8,128)(2,1)S(1)} %collective-permute-done.31.refs_5_), channel_id=1, source_target_pairs={{1,0},{5,4},{9,8},{13,12},{17,16},{21,20},{25,24},{29,28}} | collective-permute-start | bytes 3145736 | tf_op jit(solution)/shard_map/ppermute | solution.py:40
  473.3 277.0 %reduce-scatter.9.cloned.1.call-start = ((), (), s32[]{:S(2)}) async-start(), calls=%async_computation.19 | async-start | bytes 5242880 | tf_op jit(solution)/shard_map/reduce_scatter | solution.py:806
  505.0 24.0 %collective-permute-start.34 = (bf16[4,256,2048]{2,1,0:T(8,128)(2,1)}, bf16[4,256,2048]{2,1,0:T(8,128)(2,1)}, u32[]{:S(2)}, u32[]{:S(2)}) collective-permute-start(bf16[4,256,2048]{2,1,0:T(8,128)(2,1)} %get-tuple-element.483), channel_id=1, source_target_pairs={{0,4},{4,0},{8,12},{12,8},{16,20},{20,16},{24,28},{28,24},{1,5},{5... | collective-permute-start | bytes 12582920 | tf_op jit(solution)/shard_map/ppermute | solution.py:885
  508.1 20.8 %all-to-all-start.3 = ((bf16[8,32,2048]{2,1,0:T(8,128)(2,1)}), bf16[8,32,2048]{2,1,0:T(8,128)(2,1)S(1)}, u32[]{:S(2)}, u32[]{:S(2)}) async-start(bf16[8,32,2048]{2,1,0:T(8,128)(2,1)} %bitcast.130), calls=%async_computation.4 | async-start | bytes 2097152 | tf_op jit(solution)/shard_map/all_to_all | solution.py:661
  554.7 60.2 %collective-permute-start.35 = (bf16[4,256,2048]{2,1,0:T(8,128)(2,1)}, bf16[4,256,2048]{2,1,0:T(8,128)(2,1)}, u32[]{:S(2)}, u32[]{:S(2)}) collective-permute-start(bf16[4,256,2048]{2,1,0:T(8,128)(2,1)} %get-tuple-element.508), channel_id=1, source_target_pairs={{0,4},{4,0},{8,12},{12,8},{16,20},{20,16},{24,28},{28,24},{1,5},{5... | collective-permute-start | bytes 12582920 | tf_op jit(solution)/shard_map/ppermute | solution.py:885
  561.6 53.3 %all-to-all-start.4 = ((bf16[4,256,2048]{2,1,0:T(8,128)(2,1)}), bf16[4,256,2048]{2,1,0:T(8,128)(2,1)}, u32[]{:S(2)}, u32[]{:S(2)}) async-start(bf16[4,256,2048]{2,1,0:T(8,128)(2,1)} %add_convert_fusion.1), calls=%async_computation.5 | async-start | bytes 8388608 | tf_op jit(solution)/shard_map/all_to_all | solution.py:891
  622.9 52.6 %all-to-all-start.5 = ((bf16[4,256,2048]{2,1,0:T(8,128)(2,1)}), bf16[4,256,2048]{2,1,0:T(8,128)(2,1)}, u32[]{:S(2)}, u32[]{:S(2)}) async-start(bf16[4,256,2048]{2,1,0:T(8,128)(2,1)} %add_convert_fusion), calls=%async_computation.7 | async-start | bytes 8388608 | tf_op jit(solution)/shard_map/all_to_all | solution.py:891
  627.8 151.7 %reduce-scatter.11.cloned.1.call-start = ((), (), s32[]{:S(2)}) async-start(), calls=%async_computation.20 | async-start | bytes 5242880 | tf_op jit(solution)/shard_map/reduce_scatter | solution.py:806
  648.3 27.2 %collective-permute-start.36 = (bf16[4,256,1536]{2,1,0:T(8,128)(2,1)}, bf16[4,256,1536]{2,1,0:T(8,128)(2,1)}, u32[]{:S(2)}, u32[]{:S(2)}) collective-permute-start(bf16[4,256,1536]{2,1,0:T(8,128)(2,1)} %get-tuple-element.536), channel_id=1, source_target_pairs={{0,4},{4,0},{8,12},{12,8},{16,20},{20,16},{24,28},{28,24},{1,5},{5... | collective-permute-start | bytes 9437192 | tf_op jit(solution)/shard_map/ppermute | solution.py:885
  660.8 14.7 %collective-permute-start.37 = (bf16[4,64,2048]{2,1,0:T(8,128)(2,1)}, bf16[4,64,2048]{2,1,0:T(8,128)(2,1)S(1)}, u32[]{:S(2)}, u32[]{:S(2)}) collective-permute-start(bf16[4,64,2048]{2,1,0:T(8,128)(2,1)} %bitcast.147), channel_id=1, source_target_pairs={{0,4},{4,0},{8,12},{12,8},{16,20},{20,16},{24,28},{28,24},{1,5},{5... | collective-permute-start | bytes 3145736 | tf_op jit(solution)/shard_map/ppermute | solution.py:885
  661.6 13.9 %collective-permute-start.38 = (f32[4,1728]{1,0:T(4,128)S(1)}, f32[4,1728]{1,0:T(4,128)S(1)}, u32[]{:S(2)}, u32[]{:S(2)}) collective-permute-start(f32[4,1728]{1,0:T(4,128)S(1)} %slice_select_fusion), channel_id=1, source_target_pairs={{0,16},{4,20},{8,24},{12,28},{16,0},{20,4},{24,8},{28,12},{1,17},{... | collective-permute-start | bytes 82952 | tf_op jit(solution)/shard_map/ppermute | solution.py:87
  677.1 18.9 %all-to-all-start.6 = ((bf16[8,32,2048]{2,1,0:T(8,128)(2,1)}), bf16[8,32,2048]{2,1,0:T(8,128)(2,1)S(1)}, u32[]{:S(2)}, u32[]{:S(2)}) async-start(bf16[8,32,2048]{2,1,0:T(8,128)(2,1)} %bitcast.49), calls=%async_computation.8 | async-start | bytes 2097152 | tf_op jit(solution)/shard_map/all_to_all | solution.py:661
  697.1 40.4 %all-to-all-start.7 = ((bf16[4,256,1536]{2,1,0:T(8,128)(2,1)}), bf16[4,256,1536]{2,1,0:T(8,128)(2,1)}, u32[]{:S(2)}, u32[]{:S(2)}) async-start(bf16[4,256,1536]{2,1,0:T(8,128)(2,1)} %add_convert_fusion.2), calls=%async_computation.9 | async-start | bytes 6291456 | tf_op jit(solution)/shard_map/all_to_all | solution.py:891
  701.7 35.7 %collective-permute-start.39 = (f32[2,1728]{1,0:T(2,128)S(1)}, f32[2,1728]{1,0:T(2,128)S(1)}, u32[]{:S(2)}, u32[]{:S(2)}) collective-permute-start(f32[2,1728]{1,0:T(2,128)S(1)} %broadcast_select_fusion.2), channel_id=1, source_target_pairs={{0,8},{4,12},{8,0},{12,4},{16,24},{20,28},{24,16},{28,20},{1,9},{5... | collective-permute-start | bytes 41480 | tf_op jit(solution)/shard_map/ppermute | solution.py:87
  738.9 16.7 %all-to-all-start.8 = ((bf16[4,64,2048]{2,1,0:T(8,128)(2,1)}), bf16[4,64,2048]{2,1,0:T(8,128)(2,1)}, u32[]{:S(2)}, u32[]{:S(2)}) async-start(bf16[4,64,2048]{2,1,0:T(8,128)(2,1)} %add_convert_fusion.3), calls=%async_computation.10 | async-start | bytes 2097152 | tf_op jit(solution)/shard_map/all_to_all | solution.py:891
  743.3 6.9 collective-permute-start.40
  760.6 18.9 %all-to-all-start.9 = ((bf16[8,32,2048]{2,1,0:T(8,128)(2,1)}), bf16[8,32,2048]{2,1,0:T(8,128)(2,1)S(1)}, u32[]{:S(2)}, u32[]{:S(2)}) async-start(bf16[8,32,2048]{2,1,0:T(8,128)(2,1)} %bitcast.125), calls=%async_computation.12 | async-start | bytes 2097152 | tf_op jit(solution)/shard_map/all_to_all | solution.py:661
  764.4 10.8 %collective-permute-start.41 = (f32[320]{0:T(512)S(1)}, f32[320]{0:T(512)S(1)}, u32[]{:S(2)}, u32[]{:S(2)}) collective-permute-start(f32[320]{0:T(512)S(1)} %get-tuple-element.610), channel_id=1, source_target_pairs={{0,1},{1,2},{2,3},{3,0},{4,5},{5,6},{6,7},{7,4},{8,9},{9,10},{10,1... | collective-permute-start | bytes 3848 | tf_op jit(solution)/shard_map/ppermute | solution.py:114
  768.8 6.4 collective-permute-start.43
  770.3 4.9 collective-permute-start.42
  783.8 19.8 %all-to-all-start.10 = ((bf16[8,32,2048]{2,1,0:T(8,128)(2,1)}), bf16[8,32,2048]{2,1,0:T(8,128)(2,1)}, u32[]{:S(2)}, u32[]{:S(2)}) async-start(bf16[8,32,2048]{2,1,0:T(8,128)(2,1)} %bitcast.55), calls=%async_computation.14 | async-start | bytes 2097152 | tf_op jit(solution)/shard_map/all_to_all | solution.py:661
  (47 other events, 606.8 us)
Sparse Core Ops, SparseCore 0:
  32.8 90.6 all-gather.4
  130.9 26.9 all-gather.8
  160.3 71.6 all-gather.6
  331.2 104.9 reduce-scatter.4
  473.4 80.4 reduce-scatter.6
  556.0 77.2 reduce-scatter.8
  661.4 81.4 reduce-scatter.10

commit v3 on v2

--- a/solution.py
+++ b/solution.py
@@ -18,6 +18,7 @@
 BF = jnp.bfloat16
 F32 = jnp.float32
 FAR = 1 << 20
+SHARE = 4096
 
 
 class GatherChain:
@@ -44,54 +45,6 @@
 
     def set_live(self, values):
         self.left[-1], self.right[-1] = values
-
-
-class SmallGather:
-    def __init__(self, x, axis, n):
-        self.out, self.axis, self.n, self.bit = x[None], axis, n, 1
-        self.me = lax.axis_index(axis)
-
-    def steps(self):
-        return self.n.bit_length() - 1
-
-    def step(self):
-        bit, out = self.bit, self.out
-        other = lax.ppermute(out, self.axis, [(i, i ^ bit) for i in range(self.n)])
-        high = (self.me & bit) != 0
-        self.out = jnp.concatenate(
-            [jnp.where(high, other, out), jnp.where(high, out, other)], axis=0
-        )
-        self.bit *= 2
-
-    def live(self):
-        return [self.out]
-
-    def set_live(self, values):
-        self.out = values[0]
-
-
-class SmallScatter:
-    def __init__(self, x, axis, n):
-        self.out, self.axis, self.n, self.bit = x, axis, n, n // 2
-        self.me = lax.axis_index(axis)
-
-    def steps(self):
-        return self.n.bit_length() - 1
-
-    def step(self):
-        bit, x = self.bit, self.out
-        low, high = x[:bit], x[bit:]
-        mine_high = (self.me & bit) != 0
-        sent = jnp.where(mine_high, low, high)
-        kept = jnp.where(mine_high, high, low)
-        self.out = kept + lax.ppermute(sent, self.axis, [(i, i ^ bit) for i in range(self.n)])
-        self.bit //= 2
-
-    def live(self):
-        return [self.out]
-
-    def set_live(self, values):
-        self.out = values[0]
 
 
 def shifts(n):
@@ -324,7 +277,11 @@
 
 
 def cost(flops, moved, special=0):
-    return pl.CostEstimate(flops=int(flops) // 16, bytes_accessed=int(moved) // 16, transcendentals=int(special) // 16)
+    return pl.CostEstimate(
+        flops=int(flops) // SHARE,
+        bytes_accessed=int(moved) // SHARE,
+        transcendentals=int(special) // SHARE,
+    )
 
 
 def norm_qkv(chain, vectors, bias, w, n_qkv):
@@ -658,9 +615,8 @@
         return lax.all_to_all(x, "dp", split_axis=0, concat_axis=0, tiled=True).reshape(rows, width)
 
     def undeal(x):
-        return lax.all_to_all(
-            x.reshape(seqs, piece, width), "dp", split_axis=0, concat_axis=0, tiled=True
-        )
+        x = x.reshape(x.shape[0], seqs, piece, width)
+        return lax.all_to_all(x, "dp", split_axis=1, concat_axis=1, tiled=True)
 
     env = {}
 
@@ -685,10 +641,11 @@
         return lax.optimization_barrier((x, env["mark"]))[0]
 
     eighth = width // (n_d * n_t)
-    n_six = 6 * n_t * eighth
+    n_six = 6 * eighth
     env["x0"] = deal(hidden_in[0])
     env["mark"] = jnp.concatenate(
         [attn_gain, attn_shift, ffn_gain, ffn_shift, dense_bias, fc2_bias]
+        + [qkv_bias.reshape(-1), fc1_bias.reshape(-1)]
     )
     stage([])
 
@@ -730,17 +687,29 @@
 
         return fn
 
+    def vectors_over_dp():
+        env["small"] = direct_gather(env["mark"], "dp", n_d)
+
     def vectors_over_tensor():
-        vectors = direct_gather(env["mark"], "tensor", n_t)
-        env["six"] = jnp.concatenate(
-            [vectors.reshape(-1), qkv_bias.reshape(-1), fc1_bias.reshape(-1)]
+        six = env["small"][:, :n_six].reshape(-1)
+        env["six"] = direct_gather(six, "tensor", n_t)
+
+    def vectors_whole():
+        vectors = env.pop("six").reshape(n_t, n_d, 6, eighth).transpose(2, 1, 0, 3)
+        env["vectors"] = vectors.reshape(6, width).astype(F32)
+        rest = env.pop("small")[:, n_six:].astype(F32)
+        n_qb = qkv_bias.size
+        env["bias"] = jnp.concatenate(
+            [
+                rest[:, :n_qb].reshape(n_d, heads, -1).transpose(1, 0, 2).reshape(1, -1),
+                rest[:, n_qb:].reshape(n_d, heads, -1).transpose(1, 0, 2).reshape(1, -1),
+            ],
+            axis=1,
         )
 
-    def vectors_over_dp():
-        env["six"] = direct_gather(env["six"], "dp", n_d)
-
-    def deal_x1():
-        pending["x1"] = deal(after(hidden_in[1]))
+    def deal_two():
+        two = jnp.stack([after(hidden_in[1]), cotangent[0]])
+        pending["two"] = lax.all_to_all(two, "dp", split_axis=1, concat_axis=1, tiled=True)
 
     last = n_t - 2
 
@@ -752,25 +721,15 @@
     for i in range(n_t - 1):
         stage(
             [chains["x0"]],
-            at(i, [vectors_over_tensor, deal_x1], [vectors_over_dp, join("x1")]),
+            at(i, [vectors_over_dp], [vectors_over_tensor, deal_two], [vectors_whole, join("two")]),
         )
     w_fc2 = lax.all_gather(after(fc2_weight.T), "dp", axis=0, tiled=True)
     w_dense = lax.all_gather(after(dense_weight), "dp", axis=0, tiled=False)
-    own_x = [env.pop("x0"), env.pop("x1")]
-    six = env.pop("six")
-    vectors = six[:, :n_six].reshape(n_d, n_t, 6, eighth).transpose(2, 0, 1, 3)
-    vectors = vectors.reshape(6, width).astype(F32)
+    two = env.pop("two").reshape(2, rows, width)
+    own_x, own_g = [env.pop("x0"), two[0]], [two[1], None]
+    env["mark"] = vectors = env.pop("vectors")
     out_shift = vectors[4] + vectors[5]
-    rest = six[:, n_six:].astype(F32)
     n_qb = qkv_bias.size
-    bias = jnp.concatenate(
-        [
-            rest[:, :n_qb].reshape(n_d, heads, -1).transpose(1, 0, 2).reshape(1, -1),
-            rest[:, n_qb:].reshape(n_d, heads, -1).transpose(1, 0, 2).reshape(1, -1),
-        ],
-        axis=1,
-    )
-    env["mark"], env["bias"] = vectors, bias
 
     def norm_qkv_of(m):
         def fn():
@@ -806,12 +765,8 @@
         return lax.psum_scatter(env.pop(name), "tensor", scatter_dimension=0, tiled=True)
 
     def output_of(m):
-        def fn():
-            total = env.pop(f"so{m}").astype(F32)
-            out = (own_x[m].astype(F32) + total + out_shift).astype(BF)
-            env[f"output{m}"] = undeal(out)
-
-        return fn
+        total = env.pop(f"so{m}").astype(F32)
+        return (own_x[m].astype(F32) + total + out_shift).astype(BF)
 
     def arrange_g(m):
         def fn():
@@ -848,17 +803,17 @@
         return fn
 
     def input_of(m):
-        def fn():
-            total = env.pop(f"si{m}").astype(F32)
-            unit, scaling = unit_of(own_x[m].astype(F32))
-            back = scaling * (
-                total
-                - jnp.mean(total, axis=-1, keepdims=True)
-                - unit * jnp.mean(total * unit, axis=-1, keepdims=True)
-            )
-            env[f"input{m}"] = undeal((own_g[m].astype(F32) + back).astype(BF))
-
-        return fn
+        total = env.pop(f"si{m}").astype(F32)
+        unit, scaling = unit_of(own_x[m].astype(F32))
+        back = scaling * (
+            total
+            - jnp.mean(total, axis=-1, keepdims=True)
+            - unit * jnp.mean(total * unit, axis=-1, keepdims=True)
+        )
+        return (own_g[m].astype(F32) + back).astype(BF)
+
+    def output_rows():
+        pending["rows"] = undeal(jnp.stack([output_of(0), output_of(1)]))
 
     def pair(key):
         return [env[f"{key}{m}"] for m in range(micros)]
@@ -919,62 +874,82 @@
     def dense_final():
         env["grad_dense"] = summed("wd").reshape(heads, -1, width)
 
+    def steps_of(these, *plan):
+        for i in range(these[0].steps()):
+            stage(these, at(i, *plan))
+
     def gather_chain(name, x):
         chains[name] = GatherChain(after(x), "tensor", n_t)
         return chains[name]
 
     def deal_g():
-        pending["g"] = lax.all_to_all(after(cotangent), "dp", split_axis=1, concat_axis=1, tiled=True)
+        env["own_g1"] = deal(after(cotangent[1]))
 
     def spread_later(*keys):
         for key in keys:
             pending[key] = spread(key)
 
-    def steps_of(chain, *plan):
-        for i in range(chain.steps()):
-            stage([chain], at(i, *plan))
+    def steps_of(these, *plan):
+        for i in range(these[0].steps()):
+            stage(these, at(i, *plan))
 
     steps_of(
-        gather_chain("x1", own_x[1]), [norm_qkv_of(0)], [attend_of(0), hidden(0), deal_g], [join("g")]
+        [gather_chain("x1", own_x[1]), gather_chain("g0", own_g[0])],
+        [norm_qkv_of(0), hidden(0)],
+        [attend_of(0), deal_g],
+        [branch(0)],
     )
-    own_g = list(env.pop("g").reshape(micros, rows, width))
+    own_g[1] = env.pop("own_g1")
     steps_of(
-        gather_chain("g0", own_g[0]), [branch(0)], [norm_qkv_of(1)], [attend_of(1), hidden(1)]
+        [gather_chain("g1", own_g[1])],
+        [norm_qkv_of(1)],
+        [hidden(1), attend_of(1)],
+        [branch(1), arrange_g(0)],
     )
     pending["so0"] = scattered_rows("branch0")
-    steps_of(
-        gather_chain("g1", own_g[1]),
-        [branch(1), arrange_g(0)],
-        [back_in(0), back_attend(0)],
-        [back_out(0), join("so0")],
+    pending["so1"] = scattered_rows("branch1")
+    stage(
+        [], [arrange_g(1), dense_grads, swapped("wd"), fc2_grads, swapped("w2"), back_in(0)]
     )
-    pending["so1"] = scattered_rows("branch1")
+    spread_later("w2")
+    stage([], [back_attend(0), back_out(0), back_in(1), join("w2", "so0")])
     pending["si0"] = scattered_rows("e0")
-    stage([], [arrange_g(1), fc2_grads, swapped("w2"), back_in(1), output_of(0)])
-    spread_later("w2")
-    stage([], [fc1_grads, swapped("w1"), back_attend(1), back_out(1), join("w2", "so1")])
+    spread_later("wd")
+    stage([], [fc1_grads, swapped("w1"), join("wd")])
+    spread_later("w1")
+    stage(
+        [],
+        [
+            back_attend(1),
+            qkv_grads,
+            swapped("wq"),
+            back_out(1),
+            join("w1", "so1"),
+        ],
+    )
     pending["si1"] = scattered_rows("e1")
-    spread_later("w1")
+    spread_later("wq")
     sums = jnp.concatenate([env["sums0"] + env["sums1"], sum_g[None]], axis=0)
     sums = sums.reshape(5, n_d, n_t, eighth).transpose(1, 2, 0, 3).reshape(n_d, -1)
     qkvb = (env["bq0"] + env["bq1"]).reshape(heads, n_d, -1).transpose(1, 0, 2).reshape(n_d, -1)
     fc1b = (env["b10"] + env["b11"]).reshape(heads, n_d, -1).transpose(1, 0, 2).reshape(n_d, -1)
-    small = SmallScatter(jnp.concatenate([sums, qkvb, fc1b], axis=1), "dp", n_d)
-    stage([small], [qkv_grads, swapped("wq"), dense_grads, swapped("wd"), fc2_final, join("w1")])
-    spread_later("wq")
-    stage([small], [output_of(1), fc1_final, join("wq")])
-    spread_later("wd")
-    stage([small], [qkv_final, join("wd", "si0")])
-    while small.bit:
-        stage([small])
-    small_out = small.out[0]
+    small = jnp.concatenate([sums, qkvb, fc1b], axis=1)
     n_sum = 5 * n_t * eighth
-    env["mine"] = direct_scatter(small_out[:n_sum].reshape(n_t, 5 * eighth), "tensor", n_t)
-    stage([], [input_of(0), dense_final, join("si1")])
-    input_of(1)()
-
-    outputs = pair("output")
-    grads_in = pair("input")
+
+    def small_over_dp():
+        env["small"] = direct_scatter(small, "dp", n_d)
+
+    def small_over_tensor():
+        env["mine"] = direct_scatter(env["small"][:n_sum].reshape(n_t, -1), "tensor", n_t)
+
+    stage([], [small_over_dp, fc2_final, fc1_final, dense_final, join("wq", "si0")])
+    output_rows()
+    stage([], [small_over_tensor, qkv_final, join("rows")])
+    stage([], [join("si1")])
+    grads_in = undeal(jnp.stack([input_of(0), input_of(1)]))
+    small_out = env["small"]
+
+    outputs = env["rows"]
 
     small = small_out
     mine = env["mine"].reshape(5, eighth)
@@ -982,8 +957,8 @@
     fc1b = small[n_sum + n_qb :].reshape(heads, -1)
 
     return (
-        jnp.stack(outputs),
-        jnp.stack(grads_in),
+        outputs,
+        grads_in,
         mine[0],
         mine[1],
         mine[2],

time: 825 us -> 749 us (0.908)
  waiting for transfers between devices: 254 us -> 166 us
  blocking collectives: 0 us -> 19.4 us
    ppermute x12, waiting for transfers between devices: 120 us -> 46.3 us  [step(): self.right.append(lax.ppermute(to_left, self.axis, pairs))]
    ppermute x3 -> x0, waiting for transfers between devices: 36.6 us -> none  [step(): lax.ppermute(sent, self.axis, [(i, i ^ bit) for i in range(self.n)])]
    all_to_all x5 -> x3, waiting for transfers between devices: 23.1 us -> 52.8 us  [the longest x2 27.7 us: undeal(): return lax.all_to_all(x, 'dp', split_axis=1, concat_axis=1, tiled=True)]
    ppermute x10, waiting for transfers between devices: 38.2 us -> 12.7 us  [direct_gather(): got = jnp.stack([x] + [lax.ppermute(x, axis, pairs) for pairs in shifts(n)])]
    ppermute x3 -> x10, waiting for transfers between devices: 0.01 us -> 22.7 us  [direct_scatter(): total = total + lax.ppermute(sent, axis, pairs)]
    all_to_all x4 -> x3, waiting for transfers between devices: 19.5 us -> 0.01 us  [spread(): lax.all_to_all(both_cores.astype(BF), 'dp', split_axis=0, concat_axis=0,...]
    all_to_all x0 -> x1, blocking collectives: none -> 19.4 us  [spread(): lax.all_to_all(both_cores.astype(BF), 'dp', split_axis=0, concat_axis=0,...]
    all_to_all x2, waiting for transfers between devices: 15.2 us -> 28.7 us  [deal(): lax.all_to_all(x, 'dp', split_axis=0, concat_axis=0, tiled=True)]
  transfers between devices with their start and end apart: 62 -> 63, of which waited for: 22 -> 20; matrix products, arithmetic and copies ran while one was open for 9% -> 10% of each run, Pallas kernels for 39% -> 43%
where the time goes in v3:
time: 749 us; the launch traced here: 739 us
  Pallas kernels  317 us (42%)
  waiting for transfers between devices  166 us (22%)
  starting transfers between devices  124 us (17%)
  other arithmetic  62.2 us (8%)
  local copies, waits for them, and re-layouts  34.1 us (5%)
  blocking collectives  19.4 us (3%)
  between operations  15.9 us (2%)
    pallas_call x3, Pallas kernels, grad_of(): pl.pallas_call(functools.partial(grad_kernel, len(lhs)), grid_spec=pltpu....  70.8 us
    ppermute x12, waiting for transfers between devices, step(): self.right.append(lax.ppermute(to_left, self.axis, pairs))  46.3 us
    pallas_call x2, Pallas kernels, back_out_of(): pl.pallas_call(back_out_kernel, grid=(width // tile,), in_specs=[pl.Block...  45.1 us
    pallas_call x2, Pallas kernels, hidden_of(): pl.pallas_call(hidden_kernel, grid=(n_ff // tile,), in_specs=[resident(tw...  39.6 us
    ppermute x12, starting transfers between devices, step(): self.left.append(lax.ppermute(to_right, self.axis, pairs))  39.5 us
    pallas_call x2, Pallas kernels, norm_qkv(): pl.pallas_call(functools.partial(norm_qkv_kernel, len(blocks)), grid_spec...  38.3 us
    pallas_call x2, Pallas kernels, back_in_of(): pl.pallas_call(back_in_kernel, grid=(n_ff // tile,), in_specs=[resident(g...  34.1 us
    pallas_call x2, Pallas kernels, branch_of(): pl.pallas_call(branch_kernel, grid=(width // tile,), in_specs=[resident(m...  32.2 us
  transfers between devices with their start and end apart: 63, of which 20 were waited for; matrix products, arithmetic and copies ran while one was open for 10% of the time, Pallas kernels for 43%

profile of v3, /device:TPU:0, one launch (start us, length us, event | category | flops | bytes accessed | tf_op | source)
XLA Modules:
  0.0 738.8 jit_solution(16140313375526314558)
XLA Ops:
  7.2 3.1 slice_bitcast_fusion.2
  10.4 5.3 all-to-all-start
  16.0 15.1 %all-to-all-done = bf16[8,32,2048]{2,1,0:T(8,128)(2,1)S(1)} async-done(((bf16[8,32,2048]{2,1,0:T(8,128)(2,1)}), bf16[8,32,2048]{2,1,0:T(8,128)(2,1)S(1)}, u32[]{:S(2)}, u32[]{:S(2)}) %all-to-all-start) | async-done | bytes 1048608 | tf_op jit(solution)/shard_map/all_to_all | solution.py:615
  31.2 2.9 pad_maximum_fusion.3
  35.4 5.6 collective-permute-start.7
  52.8 5.5 collective-permute-done.8.refs_4_
  62.2 3.1 pad_maximum_fusion
  65.3 4.9 all-to-all-start.1
  70.3 5.7 collective-permute-start.11
  76.0 3.5 collective-permute-start.10
  81.5 6.2 collective-permute-done.11
  94.1 25.1 %all-to-all-done.1 = bf16[2,8,32,2048]{3,2,0,1:T(8,128)(2,1)S(1)} async-done(((bf16[2,8,32,2048]{3,2,0,1:T(8,128)(2,1)}), bf16[2,8,32,2048]{3,2,0,1:T(8,128)(2,1)S(1)}, u32[]{:S(2)}, u32[]{:S(2)}) %all-to-all-start.1) | async-done | bytes 2097184 | tf_op jit(solution)/shard_map/all_to_all | solution.py:712
  124.1 10.0 %collective-permute-start.18 = (bf16[256,2048]{1,0:T(8,128)(2,1)}, bf16[256,2048]{1,0:T(8,128)(2,1)}, u32[]{:S(2)}, u32[]{:S(2)}) collective-permute-start(bf16[256,2048]{1,0:T(8,128)(2,1)} %bitcast.15.refs_0_), channel_id=1, source_target_pairs={{0,1},{1,2},{2,3},{4,5},{5,6},{6,7},{8,9},{9,10},{10,11},{12,13},{... | collective-permute-start | bytes 3145736 | tf_op jit(solution)/shard_map/ppermute | solution.py:39
  135.4 6.1 collective-permute-start.16
  144.8 3.0 fusion.22
  147.8 19.2 %norm_qkv.2 = (bf16[4,256,2048]{2,1,0:T(8,128)(2,1)}, bf16[4,256,2048]{2,1,0:T(8,128)(2,1)}, bf16[4,256,2048]{2,1,0:T(8,128)(2,1)}, f32[4,256,1536]{2,1,0:T(8,128)}) custom-call(s32[2]{0:T(128)} %pad_add_fusion.2.me_ref, f32[6,2048]{1,0:T(8,128)} %reshape.550.vectors_ref, f32[1,3584]{1,0:T(1,128)} %pad_maximum_fusion.5.bias_ref, ...), custom_call_target="tpu_custom_call" | custom-call | flops 1572864 | bytes 6656 | tf_op jit(solution)/shard_map/norm_qkv/pallas_call | solution.py:302
  166.9 19.8 %hidden.2 = (bf16[1024,2048]{1,0:T(8,128)(2,1)}, bf16[1024,2048]{1,0:T(8,128)(2,1)}) custom-call(bf16[1024,2048]{1,0:T(8,128)(2,1)} %bitcast.127, bf16[2048,3584]{1,0:T(8,128)(2,1)} %all-gather.5.cloned.1.call-done.refs_7_.w_ref, f32[1,3584]{1,0:T(1,128)} %pad_maximum_fusion.5.bias_ref), custom_call_target="tpu_custom_call" | custom-call | flops 2097152 | bytes 6144 | tf_op jit(solution)/shard_map/hidden/pallas_call | solution.py:328
  192.9 3.6 all-to-all-start.2
  198.8 7.9 %attend.2 = (bf16[4,256,1536]{2,1,0:T(8,128)(2,1)S(1)}, bf16[4,256,512]{2,1,0:T(8,128)(2,1)S(1)}) custom-call(s32[4,256,1]{2,1,0:T(8,128)S(1)} %multiply_add_fusion.posq_ref, s32[4,1,1024]{2,1,0:T(1,128)S(1)} %pad_add_fusion.posk_ref, f32[4,256,128]{2,1,0:T(8,128)S(1)} %maximum_maximum_fusion.cos_ref, f32[4,256,128]{2,1,0:T(8,128)S(1)} %maximum_maximum_fusion.1.sin_ref, ...), custom_call_target="tpu_custom_call" | custom-call | flops 1073741824 | bytes 12582912 | tf_op jit(solution)/shard_map/attend/pallas_call | solution.py:171
  209.3 13.6 %all-to-all-done.2 = bf16[8,32,2048]{2,1,0:T(8,128)(2,1)S(1)} async-done(((bf16[8,32,2048]{2,1,0:T(8,128)(2,1)}), bf16[8,32,2048]{2,1,0:T(8,128)(2,1)S(1)}, u32[]{:S(2)}, u32[]{:S(2)}) %all-to-all-start.2) | async-done | bytes 1048608 | tf_op jit(solution)/shard_map/all_to_all | solution.py:615
  222.9 15.2 %collective-permute-done.23.refs_5_ = bf16[256,2048]{1,0:T(8,128)(2,1)} collective-permute-done((bf16[256,2048]{1,0:T(8,128)(2,1)}, bf16[256,2048]{1,0:T(8,128)(2,1)}, u32[]{:S(2)}, u32[]{:S(2)}) %collective-permute-start.23) | collective-permute-done | bytes 1048608 | tf_op jit(solution)/shard_map/ppermute | solution.py:41
  244.1 16.1 %branch.2 = bf16[1024,2048]{1,0:T(8,128)(2,1)} custom-call(bf16[1024,512]{1,0:T(8,128)(2,1)} %bitcast.101, bf16[1024,2048]{1,0:T(8,128)(2,1)} %get-tuple-element.393.act_ref.refs_2_, bf16[8,2,32,2048]{3,2,1,0:T(8,128)(2,1)} %bitcast.120, bf16[2048,2048]{1,0:T(8,128)(2,1)} %all-gather.7.cloned.1.call-done.w_ref), custom_call_target="tpu_custom_call" | custom-call | flops 2621440 | bytes 5120 | tf_op jit(solution)/shard_map/branch/pallas_call | solution.py:406
  260.2 7.9 %collective-permute-done.25.refs_6_ = bf16[256,2048]{1,0:T(8,128)(2,1)} collective-permute-done((bf16[256,2048]{1,0:T(8,128)(2,1)}, bf16[256,2048]{1,0:T(8,128)(2,1)}, u32[]{:S(2)}, u32[]{:S(2)}) %collective-permute-start.25) | collective-permute-done | bytes 1048608 | tf_op jit(solution)/shard_map/ppermute | solution.py:41
  268.1 17.7 %collective-permute-done.27.refs_6_ = bf16[256,2048]{1,0:T(8,128)(2,1)} collective-permute-done((bf16[256,2048]{1,0:T(8,128)(2,1)}, bf16[256,2048]{1,0:T(8,128)(2,1)}, u32[]{:S(2)}, u32[]{:S(2)}) %collective-permute-start.27) | collective-permute-done | bytes 1048608 | tf_op jit(solution)/shard_map/ppermute | solution.py:41
  287.1 5.6 collective-permute-start.28
  292.7 19.2 %norm_qkv.3 = (bf16[4,256,2048]{2,1,0:T(8,128)(2,1)}, bf16[4,256,2048]{2,1,0:T(8,128)(2,1)}, bf16[4,256,2048]{2,1,0:T(8,128)(2,1)}, f32[4,256,1536]{2,1,0:T(8,128)}) custom-call(s32[2]{0:T(128)} %pad_add_fusion.2.me_ref, f32[6,2048]{1,0:T(8,128)} %reshape.550.vectors_ref, f32[1,3584]{1,0:T(1,128)} %pad_maximum_fusion.5.bias_ref, ...), custom_call_target="tpu_custom_call" | custom-call | flops 1572864 | bytes 6656 | tf_op jit(solution)/shard_map/norm_qkv/pallas_call | solution.py:302
  314.4 19.8 %hidden.3 = (bf16[1024,2048]{1,0:T(8,128)(2,1)}, bf16[1024,2048]{1,0:T(8,128)(2,1)}) custom-call(bf16[1024,2048]{1,0:T(8,128)(2,1)} %bitcast.129, bf16[2048,3584]{1,0:T(8,128)(2,1)} %all-gather.5.cloned.1.call-done.refs_7_.w_ref, f32[1,3584]{1,0:T(1,128)} %pad_maximum_fusion.5.bias_ref), custom_call_target="tpu_custom_call" | custom-call | flops 2097152 | bytes 6144 | tf_op jit(solution)/shard_map/hidden/pallas_call | solution.py:328
  334.2 7.9 %attend.3 = (bf16[4,256,1536]{2,1,0:T(8,128)(2,1)S(1)}, bf16[4,256,512]{2,1,0:T(8,128)(2,1)S(1)}) custom-call(s32[4,256,1]{2,1,0:T(8,128)S(1)} %multiply_add_fusion.posq_ref, s32[4,1,1024]{2,1,0:T(1,128)S(1)} %pad_add_fusion.1.posk_ref, f32[4,256,128]{2,1,0:T(8,128)S(1)} %maximum_maximum_fusion.cos_ref, f32[4,256,128]{2,1,0:T(8,128)S(1)} %maximum_maximum_fusion.1.sin_ref, ...), custom_call_target="tpu_custom_call" | custom-call | flops 1073741824 | bytes 12582912 | tf_op jit(solution)/shard_map/attend/pallas_call | solution.py:171
  347.8 6.1 arrange.2
  353.9 16.1 %branch.3 = bf16[1024,2048]{1,0:T(8,128)(2,1)} custom-call(bf16[1024,512]{1,0:T(8,128)(2,1)} %bitcast.103, bf16[1024,2048]{1,0:T(8,128)(2,1)} %get-tuple-element.399.act_ref.refs_3_, bf16[8,2,32,2048]{3,2,1,0:T(8,128)(2,1)} %bitcast.121, bf16[2048,2048]{1,0:T(8,128)(2,1)} %all-gather.7.cloned.1.call-done.w_ref), custom_call_target="tpu_custom_call" | custom-call | flops 2621440 | bytes 5120 | tf_op jit(solution)/shard_map/branch/pallas_call | solution.py:406
  370.6 6.1 arrange.3
  376.7 25.4 %grad_fc2.1 = (bf16[4,256,2048]{2,1,0:T(8,128)(2,1)}, bf16[4,256,2048]{2,1,0:T(8,128)(2,1)}) custom-call(s32[1]{0:T(128)} %bitcast.37.me_ref, bf16[1024,2048]{1,0:T(8,128)(2,1)} %bitcast.107, bf16[1024,2048]{1,0:T(8,128)(2,1)} %bitcast.110, bf16[1024,2048]{1,0:T(8,128)(2,1)} %get-tuple-element.393.act_ref.refs_2_, ...), custom_call_target="tpu_custom_call" | custom-call | flops 4194304 | bytes 6144 | tf_op jit(solution)/shard_map/grad_fc2/pallas_call | solution.py:526
  402.1 9.5 %grad_dense.1 = (bf16[4,2,32,2048]{3,2,1,0:T(8,128)(2,1)}, bf16[4,2,32,2048]{3,2,1,0:T(8,128)(2,1)}) custom-call(s32[1]{0:T(128)} %bitcast.37.me_ref, bf16[1024,512]{1,0:T(8,128)(2,1)} %bitcast.102, bf16[1024,512]{1,0:T(8,128)(2,1)} %bitcast.104, bf16[1024,2048]{1,0:T(8,128)(2,1)} %bitcast.108, bf16[1024,2048]{1,0:T(8,128)(2,1)} %bitcast.111), custom_call_target="tpu_custom_call" | custom-call | flops 1048576 | bytes 3072 | tf_op jit(solution)/shard_map/grad_dense/pallas_call | solution.py:564
  412.1 17.2 %back_in.2 = (bf16[1024,512]{1,0:T(8,128)(2,1)}, bf16[1024,2048]{1,0:T(8,128)(2,1)}, f32[1,2048]{1,0:T(1,128)}) custom-call(bf16[1024,2048]{1,0:T(8,128)(2,1)} %bitcast.109, bf16[8,2,32,2048]{3,2,1,0:T(8,128)(2,1)} %bitcast.122, bf16[2048,2048]{1,0:T(8,128)(2,1)} %all-gather.7.cloned.1.call-done.w_ref, bf16[1024,2048]{1,0:T(8,128)(2,1)} %get-tuple-element.410.slope_ref), custom_call_target="tpu_custom_call" | custom-call | flops 2621440 | bytes 5120 | tf_op jit(solution)/shard_map/back_in/pallas_call | solution.py:440
  429.3 6.8 add_convert_fusion.1
  436.1 4.9 all-to-all-start.3
  441.3 17.0 %back_in.3 = (bf16[1024,512]{1,0:T(8,128)(2,1)}, bf16[1024,2048]{1,0:T(8,128)(2,1)}, f32[1,2048]{1,0:T(1,128)}) custom-call(bf16[1024,2048]{1,0:T(8,128)(2,1)} %bitcast.112, bf16[8,2,32,2048]{3,2,1,0:T(8,128)(2,1)} %bitcast.123, bf16[2048,2048]{1,0:T(8,128)(2,1)} %all-gather.7.cloned.1.call-done.w_ref, bf16[1024,2048]{1,0:T(8,128)(2,1)} %get-tuple-element.433.slope_ref), custom_call_target="tpu_custom_call" | custom-call | flops 2621440 | bytes 5120 | tf_op jit(solution)/shard_map/back_in/pallas_call | solution.py:440
  458.2 9.7 %attend_back.2 = (bf16[4,256,1536]{2,1,0:T(8,128)(2,1)S(1)}, f32[2,1,768]{2,1,0:T(1,128)S(1)}) custom-call(s32[4,256,1]{2,1,0:T(8,128)S(1)} %multiply_add_fusion.posq_ref, s32[4,1,1024]{2,1,0:T(1,128)S(1)} %pad_add_fusion.posk_ref, f32[4,256,128]{2,1,0:T(8,128)S(1)} %maximum_maximum_fusion.cos_ref, f32[4,256,128]{2,1,0:T(8,128)S(1)} %maximum_maximum_fusion.1.sin_ref, ...), custom_call_target="tpu_custom_call" | custom-call | flops 2684354560 | bytes 7864320 | tf_op jit(solution)/shard_map/attend_back/pallas_call | solution.py:192
  469.6 22.5 %back_out.2 = (bf16[1024,2048]{1,0:T(8,128)(2,1)}, f32[4,2048]{1,0:T(4,128)}) custom-call(f32[6,2048]{1,0:T(8,128)} %reshape.550.vectors_ref, bf16[1024,1536]{1,0:T(8,128)(2,1)} %bitcast.97, bf16[1024,2048]{1,0:T(8,128)(2,1)} %get-tuple-element.447.pre_ref.refs_2_, bf16[2048,3584]{1,0:T(8,128)(2,1)} %all-gather.5.cloned.1.call-done.refs_7_.w_ref, ...), custom_call_target="tpu_custom_call" | custom-call | flops 3670016 | bytes 7680 | tf_op jit(solution)/shard_map/back_out/pallas_call | solution.py:481
  492.2 25.5 %grad_fc1.1 = (bf16[4,256,2048]{2,1,0:T(8,128)(2,1)}, bf16[4,256,2048]{2,1,0:T(8,128)(2,1)}) custom-call(s32[1]{0:T(128)} %bitcast.37.me_ref, bf16[1024,2048]{1,0:T(8,128)(2,1)} %bitcast.128, bf16[1024,2048]{1,0:T(8,128)(2,1)} %bitcast.130, bf16[1024,2048]{1,0:T(8,128)(2,1)} %get-tuple-element.447.pre_ref.refs_2_, ...), custom_call_target="tpu_custom_call" | custom-call | flops 4194304 | bytes 6144 | tf_op jit(solution)/shard_map/grad_fc1/pallas_call | solution.py:526
  518.1 19.4 %all_to_all.45 = bf16[4,64,2048]{2,1,0:T(8,128)(2,1)} all-to-all(bf16[4,64,2048]{2,1,0:T(8,128)(2,1)S(1)} %add_convert_fusion.3), channel_id=1, replica_groups={{0,8,16,24},{4,12,20,28},{1,9,17,25},{5,13,21,29},{2,10,18,26},{6,14,22..., dimensions={0} | all-to-all | bytes 2097152 | tf_op jit(solution)/shard_map/all_to_all | solution.py:846
  537.5 4.1 add_convert_fusion
  541.6 5.0 all-to-all-start.5
  546.6 9.7 %attend_back.3 = (bf16[4,256,1536]{2,1,0:T(8,128)(2,1)S(1)}, f32[2,1,768]{2,1,0:T(1,128)S(1)}) custom-call(s32[4,256,1]{2,1,0:T(8,128)S(1)} %multiply_add_fusion.posq_ref, s32[4,1,1024]{2,1,0:T(1,128)S(1)} %pad_add_fusion.1.posk_ref, f32[4,256,128]{2,1,0:T(8,128)S(1)} %maximum_maximum_fusion.cos_ref, f32[4,256,128]{2,1,0:T(8,128)S(1)} %maximum_maximum_fusion.1.sin_ref, ...), custom_call_target="tpu_custom_call" | custom-call | flops 2684354560 | bytes 7864320 | tf_op jit(solution)/shard_map/attend_back/pallas_call | solution.py:192
  558.0 20.0 %grad_qkv.1 = (bf16[4,256,1536]{2,1,0:T(8,128)(2,1)}, bf16[4,256,1536]{2,1,0:T(8,128)(2,1)}) custom-call(s32[1]{0:T(128)} %bitcast.37.me_ref, bf16[1024,2048]{1,0:T(8,128)(2,1)} %bitcast.136, bf16[1024,2048]{1,0:T(8,128)(2,1)} %bitcast.139, bf16[1024,1536]{1,0:T(8,128)(2,1)} %bitcast.98, bf16[1024,1536]{1,0:T(8,128)(2,1)} %bitcast.99), custom_call_target="tpu_custom_call" | custom-call | flops 3145728 | bytes 5120 | tf_op jit(solution)/shard_map/grad_qkv/pallas_call | solution.py:526
  578.0 22.6 %back_out.3 = (bf16[1024,2048]{1,0:T(8,128)(2,1)}, f32[4,2048]{1,0:T(4,128)}) custom-call(f32[6,2048]{1,0:T(8,128)} %reshape.550.vectors_ref, bf16[1024,1536]{1,0:T(8,128)(2,1)} %bitcast.100, bf16[1024,2048]{1,0:T(8,128)(2,1)} %get-tuple-element.468.refs_3_.pre_ref, bf16[2048,3584]{1,0:T(8,128)(2,1)} %all-gather.5.cloned.1.call-done.refs_7_.w_ref, ...), custom_call_target="tpu_custom_call" | custom-call | flops 3670016 | bytes 7680 | tf_op jit(solution)/shard_map/back_out/pallas_call | solution.py:481
  600.7 5.4 add_convert_fusion.2
  606.0 4.7 all-to-all-start.6
  615.5 2.5 collective-permute-start.44
  620.5 4.5 convert_reduce_fusion.1
  625.0 4.6 convert_reduce_fusion
  629.6 19.1 %collective-permute-done.38 = f32[1728]{0:T(1024)S(1)} collective-permute-done((f32[1728]{0:T(1024)S(1)}, f32[1728]{0:T(1024)S(1)}, u32[]{:S(2)}, u32[]{:S(2)}) %collective-permute-start.38) | collective-permute-done | bytes 6944 | tf_op jit(solution)/shard_map/ppermute | solution.py:67
  653.3 2.5 fusion.7
  657.3 4.4 all-to-all-start.7
  665.1 4.5 collective-permute-start.45
  669.6 3.8 collective-permute-start.46
  673.4 3.6 convert_reduce_fusion.2
  677.1 3.2 reshape.547
  680.3 8.1 %all-to-all-done.7 = bf16[2,8,32,2048]{3,2,0,1:T(8,128)(2,1)} async-done(((bf16[2,8,32,2048]{3,2,0,1:T(8,128)(2,1)}), bf16[2,8,32,2048]{3,2,0,1:T(8,128)(2,1)}, u32[]{:S(2)}, u32[]{:S(2)}) %all-to-all-start.7) | async-done | bytes 2097184 | tf_op jit(solution)/shard_map/all_to_all | solution.py:619
  692.2 2.2 fusion.6
  696.8 4.4 all-to-all-start.8
  701.2 3.3 copy.59
  708.2 19.6 %all-to-all-done.8 = bf16[2,8,32,2048]{3,2,0,1:T(8,128)(2,1)} async-done(((bf16[2,8,32,2048]{3,2,0,1:T(8,128)(2,1)}), bf16[2,8,32,2048]{3,2,0,1:T(8,128)(2,1)}, u32[]{:S(2)}, u32[]{:S(2)}) %all-to-all-start.8) | async-done | bytes 2097184 | tf_op jit(solution)/shard_map/all_to_all | solution.py:619
  727.9 3.2 copy.60
  (307 shorter events, 93.5 us)
Async XLA Ops:
  10.4 20.7 %all-to-all-start = ((bf16[8,32,2048]{2,1,0:T(8,128)(2,1)}), bf16[8,32,2048]{2,1,0:T(8,128)(2,1)S(1)}, u32[]{:S(2)}, u32[]{:S(2)}) async-start(bf16[8,32,2048]{2,1,0:T(8,128)(2,1)} %get-tuple-element.575), calls=%async_computation | async-start | bytes 2097152 | tf_op jit(solution)/shard_map/all_to_all | solution.py:615
  15.7 132.1 %all-gather.5.cloned.1.call-start = ((), (), s32[]{:S(2)}) async-start(), calls=%async_computation.13 | async-start | bytes 16515072 | tf_op jit(solution)/shard_map/all_gather | solution.py:654
  34.1 24.1 %collective-permute-start.8 = (bf16[256,2048]{1,0:T(8,128)(2,1)S(1)}, bf16[256,2048]{1,0:T(8,128)(2,1)}, u32[]{:S(2)}, u32[]{:S(2)}) collective-permute-start(bf16[256,2048]{1,0:T(8,128)(2,1)S(1)} %bitcast.113), channel_id=1, source_target_pairs={{1,0},{2,1},{3,2},{5,4},{6,5},{7,6},{9,8},{10,9},{11,10},{13,12},{... | collective-permute-start | bytes 3145736 | tf_op jit(solution)/shard_map/ppermute | solution.py:41
  35.4 23.9 %collective-permute-start.7 = (bf16[256,2048]{1,0:T(8,128)(2,1)S(1)}, bf16[256,2048]{1,0:T(8,128)(2,1)}, u32[]{:S(2)}, u32[]{:S(2)}) collective-permute-start(bf16[256,2048]{1,0:T(8,128)(2,1)S(1)} %bitcast.114), channel_id=1, source_target_pairs={{0,1},{1,2},{2,3},{4,5},{5,6},{6,7},{8,9},{9,10},{10,11},{12,13},{... | collective-permute-start | bytes 3145736 | tf_op jit(solution)/shard_map/ppermute | solution.py:39
  42.5 1.8 collective-permute-start.6
  42.5 3.6 collective-permute-start.5
  43.1 3.6 collective-permute-start.4
  44.3 4.3 collective-permute-start.3
  46.1 3.0 collective-permute-start.2
  46.7 4.5 collective-permute-start.1
  48.6 4.0 collective-permute-start
  59.3 30.1 %collective-permute-start.12 = (bf16[256,2048]{1,0:T(8,128)(2,1)}, bf16[256,2048]{1,0:T(8,128)(2,1)}, u32[]{:S(2)}, u32[]{:S(2)}) collective-permute-start(bf16[256,2048]{1,0:T(8,128)(2,1)} %collective-permute-done.7.refs_1_), channel_id=1, source_target_pairs={{1,2},{2,3},{5,6},{6,7},{9,10},{10,11},{13,14},{14,15},{17,18},{18... | collective-permute-start | bytes 3145736 | tf_op jit(solution)/shard_map/ppermute | solution.py:39
  61.0 28.4 %collective-permute-start.13 = (bf16[256,2048]{1,0:T(8,128)(2,1)}, bf16[256,2048]{1,0:T(8,128)(2,1)}, u32[]{:S(2)}, u32[]{:S(2)}) collective-permute-start(bf16[256,2048]{1,0:T(8,128)(2,1)} %collective-permute-done.8.refs_4_), channel_id=1, source_target_pairs={{1,0},{2,1},{5,4},{6,5},{9,8},{10,9},{13,12},{14,13},{17,16},{18,1... | collective-permute-start | bytes 3145736 | tf_op jit(solution)/shard_map/ppermute | solution.py:41
  65.3 54.0 %all-to-all-start.1 = ((bf16[2,8,32,2048]{3,2,0,1:T(8,128)(2,1)}), bf16[2,8,32,2048]{3,2,0,1:T(8,128)(2,1)S(1)}, u32[]{:S(2)}, u32[]{:S(2)}) async-start(bf16[2,8,32,2048]{3,2,0,1:T(8,128)(2,1)} %pad_maximum_fusion), calls=%async_computation.1 | async-start | bytes 4194304 | tf_op jit(solution)/shard_map/all_to_all | solution.py:712
  70.2 173.8 %all-gather.9.cloned.1.call-start = ((), (), s32[]{:S(2)}) async-start(), calls=%async_computation.19 | async-start | bytes 2359296 | tf_op jit(solution)/shard_map/all_gather | solution.py:727
  70.3 17.4 %collective-permute-start.11 = (bf16[3072]{0:T(1024)(128)(2,1)S(1)}, bf16[3072]{0:T(1024)(128)(2,1)S(1)}, u32[]{:S(2)}, u32[]{:S(2)}) collective-permute-start(bf16[3072]{0:T(1024)(128)(2,1)S(1)} %reshape.511), channel_id=1, source_target_pairs={{0,3},{1,0},{2,1},{3,2},{4,7},{5,4},{6,5},{7,6},{8,11},{9,8},{10,9... | collective-permute-start | bytes 18440 | tf_op jit(solution)/shard_map/ppermute | solution.py:56
  76.0 13.0 %collective-permute-start.10 = (bf16[3072]{0:T(1024)(128)(2,1)S(1)}, bf16[3072]{0:T(1024)(128)(2,1)S(1)}, u32[]{:S(2)}, u32[]{:S(2)}) collective-permute-start(bf16[3072]{0:T(1024)(128)(2,1)S(1)} %reshape.511), channel_id=1, source_target_pairs={{0,2},{1,3},{2,0},{3,1},{4,6},{5,7},{6,4},{7,5},{8,10},{9,11},{10,... | collective-permute-start | bytes 18440 | tf_op jit(solution)/shard_map/ppermute | solution.py:56
  79.5 9.5 %collective-permute-start.9 = (bf16[3072]{0:T(1024)(128)(2,1)S(1)}, bf16[3072]{0:T(1024)(128)(2,1)S(1)}, u32[]{:S(2)}, u32[]{:S(2)}) collective-permute-start(bf16[3072]{0:T(1024)(128)(2,1)S(1)} %reshape.511), channel_id=1, source_target_pairs={{0,1},{1,2},{2,3},{3,0},{4,5},{5,6},{6,7},{7,4},{8,9},{9,10},{10,1... | collective-permute-start | bytes 18440 | tf_op jit(solution)/shard_map/ppermute | solution.py:56
  89.4 29.9 %collective-permute-start.14 = (bf16[256,2048]{1,0:T(8,128)(2,1)}, bf16[256,2048]{1,0:T(8,128)(2,1)}, u32[]{:S(2)}, u32[]{:S(2)}) collective-permute-start(bf16[256,2048]{1,0:T(8,128)(2,1)} %collective-permute-done.12.refs_2_), channel_id=1, source_target_pairs={{2,3},{6,7},{10,11},{14,15},{18,19},{22,23},{26,27},{30,31}} | collective-permute-start | bytes 3145736 | tf_op jit(solution)/shard_map/ppermute | solution.py:39
  91.1 28.2 %collective-permute-start.15 = (bf16[256,2048]{1,0:T(8,128)(2,1)}, bf16[256,2048]{1,0:T(8,128)(2,1)}, u32[]{:S(2)}, u32[]{:S(2)}) collective-permute-start(bf16[256,2048]{1,0:T(8,128)(2,1)} %collective-permute-done.13.refs_5_), channel_id=1, source_target_pairs={{1,0},{5,4},{9,8},{13,12},{17,16},{21,20},{25,24},{29,28}} | collective-permute-start | bytes 3145736 | tf_op jit(solution)/shard_map/ppermute | solution.py:41
  119.3 124.8 %all-gather.7.cloned.1.call-start = ((), (), s32[]{:S(2)}) async-start(), calls=%async_computation.14 | async-start | bytes 9437184 | tf_op jit(solution)/shard_map/all_gather | solution.py:726
  122.8 63.9 %collective-permute-start.19 = (bf16[256,2048]{1,0:T(8,128)(2,1)}, bf16[256,2048]{1,0:T(8,128)(2,1)}, u32[]{:S(2)}, u32[]{:S(2)}) collective-permute-start(bf16[256,2048]{1,0:T(8,128)(2,1)} %bitcast.15.refs_0_), channel_id=1, source_target_pairs={{1,0},{2,1},{3,2},{5,4},{6,5},{7,6},{9,8},{10,9},{11,10},{13,12},{... | collective-permute-start | bytes 3145736 | tf_op jit(solution)/shard_map/ppermute | solution.py:41
  124.1 62.6 %collective-permute-start.18 = (bf16[256,2048]{1,0:T(8,128)(2,1)}, bf16[256,2048]{1,0:T(8,128)(2,1)}, u32[]{:S(2)}, u32[]{:S(2)}) collective-permute-start(bf16[256,2048]{1,0:T(8,128)(2,1)} %bitcast.15.refs_0_), channel_id=1, source_target_pairs={{0,1},{1,2},{2,3},{4,5},{5,6},{6,7},{8,9},{9,10},{10,11},{12,13},{... | collective-permute-start | bytes 3145736 | tf_op jit(solution)/shard_map/ppermute | solution.py:39
  134.1 52.6 %collective-permute-start.17 = (bf16[256,2048]{1,0:T(8,128)(2,1)S(1)}, bf16[256,2048]{1,0:T(8,128)(2,1)}, u32[]{:S(2)}, u32[]{:S(2)}) collective-permute-start(bf16[256,2048]{1,0:T(8,128)(2,1)S(1)} %bitcast.124), channel_id=1, source_target_pairs={{1,0},{2,1},{3,2},{5,4},{6,5},{7,6},{9,8},{10,9},{11,10},{13,12},{... | collective-permute-start | bytes 3145736 | tf_op jit(solution)/shard_map/ppermute | solution.py:41
  135.4 51.3 %collective-permute-start.16 = (bf16[256,2048]{1,0:T(8,128)(2,1)S(1)}, bf16[256,2048]{1,0:T(8,128)(2,1)}, u32[]{:S(2)}, u32[]{:S(2)}) collective-permute-start(bf16[256,2048]{1,0:T(8,128)(2,1)S(1)} %bitcast.125), channel_id=1, source_target_pairs={{0,1},{1,2},{2,3},{4,5},{5,6},{6,7},{8,9},{9,10},{10,11},{12,13},{... | collective-permute-start | bytes 3145736 | tf_op jit(solution)/shard_map/ppermute | solution.py:39
  186.7 36.2 %collective-permute-start.20 = (bf16[256,2048]{1,0:T(8,128)(2,1)}, bf16[256,2048]{1,0:T(8,128)(2,1)}, u32[]{:S(2)}, u32[]{:S(2)}) collective-permute-start(bf16[256,2048]{1,0:T(8,128)(2,1)} %collective-permute-done.16.refs_1_), channel_id=1, source_target_pairs={{1,2},{2,3},{5,6},{6,7},{9,10},{10,11},{13,14},{14,15},{17,18},{18... | collective-permute-start | bytes 3145736 | tf_op jit(solution)/shard_map/ppermute | solution.py:39
  188.4 34.5 %collective-permute-start.21 = (bf16[256,2048]{1,0:T(8,128)(2,1)}, bf16[256,2048]{1,0:T(8,128)(2,1)}, u32[]{:S(2)}, u32[]{:S(2)}) collective-permute-start(bf16[256,2048]{1,0:T(8,128)(2,1)} %collective-permute-done.17.refs_4_), channel_id=1, source_target_pairs={{1,0},{2,1},{5,4},{6,5},{9,8},{10,9},{13,12},{14,13},{17,16},{18,1... | collective-permute-start | bytes 3145736 | tf_op jit(solution)/shard_map/ppermute | solution.py:41
  189.7 33.3 %collective-permute-start.22 = (bf16[256,2048]{1,0:T(8,128)(2,1)}, bf16[256,2048]{1,0:T(8,128)(2,1)}, u32[]{:S(2)}, u32[]{:S(2)}) collective-permute-start(bf16[256,2048]{1,0:T(8,128)(2,1)} %collective-permute-done.18.refs_1_), channel_id=1, source_target_pairs={{1,2},{2,3},{5,6},{6,7},{9,10},{10,11},{13,14},{14,15},{17,18},{18... | collective-permute-start | bytes 3145736 | tf_op jit(solution)/shard_map/ppermute | solution.py:39
  191.3 46.8 %collective-permute-start.23 = (bf16[256,2048]{1,0:T(8,128)(2,1)}, bf16[256,2048]{1,0:T(8,128)(2,1)}, u32[]{:S(2)}, u32[]{:S(2)}) collective-permute-start(bf16[256,2048]{1,0:T(8,128)(2,1)} %collective-permute-done.19.refs_4_), channel_id=1, source_target_pairs={{1,0},{2,1},{5,4},{6,5},{9,8},{10,9},{13,12},{14,13},{17,16},{18,1... | collective-permute-start | bytes 3145736 | tf_op jit(solution)/shard_map/ppermute | solution.py:41
  192.9 30.0 %all-to-all-start.2 = ((bf16[8,32,2048]{2,1,0:T(8,128)(2,1)}), bf16[8,32,2048]{2,1,0:T(8,128)(2,1)S(1)}, u32[]{:S(2)}, u32[]{:S(2)}) async-start(bf16[8,32,2048]{2,1,0:T(8,128)(2,1)} %get-tuple-element.309), calls=%async_computation.2 | async-start | bytes 2097152 | tf_op jit(solution)/shard_map/all_to_all | solution.py:615
  196.5 295.7 %reduce-scatter.5.cloned.1.call-start = ((), (), s32[]{:S(2)}) async-start(), calls=%async_computation.15 | async-start | bytes 5242880 | tf_op jit(solution)/shard_map/reduce_scatter | solution.py:765
  222.9 64.2 %copy-start.13 = (bf16[8,32,2048]{2,1,0:T(8,128)(2,1)}, bf16[8,32,2048]{2,1,0:T(8,128)(2,1)S(1)}, u32[]{:S(2)}) copy-start(bf16[8,32,2048]{2,1,0:T(8,128)(2,1)S(1)} %all-to-all-done.2) | copy-start | bytes 3145732
  238.1 22.1 %collective-permute-start.24 = (bf16[256,2048]{1,0:T(8,128)(2,1)}, bf16[256,2048]{1,0:T(8,128)(2,1)}, u32[]{:S(2)}, u32[]{:S(2)}) collective-permute-start(bf16[256,2048]{1,0:T(8,128)(2,1)} %collective-permute-done.20.refs_2_), channel_id=1, source_target_pairs={{2,3},{6,7},{10,11},{14,15},{18,19},{22,23},{26,27},{30,31}} | collective-permute-start | bytes 3145736 | tf_op jit(solution)/shard_map/ppermute | solution.py:39
  239.8 28.3 %collective-permute-start.25 = (bf16[256,2048]{1,0:T(8,128)(2,1)}, bf16[256,2048]{1,0:T(8,128)(2,1)}, u32[]{:S(2)}, u32[]{:S(2)}) collective-permute-start(bf16[256,2048]{1,0:T(8,128)(2,1)} %collective-permute-done.21.refs_5_), channel_id=1, source_target_pairs={{1,0},{5,4},{9,8},{13,12},{17,16},{21,20},{25,24},{29,28}} | collective-permute-start | bytes 3145736 | tf_op jit(solution)/shard_map/ppermute | solution.py:41
  241.1 27.0 %collective-permute-start.26 = (bf16[256,2048]{1,0:T(8,128)(2,1)}, bf16[256,2048]{1,0:T(8,128)(2,1)}, u32[]{:S(2)}, u32[]{:S(2)}) collective-permute-start(bf16[256,2048]{1,0:T(8,128)(2,1)} %collective-permute-done.22.refs_2_), channel_id=1, source_target_pairs={{2,3},{6,7},{10,11},{14,15},{18,19},{22,23},{26,27},{30,31}} | collective-permute-start | bytes 3145736 | tf_op jit(solution)/shard_map/ppermute | solution.py:39
  242.8 43.1 %collective-permute-start.27 = (bf16[256,2048]{1,0:T(8,128)(2,1)}, bf16[256,2048]{1,0:T(8,128)(2,1)}, u32[]{:S(2)}, u32[]{:S(2)}) collective-permute-start(bf16[256,2048]{1,0:T(8,128)(2,1)} %collective-permute-done.23.refs_5_), channel_id=1, source_target_pairs={{1,0},{5,4},{9,8},{13,12},{17,16},{21,20},{25,24},{29,28}} | collective-permute-start | bytes 3145736 | tf_op jit(solution)/shard_map/ppermute | solution.py:41
  285.8 26.0 %collective-permute-start.29 = (bf16[256,2048]{1,0:T(8,128)(2,1)S(1)}, bf16[256,2048]{1,0:T(8,128)(2,1)}, u32[]{:S(2)}, u32[]{:S(2)}) collective-permute-start(bf16[256,2048]{1,0:T(8,128)(2,1)S(1)} %bitcast.131), channel_id=1, source_target_pairs={{1,0},{2,1},{3,2},{5,4},{6,5},{7,6},{9,8},{10,9},{11,10},{13,12},{... | collective-permute-start | bytes 3145736 | tf_op jit(solution)/shard_map/ppermute | solution.py:41
  287.1 24.7 %collective-permute-start.28 = (bf16[256,2048]{1,0:T(8,128)(2,1)S(1)}, bf16[256,2048]{1,0:T(8,128)(2,1)}, u32[]{:S(2)}, u32[]{:S(2)}) collective-permute-start(bf16[256,2048]{1,0:T(8,128)(2,1)S(1)} %bitcast.132), channel_id=1, source_target_pairs={{0,1},{1,2},{2,3},{4,5},{5,6},{6,7},{8,9},{9,10},{10,11},{12,13},{... | collective-permute-start | bytes 3145736 | tf_op jit(solution)/shard_map/ppermute | solution.py:39
  311.9 32.9 %collective-permute-start.30 = (bf16[256,2048]{1,0:T(8,128)(2,1)}, bf16[256,2048]{1,0:T(8,128)(2,1)S(1)}, u32[]{:S(2)}, u32[]{:S(2)}) collective-permute-start(bf16[256,2048]{1,0:T(8,128)(2,1)} %collective-permute-done.28.refs_1_), channel_id=1, source_target_pairs={{1,2},{2,3},{5,6},{6,7},{9,10},{10,11},{13,14},{14,15},{17,18},{18... | collective-permute-start | bytes 3145736 | tf_op jit(solution)/shard_map/ppermute | solution.py:39
  312.6 32.2 %collective-permute-start.31 = (bf16[256,2048]{1,0:T(8,128)(2,1)}, bf16[256,2048]{1,0:T(8,128)(2,1)}, u32[]{:S(2)}, u32[]{:S(2)}) collective-permute-start(bf16[256,2048]{1,0:T(8,128)(2,1)} %collective-permute-done.29.refs_4_), channel_id=1, source_target_pairs={{1,0},{2,1},{5,4},{6,5},{9,8},{10,9},{13,12},{14,13},{17,16},{18,1... | collective-permute-start | bytes 3145736 | tf_op jit(solution)/shard_map/ppermute | solution.py:41
  344.8 25.1 %collective-permute-start.32 = (bf16[256,2048]{1,0:T(8,128)(2,1)S(1)}, bf16[256,2048]{1,0:T(8,128)(2,1)}, u32[]{:S(2)}, u32[]{:S(2)}) collective-permute-start(bf16[256,2048]{1,0:T(8,128)(2,1)S(1)} %collective-permute-done.30.refs_2_), channel_id=1, source_target_pairs={{2,3},{6,7},{10,11},{14,15},{18,19},{22,23},{26,27},{30,31}} | collective-permute-start | bytes 3145736 | tf_op jit(solution)/shard_map/ppermute | solution.py:39
  346.5 23.5 %collective-permute-start.33 = (bf16[256,2048]{1,0:T(8,128)(2,1)}, bf16[256,2048]{1,0:T(8,128)(2,1)}, u32[]{:S(2)}, u32[]{:S(2)}) collective-permute-start(bf16[256,2048]{1,0:T(8,128)(2,1)} %collective-permute-done.31.refs_5_), channel_id=1, source_target_pairs={{1,0},{5,4},{9,8},{13,12},{17,16},{21,20},{25,24},{29,28}} | collective-permute-start | bytes 3145736 | tf_op jit(solution)/shard_map/ppermute | solution.py:41
  370.0 230.6 %reduce-scatter.7.cloned.1.call-start = ((), (), s32[]{:S(2)}) async-start(), calls=%async_computation.16 | async-start | bytes 5242880 | tf_op jit(solution)/shard_map/reduce_scatter | solution.py:765
  402.1 27.2 %collective-permute-start.35 = (bf16[4,256,2048]{2,1,0:T(8,128)(2,1)}, bf16[4,256,2048]{2,1,0:T(8,128)(2,1)}, u32[]{:S(2)}, u32[]{:S(2)}) collective-permute-start(bf16[4,256,2048]{2,1,0:T(8,128)(2,1)} %get-tuple-element.409), channel_id=1, source_target_pairs={{0,4},{4,0},{8,12},{12,8},{16,20},{20,16},{24,28},{28,24},{1,5},{5... | collective-permute-start | bytes 12582920 | tf_op jit(solution)/shard_map/ppermute | solution.py:840
  411.6 17.7 %collective-permute-start.34 = (bf16[4,64,2048]{2,1,0:T(8,128)(2,1)}, bf16[4,64,2048]{2,1,0:T(8,128)(2,1)S(1)}, u32[]{:S(2)}, u32[]{:S(2)}) collective-permute-start(bf16[4,64,2048]{2,1,0:T(8,128)(2,1)} %bitcast.163), channel_id=1, source_target_pairs={{0,4},{4,0},{8,12},{12,8},{16,20},{20,16},{24,28},{28,24},{1,5},{5... | collective-permute-start | bytes 3145736 | tf_op jit(solution)/shard_map/ppermute | solution.py:840
  436.1 56.0 %all-to-all-start.3 = ((bf16[4,256,2048]{2,1,0:T(8,128)(2,1)}), bf16[4,256,2048]{2,1,0:T(8,128)(2,1)}, u32[]{:S(2)}, u32[]{:S(2)}) async-start(bf16[4,256,2048]{2,1,0:T(8,128)(2,1)} %add_convert_fusion.1), calls=%async_computation.3 | async-start | bytes 8388608 | tf_op jit(solution)/shard_map/all_to_all | solution.py:846
  441.0 212.2 %reduce-scatter.9.cloned.1.call-start = ((), (), s32[]{:S(2)}) async-start(), calls=%async_computation.17 | async-start | bytes 5242880 | tf_op jit(solution)/shard_map/reduce_scatter | solution.py:765
  517.7 19.8 %collective-permute-start.36 = (bf16[4,256,2048]{2,1,0:T(8,128)(2,1)}, bf16[4,256,2048]{2,1,0:T(8,128)(2,1)S(1)}, u32[]{:S(2)}, u32[]{:S(2)}) collective-permute-start(bf16[4,256,2048]{2,1,0:T(8,128)(2,1)} %get-tuple-element.458), channel_id=1, source_target_pairs={{0,4},{4,0},{8,12},{12,8},{16,20},{20,16},{24,28},{28,24},{1,5},{5... | collective-permute-start | bytes 12582920 | tf_op jit(solution)/shard_map/ppermute | solution.py:840
  541.6 59.0 %all-to-all-start.5 = ((bf16[4,256,2048]{2,1,0:T(8,128)(2,1)}), bf16[4,256,2048]{2,1,0:T(8,128)(2,1)}, u32[]{:S(2)}, u32[]{:S(2)}) async-start(bf16[4,256,2048]{2,1,0:T(8,128)(2,1)} %add_convert_fusion), calls=%async_computation.6 | async-start | bytes 8388608 | tf_op jit(solution)/shard_map/all_to_all | solution.py:846
  546.6 143.6 %reduce-scatter.11.cloned.1.call-start = ((), (), s32[]{:S(2)}) async-start(), calls=%async_computation.18 | async-start | bytes 5242880 | tf_op jit(solution)/shard_map/reduce_scatter | solution.py:765
  578.0 22.6 %collective-permute-start.37 = (bf16[4,256,1536]{2,1,0:T(8,128)(2,1)}, bf16[4,256,1536]{2,1,0:T(8,128)(2,1)}, u32[]{:S(2)}, u32[]{:S(2)}) collective-permute-start(bf16[4,256,1536]{2,1,0:T(8,128)(2,1)} %get-tuple-element.478), channel_id=1, source_target_pairs={{0,4},{4,0},{8,12},{12,8},{16,20},{20,16},{24,28},{28,24},{1,5},{5... | collective-permute-start | bytes 9437192 | tf_op jit(solution)/shard_map/ppermute | solution.py:840
  606.0 47.2 %all-to-all-start.6 = ((bf16[4,256,1536]{2,1,0:T(8,128)(2,1)}), bf16[4,256,1536]{2,1,0:T(8,128)(2,1)}, u32[]{:S(2)}, u32[]{:S(2)}) async-start(bf16[4,256,1536]{2,1,0:T(8,128)(2,1)} %add_convert_fusion.2), calls=%async_computation.8 | async-start | bytes 6291456 | tf_op jit(solution)/shard_map/all_to_all | solution.py:846
  615.0 33.7 %collective-permute-start.38 = (f32[1728]{0:T(1024)S(1)}, f32[1728]{0:T(1024)S(1)}, u32[]{:S(2)}, u32[]{:S(2)}) collective-permute-start(f32[1728]{0:T(1024)S(1)} %get-tuple-element.558), channel_id=1, source_target_pairs={{0,4},{4,8},{8,12},{12,16},{16,20},{20,24},{24,28},{28,0},{1,5},{5... | collective-permute-start | bytes 20744 | tf_op jit(solution)/shard_map/ppermute | solution.py:67
  615.5 33.2 %collective-permute-start.44 = (f32[1728]{0:T(1024)S(1)}, f32[1728]{0:T(1024)S(1)}, u32[]{:S(2)}, u32[]{:S(2)}) collective-permute-start(f32[1728]{0:T(1024)S(1)} %get-tuple-element.559), channel_id=1, source_target_pairs={{0,28},{4,0},{8,4},{12,8},{16,12},{20,16},{24,20},{28,24},{1,29},{... | collective-permute-start | bytes 20744 | tf_op jit(solution)/shard_map/ppermute | solution.py:67
  618.0 31.7 %collective-permute-start.43 = (f32[1728]{0:T(1024)S(1)}, f32[1728]{0:T(1024)S(1)}, u32[]{:S(2)}, u32[]{:S(2)}) collective-permute-start(f32[1728]{0:T(1024)S(1)} %get-tuple-element.560), channel_id=1, source_target_pairs={{0,24},{4,28},{8,0},{12,4},{16,8},{20,12},{24,16},{28,20},{1,25},{... | collective-permute-start | bytes 20744 | tf_op jit(solution)/shard_map/ppermute | solution.py:67
  619.6 30.1 %collective-permute-start.42 = (f32[1728]{0:T(1024)S(1)}, f32[1728]{0:T(1024)S(1)}, u32[]{:S(2)}, u32[]{:S(2)}) collective-permute-start(f32[1728]{0:T(1024)S(1)} %get-tuple-element.561), channel_id=1, source_target_pairs={{0,20},{4,24},{8,28},{12,0},{16,4},{20,8},{24,12},{28,16},{1,21},{... | collective-permute-start | bytes 20744 | tf_op jit(solution)/shard_map/ppermute | solution.py:67
  619.8 29.9 %collective-permute-start.41 = (f32[1728]{0:T(1024)S(1)}, f32[1728]{0:T(1024)S(1)}, u32[]{:S(2)}, u32[]{:S(2)}) collective-permute-start(f32[1728]{0:T(1024)S(1)} %get-tuple-element.562), channel_id=1, source_target_pairs={{0,16},{4,20},{8,24},{12,28},{16,0},{20,4},{24,8},{28,12},{1,17},{... | collective-permute-start | bytes 20744 | tf_op jit(solution)/shard_map/ppermute | solution.py:67
  648.7 3.1 collective-permute-start.40
  648.7 4.5 collective-permute-start.39
  657.3 31.0 %all-to-all-start.7 = ((bf16[2,8,32,2048]{3,2,0,1:T(8,128)(2,1)}), bf16[2,8,32,2048]{3,2,0,1:T(8,128)(2,1)}, u32[]{:S(2)}, u32[]{:S(2)}) async-start(bf16[2,8,32,2048]{3,2,0,1:T(8,128)(2,1)} %pad_maximum_fusion.1), calls=%async_computation.10 | async-start | bytes 4194304 | tf_op jit(solution)/shard_map/all_to_all | solution.py:619
  665.1 15.1 %collective-permute-start.45 = (f32[320]{0:T(512)S(1)}, f32[320]{0:T(512)S(1)}, u32[]{:S(2)}, u32[]{:S(2)}) collective-permute-start(f32[320]{0:T(512)S(1)} %get-tuple-element.566), channel_id=1, source_target_pairs={{0,1},{1,2},{2,3},{3,0},{4,5},{5,6},{6,7},{7,4},{8,9},{9,10},{10,1... | collective-permute-start | bytes 3848 | tf_op jit(solution)/shard_map/ppermute | solution.py:67
  669.6 10.7 %collective-permute-start.47 = (f32[320]{0:T(512)S(1)}, f32[320]{0:T(512)S(1)}, u32[]{:S(2)}, u32[]{:S(2)}) collective-permute-start(f32[320]{0:T(512)S(1)} %get-tuple-element.567), channel_id=1, source_target_pairs={{0,3},{1,0},{2,1},{3,2},{4,7},{5,4},{6,5},{7,6},{8,11},{9,8},{10,9... | collective-permute-start | bytes 3848 | tf_op jit(solution)/shard_map/ppermute | solution.py:67
  669.6 10.7 %collective-permute-start.46 = (f32[320]{0:T(512)S(1)}, f32[320]{0:T(512)S(1)}, u32[]{:S(2)}, u32[]{:S(2)}) collective-permute-start(f32[320]{0:T(512)S(1)} %get-tuple-element.568), channel_id=1, source_target_pairs={{0,2},{1,3},{2,0},{3,1},{4,6},{5,7},{6,4},{7,5},{8,10},{9,11},{10,... | collective-permute-start | bytes 3848 | tf_op jit(solution)/shard_map/ppermute | solution.py:67
  696.8 31.0 %all-to-all-start.8 = ((bf16[2,8,32,2048]{3,2,0,1:T(8,128)(2,1)}), bf16[2,8,32,2048]{3,2,0,1:T(8,128)(2,1)}, u32[]{:S(2)}, u32[]{:S(2)}) async-start(bf16[2,8,32,2048]{3,2,0,1:T(8,128)(2,1)} %pad_maximum_fusion.2), calls=%async_computation.12 | async-start | bytes 4194304 | tf_op jit(solution)/shard_map/all_to_all | solution.py:619
  (43 other events, 518.8 us)
Sparse Core Ops, SparseCore 0:
  34.2 102.9 all-gather.4
  139.1 27.9 all-gather.8
  169.6 65.6 all-gather.6
  370.1 81.2 reduce-scatter.4
  453.6 77.2 reduce-scatter.6
  533.1 77.2 reduce-scatter.8
  612.8 77.3 reduce-scatter.10

commit v4 on v3

--- a/solution.py
+++ b/solution.py
@@ -390,7 +390,8 @@
     return dense_ref[:, h].reshape(n * e, cols)
 
 
-def branch_kernel(mixed_ref, act_ref, dense_ref, w_ref, out_ref):
+def branch_kernel(mixed_ref, act_ref, dense_ref, w_ref, *refs):
+    out_ref = refs[-1]
     total = nt(act_ref[...], w_ref[...])
     for h in range(dense_ref.shape[1]):
         total += jnp.dot(
@@ -398,11 +399,12 @@
             head_rows(dense_ref, h),
             preferred_element_type=F32,
         )
-    out_ref[...] = total.astype(BF)
-
-
-def branch_of(mixed, act, dense, w_fc2):
+    out_ref[...] = total.astype(BF).reshape(out_ref.shape)
+
+
+def branch_of(mixed, act, dense, w_fc2, slot, shape, before=None):
     total, width, tile = act.shape[0], w_fc2.shape[0], 512
+    parts, _, rows, _ = shape
     return pl.pallas_call(
         branch_kernel,
         grid=(width // tile,),
@@ -411,13 +413,15 @@
             resident(act.shape),
             pl.BlockSpec(dense.shape[:3] + (tile,), lambda j: (0, 0, 0, j)),
             pl.BlockSpec((tile, w_fc2.shape[1]), lambda j: (j, 0)),
-        ],
-        out_specs=pl.BlockSpec((total, tile), lambda j: (0, j)),
-        out_shape=jax.ShapeDtypeStruct((total, width), BF),
+        ]
+        + ([] if before is None else [pl.BlockSpec(memory_space=pl.ANY)]),
+        out_specs=pl.BlockSpec((parts, 1, rows, tile), lambda j: (0, slot, 0, j)),
+        out_shape=jax.ShapeDtypeStruct(shape, BF),
+        input_output_aliases={} if before is None else {4: 0},
         cost_estimate=cost(2 * total * (dense.size + w_fc2.size), 2 * (act.size * 3 + w_fc2.size)),
         compiler_params=big(),
         name="branch",
-    )(mixed, act, dense, w_fc2)
+    )(mixed, act, dense, w_fc2, *([] if before is None else [before]))
 
 
 def back_in_kernel(g_ref, dense_ref, w_ref, slope_ref, dmix_ref, pre_ref, bias_ref):
@@ -500,49 +504,37 @@
 
 
 def grad_kernel(count, me_ref, *refs):
-    lhs, rhs, (sent_ref, kept_ref) = refs[:count], refs[count : 2 * count], refs[-2:]
+    lhs, rhs, out_ref = refs[:count], refs[count : 2 * count], refs[-1]
     total = tn(lhs[0][...], rhs[0][...])
     for a, b in zip(lhs[1:], rhs[1:]):
         total += tn(a[...], b[...])
-    step, half = pl.program_id(0), pl.num_programs(0) // 2
-
-    @pl.when(step < half)
-    def _():
-        sent_ref[0] = total.astype(BF)
-
-    @pl.when(step >= half)
-    def _():
-        kept_ref[0] = total.astype(BF)
-
-
-def grad_of(parity, lhs, rhs, cuts, name):
+    if len(refs) > 2 * count + 1:
+        total += refs[2 * count][0].astype(F32)
+    out_ref[0] = total.astype(BF)
+
+
+def grad_of(parity, lhs, rhs, cuts, name, got=None):
     total, m = lhs[0].shape
     n, tile, half = rhs[0].shape[1], m // cuts, cuts // 2
-    shape = jax.ShapeDtypeStruct((half, tile, n), BF)
-
-    def left(j, me):
-        return (0, jnp.where(j < half, 2 * j + 1 - me[0], 2 * (j - half) + me[0]))
-
+    block = pl.BlockSpec((1, tile, n), lambda j, me: (j, 0, 0))
     return pl.pallas_call(
         functools.partial(grad_kernel, len(lhs)),
         grid_spec=pltpu.PrefetchScalarGridSpec(
             num_scalar_prefetch=1,
-            grid=(cuts,),
-            in_specs=[pl.BlockSpec((total, tile), left)] * len(lhs)
+            grid=(half,),
+            in_specs=[pl.BlockSpec((total, tile), lambda j, me: (0, 2 * j + me[0]))] * len(lhs)
             + [
                 pl.BlockSpec(r.shape, lambda j, me: (0, 0), pipeline_mode=pl.Buffered(1))
                 for r in rhs
-            ],
-            out_specs=[
-                pl.BlockSpec((1, tile, n), lambda j, me: (jnp.minimum(j, half - 1), 0, 0)),
-                pl.BlockSpec((1, tile, n), lambda j, me: (jnp.maximum(j - half, 0), 0, 0)),
-            ],
+            ]
+            + ([] if got is None else [block]),
+            out_specs=block,
         ),
-        out_shape=[shape, shape],
-        cost_estimate=cost(2 * len(lhs) * total * m * n, 4 * total * (m + n) + 2 * m * n),
+        out_shape=jax.ShapeDtypeStruct((half, tile, n), BF),
+        cost_estimate=cost(len(lhs) * total * m * n, 4 * total * (m + n) + 2 * m * n),
         compiler_params=big(),
         name=name,
-    )(parity, *lhs, *rhs)
+    )(parity, *lhs, *rhs, *([] if got is None else [got]))
 
 
 def head_grad_kernel(count, me_ref, *refs):
@@ -647,11 +639,11 @@
         [attn_gain, attn_shift, ffn_gain, ffn_shift, dense_bias, fc2_bias]
         + [qkv_bias.reshape(-1), fc1_bias.reshape(-1)]
     )
+    n_qkv = heads * 3 * HD
+    env["near"] = jnp.concatenate([qkv_weight.reshape(-1, n_qkv), fc1_weight], axis=1)
     stage([])
 
-    n_qkv = heads * 3 * HD
-    near = jnp.concatenate([after(qkv_weight).reshape(-1, n_qkv), after(fc1_weight)], axis=1)
-    w_near = lax.all_gather(near, "dp", axis=0, tiled=True)
+    w_near = lax.all_gather(env.pop("near"), "dp", axis=0, tiled=True)
 
     parts = jnp.arange(n_t, dtype=jnp.int32)
     local = jnp.arange(rows, dtype=jnp.int32)
@@ -756,16 +748,24 @@
 
     def branch(m):
         def fn():
-            parts = branch_of(env[f"mixed{m}"], env[f"act{m}"], w_dense, w_fc2)
-            env[f"branch{m}"] = parts
+            env["branch"] = branch_of(
+                env[f"mixed{m}"],
+                env[f"act{m}"],
+                w_dense,
+                w_fc2,
+                m,
+                (n_t, micros, rows, width),
+                env.get("branch"),
+            )
 
         return fn
 
     def scattered_rows(name):
-        return lax.psum_scatter(env.pop(name), "tensor", scatter_dimension=0, tiled=True)
+        terms = env.pop(name).reshape(-1, width)
+        return lax.psum_scatter(terms, "tensor", scatter_dimension=0, tiled=True)
 
     def output_of(m):
-        total = env.pop(f"so{m}").astype(F32)
+        total = env["so"].reshape(micros, rows, width)[m].astype(F32)
         return (own_x[m].astype(F32) + total + out_shift).astype(BF)
 
     def arrange_g(m):
@@ -822,19 +822,35 @@
     swap = [(i, i ^ 1) for i in range(n_d)]
     same_parity = [list(range(p, n_d, 2)) for p in range(2)]
 
-    def fc2_grads():
-        env["w2_sent"], env["w2_kept"] = grad_of(parity, pair("g"), pair("act"), n_d, "grad_fc2")
+    sides = {"w2": ("g", "act"), "w1": ("two", "pre"), "wq": ("one", "dqkv")}
+
+    def sent_grads(key):
+        def fn():
+            lhs, rhs = (pair(side) for side in sides[key])
+            sent = grad_of(1 - parity, lhs, rhs, n_d, f"grad_{key}_sent")
+            env[f"{key}_got"] = lax.ppermute(sent, "dp", swap)
+
+        return fn
+
+    def sent_only(key):
+        def fn():
+            lhs, rhs = (pair(side) for side in sides[key])
+            env[f"{key}_sent"] = grad_of(1 - parity, lhs, rhs, n_d, f"grad_{key}_sent")
+
+        return fn
+
+    def kept_grads(key):
+        def fn():
+            lhs, rhs = (pair(side) for side in sides[key])
+            got = env.pop(f"{key}_got")
+            env[f"{key}_pair"] = grad_of(parity, lhs, rhs, n_d, f"grad_{key}_kept", got)
+
+        return fn
 
     def dense_grads():
         halves = head_grad_of(parity, pair("mixed"), pair("g"), n_d, "grad_dense")
         env["wd_sent"], env["wd_kept"] = (h.reshape(n_d // 2, -1, width) for h in halves)
 
-    def fc1_grads():
-        env["w1_sent"], env["w1_kept"] = grad_of(parity, pair("two"), pair("pre"), n_d, "grad_fc1")
-
-    def qkv_grads():
-        env["wq_sent"], env["wq_kept"] = grad_of(parity, pair("one"), pair("dqkv"), n_d, "grad_qkv")
-
     def swapped(key):
         def fn():
             env[f"{key}_got"] = lax.ppermute(env.pop(f"{key}_sent"), "dp", swap)
@@ -842,22 +858,18 @@
         return fn
 
     def spread(key):
-        both_cores = env.pop(f"{key}_kept").astype(F32) + env.pop(f"{key}_got").astype(F32)
+        if f"{key}_pair" in env:
+            pair_sums = env.pop(f"{key}_pair")
+        else:
+            pair_sums = env.pop(f"{key}_kept").astype(F32) + env.pop(f"{key}_got").astype(F32)
         return lax.all_to_all(
-            both_cores.astype(BF),
+            pair_sums.astype(BF),
             "dp",
             split_axis=0,
             concat_axis=0,
             axis_index_groups=same_parity,
             tiled=True,
         )
-
-    def both(*fns):
-        def fn():
-            for each in fns:
-                each()
-
-        return fn
 
     def summed(key):
         return jnp.sum(env.pop(key).astype(F32), axis=0)
@@ -906,28 +918,19 @@
         [hidden(1), attend_of(1)],
         [branch(1), arrange_g(0)],
     )
-    pending["so0"] = scattered_rows("branch0")
-    pending["so1"] = scattered_rows("branch1")
-    stage(
-        [], [arrange_g(1), dense_grads, swapped("wd"), fc2_grads, swapped("w2"), back_in(0)]
-    )
+    pending["so"] = scattered_rows("branch")
+    stage([], [arrange_g(1), sent_grads("w2"), back_in(0)])
+    stage([], [kept_grads("w2")])
     spread_later("w2")
-    stage([], [back_attend(0), back_out(0), back_in(1), join("w2", "so0")])
+    stage([], [back_attend(0), back_out(0), back_in(1), join("w2")])
     pending["si0"] = scattered_rows("e0")
-    spread_later("wd")
-    stage([], [fc1_grads, swapped("w1"), join("wd")])
+    stage([], [sent_grads("w1"), back_attend(1)])
+    stage([], [kept_grads("w1")])
     spread_later("w1")
-    stage(
-        [],
-        [
-            back_attend(1),
-            qkv_grads,
-            swapped("wq"),
-            back_out(1),
-            join("w1", "so1"),
-        ],
-    )
+    stage([], [sent_only("wq"), back_out(1), join("w1", "so")])
     pending["si1"] = scattered_rows("e1")
+    output_rows()
+    stage([], [swapped("wq"), dense_grads, kept_grads("wq"), join("rows")])
     spread_later("wq")
     sums = jnp.concatenate([env["sums0"] + env["sums1"], sum_g[None]], axis=0)
     sums = sums.reshape(5, n_d, n_t, eighth).transpose(1, 2, 0, 3).reshape(n_d, -1)
@@ -937,16 +940,21 @@
     n_sum = 5 * n_t * eighth
 
     def small_over_dp():
-        env["small"] = direct_scatter(small, "dp", n_d)
+        for s, pairs in enumerate(shifts(n_d), 1):
+            sent = lax.dynamic_index_in_dim(small, (my_d + s) % n_d, 0, keepdims=False)
+            env[f"small{s}"] = lax.ppermute(sent, "dp", pairs)
+        env["small0"] = lax.dynamic_index_in_dim(small, my_d, 0, keepdims=False)
 
     def small_over_tensor():
+        env["small"] = sum(env.pop(f"small{s}") for s in range(n_d))
         env["mine"] = direct_scatter(env["small"][:n_sum].reshape(n_t, -1), "tensor", n_t)
 
-    stage([], [small_over_dp, fc2_final, fc1_final, dense_final, join("wq", "si0")])
-    output_rows()
-    stage([], [small_over_tensor, qkv_final, join("rows")])
+    stage([], [small_over_dp, swapped("wd"), fc2_final, fc1_final, join("wq", "si0")])
+    spread_later("wd")
+    stage([], [qkv_final, small_over_tensor, join("wd")])
     stage([], [join("si1")])
     grads_in = undeal(jnp.stack([input_of(0), input_of(1)]))
+    dense_final()
     small_out = env["small"]
 
     outputs = env["rows"]

time: 749 us -> 735 us (0.981)
  other arithmetic: 62.2 us -> 41.9 us
  blocking collectives: 19.4 us -> 0 us
  Pallas kernels: 317 us -> 329 us
  waiting for transfers between devices: 166 us -> 178 us
  local copies, waits for them, and re-layouts: 34.1 us -> 42.3 us
    ppermute x0 -> x9, waiting for transfers between devices: none -> 24.4 us  [the longest x7 24.4 us: small_over_dp(): env[f'small{s}'] = lax.ppermute(sent, 'dp', pairs)]
    ppermute x10 -> x3, waiting for transfers between devices: 22.7 us -> 0.01 us  [direct_scatter(): total = total + lax.ppermute(sent, axis, pairs)]
    all_to_all x1 -> x0, blocking collectives: 19.4 us -> none  [spread(): lax.all_to_all(both_cores.astype(BF), 'dp', split_axis=0, concat_axis=0,...]
    all_to_all x3 -> x4, waiting for transfers between devices: 0.01 us -> 16.7 us  [spread(): lax.all_to_all(pair_sums.astype(BF), 'dp', split_axis=0, concat_axis=0, a...]
    convert_element_type x4 -> x1, other arithmetic: 16.7 us -> 1.38 us  [spread(): pair_sums.astype(BF)]
    pallas_call x3 -> x6, Pallas kernels: 70.8 us -> 82 us  [grad_of(): pl.pallas_call(functools.partial(grad_kernel, len(lhs)), grid_spec=pltpu....]
    all_to_all x3 -> x4, starting transfers between devices: 14.5 us -> 22.6 us  [spread(): lax.all_to_all(pair_sums.astype(BF), 'dp', split_axis=0, concat_axis=0, a...]
    ppermute x12, starting transfers between devices: 39.5 us -> 31.6 us  [step(): self.left.append(lax.ppermute(to_right, self.axis, pairs))]
  transfers between devices with their start and end apart: 63 -> 63, of which waited for: 20 -> 21; matrix products, arithmetic and copies ran while one was open for 10% -> 8% of each run, Pallas kernels for 43% -> 45%
where the time goes in v4:
time: 735 us; the launch traced here: 726 us
  Pallas kernels  329 us (45%)
  waiting for transfers between devices  178 us (24%)
  starting transfers between devices  119 us (16%)
  local copies, waits for them, and re-layouts  42.3 us (6%)
  other arithmetic  41.9 us (6%)
  between operations  15.9 us (2%)
    pallas_call x6, Pallas kernels, grad_of(): pl.pallas_call(functools.partial(grad_kernel, len(lhs)), grid_spec=pltpu....  82 us
    pallas_call x2, Pallas kernels, back_out_of(): pl.pallas_call(back_out_kernel, grid=(width // tile,), in_specs=[pl.Block...  45.2 us
    ppermute x12, waiting for transfers between devices, step(): self.right.append(lax.ppermute(to_left, self.axis, pairs))  43.9 us
    pallas_call x2, Pallas kernels, hidden_of(): pl.pallas_call(hidden_kernel, grid=(n_ff // tile,), in_specs=[resident(tw...  39.6 us
    pallas_call x2, Pallas kernels, norm_qkv(): pl.pallas_call(functools.partial(norm_qkv_kernel, len(blocks)), grid_spec...  38.3 us
    pallas_call x2, Pallas kernels, back_in_of(): pl.pallas_call(back_in_kernel, grid=(n_ff // tile,), in_specs=[resident(g...  34.2 us
    pallas_call x2, Pallas kernels, branch_of(): pl.pallas_call(branch_kernel, grid=(width // tile,), in_specs=[resident(m...  32.2 us
    ppermute x12, starting transfers between devices, step(): self.left.append(lax.ppermute(to_right, self.axis, pairs))  31.6 us
  transfers between devices with their start and end apart: 63, of which 21 were waited for; matrix products, arithmetic and copies ran while one was open for 8% of the time, Pallas kernels for 45%

profile of v4, /device:TPU:0, one launch (start us, length us, event | category | flops | bytes accessed | tf_op | source)
XLA Modules:
  0.0 725.7 jit_solution(14406515152994960213)
XLA Ops:
  7.2 3.1 slice_bitcast_fusion.2
  10.4 5.3 all-to-all-start
  16.9 2.9 pad_maximum_fusion.3
  19.9 11.2 %all-to-all-done = bf16[8,32,2048]{2,1,0:T(8,128)(2,1)S(1)} async-done(((bf16[8,32,2048]{2,1,0:T(8,128)(2,1)}), bf16[8,32,2048]{2,1,0:T(8,128)(2,1)S(1)}, u32[]{:S(2)}, u32[]{:S(2)}) %all-to-all-start) | async-done | bytes 1048608 | tf_op jit(solution)/shard_map/all_to_all | solution.py:607
  31.1 4.5 collective-permute-start.7
  48.0 6.2 collective-permute-done.7.refs_1_
  54.2 5.2 collective-permute-done.8.refs_4_
  62.4 3.1 pad_maximum_fusion
  65.5 4.9 all-to-all-start.1
  70.5 4.2 collective-permute-start.9
  74.7 3.0 collective-permute-start.10
  77.7 2.8 collective-permute-start.11
  80.6 6.6 collective-permute-done.10
  92.2 27.6 %all-to-all-done.1 = bf16[2,8,32,2048]{3,2,0,1:T(8,128)(2,1)S(1)} async-done(((bf16[2,8,32,2048]{3,2,0,1:T(8,128)(2,1)}), bf16[2,8,32,2048]{3,2,0,1:T(8,128)(2,1)S(1)}, u32[]{:S(2)}, u32[]{:S(2)}) %all-to-all-start.1) | async-done | bytes 2097184 | tf_op jit(solution)/shard_map/all_to_all | solution.py:704
  123.4 7.0 collective-permute-start.16
  131.7 6.0 collective-permute-start.18
  142.5 3.0 fusion.20
  145.4 19.2 %norm_qkv.2 = (bf16[4,256,2048]{2,1,0:T(8,128)(2,1)}, bf16[4,256,2048]{2,1,0:T(8,128)(2,1)}, bf16[4,256,2048]{2,1,0:T(8,128)(2,1)}, f32[4,256,1536]{2,1,0:T(8,128)}) custom-call(s32[2]{0:T(128)} %pad_add_fusion.2.me_ref, f32[6,2048]{1,0:T(8,128)} %reshape.583.vectors_ref, f32[1,3584]{1,0:T(1,128)} %pad_maximum_fusion.5.bias_ref, ...), custom_call_target="tpu_custom_call" | custom-call | flops 1572864 | bytes 6656 | tf_op jit(solution)/shard_map/norm_qkv/pallas_call | solution.py:302
  164.6 19.8 %hidden.2 = (bf16[1024,2048]{1,0:T(8,128)(2,1)}, bf16[1024,2048]{1,0:T(8,128)(2,1)}) custom-call(bf16[1024,2048]{1,0:T(8,128)(2,1)} %bitcast.121, bf16[2048,3584]{1,0:T(8,128)(2,1)} %all-gather.5.cloned.1.call-done.refs_7_.w_ref, f32[1,3584]{1,0:T(1,128)} %pad_maximum_fusion.5.bias_ref), custom_call_target="tpu_custom_call" | custom-call | flops 2097152 | bytes 6144 | tf_op jit(solution)/shard_map/hidden/pallas_call | solution.py:328
  190.5 3.6 all-to-all-start.2
  196.1 7.9 %attend.2 = (bf16[4,256,1536]{2,1,0:T(8,128)(2,1)S(1)}, bf16[4,256,512]{2,1,0:T(8,128)(2,1)S(1)}) custom-call(s32[4,256,1]{2,1,0:T(8,128)S(1)} %multiply_add_fusion.posq_ref, s32[4,1,1024]{2,1,0:T(1,128)S(1)} %pad_add_fusion.posk_ref, f32[4,256,128]{2,1,0:T(8,128)S(1)} %maximum_maximum_fusion.cos_ref, f32[4,256,128]{2,1,0:T(8,128)S(1)} %maximum_maximum_fusion.1.sin_ref, ...), custom_call_target="tpu_custom_call" | custom-call | flops 1073741824 | bytes 12582912 | tf_op jit(solution)/shard_map/attend/pallas_call | solution.py:171
  206.6 14.0 %all-to-all-done.2 = bf16[8,32,2048]{2,1,0:T(8,128)(2,1)S(1)} async-done(((bf16[8,32,2048]{2,1,0:T(8,128)(2,1)}), bf16[8,32,2048]{2,1,0:T(8,128)(2,1)S(1)}, u32[]{:S(2)}, u32[]{:S(2)}) %all-to-all-start.2) | async-done | bytes 1048608 | tf_op jit(solution)/shard_map/all_to_all | solution.py:607
  220.6 14.0 %collective-permute-done.23.refs_5_ = bf16[256,2048]{1,0:T(8,128)(2,1)} collective-permute-done((bf16[256,2048]{1,0:T(8,128)(2,1)}, bf16[256,2048]{1,0:T(8,128)(2,1)}, u32[]{:S(2)}, u32[]{:S(2)}) %collective-permute-start.23) | collective-permute-done | bytes 1048608 | tf_op jit(solution)/shard_map/ppermute | solution.py:41
  240.7 16.1 %branch.2.refs_0_ = bf16[4,2,256,2048]{3,2,1,0:T(8,128)(2,1)} custom-call(bf16[1024,512]{1,0:T(8,128)(2,1)} %bitcast.106, bf16[1024,2048]{1,0:T(8,128)(2,1)} %get-tuple-element.472.act_ref.refs_2_, bf16[8,2,32,2048]{3,2,1,0:T(8,128)(2,1)} %bitcast.134, bf16[2048,2048]{1,0:T(8,128)(2,1)} %all-gather.7.cloned.1.call-done.w_ref), custom_call_target="tpu_custom_call" | custom-call | flops 2621440 | bytes 5120 | tf_op jit(solution)/shard_map/branch/pallas_call | solution.py:408
  256.8 7.8 %collective-permute-done.25.refs_6_ = bf16[256,2048]{1,0:T(8,128)(2,1)} collective-permute-done((bf16[256,2048]{1,0:T(8,128)(2,1)}, bf16[256,2048]{1,0:T(8,128)(2,1)}, u32[]{:S(2)}, u32[]{:S(2)}) %collective-permute-start.25) | collective-permute-done | bytes 1048608 | tf_op jit(solution)/shard_map/ppermute | solution.py:41
  264.6 16.4 %collective-permute-done.27.refs_6_ = bf16[256,2048]{1,0:T(8,128)(2,1)} collective-permute-done((bf16[256,2048]{1,0:T(8,128)(2,1)}, bf16[256,2048]{1,0:T(8,128)(2,1)}, u32[]{:S(2)}, u32[]{:S(2)}) %collective-permute-start.27) | collective-permute-done | bytes 1048608 | tf_op jit(solution)/shard_map/ppermute | solution.py:41
  281.0 2.5 collective-permute-start.28
  284.8 19.2 %norm_qkv.3 = (bf16[4,256,2048]{2,1,0:T(8,128)(2,1)}, bf16[4,256,2048]{2,1,0:T(8,128)(2,1)}, bf16[4,256,2048]{2,1,0:T(8,128)(2,1)}, f32[4,256,1536]{2,1,0:T(8,128)}) custom-call(s32[2]{0:T(128)} %pad_add_fusion.2.me_ref, f32[6,2048]{1,0:T(8,128)} %reshape.583.vectors_ref, f32[1,3584]{1,0:T(1,128)} %pad_maximum_fusion.5.bias_ref, ...), custom_call_target="tpu_custom_call" | custom-call | flops 1572864 | bytes 6656 | tf_op jit(solution)/shard_map/norm_qkv/pallas_call | solution.py:302
  306.7 19.7 %hidden.3 = (bf16[1024,2048]{1,0:T(8,128)(2,1)}, bf16[1024,2048]{1,0:T(8,128)(2,1)}) custom-call(bf16[1024,2048]{1,0:T(8,128)(2,1)} %bitcast.124, bf16[2048,3584]{1,0:T(8,128)(2,1)} %all-gather.5.cloned.1.call-done.refs_7_.w_ref, f32[1,3584]{1,0:T(1,128)} %pad_maximum_fusion.5.bias_ref), custom_call_target="tpu_custom_call" | custom-call | flops 2097152 | bytes 6144 | tf_op jit(solution)/shard_map/hidden/pallas_call | solution.py:328
  326.4 7.8 %attend.3 = (bf16[4,256,1536]{2,1,0:T(8,128)(2,1)S(1)}, bf16[4,256,512]{2,1,0:T(8,128)(2,1)S(1)}) custom-call(s32[4,256,1]{2,1,0:T(8,128)S(1)} %multiply_add_fusion.posq_ref, s32[4,1,1024]{2,1,0:T(1,128)S(1)} %pad_add_fusion.1.posk_ref, f32[4,256,128]{2,1,0:T(8,128)S(1)} %maximum_maximum_fusion.cos_ref, f32[4,256,128]{2,1,0:T(8,128)S(1)} %maximum_maximum_fusion.1.sin_ref, ...), custom_call_target="tpu_custom_call" | custom-call | flops 1073741824 | bytes 12582912 | tf_op jit(solution)/shard_map/attend/pallas_call | solution.py:171
  339.5 6.1 arrange.2
  345.6 16.1 %branch.3 = bf16[4,2,256,2048]{3,2,1,0:T(8,128)(2,1)} custom-call(bf16[1024,512]{1,0:T(8,128)(2,1)} %bitcast.108, bf16[1024,2048]{1,0:T(8,128)(2,1)} %get-tuple-element.478.act_ref.refs_3_, bf16[8,2,32,2048]{3,2,1,0:T(8,128)(2,1)} %bitcast.135, bf16[2048,2048]{1,0:T(8,128)(2,1)} %all-gather.7.cloned.1.call-done.w_ref, ...), custom_call_target="tpu_custom_call", output_to_operand_aliasing={{}: (4, {})} | custom-call | flops 2621440 | bytes 5120 | tf_op jit(solution)/shard_map/branch/pallas_call | solution.py:408
  363.7 6.1 arrange.3
  369.8 14.4 %grad_w2_sent.1 = bf16[4,256,2048]{2,1,0:T(8,128)(2,1)} custom-call(s32[1]{0:T(128)S(6)} %sub.109.me_ref, bf16[1024,2048]{1,0:T(8,128)(2,1)} %bitcast.112, bf16[1024,2048]{1,0:T(8,128)(2,1)} %bitcast.116, bf16[1024,2048]{1,0:T(8,128)(2,1)} %get-tuple-element.472.act_ref.refs_2_, bf16[1024,2048]{1,0:T(8,128)(2,1)} %get-tuple-element.478.act_ref.refs_3_), custom_call_target="tpu_custom_call" | custom-call | flops 2097152 | bytes 6144 | tf_op jit(solution)/shard_map/grad_w2_sent/pallas_call | solution.py:520
  384.2 17.0 %back_in.2 = (bf16[1024,512]{1,0:T(8,128)(2,1)}, bf16[1024,2048]{1,0:T(8,128)(2,1)}, f32[1,2048]{1,0:T(1,128)}) custom-call(bf16[1024,2048]{1,0:T(8,128)(2,1)} %bitcast.113, bf16[8,2,32,2048]{3,2,1,0:T(8,128)(2,1)} %bitcast.136, bf16[2048,2048]{1,0:T(8,128)(2,1)} %all-gather.7.cloned.1.call-done.w_ref, bf16[1024,2048]{1,0:T(8,128)(2,1)} %get-tuple-element.464.slope_ref), custom_call_target="tpu_custom_call" | custom-call | flops 2621440 | bytes 5120 | tf_op jit(solution)/shard_map/back_in/pallas_call | solution.py:444
  403.2 14.9 %grad_w2_kept.1 = bf16[4,256,2048]{2,1,0:T(8,128)(2,1)} custom-call(s32[1]{0:T(128)} %bitcast.37.me_ref, bf16[1024,2048]{1,0:T(8,128)(2,1)} %bitcast.114, bf16[1024,2048]{1,0:T(8,128)(2,1)} %bitcast.117, bf16[1024,2048]{1,0:T(8,128)(2,1)} %get-tuple-element.472.act_ref.refs_2_, bf16[1024,2048]{1,0:T(8,128)(2,1)} %get-tuple-element.478.act_ref.refs_3_, ...), custom_call_target="tpu_custom_call" | custom-call | flops 2097152 | bytes 6144 | tf_op jit(solution)/shard_map/grad_w2_kept/pallas_call | solution.py:520
  418.1 8.3 %all-to-all-start.3 = ((bf16[4,256,2048]{2,1,0:T(8,128)(2,1)}), bf16[4,256,2048]{2,1,0:T(8,128)(2,1)}, u32[]{:S(2)}, u32[]{:S(2)}) async-start(bf16[4,256,2048]{2,1,0:T(8,128)(2,1)} %grad_w2_kept.1), calls=%async_computation.3 | async-start | bytes 8388608 | tf_op jit(solution)/shard_map/all_to_all | solution.py:865
  426.6 17.3 %back_in.3 = (bf16[1024,512]{1,0:T(8,128)(2,1)}, bf16[1024,2048]{1,0:T(8,128)(2,1)}, f32[1,2048]{1,0:T(1,128)}) custom-call(bf16[1024,2048]{1,0:T(8,128)(2,1)} %bitcast.118, bf16[8,2,32,2048]{3,2,1,0:T(8,128)(2,1)} %bitcast.137, bf16[2048,2048]{1,0:T(8,128)(2,1)} %all-gather.7.cloned.1.call-done.w_ref, bf16[1024,2048]{1,0:T(8,128)(2,1)} %get-tuple-element.508.slope_ref), custom_call_target="tpu_custom_call" | custom-call | flops 2621440 | bytes 5120 | tf_op jit(solution)/shard_map/back_in/pallas_call | solution.py:444
  443.9 9.7 %attend_back.2 = (bf16[4,256,1536]{2,1,0:T(8,128)(2,1)S(1)}, f32[2,1,768]{2,1,0:T(1,128)S(1)}) custom-call(s32[4,256,1]{2,1,0:T(8,128)S(1)} %multiply_add_fusion.posq_ref, s32[4,1,1024]{2,1,0:T(1,128)S(1)} %pad_add_fusion.posk_ref, f32[4,256,128]{2,1,0:T(8,128)S(1)} %maximum_maximum_fusion.cos_ref, f32[4,256,128]{2,1,0:T(8,128)S(1)} %maximum_maximum_fusion.1.sin_ref, ...), custom_call_target="tpu_custom_call" | custom-call | flops 2684354560 | bytes 7864320 | tf_op jit(solution)/shard_map/attend_back/pallas_call | solution.py:192
  455.2 22.6 %back_out.2 = (bf16[1024,2048]{1,0:T(8,128)(2,1)}, f32[4,2048]{1,0:T(4,128)}) custom-call(f32[6,2048]{1,0:T(8,128)} %reshape.583.vectors_ref, bf16[1024,1536]{1,0:T(8,128)(2,1)} %bitcast.100, bf16[1024,2048]{1,0:T(8,128)(2,1)} %get-tuple-element.545.pre_ref.refs_2_, bf16[2048,3584]{1,0:T(8,128)(2,1)} %all-gather.5.cloned.1.call-done.refs_7_.w_ref, ...), custom_call_target="tpu_custom_call" | custom-call | flops 3670016 | bytes 7680 | tf_op jit(solution)/shard_map/back_out/pallas_call | solution.py:485
  477.9 14.4 %grad_w1_sent.1 = bf16[4,256,2048]{2,1,0:T(8,128)(2,1)} custom-call(s32[1]{0:T(128)S(6)} %sub.109.me_ref, bf16[1024,2048]{1,0:T(8,128)(2,1)} %bitcast.122, bf16[1024,2048]{1,0:T(8,128)(2,1)} %bitcast.125, bf16[1024,2048]{1,0:T(8,128)(2,1)} %get-tuple-element.545.pre_ref.refs_2_, bf16[1024,2048]{1,0:T(8,128)(2,1)} %get-tuple-element.567.refs_3_.pre_ref), custom_call_target="tpu_custom_call" | custom-call | flops 2097152 | bytes 6144 | tf_op jit(solution)/shard_map/grad_w1_sent/pallas_call | solution.py:520
  492.5 9.9 %attend_back.3 = (bf16[4,256,1536]{2,1,0:T(8,128)(2,1)S(1)}, f32[2,1,768]{2,1,0:T(1,128)S(1)}) custom-call(s32[4,256,1]{2,1,0:T(8,128)S(1)} %multiply_add_fusion.posq_ref, s32[4,1,1024]{2,1,0:T(1,128)S(1)} %pad_add_fusion.1.posk_ref, f32[4,256,128]{2,1,0:T(8,128)S(1)} %maximum_maximum_fusion.cos_ref, f32[4,256,128]{2,1,0:T(8,128)S(1)} %maximum_maximum_fusion.1.sin_ref, ...), custom_call_target="tpu_custom_call" | custom-call | flops 2684354560 | bytes 7864320 | tf_op jit(solution)/shard_map/attend_back/pallas_call | solution.py:192
  504.0 14.8 %grad_w1_kept.1 = bf16[4,256,2048]{2,1,0:T(8,128)(2,1)} custom-call(s32[1]{0:T(128)} %bitcast.37.me_ref, bf16[1024,2048]{1,0:T(8,128)(2,1)} %bitcast.123, bf16[1024,2048]{1,0:T(8,128)(2,1)} %bitcast.126, bf16[1024,2048]{1,0:T(8,128)(2,1)} %get-tuple-element.545.pre_ref.refs_2_, bf16[1024,2048]{1,0:T(8,128)(2,1)} %get-tuple-element.567.refs_3_.pre_ref, ...), custom_call_target="tpu_custom_call" | custom-call | flops 2097152 | bytes 6144 | tf_op jit(solution)/shard_map/grad_w1_kept/pallas_call | solution.py:520
  518.8 5.3 all-to-all-start.4
  524.1 11.4 %grad_wq_sent.1 = bf16[4,256,1536]{2,1,0:T(8,128)(2,1)} custom-call(s32[1]{0:T(128)S(6)} %sub.109.me_ref, bf16[1024,2048]{1,0:T(8,128)(2,1)} %bitcast.138, bf16[1024,2048]{1,0:T(8,128)(2,1)} %bitcast.140, bf16[1024,1536]{1,0:T(8,128)(2,1)} %bitcast.101, bf16[1024,1536]{1,0:T(8,128)(2,1)} %bitcast.103), custom_call_target="tpu_custom_call" | custom-call | flops 1572864 | bytes 5120 | tf_op jit(solution)/shard_map/grad_wq_sent/pallas_call | solution.py:520
  535.5 22.6 %back_out.3 = (bf16[1024,2048]{1,0:T(8,128)(2,1)}, f32[4,2048]{1,0:T(4,128)}) custom-call(f32[6,2048]{1,0:T(8,128)} %reshape.583.vectors_ref, bf16[1024,1536]{1,0:T(8,128)(2,1)} %bitcast.104, bf16[1024,2048]{1,0:T(8,128)(2,1)} %get-tuple-element.567.refs_3_.pre_ref, bf16[2048,3584]{1,0:T(8,128)(2,1)} %all-gather.5.cloned.1.call-done.refs_7_.w_ref, ...), custom_call_target="tpu_custom_call" | custom-call | flops 3670016 | bytes 7680 | tf_op jit(solution)/shard_map/back_out/pallas_call | solution.py:485
  558.1 15.8 %all-to-all-done.4 = bf16[4,256,2048]{2,1,0:T(8,128)(2,1)} async-done(((bf16[4,256,2048]{2,1,0:T(8,128)(2,1)}), bf16[4,256,2048]{2,1,0:T(8,128)(2,1)}, u32[]{:S(2)}, u32[]{:S(2)}) %all-to-all-start.4) | async-done | bytes 4194336 | tf_op jit(solution)/shard_map/all_to_all | solution.py:865
  579.8 3.9 all-to-all-start.5
  583.7 9.6 %grad_dense.1 = (bf16[4,2,32,2048]{3,2,1,0:T(8,128)(2,1)}, bf16[4,2,32,2048]{3,2,1,0:T(8,128)(2,1)}) custom-call(s32[1]{0:T(128)} %bitcast.37.me_ref, bf16[1024,512]{1,0:T(8,128)(2,1)} %bitcast.107, bf16[1024,512]{1,0:T(8,128)(2,1)} %bitcast.109, bf16[1024,2048]{1,0:T(8,128)(2,1)} %bitcast.115, bf16[1024,2048]{1,0:T(8,128)(2,1)} %bitcast.119), custom_call_target="tpu_custom_call" | custom-call | flops 1048576 | bytes 3072 | tf_op jit(solution)/shard_map/grad_dense/pallas_call | solution.py:556
  593.2 11.9 %grad_wq_kept.1 = bf16[4,256,1536]{2,1,0:T(8,128)(2,1)} custom-call(s32[1]{0:T(128)} %bitcast.37.me_ref, bf16[1024,2048]{1,0:T(8,128)(2,1)} %bitcast.139, bf16[1024,2048]{1,0:T(8,128)(2,1)} %bitcast.141, bf16[1024,1536]{1,0:T(8,128)(2,1)} %bitcast.102, bf16[1024,1536]{1,0:T(8,128)(2,1)} %bitcast.105, bf16[4,256,1536]{2,1,0:T(8,128)(2,1)} %collective-permute-done.36.refs_4_), custom_call_target="tpu_custom_call" | custom-call | flops 1572864 | bytes 5120 | tf_op jit(solution)/shard_map/grad_wq_kept/pallas_call | solution.py:520
  605.2 5.0 all-to-all-done.5
  611.6 4.8 all-to-all-start.6
  622.3 4.5 convert_reduce_fusion.1
  627.4 21.2 %collective-permute-done.37 = f32[1728]{0:T(1024)S(1)} collective-permute-done((f32[1728]{0:T(1024)S(1)}, f32[1728]{0:T(1024)S(1)}, u32[]{:S(2)}, u32[]{:S(2)}) %collective-permute-start.37) | collective-permute-done | bytes 6944 | tf_op jit(solution)/shard_map/ppermute | solution.py:945
  648.6 3.3 collective-permute-done.38
  652.6 4.5 convert_reduce_fusion
  658.5 4.3 all-to-all-start.7
  666.1 2.8 collective-permute-start.47
  668.9 3.6 convert_reduce_fusion.2
  672.6 3.5 reshape.578
  683.6 4.4 all-to-all-start.8
  688.0 3.3 copy.60
  697.2 17.4 %all-to-all-done.8 = bf16[2,8,32,2048]{3,2,0,1:T(8,128)(2,1)} async-done(((bf16[2,8,32,2048]{3,2,0,1:T(8,128)(2,1)}), bf16[2,8,32,2048]{3,2,0,1:T(8,128)(2,1)}, u32[]{:S(2)}, u32[]{:S(2)}) %all-to-all-start.8) | async-done | bytes 2097184 | tf_op jit(solution)/shard_map/all_to_all | solution.py:611
  714.7 3.2 copy.61
  (307 shorter events, 97.2 us)
Async XLA Ops:
  10.4 20.7 %all-to-all-start = ((bf16[8,32,2048]{2,1,0:T(8,128)(2,1)}), bf16[8,32,2048]{2,1,0:T(8,128)(2,1)S(1)}, u32[]{:S(2)}, u32[]{:S(2)}) async-start(bf16[8,32,2048]{2,1,0:T(8,128)(2,1)} %get-tuple-element.695), calls=%async_computation | async-start | bytes 2097152 | tf_op jit(solution)/shard_map/all_to_all | solution.py:607
  15.7 129.8 %all-gather.5.cloned.1.call-start = ((), (), s32[]{:S(2)}) async-start(), calls=%async_computation.12 | async-start | bytes 16515072 | tf_op jit(solution)/shard_map/all_gather | solution.py:646
  31.1 23.1 %collective-permute-start.7 = (bf16[256,2048]{1,0:T(8,128)(2,1)S(1)}, bf16[256,2048]{1,0:T(8,128)(2,1)}, u32[]{:S(2)}, u32[]{:S(2)}) collective-permute-start(bf16[256,2048]{1,0:T(8,128)(2,1)S(1)} %bitcast.127), channel_id=1, source_target_pairs={{0,1},{1,2},{2,3},{4,5},{5,6},{6,7},{8,9},{9,10},{10,11},{12,13},{... | collective-permute-start | bytes 3145736 | tf_op jit(solution)/shard_map/ppermute | solution.py:39
  35.7 23.8 %collective-permute-start.8 = (bf16[256,2048]{1,0:T(8,128)(2,1)S(1)}, bf16[256,2048]{1,0:T(8,128)(2,1)}, u32[]{:S(2)}, u32[]{:S(2)}) collective-permute-start(bf16[256,2048]{1,0:T(8,128)(2,1)S(1)} %bitcast.128), channel_id=1, source_target_pairs={{1,0},{2,1},{3,2},{5,4},{6,5},{7,6},{9,8},{10,9},{11,10},{13,12},{... | collective-permute-start | bytes 3145736 | tf_op jit(solution)/shard_map/ppermute | solution.py:41
  38.4 3.9 collective-permute-start
  38.4 4.6 collective-permute-start.1
  39.0 4.1 collective-permute-start.2
  42.3 3.6 collective-permute-start.3
  43.1 3.6 collective-permute-start.4
  43.1 3.6 collective-permute-start.5
  45.9 1.9 collective-permute-start.6
  59.4 28.0 %collective-permute-start.12 = (bf16[256,2048]{1,0:T(8,128)(2,1)}, bf16[256,2048]{1,0:T(8,128)(2,1)}, u32[]{:S(2)}, u32[]{:S(2)}) collective-permute-start(bf16[256,2048]{1,0:T(8,128)(2,1)} %collective-permute-done.7.refs_1_), channel_id=1, source_target_pairs={{1,2},{2,3},{5,6},{6,7},{9,10},{10,11},{13,14},{14,15},{17,18},{18... | collective-permute-start | bytes 3145736 | tf_op jit(solution)/shard_map/ppermute | solution.py:39
  61.1 26.3 %collective-permute-start.13 = (bf16[256,2048]{1,0:T(8,128)(2,1)}, bf16[256,2048]{1,0:T(8,128)(2,1)}, u32[]{:S(2)}, u32[]{:S(2)}) collective-permute-start(bf16[256,2048]{1,0:T(8,128)(2,1)} %collective-permute-done.8.refs_4_), channel_id=1, source_target_pairs={{1,0},{2,1},{5,4},{6,5},{9,8},{10,9},{13,12},{14,13},{17,16},{18,1... | collective-permute-start | bytes 3145736 | tf_op jit(solution)/shard_map/ppermute | solution.py:41
  65.5 54.3 %all-to-all-start.1 = ((bf16[2,8,32,2048]{3,2,0,1:T(8,128)(2,1)}), bf16[2,8,32,2048]{3,2,0,1:T(8,128)(2,1)S(1)}, u32[]{:S(2)}, u32[]{:S(2)}) async-start(bf16[2,8,32,2048]{3,2,0,1:T(8,128)(2,1)} %pad_maximum_fusion), calls=%async_computation.1 | async-start | bytes 4194304 | tf_op jit(solution)/shard_map/all_to_all | solution.py:704
  70.4 170.2 %all-gather.9.cloned.1.call-start = ((), (), s32[]{:S(2)}) async-start(), calls=%async_computation.17 | async-start | bytes 2359296 | tf_op jit(solution)/shard_map/all_gather | solution.py:719
  70.5 10.1 %collective-permute-start.9 = (bf16[3072]{0:T(1024)(128)(2,1)S(1)}, bf16[3072]{0:T(1024)(128)(2,1)S(1)}, u32[]{:S(2)}, u32[]{:S(2)}) collective-permute-start(bf16[3072]{0:T(1024)(128)(2,1)S(1)} %reshape.544), channel_id=1, source_target_pairs={{0,1},{1,2},{2,3},{3,0},{4,5},{5,6},{6,7},{7,4},{8,9},{9,10},{10,1... | collective-permute-start | bytes 18440 | tf_op jit(solution)/shard_map/ppermute | solution.py:56
  74.7 12.4 %collective-permute-start.10 = (bf16[3072]{0:T(1024)(128)(2,1)S(1)}, bf16[3072]{0:T(1024)(128)(2,1)S(1)}, u32[]{:S(2)}, u32[]{:S(2)}) collective-permute-start(bf16[3072]{0:T(1024)(128)(2,1)S(1)} %reshape.544), channel_id=1, source_target_pairs={{0,2},{1,3},{2,0},{3,1},{4,6},{5,7},{6,4},{7,5},{8,10},{9,11},{10,... | collective-permute-start | bytes 18440 | tf_op jit(solution)/shard_map/ppermute | solution.py:56
  77.7 9.5 %collective-permute-start.11 = (bf16[3072]{0:T(1024)(128)(2,1)S(1)}, bf16[3072]{0:T(1024)(128)(2,1)S(1)}, u32[]{:S(2)}, u32[]{:S(2)}) collective-permute-start(bf16[3072]{0:T(1024)(128)(2,1)S(1)} %reshape.544), channel_id=1, source_target_pairs={{0,3},{1,0},{2,1},{3,2},{4,7},{5,4},{6,5},{7,6},{8,11},{9,8},{10,9... | collective-permute-start | bytes 18440 | tf_op jit(solution)/shard_map/ppermute | solution.py:56
  87.5 32.3 %collective-permute-start.14 = (bf16[256,2048]{1,0:T(8,128)(2,1)}, bf16[256,2048]{1,0:T(8,128)(2,1)}, u32[]{:S(2)}, u32[]{:S(2)}) collective-permute-start(bf16[256,2048]{1,0:T(8,128)(2,1)} %collective-permute-done.12.refs_2_), channel_id=1, source_target_pairs={{2,3},{6,7},{10,11},{14,15},{18,19},{22,23},{26,27},{30,31}} | collective-permute-start | bytes 3145736 | tf_op jit(solution)/shard_map/ppermute | solution.py:39
  89.1 30.7 %collective-permute-start.15 = (bf16[256,2048]{1,0:T(8,128)(2,1)}, bf16[256,2048]{1,0:T(8,128)(2,1)}, u32[]{:S(2)}, u32[]{:S(2)}) collective-permute-start(bf16[256,2048]{1,0:T(8,128)(2,1)} %collective-permute-done.13.refs_5_), channel_id=1, source_target_pairs={{1,0},{5,4},{9,8},{13,12},{17,16},{21,20},{25,24},{29,28}} | collective-permute-start | bytes 3145736 | tf_op jit(solution)/shard_map/ppermute | solution.py:41
  119.8 120.8 %all-gather.7.cloned.1.call-start = ((), (), s32[]{:S(2)}) async-start(), calls=%async_computation.13 | async-start | bytes 9437184 | tf_op jit(solution)/shard_map/all_gather | solution.py:718
  123.4 61.1 %collective-permute-start.16 = (bf16[256,2048]{1,0:T(8,128)(2,1)S(1)}, bf16[256,2048]{1,0:T(8,128)(2,1)}, u32[]{:S(2)}, u32[]{:S(2)}) collective-permute-start(bf16[256,2048]{1,0:T(8,128)(2,1)S(1)} %bitcast.142), channel_id=1, source_target_pairs={{0,1},{1,2},{2,3},{4,5},{5,6},{6,7},{8,9},{9,10},{10,11},{12,13},{... | collective-permute-start | bytes 3145736 | tf_op jit(solution)/shard_map/ppermute | solution.py:39
  130.4 54.0 %collective-permute-start.17 = (bf16[256,2048]{1,0:T(8,128)(2,1)S(1)}, bf16[256,2048]{1,0:T(8,128)(2,1)}, u32[]{:S(2)}, u32[]{:S(2)}) collective-permute-start(bf16[256,2048]{1,0:T(8,128)(2,1)S(1)} %bitcast.143), channel_id=1, source_target_pairs={{1,0},{2,1},{3,2},{5,4},{6,5},{7,6},{9,8},{10,9},{11,10},{13,12},{... | collective-permute-start | bytes 3145736 | tf_op jit(solution)/shard_map/ppermute | solution.py:41
  131.7 52.7 %collective-permute-start.18 = (bf16[256,2048]{1,0:T(8,128)(2,1)}, bf16[256,2048]{1,0:T(8,128)(2,1)}, u32[]{:S(2)}, u32[]{:S(2)}) collective-permute-start(bf16[256,2048]{1,0:T(8,128)(2,1)} %bitcast.15.refs_0_), channel_id=1, source_target_pairs={{0,1},{1,2},{2,3},{4,5},{5,6},{6,7},{8,9},{9,10},{10,11},{12,13},{... | collective-permute-start | bytes 3145736 | tf_op jit(solution)/shard_map/ppermute | solution.py:39
  137.8 46.7 %collective-permute-start.19 = (bf16[256,2048]{1,0:T(8,128)(2,1)}, bf16[256,2048]{1,0:T(8,128)(2,1)}, u32[]{:S(2)}, u32[]{:S(2)}) collective-permute-start(bf16[256,2048]{1,0:T(8,128)(2,1)} %bitcast.15.refs_0_), channel_id=1, source_target_pairs={{1,0},{2,1},{3,2},{5,4},{6,5},{7,6},{9,8},{10,9},{11,10},{13,12},{... | collective-permute-start | bytes 3145736 | tf_op jit(solution)/shard_map/ppermute | solution.py:41
  184.5 36.1 %collective-permute-start.20 = (bf16[256,2048]{1,0:T(8,128)(2,1)}, bf16[256,2048]{1,0:T(8,128)(2,1)}, u32[]{:S(2)}, u32[]{:S(2)}) collective-permute-start(bf16[256,2048]{1,0:T(8,128)(2,1)} %collective-permute-done.16.refs_1_), channel_id=1, source_target_pairs={{1,2},{2,3},{5,6},{6,7},{9,10},{10,11},{13,14},{14,15},{17,18},{18... | collective-permute-start | bytes 3145736 | tf_op jit(solution)/shard_map/ppermute | solution.py:39
  186.1 34.5 %collective-permute-start.21 = (bf16[256,2048]{1,0:T(8,128)(2,1)}, bf16[256,2048]{1,0:T(8,128)(2,1)}, u32[]{:S(2)}, u32[]{:S(2)}) collective-permute-start(bf16[256,2048]{1,0:T(8,128)(2,1)} %collective-permute-done.17.refs_4_), channel_id=1, source_target_pairs={{1,0},{2,1},{5,4},{6,5},{9,8},{10,9},{13,12},{14,13},{17,16},{18,1... | collective-permute-start | bytes 3145736 | tf_op jit(solution)/shard_map/ppermute | solution.py:41
  187.4 33.2 %collective-permute-start.22 = (bf16[256,2048]{1,0:T(8,128)(2,1)}, bf16[256,2048]{1,0:T(8,128)(2,1)}, u32[]{:S(2)}, u32[]{:S(2)}) collective-permute-start(bf16[256,2048]{1,0:T(8,128)(2,1)} %collective-permute-done.18.refs_1_), channel_id=1, source_target_pairs={{1,2},{2,3},{5,6},{6,7},{9,10},{10,11},{13,14},{14,15},{17,18},{18... | collective-permute-start | bytes 3145736 | tf_op jit(solution)/shard_map/ppermute | solution.py:39
  189.0 45.6 %collective-permute-start.23 = (bf16[256,2048]{1,0:T(8,128)(2,1)}, bf16[256,2048]{1,0:T(8,128)(2,1)}, u32[]{:S(2)}, u32[]{:S(2)}) collective-permute-start(bf16[256,2048]{1,0:T(8,128)(2,1)} %collective-permute-done.19.refs_4_), channel_id=1, source_target_pairs={{1,0},{2,1},{5,4},{6,5},{9,8},{10,9},{13,12},{14,13},{17,16},{18,1... | collective-permute-start | bytes 3145736 | tf_op jit(solution)/shard_map/ppermute | solution.py:41
  190.5 30.1 %all-to-all-start.2 = ((bf16[8,32,2048]{2,1,0:T(8,128)(2,1)}), bf16[8,32,2048]{2,1,0:T(8,128)(2,1)S(1)}, u32[]{:S(2)}, u32[]{:S(2)}) async-start(bf16[8,32,2048]{2,1,0:T(8,128)(2,1)} %get-tuple-element.367), calls=%async_computation.2 | async-start | bytes 2097152 | tf_op jit(solution)/shard_map/all_to_all | solution.py:607
  194.1 379.8 %reduce-scatter.4.cloned.1.call-start = ((), (), s32[]{:S(2)}) async-start(), calls=%async_computation.14 | async-start | bytes 10485760 | tf_op jit(solution)/shard_map/reduce_scatter | solution.py:765
  220.6 62.9 %copy-start.14 = (bf16[8,32,2048]{2,1,0:T(8,128)(2,1)}, bf16[8,32,2048]{2,1,0:T(8,128)(2,1)S(1)}, u32[]{:S(2)}) copy-start(bf16[8,32,2048]{2,1,0:T(8,128)(2,1)S(1)} %all-to-all-done.2) | copy-start | bytes 3145732
  234.6 22.2 %collective-permute-start.24 = (bf16[256,2048]{1,0:T(8,128)(2,1)}, bf16[256,2048]{1,0:T(8,128)(2,1)}, u32[]{:S(2)}, u32[]{:S(2)}) collective-permute-start(bf16[256,2048]{1,0:T(8,128)(2,1)} %collective-permute-done.20.refs_2_), channel_id=1, source_target_pairs={{2,3},{6,7},{10,11},{14,15},{18,19},{22,23},{26,27},{30,31}} | collective-permute-start | bytes 3145736 | tf_op jit(solution)/shard_map/ppermute | solution.py:39
  236.3 28.3 %collective-permute-start.25 = (bf16[256,2048]{1,0:T(8,128)(2,1)}, bf16[256,2048]{1,0:T(8,128)(2,1)}, u32[]{:S(2)}, u32[]{:S(2)}) collective-permute-start(bf16[256,2048]{1,0:T(8,128)(2,1)} %collective-permute-done.21.refs_5_), channel_id=1, source_target_pairs={{1,0},{5,4},{9,8},{13,12},{17,16},{21,20},{25,24},{29,28}} | collective-permute-start | bytes 3145736 | tf_op jit(solution)/shard_map/ppermute | solution.py:41
  237.6 27.0 %collective-permute-start.26 = (bf16[256,2048]{1,0:T(8,128)(2,1)}, bf16[256,2048]{1,0:T(8,128)(2,1)}, u32[]{:S(2)}, u32[]{:S(2)}) collective-permute-start(bf16[256,2048]{1,0:T(8,128)(2,1)} %collective-permute-done.22.refs_2_), channel_id=1, source_target_pairs={{2,3},{6,7},{10,11},{14,15},{18,19},{22,23},{26,27},{30,31}} | collective-permute-start | bytes 3145736 | tf_op jit(solution)/shard_map/ppermute | solution.py:39
  239.3 41.7 %collective-permute-start.27 = (bf16[256,2048]{1,0:T(8,128)(2,1)}, bf16[256,2048]{1,0:T(8,128)(2,1)}, u32[]{:S(2)}, u32[]{:S(2)}) collective-permute-start(bf16[256,2048]{1,0:T(8,128)(2,1)} %collective-permute-done.23.refs_5_), channel_id=1, source_target_pairs={{1,0},{5,4},{9,8},{13,12},{17,16},{21,20},{25,24},{29,28}} | collective-permute-start | bytes 3145736 | tf_op jit(solution)/shard_map/ppermute | solution.py:41
  281.0 22.9 %collective-permute-start.28 = (bf16[256,2048]{1,0:T(8,128)(2,1)S(1)}, bf16[256,2048]{1,0:T(8,128)(2,1)}, u32[]{:S(2)}, u32[]{:S(2)}) collective-permute-start(bf16[256,2048]{1,0:T(8,128)(2,1)S(1)} %bitcast.145), channel_id=1, source_target_pairs={{0,1},{1,2},{2,3},{4,5},{5,6},{6,7},{8,9},{9,10},{10,11},{12,13},{... | collective-permute-start | bytes 3145736 | tf_op jit(solution)/shard_map/ppermute | solution.py:39
  283.5 20.9 %collective-permute-start.29 = (bf16[256,2048]{1,0:T(8,128)(2,1)S(1)}, bf16[256,2048]{1,0:T(8,128)(2,1)}, u32[]{:S(2)}, u32[]{:S(2)}) collective-permute-start(bf16[256,2048]{1,0:T(8,128)(2,1)S(1)} %bitcast.146), channel_id=1, source_target_pairs={{1,0},{2,1},{3,2},{5,4},{6,5},{7,6},{9,8},{10,9},{11,10},{13,12},{... | collective-permute-start | bytes 3145736 | tf_op jit(solution)/shard_map/ppermute | solution.py:41
  304.4 32.6 %collective-permute-start.30 = (bf16[256,2048]{1,0:T(8,128)(2,1)}, bf16[256,2048]{1,0:T(8,128)(2,1)S(1)}, u32[]{:S(2)}, u32[]{:S(2)}) collective-permute-start(bf16[256,2048]{1,0:T(8,128)(2,1)} %collective-permute-done.28.refs_1_), channel_id=1, source_target_pairs={{1,2},{2,3},{5,6},{6,7},{9,10},{10,11},{13,14},{14,15},{17,18},{18... | collective-permute-start | bytes 3145736 | tf_op jit(solution)/shard_map/ppermute | solution.py:39
  305.2 31.9 %collective-permute-start.31 = (bf16[256,2048]{1,0:T(8,128)(2,1)}, bf16[256,2048]{1,0:T(8,128)(2,1)}, u32[]{:S(2)}, u32[]{:S(2)}) collective-permute-start(bf16[256,2048]{1,0:T(8,128)(2,1)} %collective-permute-done.29.refs_4_), channel_id=1, source_target_pairs={{1,0},{2,1},{5,4},{6,5},{9,8},{10,9},{13,12},{14,13},{17,16},{18,1... | collective-permute-start | bytes 3145736 | tf_op jit(solution)/shard_map/ppermute | solution.py:41
  337.0 24.6 %collective-permute-start.32 = (bf16[256,2048]{1,0:T(8,128)(2,1)S(1)}, bf16[256,2048]{1,0:T(8,128)(2,1)S(1)}, u32[]{:S(2)}, u32[]{:S(2)}) collective-permute-start(bf16[256,2048]{1,0:T(8,128)(2,1)S(1)} %collective-permute-done.30.refs_2_), channel_id=1, source_target_pairs={{2,3},{6,7},{10,11},{14,15},{18,19},{22,23},{26,27},{30,31}} | collective-permute-start | bytes 3145736 | tf_op jit(solution)/shard_map/ppermute | solution.py:39
  337.7 24.9 %collective-permute-start.33 = (bf16[256,2048]{1,0:T(8,128)(2,1)}, bf16[256,2048]{1,0:T(8,128)(2,1)S(1)}, u32[]{:S(2)}, u32[]{:S(2)}) collective-permute-start(bf16[256,2048]{1,0:T(8,128)(2,1)} %collective-permute-done.31.refs_5_), channel_id=1, source_target_pairs={{1,0},{5,4},{9,8},{13,12},{17,16},{21,20},{25,24},{29,28}} | collective-permute-start | bytes 3145736 | tf_op jit(solution)/shard_map/ppermute | solution.py:41
  384.2 17.0 %collective-permute-start.34 = (bf16[4,256,2048]{2,1,0:T(8,128)(2,1)}, bf16[4,256,2048]{2,1,0:T(8,128)(2,1)S(1)}, u32[]{:S(2)}, u32[]{:S(2)}) collective-permute-start(bf16[4,256,2048]{2,1,0:T(8,128)(2,1)} %grad_w2_sent.1), channel_id=1, source_target_pairs={{0,4},{4,0},{8,12},{12,8},{16,20},{20,16},{24,28},{28,24},{1,5},{5... | collective-permute-start | bytes 12582920 | tf_op jit(solution)/shard_map/ppermute | solution.py:831
  418.1 59.7 %all-to-all-start.3 = ((bf16[4,256,2048]{2,1,0:T(8,128)(2,1)}), bf16[4,256,2048]{2,1,0:T(8,128)(2,1)}, u32[]{:S(2)}, u32[]{:S(2)}) async-start(bf16[4,256,2048]{2,1,0:T(8,128)(2,1)} %grad_w2_kept.1), calls=%async_computation.3 | async-start | bytes 8388608 | tf_op jit(solution)/shard_map/all_to_all | solution.py:865
  426.5 230.6 %reduce-scatter.6.cloned.1.call-start = ((), (), s32[]{:S(2)}) async-start(), calls=%async_computation.15 | async-start | bytes 5242880 | tf_op jit(solution)/shard_map/reduce_scatter | solution.py:765
  492.3 11.7 %collective-permute-start.35 = (bf16[4,256,2048]{2,1,0:T(8,128)(2,1)}, bf16[4,256,2048]{2,1,0:T(8,128)(2,1)}, u32[]{:S(2)}, u32[]{:S(2)}) collective-permute-start(bf16[4,256,2048]{2,1,0:T(8,128)(2,1)} %grad_w1_sent.1), channel_id=1, source_target_pairs={{0,4},{4,0},{8,12},{12,8},{16,20},{20,16},{24,28},{28,24},{1,5},{5... | collective-permute-start | bytes 12582920 | tf_op jit(solution)/shard_map/ppermute | solution.py:831
  518.8 55.1 %all-to-all-start.4 = ((bf16[4,256,2048]{2,1,0:T(8,128)(2,1)}), bf16[4,256,2048]{2,1,0:T(8,128)(2,1)}, u32[]{:S(2)}, u32[]{:S(2)}) async-start(bf16[4,256,2048]{2,1,0:T(8,128)(2,1)} %grad_w1_kept.1), calls=%async_computation.4 | async-start | bytes 8388608 | tf_op jit(solution)/shard_map/all_to_all | solution.py:865
  524.1 153.0 %reduce-scatter.8.cloned.1.call-start = ((), (), s32[]{:S(2)}) async-start(), calls=%async_computation.16 | async-start | bytes 5242880 | tf_op jit(solution)/shard_map/reduce_scatter | solution.py:765
  576.0 17.2 %collective-permute-start.36 = (bf16[4,256,1536]{2,1,0:T(8,128)(2,1)}, bf16[4,256,1536]{2,1,0:T(8,128)(2,1)}, u32[]{:S(2)}, u32[]{:S(2)}) collective-permute-start(bf16[4,256,1536]{2,1,0:T(8,128)(2,1)} %grad_wq_sent.1), channel_id=1, source_target_pairs={{0,4},{4,0},{8,12},{12,8},{16,20},{20,16},{24,28},{28,24},{1,5},{5... | collective-permute-start | bytes 9437192 | tf_op jit(solution)/shard_map/ppermute | solution.py:856
  579.8 30.4 %all-to-all-start.5 = ((bf16[2,8,32,2048]{3,2,0,1:T(8,128)(2,1)}), bf16[2,8,32,2048]{3,2,0,1:T(8,128)(2,1)S(1)}, u32[]{:S(2)}, u32[]{:S(2)}) async-start(bf16[2,8,32,2048]{3,2,0,1:T(8,128)(2,1)} %pad_maximum_fusion.1), calls=%async_computation.6 | async-start | bytes 4194304 | tf_op jit(solution)/shard_map/all_to_all | solution.py:611
  611.6 45.6 %all-to-all-start.6 = ((bf16[4,256,1536]{2,1,0:T(8,128)(2,1)}), bf16[4,256,1536]{2,1,0:T(8,128)(2,1)}, u32[]{:S(2)}, u32[]{:S(2)}) async-start(bf16[4,256,1536]{2,1,0:T(8,128)(2,1)} %grad_wq_kept.1), calls=%async_computation.7 | async-start | bytes 6291456 | tf_op jit(solution)/shard_map/all_to_all | solution.py:865
  617.1 40.0 %collective-permute-start.44 = (bf16[4,64,2048]{2,1,0:T(8,128)(2,1)}, bf16[4,64,2048]{2,1,0:T(8,128)(2,1)S(1)}, u32[]{:S(2)}, u32[]{:S(2)}) collective-permute-start(bf16[4,64,2048]{2,1,0:T(8,128)(2,1)} %bitcast.175), channel_id=1, source_target_pairs={{0,4},{4,0},{8,12},{12,8},{16,20},{20,16},{24,28},{28,24},{1,5},{5... | collective-permute-start | bytes 3145736 | tf_op jit(solution)/shard_map/ppermute | solution.py:856
  617.9 30.7 %collective-permute-start.37 = (f32[1728]{0:T(1024)S(1)}, f32[1728]{0:T(1024)S(1)}, u32[]{:S(2)}, u32[]{:S(2)}) collective-permute-start(f32[1728]{0:T(1024)S(1)} %get-tuple-element.683), channel_id=1, source_target_pairs={{0,4},{4,8},{8,12},{12,16},{16,20},{20,24},{24,28},{28,0},{1,5},{5... | collective-permute-start | bytes 20744 | tf_op jit(solution)/shard_map/ppermute | solution.py:945
  618.5 33.4 %collective-permute-start.38 = (f32[1728]{0:T(1024)S(1)}, f32[1728]{0:T(1024)S(1)}, u32[]{:S(2)}, u32[]{:S(2)}) collective-permute-start(f32[1728]{0:T(1024)S(1)} %get-tuple-element.682), channel_id=1, source_target_pairs={{0,8},{4,12},{8,16},{12,20},{16,24},{20,28},{24,0},{28,4},{1,9},{5... | collective-permute-start | bytes 20744 | tf_op jit(solution)/shard_map/ppermute | solution.py:945
  620.4 31.4 %collective-permute-start.39 = (f32[1728]{0:T(1024)S(1)}, f32[1728]{0:T(1024)S(1)}, u32[]{:S(2)}, u32[]{:S(2)}) collective-permute-start(f32[1728]{0:T(1024)S(1)} %get-tuple-element.681), channel_id=1, source_target_pairs={{0,12},{4,16},{8,20},{12,24},{16,28},{20,0},{24,4},{28,8},{1,13},{... | collective-permute-start | bytes 20744 | tf_op jit(solution)/shard_map/ppermute | solution.py:945
  626.8 30.3 %collective-permute-start.40 = (f32[1728]{0:T(1024)S(1)}, f32[1728]{0:T(1024)S(1)}, u32[]{:S(2)}, u32[]{:S(2)}) collective-permute-start(f32[1728]{0:T(1024)S(1)} %get-tuple-element.680), channel_id=1, source_target_pairs={{0,16},{4,20},{8,24},{12,28},{16,0},{20,4},{24,8},{28,12},{1,17},{... | collective-permute-start | bytes 20744 | tf_op jit(solution)/shard_map/ppermute | solution.py:945
  648.6 8.5 %collective-permute-start.41 = (f32[1728]{0:T(1024)S(1)}, f32[1728]{0:T(1024)S(1)}, u32[]{:S(2)}, u32[]{:S(2)}) collective-permute-start(f32[1728]{0:T(1024)S(1)} %get-tuple-element.679), channel_id=1, source_target_pairs={{0,20},{4,24},{8,28},{12,0},{16,4},{20,8},{24,12},{28,16},{1,21},{... | collective-permute-start | bytes 20744 | tf_op jit(solution)/shard_map/ppermute | solution.py:945
  651.8 5.3 collective-permute-start.42
  651.8 5.3 collective-permute-start.43
  658.5 18.5 %all-to-all-start.7 = ((bf16[4,64,2048]{2,1,0:T(8,128)(2,1)}), bf16[4,64,2048]{2,1,0:T(8,128)(2,1)}, u32[]{:S(2)}, u32[]{:S(2)}) async-start(bf16[4,64,2048]{2,1,0:T(8,128)(2,1)} %add_convert_fusion), calls=%async_computation.9 | async-start | bytes 2097152 | tf_op jit(solution)/shard_map/all_to_all | solution.py:865
  663.0 13.1 %collective-permute-start.45 = (f32[320]{0:T(512)S(1)}, f32[320]{0:T(512)S(1)}, u32[]{:S(2)}, u32[]{:S(2)}) collective-permute-start(f32[320]{0:T(512)S(1)} %get-tuple-element.684), channel_id=1, source_target_pairs={{0,1},{1,2},{2,3},{3,0},{4,5},{5,6},{6,7},{7,4},{8,9},{9,10},{10,1... | collective-permute-start | bytes 3848 | tf_op jit(solution)/shard_map/ppermute | solution.py:67
  664.9 11.2 %collective-permute-start.46 = (f32[320]{0:T(512)S(1)}, f32[320]{0:T(512)S(1)}, u32[]{:S(2)}, u32[]{:S(2)}) collective-permute-start(f32[320]{0:T(512)S(1)} %get-tuple-element.686), channel_id=1, source_target_pairs={{0,2},{1,3},{2,0},{3,1},{4,6},{5,7},{6,4},{7,5},{8,10},{9,11},{10,... | collective-permute-start | bytes 3848 | tf_op jit(solution)/shard_map/ppermute | solution.py:67
  666.1 10.0 %collective-permute-start.47 = (f32[320]{0:T(512)S(1)}, f32[320]{0:T(512)S(1)}, u32[]{:S(2)}, u32[]{:S(2)}) collective-permute-start(f32[320]{0:T(512)S(1)} %get-tuple-element.685), channel_id=1, source_target_pairs={{0,3},{1,0},{2,1},{3,2},{4,7},{5,4},{6,5},{7,6},{8,11},{9,8},{10,9... | collective-permute-start | bytes 3848 | tf_op jit(solution)/shard_map/ppermute | solution.py:67
  683.6 31.0 %all-to-all-start.8 = ((bf16[2,8,32,2048]{3,2,0,1:T(8,128)(2,1)}), bf16[2,8,32,2048]{3,2,0,1:T(8,128)(2,1)}, u32[]{:S(2)}, u32[]{:S(2)}) async-start(bf16[2,8,32,2048]{3,2,0,1:T(8,128)(2,1)} %pad_maximum_fusion.2), calls=%async_computation.11 | async-start | bytes 4194304 | tf_op jit(solution)/shard_map/all_to_all | solution.py:611
  (44 other events, 367.4 us)
Sparse Core Ops, SparseCore 0:
  31.2 103.0 all-gather.4
  136.2 27.8 all-gather.8
  166.6 65.6 all-gather.6
  363.8 149.9 reduce-scatter.3
  515.9 77.5 reduce-scatter.5
  595.7 77.3 reduce-scatter.7

commit v5 on v4

--- a/solution.py
+++ b/solution.py
@@ -922,15 +922,16 @@
     stage([], [arrange_g(1), sent_grads("w2"), back_in(0)])
     stage([], [kept_grads("w2")])
     spread_later("w2")
-    stage([], [back_attend(0), back_out(0), back_in(1), join("w2")])
+    stage([], [back_attend(0), back_out(0), back_in(1), dense_grads, join("w2")])
     pending["si0"] = scattered_rows("e0")
-    stage([], [sent_grads("w1"), back_attend(1)])
-    stage([], [kept_grads("w1")])
+    stage([], [sent_grads("w1"), swapped("wd"), back_attend(1)])
+    spread_later("wd")
+    stage([], [kept_grads("w1"), join("wd")])
     spread_later("w1")
     stage([], [sent_only("wq"), back_out(1), join("w1", "so")])
     pending["si1"] = scattered_rows("e1")
     output_rows()
-    stage([], [swapped("wq"), dense_grads, kept_grads("wq"), join("rows")])
+    stage([], [swapped("wq"), fc2_final, kept_grads("wq"), join("rows")])
     spread_later("wq")
     sums = jnp.concatenate([env["sums0"] + env["sums1"], sum_g[None]], axis=0)
     sums = sums.reshape(5, n_d, n_t, eighth).transpose(1, 2, 0, 3).reshape(n_d, -1)
@@ -949,12 +950,11 @@
         env["small"] = sum(env.pop(f"small{s}") for s in range(n_d))
         env["mine"] = direct_scatter(env["small"][:n_sum].reshape(n_t, -1), "tensor", n_t)
 
-    stage([], [small_over_dp, swapped("wd"), fc2_final, fc1_final, join("wq", "si0")])
-    spread_later("wd")
-    stage([], [qkv_final, small_over_tensor, join("wd")])
+    stage([], [small_over_dp, fc1_final, dense_final, join("wq", "si0")])
     stage([], [join("si1")])
     grads_in = undeal(jnp.stack([input_of(0), input_of(1)]))
-    dense_final()
+    small_over_tensor()
+    qkv_final()
     small_out = env["small"]
 
     outputs = env["rows"]

time: 735 us -> 732 us (level)
    unnamed x98 -> x102, local copies, waits for them, and re-layouts: 27.5 us -> 28.6 us
  transfers between devices with their start and end apart: 63 -> 63, of which waited for: 21 -> 22; matrix products, arithmetic and copies ran while one was open for 8% -> 7% of each run, Pallas kernels for 45% -> 46%
where the time goes in v5:
time: 732 us; the launch traced here: 722 us
  Pallas kernels  329 us (45%)
  waiting for transfers between devices  175 us (24%)
  starting transfers between devices  119 us (16%)
  local copies, waits for them, and re-layouts  42 us (6%)
  other arithmetic  41.3 us (6%)
  between operations  15.8 us (2%)
    pallas_call x6, Pallas kernels, grad_of(): pl.pallas_call(functools.partial(grad_kernel, len(lhs)), grid_spec=pltpu....  82.6 us
    pallas_call x2, Pallas kernels, back_out_of(): pl.pallas_call(back_out_kernel, grid=(width // tile,), in_specs=[pl.Block...  45.1 us
    ppermute x12, waiting for transfers between devices, step(): self.right.append(lax.ppermute(to_left, self.axis, pairs))  43.8 us
    pallas_call x2, Pallas kernels, hidden_of(): pl.pallas_call(hidden_kernel, grid=(n_ff // tile,), in_specs=[resident(tw...  39.6 us
    pallas_call x2, Pallas kernels, norm_qkv(): pl.pallas_call(functools.partial(norm_qkv_kernel, len(blocks)), grid_spec...  38.3 us
    pallas_call x2, Pallas kernels, back_in_of(): pl.pallas_call(back_in_kernel, grid=(n_ff // tile,), in_specs=[resident(g...  34 us
    pallas_call x2, Pallas kernels, branch_of(): pl.pallas_call(branch_kernel, grid=(width // tile,), in_specs=[resident(m...  32.2 us
    ppermute x12, starting transfers between devices, step(): self.left.append(lax.ppermute(to_right, self.axis, pairs))  31.5 us
  transfers between devices with their start and end apart: 63, of which 22 were waited for; matrix products, arithmetic and copies ran while one was open for 7% of the time, Pallas kernels for 46%

profile of v5, /device:TPU:0, one launch (start us, length us, event | category | flops | bytes accessed | tf_op | source)
XLA Modules:
  0.0 722.2 jit_solution(15926724519673792370)
XLA Ops:
  7.2 3.1 slice_bitcast_fusion.2
  10.4 5.3 all-to-all-start
  16.9 2.9 pad_maximum_fusion.3
  19.9 11.2 %all-to-all-done = bf16[8,32,2048]{2,1,0:T(8,128)(2,1)S(1)} async-done(((bf16[8,32,2048]{2,1,0:T(8,128)(2,1)}), bf16[8,32,2048]{2,1,0:T(8,128)(2,1)S(1)}, u32[]{:S(2)}, u32[]{:S(2)}) %all-to-all-start) | async-done | bytes 1048608 | tf_op jit(solution)/shard_map/all_to_all | solution.py:607
  31.1 4.5 collective-permute-start.7
  48.1 6.2 collective-permute-done.7.refs_1_
  54.2 5.2 collective-permute-done.8.refs_4_
  62.4 3.1 pad_maximum_fusion
  65.5 4.9 all-to-all-start.1
  70.5 4.2 collective-permute-start.9
  74.7 3.0 collective-permute-start.10
  77.7 2.8 collective-permute-start.11
  80.6 6.6 collective-permute-done.10
  92.2 27.6 %all-to-all-done.1 = bf16[2,8,32,2048]{3,2,0,1:T(8,128)(2,1)S(1)} async-done(((bf16[2,8,32,2048]{3,2,0,1:T(8,128)(2,1)}), bf16[2,8,32,2048]{3,2,0,1:T(8,128)(2,1)S(1)}, u32[]{:S(2)}, u32[]{:S(2)}) %all-to-all-start.1) | async-done | bytes 2097184 | tf_op jit(solution)/shard_map/all_to_all | solution.py:704
  123.4 7.1 collective-permute-start.16
  131.8 5.9 collective-permute-start.18
  142.4 3.0 fusion.20
  145.4 19.2 %norm_qkv.2 = (bf16[4,256,2048]{2,1,0:T(8,128)(2,1)}, bf16[4,256,2048]{2,1,0:T(8,128)(2,1)}, bf16[4,256,2048]{2,1,0:T(8,128)(2,1)}, f32[4,256,1536]{2,1,0:T(8,128)}) custom-call(s32[2]{0:T(128)} %pad_add_fusion.2.me_ref, f32[6,2048]{1,0:T(8,128)} %reshape.583.vectors_ref, f32[1,3584]{1,0:T(1,128)} %pad_maximum_fusion.5.bias_ref, ...), custom_call_target="tpu_custom_call" | custom-call | flops 1572864 | bytes 6656 | tf_op jit(solution)/shard_map/norm_qkv/pallas_call | solution.py:302
  164.6 19.8 %hidden.2 = (bf16[1024,2048]{1,0:T(8,128)(2,1)}, bf16[1024,2048]{1,0:T(8,128)(2,1)}) custom-call(bf16[1024,2048]{1,0:T(8,128)(2,1)} %bitcast.121, bf16[2048,3584]{1,0:T(8,128)(2,1)} %all-gather.5.cloned.1.call-done.refs_7_.w_ref, f32[1,3584]{1,0:T(1,128)} %pad_maximum_fusion.5.bias_ref), custom_call_target="tpu_custom_call" | custom-call | flops 2097152 | bytes 6144 | tf_op jit(solution)/shard_map/hidden/pallas_call | solution.py:328
  190.5 3.6 all-to-all-start.2
  196.0 7.9 %attend.2 = (bf16[4,256,1536]{2,1,0:T(8,128)(2,1)S(1)}, bf16[4,256,512]{2,1,0:T(8,128)(2,1)S(1)}) custom-call(s32[4,256,1]{2,1,0:T(8,128)S(1)} %multiply_add_fusion.posq_ref, s32[4,1,1024]{2,1,0:T(1,128)S(1)} %pad_add_fusion.posk_ref, f32[4,256,128]{2,1,0:T(8,128)S(1)} %maximum_maximum_fusion.cos_ref, f32[4,256,128]{2,1,0:T(8,128)S(1)} %maximum_maximum_fusion.1.sin_ref, ...), custom_call_target="tpu_custom_call" | custom-call | flops 1073741824 | bytes 12582912 | tf_op jit(solution)/shard_map/attend/pallas_call | solution.py:171
  206.4 14.4 %all-to-all-done.2 = bf16[8,32,2048]{2,1,0:T(8,128)(2,1)S(1)} async-done(((bf16[8,32,2048]{2,1,0:T(8,128)(2,1)}), bf16[8,32,2048]{2,1,0:T(8,128)(2,1)S(1)}, u32[]{:S(2)}, u32[]{:S(2)}) %all-to-all-start.2) | async-done | bytes 1048608 | tf_op jit(solution)/shard_map/all_to_all | solution.py:607
  220.8 13.8 %collective-permute-done.23.refs_5_ = bf16[256,2048]{1,0:T(8,128)(2,1)} collective-permute-done((bf16[256,2048]{1,0:T(8,128)(2,1)}, bf16[256,2048]{1,0:T(8,128)(2,1)}, u32[]{:S(2)}, u32[]{:S(2)}) %collective-permute-start.23) | collective-permute-done | bytes 1048608 | tf_op jit(solution)/shard_map/ppermute | solution.py:41
  240.6 16.1 %branch.2.refs_0_ = bf16[4,2,256,2048]{3,2,1,0:T(8,128)(2,1)} custom-call(bf16[1024,512]{1,0:T(8,128)(2,1)} %bitcast.106, bf16[1024,2048]{1,0:T(8,128)(2,1)} %get-tuple-element.458.act_ref.refs_2_, bf16[8,2,32,2048]{3,2,1,0:T(8,128)(2,1)} %bitcast.134, bf16[2048,2048]{1,0:T(8,128)(2,1)} %all-gather.7.cloned.1.call-done.w_ref), custom_call_target="tpu_custom_call" | custom-call | flops 2621440 | bytes 5120 | tf_op jit(solution)/shard_map/branch/pallas_call | solution.py:408
  256.7 7.8 %collective-permute-done.25.refs_6_ = bf16[256,2048]{1,0:T(8,128)(2,1)} collective-permute-done((bf16[256,2048]{1,0:T(8,128)(2,1)}, bf16[256,2048]{1,0:T(8,128)(2,1)}, u32[]{:S(2)}, u32[]{:S(2)}) %collective-permute-start.25) | collective-permute-done | bytes 1048608 | tf_op jit(solution)/shard_map/ppermute | solution.py:41
  264.6 16.4 %collective-permute-done.27.refs_6_ = bf16[256,2048]{1,0:T(8,128)(2,1)} collective-permute-done((bf16[256,2048]{1,0:T(8,128)(2,1)}, bf16[256,2048]{1,0:T(8,128)(2,1)}, u32[]{:S(2)}, u32[]{:S(2)}) %collective-permute-start.27) | collective-permute-done | bytes 1048608 | tf_op jit(solution)/shard_map/ppermute | solution.py:41
  281.0 2.4 collective-permute-start.28
  284.7 19.2 %norm_qkv.3 = (bf16[4,256,2048]{2,1,0:T(8,128)(2,1)}, bf16[4,256,2048]{2,1,0:T(8,128)(2,1)}, bf16[4,256,2048]{2,1,0:T(8,128)(2,1)}, f32[4,256,1536]{2,1,0:T(8,128)}) custom-call(s32[2]{0:T(128)} %pad_add_fusion.2.me_ref, f32[6,2048]{1,0:T(8,128)} %reshape.583.vectors_ref, f32[1,3584]{1,0:T(1,128)} %pad_maximum_fusion.5.bias_ref, ...), custom_call_target="tpu_custom_call" | custom-call | flops 1572864 | bytes 6656 | tf_op jit(solution)/shard_map/norm_qkv/pallas_call | solution.py:302
  306.6 19.8 %hidden.3 = (bf16[1024,2048]{1,0:T(8,128)(2,1)}, bf16[1024,2048]{1,0:T(8,128)(2,1)}) custom-call(bf16[1024,2048]{1,0:T(8,128)(2,1)} %bitcast.124, bf16[2048,3584]{1,0:T(8,128)(2,1)} %all-gather.5.cloned.1.call-done.refs_7_.w_ref, f32[1,3584]{1,0:T(1,128)} %pad_maximum_fusion.5.bias_ref), custom_call_target="tpu_custom_call" | custom-call | flops 2097152 | bytes 6144 | tf_op jit(solution)/shard_map/hidden/pallas_call | solution.py:328
  326.4 7.8 %attend.3 = (bf16[4,256,1536]{2,1,0:T(8,128)(2,1)S(1)}, bf16[4,256,512]{2,1,0:T(8,128)(2,1)S(1)}) custom-call(s32[4,256,1]{2,1,0:T(8,128)S(1)} %multiply_add_fusion.posq_ref, s32[4,1,1024]{2,1,0:T(1,128)S(1)} %pad_add_fusion.1.posk_ref, f32[4,256,128]{2,1,0:T(8,128)S(1)} %maximum_maximum_fusion.cos_ref, f32[4,256,128]{2,1,0:T(8,128)S(1)} %maximum_maximum_fusion.1.sin_ref, ...), custom_call_target="tpu_custom_call" | custom-call | flops 1073741824 | bytes 12582912 | tf_op jit(solution)/shard_map/attend/pallas_call | solution.py:171
  339.4 6.1 arrange.2
  345.6 16.1 %branch.3 = bf16[4,2,256,2048]{3,2,1,0:T(8,128)(2,1)} custom-call(bf16[1024,512]{1,0:T(8,128)(2,1)} %bitcast.108, bf16[1024,2048]{1,0:T(8,128)(2,1)} %get-tuple-element.464.act_ref.refs_3_, bf16[8,2,32,2048]{3,2,1,0:T(8,128)(2,1)} %bitcast.135, bf16[2048,2048]{1,0:T(8,128)(2,1)} %all-gather.7.cloned.1.call-done.w_ref, ...), custom_call_target="tpu_custom_call", output_to_operand_aliasing={{}: (4, {})} | custom-call | flops 2621440 | bytes 5120 | tf_op jit(solution)/shard_map/branch/pallas_call | solution.py:408
  363.7 6.1 arrange.3
  369.8 14.4 %grad_w2_sent.1 = bf16[4,256,2048]{2,1,0:T(8,128)(2,1)} custom-call(s32[1]{0:T(128)S(6)} %sub.109.me_ref, bf16[1024,2048]{1,0:T(8,128)(2,1)} %bitcast.112, bf16[1024,2048]{1,0:T(8,128)(2,1)} %bitcast.116, bf16[1024,2048]{1,0:T(8,128)(2,1)} %get-tuple-element.458.act_ref.refs_2_, bf16[1024,2048]{1,0:T(8,128)(2,1)} %get-tuple-element.464.act_ref.refs_3_), custom_call_target="tpu_custom_call" | custom-call | flops 2097152 | bytes 6144 | tf_op jit(solution)/shard_map/grad_w2_sent/pallas_call | solution.py:520
  384.2 16.9 %back_in.2 = (bf16[1024,512]{1,0:T(8,128)(2,1)}, bf16[1024,2048]{1,0:T(8,128)(2,1)}, f32[1,2048]{1,0:T(1,128)}) custom-call(bf16[1024,2048]{1,0:T(8,128)(2,1)} %bitcast.113, bf16[8,2,32,2048]{3,2,1,0:T(8,128)(2,1)} %bitcast.136, bf16[2048,2048]{1,0:T(8,128)(2,1)} %all-gather.7.cloned.1.call-done.w_ref, bf16[1024,2048]{1,0:T(8,128)(2,1)} %get-tuple-element.450.slope_ref), custom_call_target="tpu_custom_call" | custom-call | flops 2621440 | bytes 5120 | tf_op jit(solution)/shard_map/back_in/pallas_call | solution.py:444
  403.0 14.9 %grad_w2_kept.1 = bf16[4,256,2048]{2,1,0:T(8,128)(2,1)} custom-call(s32[1]{0:T(128)} %bitcast.37.me_ref, bf16[1024,2048]{1,0:T(8,128)(2,1)} %bitcast.114, bf16[1024,2048]{1,0:T(8,128)(2,1)} %bitcast.117, bf16[1024,2048]{1,0:T(8,128)(2,1)} %get-tuple-element.458.act_ref.refs_2_, bf16[1024,2048]{1,0:T(8,128)(2,1)} %get-tuple-element.464.act_ref.refs_3_, ...), custom_call_target="tpu_custom_call" | custom-call | flops 2097152 | bytes 6144 | tf_op jit(solution)/shard_map/grad_w2_kept/pallas_call | solution.py:520
  417.9 8.2 %all-to-all-start.3 = ((bf16[4,256,2048]{2,1,0:T(8,128)(2,1)}), bf16[4,256,2048]{2,1,0:T(8,128)(2,1)}, u32[]{:S(2)}, u32[]{:S(2)}) async-start(bf16[4,256,2048]{2,1,0:T(8,128)(2,1)} %grad_w2_kept.1), calls=%async_computation.3 | async-start | bytes 8388608 | tf_op jit(solution)/shard_map/all_to_all | solution.py:865
  426.3 9.8 %grad_dense.1 = (bf16[4,2,32,2048]{3,2,1,0:T(8,128)(2,1)}, bf16[4,2,32,2048]{3,2,1,0:T(8,128)(2,1)}) custom-call(s32[1]{0:T(128)} %bitcast.37.me_ref, bf16[1024,512]{1,0:T(8,128)(2,1)} %bitcast.107, bf16[1024,512]{1,0:T(8,128)(2,1)} %bitcast.109, bf16[1024,2048]{1,0:T(8,128)(2,1)} %bitcast.115, bf16[1024,2048]{1,0:T(8,128)(2,1)} %bitcast.118), custom_call_target="tpu_custom_call" | custom-call | flops 1048576 | bytes 3072 | tf_op jit(solution)/shard_map/grad_dense/pallas_call | solution.py:556
  436.1 17.1 %back_in.3 = (bf16[1024,512]{1,0:T(8,128)(2,1)}, bf16[1024,2048]{1,0:T(8,128)(2,1)}, f32[1,2048]{1,0:T(1,128)}) custom-call(bf16[1024,2048]{1,0:T(8,128)(2,1)} %bitcast.119, bf16[8,2,32,2048]{3,2,1,0:T(8,128)(2,1)} %bitcast.137, bf16[2048,2048]{1,0:T(8,128)(2,1)} %all-gather.7.cloned.1.call-done.w_ref, bf16[1024,2048]{1,0:T(8,128)(2,1)} %get-tuple-element.494.slope_ref), custom_call_target="tpu_custom_call" | custom-call | flops 2621440 | bytes 5120 | tf_op jit(solution)/shard_map/back_in/pallas_call | solution.py:444
  453.2 9.7 %attend_back.2 = (bf16[4,256,1536]{2,1,0:T(8,128)(2,1)S(1)}, f32[2,1,768]{2,1,0:T(1,128)S(1)}) custom-call(s32[4,256,1]{2,1,0:T(8,128)S(1)} %multiply_add_fusion.posq_ref, s32[4,1,1024]{2,1,0:T(1,128)S(1)} %pad_add_fusion.posk_ref, f32[4,256,128]{2,1,0:T(8,128)S(1)} %maximum_maximum_fusion.cos_ref, f32[4,256,128]{2,1,0:T(8,128)S(1)} %maximum_maximum_fusion.1.sin_ref, ...), custom_call_target="tpu_custom_call" | custom-call | flops 2684354560 | bytes 7864320 | tf_op jit(solution)/shard_map/attend_back/pallas_call | solution.py:192
  464.5 22.6 %back_out.2 = (bf16[1024,2048]{1,0:T(8,128)(2,1)}, f32[4,2048]{1,0:T(4,128)}) custom-call(f32[6,2048]{1,0:T(8,128)} %reshape.583.vectors_ref, bf16[1024,1536]{1,0:T(8,128)(2,1)} %bitcast.100, bf16[1024,2048]{1,0:T(8,128)(2,1)} %get-tuple-element.527.pre_ref.refs_2_, bf16[2048,3584]{1,0:T(8,128)(2,1)} %all-gather.5.cloned.1.call-done.refs_7_.w_ref, ...), custom_call_target="tpu_custom_call" | custom-call | flops 3670016 | bytes 7680 | tf_op jit(solution)/shard_map/back_out/pallas_call | solution.py:485
  487.1 14.4 %grad_w1_sent.1 = bf16[4,256,2048]{2,1,0:T(8,128)(2,1)} custom-call(s32[1]{0:T(128)S(6)} %sub.109.me_ref, bf16[1024,2048]{1,0:T(8,128)(2,1)} %bitcast.122, bf16[1024,2048]{1,0:T(8,128)(2,1)} %bitcast.125, bf16[1024,2048]{1,0:T(8,128)(2,1)} %get-tuple-element.527.pre_ref.refs_2_, bf16[1024,2048]{1,0:T(8,128)(2,1)} %get-tuple-element.547.refs_3_.pre_ref), custom_call_target="tpu_custom_call" | custom-call | flops 2097152 | bytes 6144 | tf_op jit(solution)/shard_map/grad_w1_sent/pallas_call | solution.py:520
  502.8 9.9 %attend_back.3 = (bf16[4,256,1536]{2,1,0:T(8,128)(2,1)S(1)}, f32[2,1,768]{2,1,0:T(1,128)S(1)}) custom-call(s32[4,256,1]{2,1,0:T(8,128)S(1)} %multiply_add_fusion.posq_ref, s32[4,1,1024]{2,1,0:T(1,128)S(1)} %pad_add_fusion.1.posk_ref, f32[4,256,128]{2,1,0:T(8,128)S(1)} %maximum_maximum_fusion.cos_ref, f32[4,256,128]{2,1,0:T(8,128)S(1)} %maximum_maximum_fusion.1.sin_ref, ...), custom_call_target="tpu_custom_call" | custom-call | flops 2684354560 | bytes 7864320 | tf_op jit(solution)/shard_map/attend_back/pallas_call | solution.py:192
  515.7 5.0 all-to-all-start.4
  520.7 15.5 %grad_w1_kept.1 = bf16[4,256,2048]{2,1,0:T(8,128)(2,1)} custom-call(s32[1]{0:T(128)} %bitcast.37.me_ref, bf16[1024,2048]{1,0:T(8,128)(2,1)} %bitcast.123, bf16[1024,2048]{1,0:T(8,128)(2,1)} %bitcast.126, bf16[1024,2048]{1,0:T(8,128)(2,1)} %get-tuple-element.527.pre_ref.refs_2_, bf16[1024,2048]{1,0:T(8,128)(2,1)} %get-tuple-element.547.refs_3_.pre_ref, ...), custom_call_target="tpu_custom_call" | custom-call | flops 2097152 | bytes 6144 | tf_op jit(solution)/shard_map/grad_w1_kept/pallas_call | solution.py:520
  537.2 4.9 all-to-all-start.5
  542.2 11.5 %grad_wq_sent.1 = bf16[4,256,1536]{2,1,0:T(8,128)(2,1)} custom-call(s32[1]{0:T(128)S(6)} %sub.109.me_ref, bf16[1024,2048]{1,0:T(8,128)(2,1)} %bitcast.138, bf16[1024,2048]{1,0:T(8,128)(2,1)} %bitcast.140, bf16[1024,1536]{1,0:T(8,128)(2,1)} %bitcast.101, bf16[1024,1536]{1,0:T(8,128)(2,1)} %bitcast.103), custom_call_target="tpu_custom_call" | custom-call | flops 1572864 | bytes 5120 | tf_op jit(solution)/shard_map/grad_wq_sent/pallas_call | solution.py:520
  553.7 22.6 %back_out.3 = (bf16[1024,2048]{1,0:T(8,128)(2,1)}, f32[4,2048]{1,0:T(4,128)}) custom-call(f32[6,2048]{1,0:T(8,128)} %reshape.583.vectors_ref, bf16[1024,1536]{1,0:T(8,128)(2,1)} %bitcast.104, bf16[1024,2048]{1,0:T(8,128)(2,1)} %get-tuple-element.547.refs_3_.pre_ref, bf16[2048,3584]{1,0:T(8,128)(2,1)} %all-gather.5.cloned.1.call-done.refs_7_.w_ref, ...), custom_call_target="tpu_custom_call" | custom-call | flops 3670016 | bytes 7680 | tf_op jit(solution)/shard_map/back_out/pallas_call | solution.py:485
  576.3 14.2 %all-to-all-done.5 = bf16[4,256,2048]{2,1,0:T(8,128)(2,1)} async-done(((bf16[4,256,2048]{2,1,0:T(8,128)(2,1)}), bf16[4,256,2048]{2,1,0:T(8,128)(2,1)}, u32[]{:S(2)}, u32[]{:S(2)}) %all-to-all-start.5) | async-done | bytes 4194336 | tf_op jit(solution)/shard_map/all_to_all | solution.py:865
  596.5 3.9 all-to-all-start.6
  600.3 5.2 convert_reduce_fusion.1
  605.5 11.9 %grad_wq_kept.1 = bf16[4,256,1536]{2,1,0:T(8,128)(2,1)} custom-call(s32[1]{0:T(128)} %bitcast.37.me_ref, bf16[1024,2048]{1,0:T(8,128)(2,1)} %bitcast.139, bf16[1024,2048]{1,0:T(8,128)(2,1)} %bitcast.141, bf16[1024,1536]{1,0:T(8,128)(2,1)} %bitcast.102, bf16[1024,1536]{1,0:T(8,128)(2,1)} %bitcast.105, bf16[4,256,1536]{2,1,0:T(8,128)(2,1)} %collective-permute-done.37.refs_4_), custom_call_target="tpu_custom_call" | custom-call | flops 1572864 | bytes 5120 | tf_op jit(solution)/shard_map/grad_wq_kept/pallas_call | solution.py:520
  617.4 9.5 %all-to-all-done.6 = bf16[2,8,32,2048]{3,2,0,1:T(8,128)(2,1)S(1)} async-done(((bf16[2,8,32,2048]{3,2,0,1:T(8,128)(2,1)}), bf16[2,8,32,2048]{3,2,0,1:T(8,128)(2,1)S(1)}, u32[]{:S(2)}, u32[]{:S(2)}) %all-to-all-start.6) | async-done | bytes 2097184 | tf_op jit(solution)/shard_map/all_to_all | solution.py:611
  628.2 4.8 all-to-all-start.7
  636.7 4.5 convert_reduce_fusion
  644.2 21.0 %collective-permute-done.38 = f32[1728]{0:T(1024)S(1)} collective-permute-done((f32[1728]{0:T(1024)S(1)}, f32[1728]{0:T(1024)S(1)}, u32[]{:S(2)}, u32[]{:S(2)}) %collective-permute-start.38) | collective-permute-done | bytes 6944 | tf_op jit(solution)/shard_map/ppermute | solution.py:946
  665.2 3.5 collective-permute-done.39
  670.1 2.8 reduce-scatter.8.cloned.1.call-done
  680.3 4.3 all-to-all-start.8
  688.0 2.7 collective-permute-start.47
  690.7 2.5 convert_reduce_fusion.2
  696.7 3.3 copy.60
  702.4 8.9 %all-to-all-done.8 = bf16[2,8,32,2048]{3,2,0,1:T(8,128)(2,1)} async-done(((bf16[2,8,32,2048]{3,2,0,1:T(8,128)(2,1)}), bf16[2,8,32,2048]{3,2,0,1:T(8,128)(2,1)}, u32[]{:S(2)}, u32[]{:S(2)}) %all-to-all-start.8) | async-done | bytes 2097184 | tf_op jit(solution)/shard_map/all_to_all | solution.py:611
  711.3 3.2 copy.61
  (311 shorter events, 99.7 us)
Async XLA Ops:
  10.4 20.7 %all-to-all-start = ((bf16[8,32,2048]{2,1,0:T(8,128)(2,1)}), bf16[8,32,2048]{2,1,0:T(8,128)(2,1)S(1)}, u32[]{:S(2)}, u32[]{:S(2)}) async-start(bf16[8,32,2048]{2,1,0:T(8,128)(2,1)} %get-tuple-element.667), calls=%async_computation | async-start | bytes 2097152 | tf_op jit(solution)/shard_map/all_to_all | solution.py:607
  15.7 129.7 %all-gather.5.cloned.1.call-start = ((), (), s32[]{:S(2)}) async-start(), calls=%async_computation.12 | async-start | bytes 16515072 | tf_op jit(solution)/shard_map/all_gather | solution.py:646
  31.1 23.1 %collective-permute-start.7 = (bf16[256,2048]{1,0:T(8,128)(2,1)S(1)}, bf16[256,2048]{1,0:T(8,128)(2,1)}, u32[]{:S(2)}, u32[]{:S(2)}) collective-permute-start(bf16[256,2048]{1,0:T(8,128)(2,1)S(1)} %bitcast.127), channel_id=1, source_target_pairs={{0,1},{1,2},{2,3},{4,5},{5,6},{6,7},{8,9},{9,10},{10,11},{12,13},{... | collective-permute-start | bytes 3145736 | tf_op jit(solution)/shard_map/ppermute | solution.py:39
  35.7 23.8 %collective-permute-start.8 = (bf16[256,2048]{1,0:T(8,128)(2,1)S(1)}, bf16[256,2048]{1,0:T(8,128)(2,1)}, u32[]{:S(2)}, u32[]{:S(2)}) collective-permute-start(bf16[256,2048]{1,0:T(8,128)(2,1)S(1)} %bitcast.128), channel_id=1, source_target_pairs={{1,0},{2,1},{3,2},{5,4},{6,5},{7,6},{9,8},{10,9},{11,10},{13,12},{... | collective-permute-start | bytes 3145736 | tf_op jit(solution)/shard_map/ppermute | solution.py:41
  38.4 3.9 collective-permute-start
  38.4 4.6 collective-permute-start.1
  39.0 4.1 collective-permute-start.2
  42.3 3.6 collective-permute-start.3
  43.1 3.6 collective-permute-start.4
  43.1 3.6 collective-permute-start.5
  45.9 1.9 collective-permute-start.6
  59.4 28.0 %collective-permute-start.12 = (bf16[256,2048]{1,0:T(8,128)(2,1)}, bf16[256,2048]{1,0:T(8,128)(2,1)}, u32[]{:S(2)}, u32[]{:S(2)}) collective-permute-start(bf16[256,2048]{1,0:T(8,128)(2,1)} %collective-permute-done.7.refs_1_), channel_id=1, source_target_pairs={{1,2},{2,3},{5,6},{6,7},{9,10},{10,11},{13,14},{14,15},{17,18},{18... | collective-permute-start | bytes 3145736 | tf_op jit(solution)/shard_map/ppermute | solution.py:39
  61.1 26.3 %collective-permute-start.13 = (bf16[256,2048]{1,0:T(8,128)(2,1)}, bf16[256,2048]{1,0:T(8,128)(2,1)}, u32[]{:S(2)}, u32[]{:S(2)}) collective-permute-start(bf16[256,2048]{1,0:T(8,128)(2,1)} %collective-permute-done.8.refs_4_), channel_id=1, source_target_pairs={{1,0},{2,1},{5,4},{6,5},{9,8},{10,9},{13,12},{14,13},{17,16},{18,1... | collective-permute-start | bytes 3145736 | tf_op jit(solution)/shard_map/ppermute | solution.py:41
  65.5 54.3 %all-to-all-start.1 = ((bf16[2,8,32,2048]{3,2,0,1:T(8,128)(2,1)}), bf16[2,8,32,2048]{3,2,0,1:T(8,128)(2,1)S(1)}, u32[]{:S(2)}, u32[]{:S(2)}) async-start(bf16[2,8,32,2048]{3,2,0,1:T(8,128)(2,1)} %pad_maximum_fusion), calls=%async_computation.1 | async-start | bytes 4194304 | tf_op jit(solution)/shard_map/all_to_all | solution.py:704
  70.4 170.2 %all-gather.9.cloned.1.call-start = ((), (), s32[]{:S(2)}) async-start(), calls=%async_computation.17 | async-start | bytes 2359296 | tf_op jit(solution)/shard_map/all_gather | solution.py:719
  70.5 10.1 %collective-permute-start.9 = (bf16[3072]{0:T(1024)(128)(2,1)S(1)}, bf16[3072]{0:T(1024)(128)(2,1)S(1)}, u32[]{:S(2)}, u32[]{:S(2)}) collective-permute-start(bf16[3072]{0:T(1024)(128)(2,1)S(1)} %reshape.544), channel_id=1, source_target_pairs={{0,1},{1,2},{2,3},{3,0},{4,5},{5,6},{6,7},{7,4},{8,9},{9,10},{10,1... | collective-permute-start | bytes 18440 | tf_op jit(solution)/shard_map/ppermute | solution.py:56
  74.7 12.4 %collective-permute-start.10 = (bf16[3072]{0:T(1024)(128)(2,1)S(1)}, bf16[3072]{0:T(1024)(128)(2,1)S(1)}, u32[]{:S(2)}, u32[]{:S(2)}) collective-permute-start(bf16[3072]{0:T(1024)(128)(2,1)S(1)} %reshape.544), channel_id=1, source_target_pairs={{0,2},{1,3},{2,0},{3,1},{4,6},{5,7},{6,4},{7,5},{8,10},{9,11},{10,... | collective-permute-start | bytes 18440 | tf_op jit(solution)/shard_map/ppermute | solution.py:56
  77.7 9.5 %collective-permute-start.11 = (bf16[3072]{0:T(1024)(128)(2,1)S(1)}, bf16[3072]{0:T(1024)(128)(2,1)S(1)}, u32[]{:S(2)}, u32[]{:S(2)}) collective-permute-start(bf16[3072]{0:T(1024)(128)(2,1)S(1)} %reshape.544), channel_id=1, source_target_pairs={{0,3},{1,0},{2,1},{3,2},{4,7},{5,4},{6,5},{7,6},{8,11},{9,8},{10,9... | collective-permute-start | bytes 18440 | tf_op jit(solution)/shard_map/ppermute | solution.py:56
  87.4 32.3 %collective-permute-start.14 = (bf16[256,2048]{1,0:T(8,128)(2,1)}, bf16[256,2048]{1,0:T(8,128)(2,1)}, u32[]{:S(2)}, u32[]{:S(2)}) collective-permute-start(bf16[256,2048]{1,0:T(8,128)(2,1)} %collective-permute-done.12.refs_2_), channel_id=1, source_target_pairs={{2,3},{6,7},{10,11},{14,15},{18,19},{22,23},{26,27},{30,31}} | collective-permute-start | bytes 3145736 | tf_op jit(solution)/shard_map/ppermute | solution.py:39
  89.1 30.7 %collective-permute-start.15 = (bf16[256,2048]{1,0:T(8,128)(2,1)}, bf16[256,2048]{1,0:T(8,128)(2,1)}, u32[]{:S(2)}, u32[]{:S(2)}) collective-permute-start(bf16[256,2048]{1,0:T(8,128)(2,1)} %collective-permute-done.13.refs_5_), channel_id=1, source_target_pairs={{1,0},{5,4},{9,8},{13,12},{17,16},{21,20},{25,24},{29,28}} | collective-permute-start | bytes 3145736 | tf_op jit(solution)/shard_map/ppermute | solution.py:41
  119.8 120.8 %all-gather.7.cloned.1.call-start = ((), (), s32[]{:S(2)}) async-start(), calls=%async_computation.13 | async-start | bytes 9437184 | tf_op jit(solution)/shard_map/all_gather | solution.py:718
  123.4 61.0 %collective-permute-start.16 = (bf16[256,2048]{1,0:T(8,128)(2,1)S(1)}, bf16[256,2048]{1,0:T(8,128)(2,1)}, u32[]{:S(2)}, u32[]{:S(2)}) collective-permute-start(bf16[256,2048]{1,0:T(8,128)(2,1)S(1)} %bitcast.142), channel_id=1, source_target_pairs={{0,1},{1,2},{2,3},{4,5},{5,6},{6,7},{8,9},{9,10},{10,11},{12,13},{... | collective-permute-start | bytes 3145736 | tf_op jit(solution)/shard_map/ppermute | solution.py:39
  130.5 53.9 %collective-permute-start.17 = (bf16[256,2048]{1,0:T(8,128)(2,1)S(1)}, bf16[256,2048]{1,0:T(8,128)(2,1)}, u32[]{:S(2)}, u32[]{:S(2)}) collective-permute-start(bf16[256,2048]{1,0:T(8,128)(2,1)S(1)} %bitcast.143), channel_id=1, source_target_pairs={{1,0},{2,1},{3,2},{5,4},{6,5},{7,6},{9,8},{10,9},{11,10},{13,12},{... | collective-permute-start | bytes 3145736 | tf_op jit(solution)/shard_map/ppermute | solution.py:41
  131.8 52.6 %collective-permute-start.18 = (bf16[256,2048]{1,0:T(8,128)(2,1)}, bf16[256,2048]{1,0:T(8,128)(2,1)}, u32[]{:S(2)}, u32[]{:S(2)}) collective-permute-start(bf16[256,2048]{1,0:T(8,128)(2,1)} %bitcast.15.refs_0_), channel_id=1, source_target_pairs={{0,1},{1,2},{2,3},{4,5},{5,6},{6,7},{8,9},{9,10},{10,11},{12,13},{... | collective-permute-start | bytes 3145736 | tf_op jit(solution)/shard_map/ppermute | solution.py:39
  137.7 46.7 %collective-permute-start.19 = (bf16[256,2048]{1,0:T(8,128)(2,1)}, bf16[256,2048]{1,0:T(8,128)(2,1)}, u32[]{:S(2)}, u32[]{:S(2)}) collective-permute-start(bf16[256,2048]{1,0:T(8,128)(2,1)} %bitcast.15.refs_0_), channel_id=1, source_target_pairs={{1,0},{2,1},{3,2},{5,4},{6,5},{7,6},{9,8},{10,9},{11,10},{13,12},{... | collective-permute-start | bytes 3145736 | tf_op jit(solution)/shard_map/ppermute | solution.py:41
  184.4 36.4 %collective-permute-start.20 = (bf16[256,2048]{1,0:T(8,128)(2,1)}, bf16[256,2048]{1,0:T(8,128)(2,1)}, u32[]{:S(2)}, u32[]{:S(2)}) collective-permute-start(bf16[256,2048]{1,0:T(8,128)(2,1)} %collective-permute-done.16.refs_1_), channel_id=1, source_target_pairs={{1,2},{2,3},{5,6},{6,7},{9,10},{10,11},{13,14},{14,15},{17,18},{18... | collective-permute-start | bytes 3145736 | tf_op jit(solution)/shard_map/ppermute | solution.py:39
  186.1 34.7 %collective-permute-start.21 = (bf16[256,2048]{1,0:T(8,128)(2,1)}, bf16[256,2048]{1,0:T(8,128)(2,1)}, u32[]{:S(2)}, u32[]{:S(2)}) collective-permute-start(bf16[256,2048]{1,0:T(8,128)(2,1)} %collective-permute-done.17.refs_4_), channel_id=1, source_target_pairs={{1,0},{2,1},{5,4},{6,5},{9,8},{10,9},{13,12},{14,13},{17,16},{18,1... | collective-permute-start | bytes 3145736 | tf_op jit(solution)/shard_map/ppermute | solution.py:41
  187.4 33.4 %collective-permute-start.22 = (bf16[256,2048]{1,0:T(8,128)(2,1)}, bf16[256,2048]{1,0:T(8,128)(2,1)}, u32[]{:S(2)}, u32[]{:S(2)}) collective-permute-start(bf16[256,2048]{1,0:T(8,128)(2,1)} %collective-permute-done.18.refs_1_), channel_id=1, source_target_pairs={{1,2},{2,3},{5,6},{6,7},{9,10},{10,11},{13,14},{14,15},{17,18},{18... | collective-permute-start | bytes 3145736 | tf_op jit(solution)/shard_map/ppermute | solution.py:39
  189.0 45.6 %collective-permute-start.23 = (bf16[256,2048]{1,0:T(8,128)(2,1)}, bf16[256,2048]{1,0:T(8,128)(2,1)}, u32[]{:S(2)}, u32[]{:S(2)}) collective-permute-start(bf16[256,2048]{1,0:T(8,128)(2,1)} %collective-permute-done.19.refs_4_), channel_id=1, source_target_pairs={{1,0},{2,1},{5,4},{6,5},{9,8},{10,9},{13,12},{14,13},{17,16},{18,1... | collective-permute-start | bytes 3145736 | tf_op jit(solution)/shard_map/ppermute | solution.py:41
  190.5 30.3 %all-to-all-start.2 = ((bf16[8,32,2048]{2,1,0:T(8,128)(2,1)}), bf16[8,32,2048]{2,1,0:T(8,128)(2,1)S(1)}, u32[]{:S(2)}, u32[]{:S(2)}) async-start(bf16[8,32,2048]{2,1,0:T(8,128)(2,1)} %get-tuple-element.353), calls=%async_computation.2 | async-start | bytes 2097152 | tf_op jit(solution)/shard_map/all_to_all | solution.py:607
  194.1 396.5 %reduce-scatter.4.cloned.1.call-start = ((), (), s32[]{:S(2)}) async-start(), calls=%async_computation.14 | async-start | bytes 10485760 | tf_op jit(solution)/shard_map/reduce_scatter | solution.py:765
  220.8 62.7 %copy-start.14 = (bf16[8,32,2048]{2,1,0:T(8,128)(2,1)}, bf16[8,32,2048]{2,1,0:T(8,128)(2,1)S(1)}, u32[]{:S(2)}) copy-start(bf16[8,32,2048]{2,1,0:T(8,128)(2,1)S(1)} %all-to-all-done.2) | copy-start | bytes 3145732
  234.6 22.1 %collective-permute-start.24 = (bf16[256,2048]{1,0:T(8,128)(2,1)}, bf16[256,2048]{1,0:T(8,128)(2,1)}, u32[]{:S(2)}, u32[]{:S(2)}) collective-permute-start(bf16[256,2048]{1,0:T(8,128)(2,1)} %collective-permute-done.20.refs_2_), channel_id=1, source_target_pairs={{2,3},{6,7},{10,11},{14,15},{18,19},{22,23},{26,27},{30,31}} | collective-permute-start | bytes 3145736 | tf_op jit(solution)/shard_map/ppermute | solution.py:39
  236.3 28.3 %collective-permute-start.25 = (bf16[256,2048]{1,0:T(8,128)(2,1)}, bf16[256,2048]{1,0:T(8,128)(2,1)}, u32[]{:S(2)}, u32[]{:S(2)}) collective-permute-start(bf16[256,2048]{1,0:T(8,128)(2,1)} %collective-permute-done.21.refs_5_), channel_id=1, source_target_pairs={{1,0},{5,4},{9,8},{13,12},{17,16},{21,20},{25,24},{29,28}} | collective-permute-start | bytes 3145736 | tf_op jit(solution)/shard_map/ppermute | solution.py:41
  237.6 27.0 %collective-permute-start.26 = (bf16[256,2048]{1,0:T(8,128)(2,1)}, bf16[256,2048]{1,0:T(8,128)(2,1)}, u32[]{:S(2)}, u32[]{:S(2)}) collective-permute-start(bf16[256,2048]{1,0:T(8,128)(2,1)} %collective-permute-done.22.refs_2_), channel_id=1, source_target_pairs={{2,3},{6,7},{10,11},{14,15},{18,19},{22,23},{26,27},{30,31}} | collective-permute-start | bytes 3145736 | tf_op jit(solution)/shard_map/ppermute | solution.py:39
  239.3 41.7 %collective-permute-start.27 = (bf16[256,2048]{1,0:T(8,128)(2,1)}, bf16[256,2048]{1,0:T(8,128)(2,1)}, u32[]{:S(2)}, u32[]{:S(2)}) collective-permute-start(bf16[256,2048]{1,0:T(8,128)(2,1)} %collective-permute-done.23.refs_5_), channel_id=1, source_target_pairs={{1,0},{5,4},{9,8},{13,12},{17,16},{21,20},{25,24},{29,28}} | collective-permute-start | bytes 3145736 | tf_op jit(solution)/shard_map/ppermute | solution.py:41
  281.0 22.9 %collective-permute-start.28 = (bf16[256,2048]{1,0:T(8,128)(2,1)S(1)}, bf16[256,2048]{1,0:T(8,128)(2,1)}, u32[]{:S(2)}, u32[]{:S(2)}) collective-permute-start(bf16[256,2048]{1,0:T(8,128)(2,1)S(1)} %bitcast.145), channel_id=1, source_target_pairs={{0,1},{1,2},{2,3},{4,5},{5,6},{6,7},{8,9},{9,10},{10,11},{12,13},{... | collective-permute-start | bytes 3145736 | tf_op jit(solution)/shard_map/ppermute | solution.py:39
  283.4 21.0 %collective-permute-start.29 = (bf16[256,2048]{1,0:T(8,128)(2,1)S(1)}, bf16[256,2048]{1,0:T(8,128)(2,1)}, u32[]{:S(2)}, u32[]{:S(2)}) collective-permute-start(bf16[256,2048]{1,0:T(8,128)(2,1)S(1)} %bitcast.146), channel_id=1, source_target_pairs={{1,0},{2,1},{3,2},{5,4},{6,5},{7,6},{9,8},{10,9},{11,10},{13,12},{... | collective-permute-start | bytes 3145736 | tf_op jit(solution)/shard_map/ppermute | solution.py:41
  304.4 32.6 %collective-permute-start.30 = (bf16[256,2048]{1,0:T(8,128)(2,1)}, bf16[256,2048]{1,0:T(8,128)(2,1)S(1)}, u32[]{:S(2)}, u32[]{:S(2)}) collective-permute-start(bf16[256,2048]{1,0:T(8,128)(2,1)} %collective-permute-done.28.refs_1_), channel_id=1, source_target_pairs={{1,2},{2,3},{5,6},{6,7},{9,10},{10,11},{13,14},{14,15},{17,18},{18... | collective-permute-start | bytes 3145736 | tf_op jit(solution)/shard_map/ppermute | solution.py:39
  305.1 31.9 %collective-permute-start.31 = (bf16[256,2048]{1,0:T(8,128)(2,1)}, bf16[256,2048]{1,0:T(8,128)(2,1)}, u32[]{:S(2)}, u32[]{:S(2)}) collective-permute-start(bf16[256,2048]{1,0:T(8,128)(2,1)} %collective-permute-done.29.refs_4_), channel_id=1, source_target_pairs={{1,0},{2,1},{5,4},{6,5},{9,8},{10,9},{13,12},{14,13},{17,16},{18,1... | collective-permute-start | bytes 3145736 | tf_op jit(solution)/shard_map/ppermute | solution.py:41
  337.0 24.7 %collective-permute-start.32 = (bf16[256,2048]{1,0:T(8,128)(2,1)S(1)}, bf16[256,2048]{1,0:T(8,128)(2,1)S(1)}, u32[]{:S(2)}, u32[]{:S(2)}) collective-permute-start(bf16[256,2048]{1,0:T(8,128)(2,1)S(1)} %collective-permute-done.30.refs_2_), channel_id=1, source_target_pairs={{2,3},{6,7},{10,11},{14,15},{18,19},{22,23},{26,27},{30,31}} | collective-permute-start | bytes 3145736 | tf_op jit(solution)/shard_map/ppermute | solution.py:39
  337.7 24.9 %collective-permute-start.33 = (bf16[256,2048]{1,0:T(8,128)(2,1)}, bf16[256,2048]{1,0:T(8,128)(2,1)S(1)}, u32[]{:S(2)}, u32[]{:S(2)}) collective-permute-start(bf16[256,2048]{1,0:T(8,128)(2,1)} %collective-permute-done.31.refs_5_), channel_id=1, source_target_pairs={{1,0},{5,4},{9,8},{13,12},{17,16},{21,20},{25,24},{29,28}} | collective-permute-start | bytes 3145736 | tf_op jit(solution)/shard_map/ppermute | solution.py:41
  384.2 16.9 %collective-permute-start.34 = (bf16[4,256,2048]{2,1,0:T(8,128)(2,1)}, bf16[4,256,2048]{2,1,0:T(8,128)(2,1)S(1)}, u32[]{:S(2)}, u32[]{:S(2)}) collective-permute-start(bf16[4,256,2048]{2,1,0:T(8,128)(2,1)} %grad_w2_sent.1), channel_id=1, source_target_pairs={{0,4},{4,0},{8,12},{12,8},{16,20},{20,16},{24,28},{28,24},{1,5},{5... | collective-permute-start | bytes 12582920 | tf_op jit(solution)/shard_map/ppermute | solution.py:831
  417.9 69.2 %all-to-all-start.3 = ((bf16[4,256,2048]{2,1,0:T(8,128)(2,1)}), bf16[4,256,2048]{2,1,0:T(8,128)(2,1)}, u32[]{:S(2)}, u32[]{:S(2)}) async-start(bf16[4,256,2048]{2,1,0:T(8,128)(2,1)} %grad_w2_kept.1), calls=%async_computation.3 | async-start | bytes 8388608 | tf_op jit(solution)/shard_map/all_to_all | solution.py:865
  426.1 243.6 %reduce-scatter.6.cloned.1.call-start = ((), (), s32[]{:S(2)}) async-start(), calls=%async_computation.15 | async-start | bytes 5242880 | tf_op jit(solution)/shard_map/reduce_scatter | solution.py:765
  501.5 12.8 %collective-permute-start.35 = (bf16[4,256,2048]{2,1,0:T(8,128)(2,1)}, bf16[4,256,2048]{2,1,0:T(8,128)(2,1)}, u32[]{:S(2)}, u32[]{:S(2)}) collective-permute-start(bf16[4,256,2048]{2,1,0:T(8,128)(2,1)} %grad_w1_sent.1), channel_id=1, source_target_pairs={{0,4},{4,0},{8,12},{12,8},{16,20},{20,16},{24,28},{28,24},{1,5},{5... | collective-permute-start | bytes 12582920 | tf_op jit(solution)/shard_map/ppermute | solution.py:831
  501.7 12.6 %collective-permute-start.36 = (bf16[4,64,2048]{2,1,0:T(8,128)(2,1)}, bf16[4,64,2048]{2,1,0:T(8,128)(2,1)S(1)}, u32[]{:S(2)}, u32[]{:S(2)}) collective-permute-start(bf16[4,64,2048]{2,1,0:T(8,128)(2,1)} %bitcast.175), channel_id=1, source_target_pairs={{0,4},{4,0},{8,12},{12,8},{16,20},{20,16},{24,28},{28,24},{1,5},{5... | collective-permute-start | bytes 3145736 | tf_op jit(solution)/shard_map/ppermute | solution.py:856
  515.7 20.6 %all-to-all-start.4 = ((bf16[4,64,2048]{2,1,0:T(8,128)(2,1)}), bf16[4,64,2048]{2,1,0:T(8,128)(2,1)S(1)}, u32[]{:S(2)}, u32[]{:S(2)}) async-start(bf16[4,64,2048]{2,1,0:T(8,128)(2,1)} %add_convert_fusion), calls=%async_computation.4 | async-start | bytes 2097152 | tf_op jit(solution)/shard_map/all_to_all | solution.py:865
  537.2 53.3 %all-to-all-start.5 = ((bf16[4,256,2048]{2,1,0:T(8,128)(2,1)}), bf16[4,256,2048]{2,1,0:T(8,128)(2,1)}, u32[]{:S(2)}, u32[]{:S(2)}) async-start(bf16[4,256,2048]{2,1,0:T(8,128)(2,1)} %grad_w1_kept.1), calls=%async_computation.5 | async-start | bytes 8388608 | tf_op jit(solution)/shard_map/all_to_all | solution.py:865
  542.1 130.8 %reduce-scatter.8.cloned.1.call-start = ((), (), s32[]{:S(2)}) async-start(), calls=%async_computation.16 | async-start | bytes 5242880 | tf_op jit(solution)/shard_map/reduce_scatter | solution.py:765
  592.7 12.8 %collective-permute-start.37 = (bf16[4,256,1536]{2,1,0:T(8,128)(2,1)}, bf16[4,256,1536]{2,1,0:T(8,128)(2,1)}, u32[]{:S(2)}, u32[]{:S(2)}) collective-permute-start(bf16[4,256,1536]{2,1,0:T(8,128)(2,1)} %grad_wq_sent.1), channel_id=1, source_target_pairs={{0,4},{4,0},{8,12},{12,8},{16,20},{20,16},{24,28},{28,24},{1,5},{5... | collective-permute-start | bytes 9437192 | tf_op jit(solution)/shard_map/ppermute | solution.py:856
  596.5 30.4 %all-to-all-start.6 = ((bf16[2,8,32,2048]{3,2,0,1:T(8,128)(2,1)}), bf16[2,8,32,2048]{3,2,0,1:T(8,128)(2,1)S(1)}, u32[]{:S(2)}, u32[]{:S(2)}) async-start(bf16[2,8,32,2048]{3,2,0,1:T(8,128)(2,1)} %pad_maximum_fusion.1), calls=%async_computation.7 | async-start | bytes 4194304 | tf_op jit(solution)/shard_map/all_to_all | solution.py:611
  628.2 41.8 %all-to-all-start.7 = ((bf16[4,256,1536]{2,1,0:T(8,128)(2,1)}), bf16[4,256,1536]{2,1,0:T(8,128)(2,1)}, u32[]{:S(2)}, u32[]{:S(2)}) async-start(bf16[4,256,1536]{2,1,0:T(8,128)(2,1)} %grad_wq_kept.1), calls=%async_computation.8 | async-start | bytes 6291456 | tf_op jit(solution)/shard_map/all_to_all | solution.py:865
  634.7 30.6 %collective-permute-start.38 = (f32[1728]{0:T(1024)S(1)}, f32[1728]{0:T(1024)S(1)}, u32[]{:S(2)}, u32[]{:S(2)}) collective-permute-start(f32[1728]{0:T(1024)S(1)} %get-tuple-element.655), channel_id=1, source_target_pairs={{0,4},{4,8},{8,12},{12,16},{16,20},{20,24},{24,28},{28,0},{1,5},{5... | collective-permute-start | bytes 20744 | tf_op jit(solution)/shard_map/ppermute | solution.py:946
  634.7 34.0 %collective-permute-start.39 = (f32[1728]{0:T(1024)S(1)}, f32[1728]{0:T(1024)S(1)}, u32[]{:S(2)}, u32[]{:S(2)}) collective-permute-start(f32[1728]{0:T(1024)S(1)} %get-tuple-element.654), channel_id=1, source_target_pairs={{0,8},{4,12},{8,16},{12,20},{16,24},{20,28},{24,0},{28,4},{1,9},{5... | collective-permute-start | bytes 20744 | tf_op jit(solution)/shard_map/ppermute | solution.py:946
  641.2 28.4 %collective-permute-start.40 = (f32[1728]{0:T(1024)S(1)}, f32[1728]{0:T(1024)S(1)}, u32[]{:S(2)}, u32[]{:S(2)}) collective-permute-start(f32[1728]{0:T(1024)S(1)} %get-tuple-element.653), channel_id=1, source_target_pairs={{0,12},{4,16},{8,20},{12,24},{16,28},{20,0},{24,4},{28,8},{1,13},{... | collective-permute-start | bytes 20744 | tf_op jit(solution)/shard_map/ppermute | solution.py:946
  643.5 26.1 %collective-permute-start.41 = (f32[1728]{0:T(1024)S(1)}, f32[1728]{0:T(1024)S(1)}, u32[]{:S(2)}, u32[]{:S(2)}) collective-permute-start(f32[1728]{0:T(1024)S(1)} %get-tuple-element.652), channel_id=1, source_target_pairs={{0,16},{4,20},{8,24},{12,28},{16,0},{20,4},{24,8},{28,12},{1,17},{... | collective-permute-start | bytes 20744 | tf_op jit(solution)/shard_map/ppermute | solution.py:946
  644.1 25.6 %collective-permute-start.42 = (f32[1728]{0:T(1024)S(1)}, f32[1728]{0:T(1024)S(1)}, u32[]{:S(2)}, u32[]{:S(2)}) collective-permute-start(f32[1728]{0:T(1024)S(1)} %get-tuple-element.651), channel_id=1, source_target_pairs={{0,20},{4,24},{8,28},{12,0},{16,4},{20,8},{24,12},{28,16},{1,21},{... | collective-permute-start | bytes 20744 | tf_op jit(solution)/shard_map/ppermute | solution.py:946
  665.2 4.5 collective-permute-start.43
  668.7 1.4 collective-permute-start.44
  680.3 31.0 %all-to-all-start.8 = ((bf16[2,8,32,2048]{3,2,0,1:T(8,128)(2,1)}), bf16[2,8,32,2048]{3,2,0,1:T(8,128)(2,1)}, u32[]{:S(2)}, u32[]{:S(2)}) async-start(bf16[2,8,32,2048]{3,2,0,1:T(8,128)(2,1)} %pad_maximum_fusion.2), calls=%async_computation.11 | async-start | bytes 4194304 | tf_op jit(solution)/shard_map/all_to_all | solution.py:611
  684.8 17.0 %collective-permute-start.45 = (f32[320]{0:T(512)S(1)}, f32[320]{0:T(512)S(1)}, u32[]{:S(2)}, u32[]{:S(2)}) collective-permute-start(f32[320]{0:T(512)S(1)} %get-tuple-element.656), channel_id=1, source_target_pairs={{0,1},{1,2},{2,3},{3,0},{4,5},{5,6},{6,7},{7,4},{8,9},{9,10},{10,1... | collective-permute-start | bytes 3848 | tf_op jit(solution)/shard_map/ppermute | solution.py:67
  686.3 15.5 %collective-permute-start.46 = (f32[320]{0:T(512)S(1)}, f32[320]{0:T(512)S(1)}, u32[]{:S(2)}, u32[]{:S(2)}) collective-permute-start(f32[320]{0:T(512)S(1)} %get-tuple-element.658), channel_id=1, source_target_pairs={{0,2},{1,3},{2,0},{3,1},{4,6},{5,7},{6,4},{7,5},{8,10},{9,11},{10,... | collective-permute-start | bytes 3848 | tf_op jit(solution)/shard_map/ppermute | solution.py:67
  688.0 13.8 %collective-permute-start.47 = (f32[320]{0:T(512)S(1)}, f32[320]{0:T(512)S(1)}, u32[]{:S(2)}, u32[]{:S(2)}) collective-permute-start(f32[320]{0:T(512)S(1)} %get-tuple-element.657), channel_id=1, source_target_pairs={{0,3},{1,0},{2,1},{3,2},{4,7},{5,4},{6,5},{7,6},{8,11},{9,8},{10,9... | collective-permute-start | bytes 3848 | tf_op jit(solution)/shard_map/ppermute | solution.py:67
  (46 other events, 414.4 us)
Sparse Core Ops, SparseCore 0:
  31.2 103.0 all-gather.4
  136.2 27.8 all-gather.8
  166.0 65.6 all-gather.6
  363.8 149.8 reduce-scatter.3
  515.8 77.4 reduce-scatter.5
  595.6 77.2 reduce-scatter.7

commit v6 on v5

--- a/solution.py
+++ b/solution.py
@@ -699,9 +699,12 @@
             axis=1,
         )
 
+    def stack_two():
+        env["two"] = jnp.stack([after(hidden_in[1]), cotangent[0]])
+
     def deal_two():
-        two = jnp.stack([after(hidden_in[1]), cotangent[0]])
-        pending["two"] = lax.all_to_all(two, "dp", split_axis=1, concat_axis=1, tiled=True)
+        stacked = env.pop("two")
+        pending["two"] = lax.all_to_all(stacked, "dp", split_axis=1, concat_axis=1, tiled=True)
 
     last = n_t - 2
 
@@ -713,7 +716,7 @@
     for i in range(n_t - 1):
         stage(
             [chains["x0"]],
-            at(i, [vectors_over_dp], [vectors_over_tensor, deal_two], [vectors_whole, join("two")]),
+            at(i, [vectors_over_dp, stack_two], [vectors_over_tensor, deal_two], [vectors_whole, join("two")]),
         )
     w_fc2 = lax.all_gather(after(fc2_weight.T), "dp", axis=0, tiled=True)
     w_dense = lax.all_gather(after(dense_weight), "dp", axis=0, tiled=False)

time: 732 us -> 728 us (level)
    unnamed x102 -> x104, local copies, waits for them, and re-layouts: 28.6 us -> 28.6 us
  transfers between devices with their start and end apart: 63 -> 63, of which waited for: 22 -> 20; matrix products, arithmetic and copies ran while one was open for 7% -> 7% of each run, Pallas kernels for 46% -> 46%
where the time goes in v6:
time: 728 us; the launch traced here: 719 us
  Pallas kernels  330 us (45%)
  waiting for transfers between devices  173 us (24%)
  starting transfers between devices  118 us (16%)
  local copies, waits for them, and re-layouts  41.6 us (6%)
  other arithmetic  39.4 us (5%)
  between operations  15.8 us (2%)
    pallas_call x6, Pallas kernels, grad_of(): pl.pallas_call(functools.partial(grad_kernel, len(lhs)), grid_spec=pltpu....  82.7 us
    pallas_call x2, Pallas kernels, back_out_of(): pl.pallas_call(back_out_kernel, grid=(width // tile,), in_specs=[pl.Block...  45.1 us
    ppermute x12, waiting for transfers between devices, step(): self.right.append(lax.ppermute(to_left, self.axis, pairs))  44.2 us
    pallas_call x2, Pallas kernels, hidden_of(): pl.pallas_call(hidden_kernel, grid=(n_ff // tile,), in_specs=[resident(tw...  39.6 us
    pallas_call x2, Pallas kernels, norm_qkv(): pl.pallas_call(functools.partial(norm_qkv_kernel, len(blocks)), grid_spec...  38.4 us
    pallas_call x2, Pallas kernels, back_in_of(): pl.pallas_call(back_in_kernel, grid=(n_ff // tile,), in_specs=[resident(g...  34 us
    pallas_call x2, Pallas kernels, branch_of(): pl.pallas_call(branch_kernel, grid=(width // tile,), in_specs=[resident(m...  32.2 us
    ppermute x12, starting transfers between devices, step(): self.left.append(lax.ppermute(to_right, self.axis, pairs))  31.4 us
  transfers between devices with their start and end apart: 63, of which 20 were waited for; matrix products, arithmetic and copies ran while one was open for 7% of the time, Pallas kernels for 46%

profile of v6, /device:TPU:0, one launch (start us, length us, event | category | flops | bytes accessed | tf_op | source)
XLA Modules:
  0.0 718.6 jit_solution(9463778496610120684)
XLA Ops:
  7.2 3.1 slice_bitcast_fusion.2
  10.4 5.3 all-to-all-start
  16.9 2.9 pad_maximum_fusion.3
  19.9 11.2 %all-to-all-done = bf16[8,32,2048]{2,1,0:T(8,128)(2,1)S(1)} async-done(((bf16[8,32,2048]{2,1,0:T(8,128)(2,1)}), bf16[8,32,2048]{2,1,0:T(8,128)(2,1)S(1)}, u32[]{:S(2)}, u32[]{:S(2)}) %all-to-all-start) | async-done | bytes 1048608 | tf_op jit(solution)/shard_map/all_to_all | solution.py:607
  31.1 4.6 collective-permute-start.7
  48.1 6.2 collective-permute-done.7.refs_1_
  54.4 5.2 collective-permute-done.8.refs_4_
  62.6 4.9 all-to-all-start.1
  67.6 4.1 collective-permute-start.9
  71.7 2.5 collective-permute-start.10
  74.2 2.8 collective-permute-start.11
  77.1 10.2 %collective-permute-done.10 = bf16[3072]{0:T(1024)(128)(2,1)S(1)} collective-permute-done((bf16[3072]{0:T(1024)(128)(2,1)S(1)}, bf16[3072]{0:T(1024)(128)(2,1)S(1)}, u32[]{:S(2)}, u32[]{:S(2)}) %collective-permute-start.10) | collective-permute-done | bytes 6176 | tf_op jit(solution)/shard_map/ppermute | solution.py:56
  92.3 24.2 %all-to-all-done.1 = bf16[2,8,32,2048]{3,2,0,1:T(8,128)(2,1)S(1)} async-done(((bf16[2,8,32,2048]{3,2,0,1:T(8,128)(2,1)}), bf16[2,8,32,2048]{3,2,0,1:T(8,128)(2,1)S(1)}, u32[]{:S(2)}, u32[]{:S(2)}) %all-to-all-start.1) | async-done | bytes 2097184 | tf_op jit(solution)/shard_map/all_to_all | solution.py:707
  120.1 7.4 %collective-permute-start.16 = (bf16[256,2048]{1,0:T(8,128)(2,1)S(1)}, bf16[256,2048]{1,0:T(8,128)(2,1)}, u32[]{:S(2)}, u32[]{:S(2)}) collective-permute-start(bf16[256,2048]{1,0:T(8,128)(2,1)S(1)} %bitcast.142), channel_id=1, source_target_pairs={{0,1},{1,2},{2,3},{4,5},{5,6},{6,7},{8,9},{9,10},{10,11},{12,13},{... | collective-permute-start | bytes 3145736 | tf_op jit(solution)/shard_map/ppermute | solution.py:39
  128.8 5.5 collective-permute-start.18
  139.0 3.0 fusion.20
  142.0 19.2 %norm_qkv.2 = (bf16[4,256,2048]{2,1,0:T(8,128)(2,1)}, bf16[4,256,2048]{2,1,0:T(8,128)(2,1)}, bf16[4,256,2048]{2,1,0:T(8,128)(2,1)}, f32[4,256,1536]{2,1,0:T(8,128)}) custom-call(s32[2]{0:T(128)} %pad_add_fusion.2.me_ref, f32[6,2048]{1,0:T(8,128)} %reshape.583.vectors_ref, f32[1,3584]{1,0:T(1,128)} %pad_maximum_fusion.5.bias_ref, ...), custom_call_target="tpu_custom_call" | custom-call | flops 1572864 | bytes 6656 | tf_op jit(solution)/shard_map/norm_qkv/pallas_call | solution.py:302
  161.2 19.8 %hidden.2 = (bf16[1024,2048]{1,0:T(8,128)(2,1)}, bf16[1024,2048]{1,0:T(8,128)(2,1)}) custom-call(bf16[1024,2048]{1,0:T(8,128)(2,1)} %bitcast.121, bf16[2048,3584]{1,0:T(8,128)(2,1)} %all-gather.5.cloned.1.call-done.refs_7_.w_ref, f32[1,3584]{1,0:T(1,128)} %pad_maximum_fusion.5.bias_ref), custom_call_target="tpu_custom_call" | custom-call | flops 2097152 | bytes 6144 | tf_op jit(solution)/shard_map/hidden/pallas_call | solution.py:328
  187.2 3.6 all-to-all-start.2
  192.6 8.8 %attend.2 = (bf16[4,256,1536]{2,1,0:T(8,128)(2,1)S(1)}, bf16[4,256,512]{2,1,0:T(8,128)(2,1)S(1)}) custom-call(s32[4,256,1]{2,1,0:T(8,128)S(1)} %multiply_add_fusion.posq_ref, s32[4,1,1024]{2,1,0:T(1,128)S(1)} %pad_add_fusion.posk_ref, f32[4,256,128]{2,1,0:T(8,128)S(1)} %maximum_maximum_fusion.cos_ref, f32[4,256,128]{2,1,0:T(8,128)S(1)} %maximum_maximum_fusion.1.sin_ref, ...), custom_call_target="tpu_custom_call" | custom-call | flops 1073741824 | bytes 12582912 | tf_op jit(solution)/shard_map/attend/pallas_call | solution.py:171
  204.0 12.6 %all-to-all-done.2 = bf16[8,32,2048]{2,1,0:T(8,128)(2,1)S(1)} async-done(((bf16[8,32,2048]{2,1,0:T(8,128)(2,1)}), bf16[8,32,2048]{2,1,0:T(8,128)(2,1)S(1)}, u32[]{:S(2)}, u32[]{:S(2)}) %all-to-all-start.2) | async-done | bytes 1048608 | tf_op jit(solution)/shard_map/all_to_all | solution.py:607
  216.6 14.4 %collective-permute-done.23.refs_5_ = bf16[256,2048]{1,0:T(8,128)(2,1)} collective-permute-done((bf16[256,2048]{1,0:T(8,128)(2,1)}, bf16[256,2048]{1,0:T(8,128)(2,1)}, u32[]{:S(2)}, u32[]{:S(2)}) %collective-permute-start.23) | collective-permute-done | bytes 1048608 | tf_op jit(solution)/shard_map/ppermute | solution.py:41
  237.1 16.1 %branch.2.refs_0_ = bf16[4,2,256,2048]{3,2,1,0:T(8,128)(2,1)} custom-call(bf16[1024,512]{1,0:T(8,128)(2,1)} %bitcast.106, bf16[1024,2048]{1,0:T(8,128)(2,1)} %get-tuple-element.460.act_ref.refs_2_, bf16[8,2,32,2048]{3,2,1,0:T(8,128)(2,1)} %bitcast.134, bf16[2048,2048]{1,0:T(8,128)(2,1)} %all-gather.7.cloned.1.call-done.w_ref), custom_call_target="tpu_custom_call" | custom-call | flops 2621440 | bytes 5120 | tf_op jit(solution)/shard_map/branch/pallas_call | solution.py:408
  253.2 7.8 %collective-permute-done.25.refs_6_ = bf16[256,2048]{1,0:T(8,128)(2,1)} collective-permute-done((bf16[256,2048]{1,0:T(8,128)(2,1)}, bf16[256,2048]{1,0:T(8,128)(2,1)}, u32[]{:S(2)}, u32[]{:S(2)}) %collective-permute-start.25) | collective-permute-done | bytes 1048608 | tf_op jit(solution)/shard_map/ppermute | solution.py:41
  261.0 16.3 %collective-permute-done.27.refs_6_ = bf16[256,2048]{1,0:T(8,128)(2,1)} collective-permute-done((bf16[256,2048]{1,0:T(8,128)(2,1)}, bf16[256,2048]{1,0:T(8,128)(2,1)}, u32[]{:S(2)}, u32[]{:S(2)}) %collective-permute-start.27) | collective-permute-done | bytes 1048608 | tf_op jit(solution)/shard_map/ppermute | solution.py:41
  277.4 2.4 collective-permute-start.28
  281.1 19.2 %norm_qkv.3 = (bf16[4,256,2048]{2,1,0:T(8,128)(2,1)}, bf16[4,256,2048]{2,1,0:T(8,128)(2,1)}, bf16[4,256,2048]{2,1,0:T(8,128)(2,1)}, f32[4,256,1536]{2,1,0:T(8,128)}) custom-call(s32[2]{0:T(128)} %pad_add_fusion.2.me_ref, f32[6,2048]{1,0:T(8,128)} %reshape.583.vectors_ref, f32[1,3584]{1,0:T(1,128)} %pad_maximum_fusion.5.bias_ref, ...), custom_call_target="tpu_custom_call" | custom-call | flops 1572864 | bytes 6656 | tf_op jit(solution)/shard_map/norm_qkv/pallas_call | solution.py:302
  302.9 19.8 %hidden.3 = (bf16[1024,2048]{1,0:T(8,128)(2,1)}, bf16[1024,2048]{1,0:T(8,128)(2,1)}) custom-call(bf16[1024,2048]{1,0:T(8,128)(2,1)} %bitcast.124, bf16[2048,3584]{1,0:T(8,128)(2,1)} %all-gather.5.cloned.1.call-done.refs_7_.w_ref, f32[1,3584]{1,0:T(1,128)} %pad_maximum_fusion.5.bias_ref), custom_call_target="tpu_custom_call" | custom-call | flops 2097152 | bytes 6144 | tf_op jit(solution)/shard_map/hidden/pallas_call | solution.py:328
  322.7 7.8 %attend.3 = (bf16[4,256,1536]{2,1,0:T(8,128)(2,1)S(1)}, bf16[4,256,512]{2,1,0:T(8,128)(2,1)S(1)}) custom-call(s32[4,256,1]{2,1,0:T(8,128)S(1)} %multiply_add_fusion.posq_ref, s32[4,1,1024]{2,1,0:T(1,128)S(1)} %pad_add_fusion.1.posk_ref, f32[4,256,128]{2,1,0:T(8,128)S(1)} %maximum_maximum_fusion.cos_ref, f32[4,256,128]{2,1,0:T(8,128)S(1)} %maximum_maximum_fusion.1.sin_ref, ...), custom_call_target="tpu_custom_call" | custom-call | flops 1073741824 | bytes 12582912 | tf_op jit(solution)/shard_map/attend/pallas_call | solution.py:171
  335.7 6.1 arrange.2
  341.8 16.1 %branch.3 = bf16[4,2,256,2048]{3,2,1,0:T(8,128)(2,1)} custom-call(bf16[1024,512]{1,0:T(8,128)(2,1)} %bitcast.108, bf16[1024,2048]{1,0:T(8,128)(2,1)} %get-tuple-element.466.act_ref.refs_3_, bf16[8,2,32,2048]{3,2,1,0:T(8,128)(2,1)} %bitcast.135, bf16[2048,2048]{1,0:T(8,128)(2,1)} %all-gather.7.cloned.1.call-done.w_ref, ...), custom_call_target="tpu_custom_call", output_to_operand_aliasing={{}: (4, {})} | custom-call | flops 2621440 | bytes 5120 | tf_op jit(solution)/shard_map/branch/pallas_call | solution.py:408
  360.0 6.1 arrange.3
  366.1 14.4 %grad_w2_sent.1 = bf16[4,256,2048]{2,1,0:T(8,128)(2,1)} custom-call(s32[1]{0:T(128)S(6)} %sub.109.me_ref, bf16[1024,2048]{1,0:T(8,128)(2,1)} %bitcast.112, bf16[1024,2048]{1,0:T(8,128)(2,1)} %bitcast.116, bf16[1024,2048]{1,0:T(8,128)(2,1)} %get-tuple-element.460.act_ref.refs_2_, bf16[1024,2048]{1,0:T(8,128)(2,1)} %get-tuple-element.466.act_ref.refs_3_), custom_call_target="tpu_custom_call" | custom-call | flops 2097152 | bytes 6144 | tf_op jit(solution)/shard_map/grad_w2_sent/pallas_call | solution.py:520
  380.4 17.0 %back_in.2 = (bf16[1024,512]{1,0:T(8,128)(2,1)}, bf16[1024,2048]{1,0:T(8,128)(2,1)}, f32[1,2048]{1,0:T(1,128)}) custom-call(bf16[1024,2048]{1,0:T(8,128)(2,1)} %bitcast.113, bf16[8,2,32,2048]{3,2,1,0:T(8,128)(2,1)} %bitcast.136, bf16[2048,2048]{1,0:T(8,128)(2,1)} %all-gather.7.cloned.1.call-done.w_ref, bf16[1024,2048]{1,0:T(8,128)(2,1)} %get-tuple-element.452.slope_ref), custom_call_target="tpu_custom_call" | custom-call | flops 2621440 | bytes 5120 | tf_op jit(solution)/shard_map/back_in/pallas_call | solution.py:444
  399.4 14.9 %grad_w2_kept.1 = bf16[4,256,2048]{2,1,0:T(8,128)(2,1)} custom-call(s32[1]{0:T(128)} %bitcast.37.me_ref, bf16[1024,2048]{1,0:T(8,128)(2,1)} %bitcast.114, bf16[1024,2048]{1,0:T(8,128)(2,1)} %bitcast.117, bf16[1024,2048]{1,0:T(8,128)(2,1)} %get-tuple-element.460.act_ref.refs_2_, bf16[1024,2048]{1,0:T(8,128)(2,1)} %get-tuple-element.466.act_ref.refs_3_, ...), custom_call_target="tpu_custom_call" | custom-call | flops 2097152 | bytes 6144 | tf_op jit(solution)/shard_map/grad_w2_kept/pallas_call | solution.py:520
  414.3 8.1 %all-to-all-start.3 = ((bf16[4,256,2048]{2,1,0:T(8,128)(2,1)}), bf16[4,256,2048]{2,1,0:T(8,128)(2,1)}, u32[]{:S(2)}, u32[]{:S(2)}) async-start(bf16[4,256,2048]{2,1,0:T(8,128)(2,1)} %grad_w2_kept.1), calls=%async_computation.3 | async-start | bytes 8388608 | tf_op jit(solution)/shard_map/all_to_all | solution.py:868
  422.6 9.7 %grad_dense.1 = (bf16[4,2,32,2048]{3,2,1,0:T(8,128)(2,1)}, bf16[4,2,32,2048]{3,2,1,0:T(8,128)(2,1)}) custom-call(s32[1]{0:T(128)} %bitcast.37.me_ref, bf16[1024,512]{1,0:T(8,128)(2,1)} %bitcast.107, bf16[1024,512]{1,0:T(8,128)(2,1)} %bitcast.109, bf16[1024,2048]{1,0:T(8,128)(2,1)} %bitcast.115, bf16[1024,2048]{1,0:T(8,128)(2,1)} %bitcast.118), custom_call_target="tpu_custom_call" | custom-call | flops 1048576 | bytes 3072 | tf_op jit(solution)/shard_map/grad_dense/pallas_call | solution.py:556
  432.3 17.0 %back_in.3 = (bf16[1024,512]{1,0:T(8,128)(2,1)}, bf16[1024,2048]{1,0:T(8,128)(2,1)}, f32[1,2048]{1,0:T(1,128)}) custom-call(bf16[1024,2048]{1,0:T(8,128)(2,1)} %bitcast.119, bf16[8,2,32,2048]{3,2,1,0:T(8,128)(2,1)} %bitcast.137, bf16[2048,2048]{1,0:T(8,128)(2,1)} %all-gather.7.cloned.1.call-done.w_ref, bf16[1024,2048]{1,0:T(8,128)(2,1)} %get-tuple-element.496.slope_ref), custom_call_target="tpu_custom_call" | custom-call | flops 2621440 | bytes 5120 | tf_op jit(solution)/shard_map/back_in/pallas_call | solution.py:444
  449.4 9.7 %attend_back.2 = (bf16[4,256,1536]{2,1,0:T(8,128)(2,1)S(1)}, f32[2,1,768]{2,1,0:T(1,128)S(1)}) custom-call(s32[4,256,1]{2,1,0:T(8,128)S(1)} %multiply_add_fusion.posq_ref, s32[4,1,1024]{2,1,0:T(1,128)S(1)} %pad_add_fusion.posk_ref, f32[4,256,128]{2,1,0:T(8,128)S(1)} %maximum_maximum_fusion.cos_ref, f32[4,256,128]{2,1,0:T(8,128)S(1)} %maximum_maximum_fusion.1.sin_ref, ...), custom_call_target="tpu_custom_call" | custom-call | flops 2684354560 | bytes 7864320 | tf_op jit(solution)/shard_map/attend_back/pallas_call | solution.py:192
  460.7 22.5 %back_out.2 = (bf16[1024,2048]{1,0:T(8,128)(2,1)}, f32[4,2048]{1,0:T(4,128)}) custom-call(f32[6,2048]{1,0:T(8,128)} %reshape.583.vectors_ref, bf16[1024,1536]{1,0:T(8,128)(2,1)} %bitcast.100, bf16[1024,2048]{1,0:T(8,128)(2,1)} %get-tuple-element.529.pre_ref.refs_2_, bf16[2048,3584]{1,0:T(8,128)(2,1)} %all-gather.5.cloned.1.call-done.refs_7_.w_ref, ...), custom_call_target="tpu_custom_call" | custom-call | flops 3670016 | bytes 7680 | tf_op jit(solution)/shard_map/back_out/pallas_call | solution.py:485
  483.2 14.4 %grad_w1_sent.1 = bf16[4,256,2048]{2,1,0:T(8,128)(2,1)} custom-call(s32[1]{0:T(128)S(6)} %sub.109.me_ref, bf16[1024,2048]{1,0:T(8,128)(2,1)} %bitcast.122, bf16[1024,2048]{1,0:T(8,128)(2,1)} %bitcast.125, bf16[1024,2048]{1,0:T(8,128)(2,1)} %get-tuple-element.529.pre_ref.refs_2_, bf16[1024,2048]{1,0:T(8,128)(2,1)} %get-tuple-element.549.refs_3_.pre_ref), custom_call_target="tpu_custom_call" | custom-call | flops 2097152 | bytes 6144 | tf_op jit(solution)/shard_map/grad_w1_sent/pallas_call | solution.py:520
  498.9 9.9 %attend_back.3 = (bf16[4,256,1536]{2,1,0:T(8,128)(2,1)S(1)}, f32[2,1,768]{2,1,0:T(1,128)S(1)}) custom-call(s32[4,256,1]{2,1,0:T(8,128)S(1)} %multiply_add_fusion.posq_ref, s32[4,1,1024]{2,1,0:T(1,128)S(1)} %pad_add_fusion.1.posk_ref, f32[4,256,128]{2,1,0:T(8,128)S(1)} %maximum_maximum_fusion.cos_ref, f32[4,256,128]{2,1,0:T(8,128)S(1)} %maximum_maximum_fusion.1.sin_ref, ...), custom_call_target="tpu_custom_call" | custom-call | flops 2684354560 | bytes 7864320 | tf_op jit(solution)/shard_map/attend_back/pallas_call | solution.py:192
  511.8 5.1 all-to-all-start.4
  516.9 15.6 %grad_w1_kept.1 = bf16[4,256,2048]{2,1,0:T(8,128)(2,1)} custom-call(s32[1]{0:T(128)} %bitcast.37.me_ref, bf16[1024,2048]{1,0:T(8,128)(2,1)} %bitcast.123, bf16[1024,2048]{1,0:T(8,128)(2,1)} %bitcast.126, bf16[1024,2048]{1,0:T(8,128)(2,1)} %get-tuple-element.529.pre_ref.refs_2_, bf16[1024,2048]{1,0:T(8,128)(2,1)} %get-tuple-element.549.refs_3_.pre_ref, ...), custom_call_target="tpu_custom_call" | custom-call | flops 2097152 | bytes 6144 | tf_op jit(solution)/shard_map/grad_w1_kept/pallas_call | solution.py:520
  533.4 4.9 all-to-all-start.5
  538.3 11.6 %grad_wq_sent.1 = bf16[4,256,1536]{2,1,0:T(8,128)(2,1)} custom-call(s32[1]{0:T(128)S(6)} %sub.109.me_ref, bf16[1024,2048]{1,0:T(8,128)(2,1)} %bitcast.138, bf16[1024,2048]{1,0:T(8,128)(2,1)} %bitcast.140, bf16[1024,1536]{1,0:T(8,128)(2,1)} %bitcast.101, bf16[1024,1536]{1,0:T(8,128)(2,1)} %bitcast.103), custom_call_target="tpu_custom_call" | custom-call | flops 1572864 | bytes 5120 | tf_op jit(solution)/shard_map/grad_wq_sent/pallas_call | solution.py:520
  549.9 22.6 %back_out.3 = (bf16[1024,2048]{1,0:T(8,128)(2,1)}, f32[4,2048]{1,0:T(4,128)}) custom-call(f32[6,2048]{1,0:T(8,128)} %reshape.583.vectors_ref, bf16[1024,1536]{1,0:T(8,128)(2,1)} %bitcast.104, bf16[1024,2048]{1,0:T(8,128)(2,1)} %get-tuple-element.549.refs_3_.pre_ref, bf16[2048,3584]{1,0:T(8,128)(2,1)} %all-gather.5.cloned.1.call-done.refs_7_.w_ref, ...), custom_call_target="tpu_custom_call" | custom-call | flops 3670016 | bytes 7680 | tf_op jit(solution)/shard_map/back_out/pallas_call | solution.py:485
  572.5 14.1 %all-to-all-done.5 = bf16[4,256,2048]{2,1,0:T(8,128)(2,1)} async-done(((bf16[4,256,2048]{2,1,0:T(8,128)(2,1)}), bf16[4,256,2048]{2,1,0:T(8,128)(2,1)}, u32[]{:S(2)}, u32[]{:S(2)}) %all-to-all-start.5) | async-done | bytes 4194336 | tf_op jit(solution)/shard_map/all_to_all | solution.py:868
  592.5 3.9 all-to-all-start.6
  596.4 4.8 convert_reduce_fusion.1
  601.2 11.9 %grad_wq_kept.1 = bf16[4,256,1536]{2,1,0:T(8,128)(2,1)} custom-call(s32[1]{0:T(128)} %bitcast.37.me_ref, bf16[1024,2048]{1,0:T(8,128)(2,1)} %bitcast.139, bf16[1024,2048]{1,0:T(8,128)(2,1)} %bitcast.141, bf16[1024,1536]{1,0:T(8,128)(2,1)} %bitcast.102, bf16[1024,1536]{1,0:T(8,128)(2,1)} %bitcast.105, bf16[4,256,1536]{2,1,0:T(8,128)(2,1)} %collective-permute-done.37.refs_4_), custom_call_target="tpu_custom_call" | custom-call | flops 1572864 | bytes 5120 | tf_op jit(solution)/shard_map/grad_wq_kept/pallas_call | solution.py:520
  613.1 9.9 %all-to-all-done.6 = bf16[2,8,32,2048]{3,2,0,1:T(8,128)(2,1)S(1)} async-done(((bf16[2,8,32,2048]{3,2,0,1:T(8,128)(2,1)}), bf16[2,8,32,2048]{3,2,0,1:T(8,128)(2,1)S(1)}, u32[]{:S(2)}, u32[]{:S(2)}) %all-to-all-start.6) | async-done | bytes 2097184 | tf_op jit(solution)/shard_map/all_to_all | solution.py:611
  624.3 4.8 all-to-all-start.7
  632.8 4.5 convert_reduce_fusion
  637.3 2.3 collective-permute-start.40
  640.3 21.0 %collective-permute-done.38 = f32[1728]{0:T(1024)S(1)} collective-permute-done((f32[1728]{0:T(1024)S(1)}, f32[1728]{0:T(1024)S(1)}, u32[]{:S(2)}, u32[]{:S(2)}) %collective-permute-start.38) | collective-permute-done | bytes 6944 | tf_op jit(solution)/shard_map/ppermute | solution.py:949
  661.3 3.5 collective-permute-done.39
  666.1 3.2 reduce-scatter.8.cloned.1.call-done
  676.7 4.3 all-to-all-start.8
  684.4 2.7 collective-permute-start.47
  687.1 2.5 convert_reduce_fusion.2
  693.1 3.3 copy.60
  698.8 8.9 %all-to-all-done.8 = bf16[2,8,32,2048]{3,2,0,1:T(8,128)(2,1)} async-done(((bf16[2,8,32,2048]{3,2,0,1:T(8,128)(2,1)}), bf16[2,8,32,2048]{3,2,0,1:T(8,128)(2,1)}, u32[]{:S(2)}, u32[]{:S(2)}) %all-to-all-start.8) | async-done | bytes 2097184 | tf_op jit(solution)/shard_map/all_to_all | solution.py:611
  707.7 3.2 copy.61
  (313 shorter events, 97.3 us)
Async XLA Ops:
  10.4 20.7 %all-to-all-start = ((bf16[8,32,2048]{2,1,0:T(8,128)(2,1)}), bf16[8,32,2048]{2,1,0:T(8,128)(2,1)S(1)}, u32[]{:S(2)}, u32[]{:S(2)}) async-start(bf16[8,32,2048]{2,1,0:T(8,128)(2,1)} %get-tuple-element.669), calls=%async_computation | async-start | bytes 2097152 | tf_op jit(solution)/shard_map/all_to_all | solution.py:607
  15.7 126.3 %all-gather.5.cloned.1.call-start = ((), (), s32[]{:S(2)}) async-start(), calls=%async_computation.12 | async-start | bytes 16515072 | tf_op jit(solution)/shard_map/all_gather | solution.py:646
  31.1 23.2 %collective-permute-start.7 = (bf16[256,2048]{1,0:T(8,128)(2,1)S(1)}, bf16[256,2048]{1,0:T(8,128)(2,1)}, u32[]{:S(2)}, u32[]{:S(2)}) collective-permute-start(bf16[256,2048]{1,0:T(8,128)(2,1)S(1)} %bitcast.127), channel_id=1, source_target_pairs={{0,1},{1,2},{2,3},{4,5},{5,6},{6,7},{8,9},{9,10},{10,11},{12,13},{... | collective-permute-start | bytes 3145736 | tf_op jit(solution)/shard_map/ppermute | solution.py:39
  35.8 23.8 %collective-permute-start.8 = (bf16[256,2048]{1,0:T(8,128)(2,1)S(1)}, bf16[256,2048]{1,0:T(8,128)(2,1)}, u32[]{:S(2)}, u32[]{:S(2)}) collective-permute-start(bf16[256,2048]{1,0:T(8,128)(2,1)S(1)} %bitcast.128), channel_id=1, source_target_pairs={{1,0},{2,1},{3,2},{5,4},{6,5},{7,6},{9,8},{10,9},{11,10},{13,12},{... | collective-permute-start | bytes 3145736 | tf_op jit(solution)/shard_map/ppermute | solution.py:41
  38.2 3.9 collective-permute-start
  38.2 4.6 collective-permute-start.1
  38.7 4.1 collective-permute-start.2
  42.1 3.6 collective-permute-start.3
  42.8 5.0 collective-permute-start.4
  42.8 5.1 collective-permute-start.5
  45.7 2.2 collective-permute-start.6
  59.6 28.0 %collective-permute-start.12 = (bf16[256,2048]{1,0:T(8,128)(2,1)}, bf16[256,2048]{1,0:T(8,128)(2,1)}, u32[]{:S(2)}, u32[]{:S(2)}) collective-permute-start(bf16[256,2048]{1,0:T(8,128)(2,1)} %collective-permute-done.7.refs_1_), channel_id=1, source_target_pairs={{1,2},{2,3},{5,6},{6,7},{9,10},{10,11},{13,14},{14,15},{17,18},{18... | collective-permute-start | bytes 3145736 | tf_op jit(solution)/shard_map/ppermute | solution.py:39
  61.3 26.3 %collective-permute-start.13 = (bf16[256,2048]{1,0:T(8,128)(2,1)}, bf16[256,2048]{1,0:T(8,128)(2,1)}, u32[]{:S(2)}, u32[]{:S(2)}) collective-permute-start(bf16[256,2048]{1,0:T(8,128)(2,1)} %collective-permute-done.8.refs_4_), channel_id=1, source_target_pairs={{1,0},{2,1},{5,4},{6,5},{9,8},{10,9},{13,12},{14,13},{17,16},{18,1... | collective-permute-start | bytes 3145736 | tf_op jit(solution)/shard_map/ppermute | solution.py:41
  62.6 54.0 %all-to-all-start.1 = ((bf16[2,8,32,2048]{3,2,0,1:T(8,128)(2,1)}), bf16[2,8,32,2048]{3,2,0,1:T(8,128)(2,1)S(1)}, u32[]{:S(2)}, u32[]{:S(2)}) async-start(bf16[2,8,32,2048]{3,2,0,1:T(8,128)(2,1)} %pad_maximum_fusion), calls=%async_computation.1 | async-start | bytes 4194304 | tf_op jit(solution)/shard_map/all_to_all | solution.py:707
  67.5 169.5 %all-gather.9.cloned.1.call-start = ((), (), s32[]{:S(2)}) async-start(), calls=%async_computation.17 | async-start | bytes 2359296 | tf_op jit(solution)/shard_map/all_gather | solution.py:722
  67.6 9.4 %collective-permute-start.9 = (bf16[3072]{0:T(1024)(128)(2,1)S(1)}, bf16[3072]{0:T(1024)(128)(2,1)S(1)}, u32[]{:S(2)}, u32[]{:S(2)}) collective-permute-start(bf16[3072]{0:T(1024)(128)(2,1)S(1)} %reshape.544), channel_id=1, source_target_pairs={{0,1},{1,2},{2,3},{3,0},{4,5},{5,6},{6,7},{7,4},{8,9},{9,10},{10,1... | collective-permute-start | bytes 18440 | tf_op jit(solution)/shard_map/ppermute | solution.py:56
  71.7 15.6 %collective-permute-start.10 = (bf16[3072]{0:T(1024)(128)(2,1)S(1)}, bf16[3072]{0:T(1024)(128)(2,1)S(1)}, u32[]{:S(2)}, u32[]{:S(2)}) collective-permute-start(bf16[3072]{0:T(1024)(128)(2,1)S(1)} %reshape.544), channel_id=1, source_target_pairs={{0,2},{1,3},{2,0},{3,1},{4,6},{5,7},{6,4},{7,5},{8,10},{9,11},{10,... | collective-permute-start | bytes 18440 | tf_op jit(solution)/shard_map/ppermute | solution.py:56
  74.2 13.1 %collective-permute-start.11 = (bf16[3072]{0:T(1024)(128)(2,1)S(1)}, bf16[3072]{0:T(1024)(128)(2,1)S(1)}, u32[]{:S(2)}, u32[]{:S(2)}) collective-permute-start(bf16[3072]{0:T(1024)(128)(2,1)S(1)} %reshape.544), channel_id=1, source_target_pairs={{0,3},{1,0},{2,1},{3,2},{4,7},{5,4},{6,5},{7,6},{8,11},{9,8},{10,9... | collective-permute-start | bytes 18440 | tf_op jit(solution)/shard_map/ppermute | solution.py:56
  87.6 28.9 %collective-permute-start.14 = (bf16[256,2048]{1,0:T(8,128)(2,1)}, bf16[256,2048]{1,0:T(8,128)(2,1)}, u32[]{:S(2)}, u32[]{:S(2)}) collective-permute-start(bf16[256,2048]{1,0:T(8,128)(2,1)} %collective-permute-done.12.refs_2_), channel_id=1, source_target_pairs={{2,3},{6,7},{10,11},{14,15},{18,19},{22,23},{26,27},{30,31}} | collective-permute-start | bytes 3145736 | tf_op jit(solution)/shard_map/ppermute | solution.py:39
  89.3 27.3 %collective-permute-start.15 = (bf16[256,2048]{1,0:T(8,128)(2,1)}, bf16[256,2048]{1,0:T(8,128)(2,1)}, u32[]{:S(2)}, u32[]{:S(2)}) collective-permute-start(bf16[256,2048]{1,0:T(8,128)(2,1)} %collective-permute-done.13.refs_5_), channel_id=1, source_target_pairs={{1,0},{5,4},{9,8},{13,12},{17,16},{21,20},{25,24},{29,28}} | collective-permute-start | bytes 3145736 | tf_op jit(solution)/shard_map/ppermute | solution.py:41
  116.6 120.5 %all-gather.7.cloned.1.call-start = ((), (), s32[]{:S(2)}) async-start(), calls=%async_computation.13 | async-start | bytes 9437184 | tf_op jit(solution)/shard_map/all_gather | solution.py:721
  120.1 60.9 %collective-permute-start.16 = (bf16[256,2048]{1,0:T(8,128)(2,1)S(1)}, bf16[256,2048]{1,0:T(8,128)(2,1)}, u32[]{:S(2)}, u32[]{:S(2)}) collective-permute-start(bf16[256,2048]{1,0:T(8,128)(2,1)S(1)} %bitcast.142), channel_id=1, source_target_pairs={{0,1},{1,2},{2,3},{4,5},{5,6},{6,7},{8,9},{9,10},{10,11},{12,13},{... | collective-permute-start | bytes 3145736 | tf_op jit(solution)/shard_map/ppermute | solution.py:39
  127.5 53.5 %collective-permute-start.17 = (bf16[256,2048]{1,0:T(8,128)(2,1)S(1)}, bf16[256,2048]{1,0:T(8,128)(2,1)}, u32[]{:S(2)}, u32[]{:S(2)}) collective-permute-start(bf16[256,2048]{1,0:T(8,128)(2,1)S(1)} %bitcast.143), channel_id=1, source_target_pairs={{1,0},{2,1},{3,2},{5,4},{6,5},{7,6},{9,8},{10,9},{11,10},{13,12},{... | collective-permute-start | bytes 3145736 | tf_op jit(solution)/shard_map/ppermute | solution.py:41
  128.8 52.3 %collective-permute-start.18 = (bf16[256,2048]{1,0:T(8,128)(2,1)}, bf16[256,2048]{1,0:T(8,128)(2,1)}, u32[]{:S(2)}, u32[]{:S(2)}) collective-permute-start(bf16[256,2048]{1,0:T(8,128)(2,1)} %bitcast.15.refs_0_), channel_id=1, source_target_pairs={{0,1},{1,2},{2,3},{4,5},{5,6},{6,7},{8,9},{9,10},{10,11},{12,13},{... | collective-permute-start | bytes 3145736 | tf_op jit(solution)/shard_map/ppermute | solution.py:39
  134.3 46.7 %collective-permute-start.19 = (bf16[256,2048]{1,0:T(8,128)(2,1)}, bf16[256,2048]{1,0:T(8,128)(2,1)}, u32[]{:S(2)}, u32[]{:S(2)}) collective-permute-start(bf16[256,2048]{1,0:T(8,128)(2,1)} %bitcast.15.refs_0_), channel_id=1, source_target_pairs={{1,0},{2,1},{3,2},{5,4},{6,5},{7,6},{9,8},{10,9},{11,10},{13,12},{... | collective-permute-start | bytes 3145736 | tf_op jit(solution)/shard_map/ppermute | solution.py:41
  181.1 35.6 %collective-permute-start.20 = (bf16[256,2048]{1,0:T(8,128)(2,1)}, bf16[256,2048]{1,0:T(8,128)(2,1)}, u32[]{:S(2)}, u32[]{:S(2)}) collective-permute-start(bf16[256,2048]{1,0:T(8,128)(2,1)} %collective-permute-done.16.refs_1_), channel_id=1, source_target_pairs={{1,2},{2,3},{5,6},{6,7},{9,10},{10,11},{13,14},{14,15},{17,18},{18... | collective-permute-start | bytes 3145736 | tf_op jit(solution)/shard_map/ppermute | solution.py:39
  182.7 33.9 %collective-permute-start.21 = (bf16[256,2048]{1,0:T(8,128)(2,1)}, bf16[256,2048]{1,0:T(8,128)(2,1)}, u32[]{:S(2)}, u32[]{:S(2)}) collective-permute-start(bf16[256,2048]{1,0:T(8,128)(2,1)} %collective-permute-done.17.refs_4_), channel_id=1, source_target_pairs={{1,0},{2,1},{5,4},{6,5},{9,8},{10,9},{13,12},{14,13},{17,16},{18,1... | collective-permute-start | bytes 3145736 | tf_op jit(solution)/shard_map/ppermute | solution.py:41
  184.0 32.6 %collective-permute-start.22 = (bf16[256,2048]{1,0:T(8,128)(2,1)}, bf16[256,2048]{1,0:T(8,128)(2,1)}, u32[]{:S(2)}, u32[]{:S(2)}) collective-permute-start(bf16[256,2048]{1,0:T(8,128)(2,1)} %collective-permute-done.18.refs_1_), channel_id=1, source_target_pairs={{1,2},{2,3},{5,6},{6,7},{9,10},{10,11},{13,14},{14,15},{17,18},{18... | collective-permute-start | bytes 3145736 | tf_op jit(solution)/shard_map/ppermute | solution.py:39
  185.7 45.4 %collective-permute-start.23 = (bf16[256,2048]{1,0:T(8,128)(2,1)}, bf16[256,2048]{1,0:T(8,128)(2,1)}, u32[]{:S(2)}, u32[]{:S(2)}) collective-permute-start(bf16[256,2048]{1,0:T(8,128)(2,1)} %collective-permute-done.19.refs_4_), channel_id=1, source_target_pairs={{1,0},{2,1},{5,4},{6,5},{9,8},{10,9},{13,12},{14,13},{17,16},{18,1... | collective-permute-start | bytes 3145736 | tf_op jit(solution)/shard_map/ppermute | solution.py:41
  187.2 29.5 %all-to-all-start.2 = ((bf16[8,32,2048]{2,1,0:T(8,128)(2,1)}), bf16[8,32,2048]{2,1,0:T(8,128)(2,1)S(1)}, u32[]{:S(2)}, u32[]{:S(2)}) async-start(bf16[8,32,2048]{2,1,0:T(8,128)(2,1)} %get-tuple-element.355), calls=%async_computation.2 | async-start | bytes 2097152 | tf_op jit(solution)/shard_map/all_to_all | solution.py:607
  190.7 395.9 %reduce-scatter.4.cloned.1.call-start = ((), (), s32[]{:S(2)}) async-start(), calls=%async_computation.14 | async-start | bytes 10485760 | tf_op jit(solution)/shard_map/reduce_scatter | solution.py:768
  216.6 63.2 %copy-start.14 = (bf16[8,32,2048]{2,1,0:T(8,128)(2,1)}, bf16[8,32,2048]{2,1,0:T(8,128)(2,1)S(1)}, u32[]{:S(2)}) copy-start(bf16[8,32,2048]{2,1,0:T(8,128)(2,1)S(1)} %all-to-all-done.2) | copy-start | bytes 3145732
  231.0 22.1 %collective-permute-start.24 = (bf16[256,2048]{1,0:T(8,128)(2,1)}, bf16[256,2048]{1,0:T(8,128)(2,1)}, u32[]{:S(2)}, u32[]{:S(2)}) collective-permute-start(bf16[256,2048]{1,0:T(8,128)(2,1)} %collective-permute-done.20.refs_2_), channel_id=1, source_target_pairs={{2,3},{6,7},{10,11},{14,15},{18,19},{22,23},{26,27},{30,31}} | collective-permute-start | bytes 3145736 | tf_op jit(solution)/shard_map/ppermute | solution.py:39
  232.7 28.3 %collective-permute-start.25 = (bf16[256,2048]{1,0:T(8,128)(2,1)}, bf16[256,2048]{1,0:T(8,128)(2,1)}, u32[]{:S(2)}, u32[]{:S(2)}) collective-permute-start(bf16[256,2048]{1,0:T(8,128)(2,1)} %collective-permute-done.21.refs_5_), channel_id=1, source_target_pairs={{1,0},{5,4},{9,8},{13,12},{17,16},{21,20},{25,24},{29,28}} | collective-permute-start | bytes 3145736 | tf_op jit(solution)/shard_map/ppermute | solution.py:41
  234.0 27.0 %collective-permute-start.26 = (bf16[256,2048]{1,0:T(8,128)(2,1)}, bf16[256,2048]{1,0:T(8,128)(2,1)}, u32[]{:S(2)}, u32[]{:S(2)}) collective-permute-start(bf16[256,2048]{1,0:T(8,128)(2,1)} %collective-permute-done.22.refs_2_), channel_id=1, source_target_pairs={{2,3},{6,7},{10,11},{14,15},{18,19},{22,23},{26,27},{30,31}} | collective-permute-start | bytes 3145736 | tf_op jit(solution)/shard_map/ppermute | solution.py:39
  235.7 41.6 %collective-permute-start.27 = (bf16[256,2048]{1,0:T(8,128)(2,1)}, bf16[256,2048]{1,0:T(8,128)(2,1)}, u32[]{:S(2)}, u32[]{:S(2)}) collective-permute-start(bf16[256,2048]{1,0:T(8,128)(2,1)} %collective-permute-done.23.refs_5_), channel_id=1, source_target_pairs={{1,0},{5,4},{9,8},{13,12},{17,16},{21,20},{25,24},{29,28}} | collective-permute-start | bytes 3145736 | tf_op jit(solution)/shard_map/ppermute | solution.py:41
  277.4 22.9 %collective-permute-start.28 = (bf16[256,2048]{1,0:T(8,128)(2,1)S(1)}, bf16[256,2048]{1,0:T(8,128)(2,1)}, u32[]{:S(2)}, u32[]{:S(2)}) collective-permute-start(bf16[256,2048]{1,0:T(8,128)(2,1)S(1)} %bitcast.145), channel_id=1, source_target_pairs={{0,1},{1,2},{2,3},{4,5},{5,6},{6,7},{8,9},{9,10},{10,11},{12,13},{... | collective-permute-start | bytes 3145736 | tf_op jit(solution)/shard_map/ppermute | solution.py:39
  279.8 20.9 %collective-permute-start.29 = (bf16[256,2048]{1,0:T(8,128)(2,1)S(1)}, bf16[256,2048]{1,0:T(8,128)(2,1)}, u32[]{:S(2)}, u32[]{:S(2)}) collective-permute-start(bf16[256,2048]{1,0:T(8,128)(2,1)S(1)} %bitcast.146), channel_id=1, source_target_pairs={{1,0},{2,1},{3,2},{5,4},{6,5},{7,6},{9,8},{10,9},{11,10},{13,12},{... | collective-permute-start | bytes 3145736 | tf_op jit(solution)/shard_map/ppermute | solution.py:41
  300.7 32.6 %collective-permute-start.30 = (bf16[256,2048]{1,0:T(8,128)(2,1)}, bf16[256,2048]{1,0:T(8,128)(2,1)S(1)}, u32[]{:S(2)}, u32[]{:S(2)}) collective-permute-start(bf16[256,2048]{1,0:T(8,128)(2,1)} %collective-permute-done.28.refs_1_), channel_id=1, source_target_pairs={{1,2},{2,3},{5,6},{6,7},{9,10},{10,11},{13,14},{14,15},{17,18},{18... | collective-permute-start | bytes 3145736 | tf_op jit(solution)/shard_map/ppermute | solution.py:39
  301.4 31.9 %collective-permute-start.31 = (bf16[256,2048]{1,0:T(8,128)(2,1)}, bf16[256,2048]{1,0:T(8,128)(2,1)}, u32[]{:S(2)}, u32[]{:S(2)}) collective-permute-start(bf16[256,2048]{1,0:T(8,128)(2,1)} %collective-permute-done.29.refs_4_), channel_id=1, source_target_pairs={{1,0},{2,1},{5,4},{6,5},{9,8},{10,9},{13,12},{14,13},{17,16},{18,1... | collective-permute-start | bytes 3145736 | tf_op jit(solution)/shard_map/ppermute | solution.py:41
  333.3 24.7 %collective-permute-start.32 = (bf16[256,2048]{1,0:T(8,128)(2,1)S(1)}, bf16[256,2048]{1,0:T(8,128)(2,1)S(1)}, u32[]{:S(2)}, u32[]{:S(2)}) collective-permute-start(bf16[256,2048]{1,0:T(8,128)(2,1)S(1)} %collective-permute-done.30.refs_2_), channel_id=1, source_target_pairs={{2,3},{6,7},{10,11},{14,15},{18,19},{22,23},{26,27},{30,31}} | collective-permute-start | bytes 3145736 | tf_op jit(solution)/shard_map/ppermute | solution.py:39
  334.0 24.9 %collective-permute-start.33 = (bf16[256,2048]{1,0:T(8,128)(2,1)}, bf16[256,2048]{1,0:T(8,128)(2,1)S(1)}, u32[]{:S(2)}, u32[]{:S(2)}) collective-permute-start(bf16[256,2048]{1,0:T(8,128)(2,1)} %collective-permute-done.31.refs_5_), channel_id=1, source_target_pairs={{1,0},{5,4},{9,8},{13,12},{17,16},{21,20},{25,24},{29,28}} | collective-permute-start | bytes 3145736 | tf_op jit(solution)/shard_map/ppermute | solution.py:41
  380.4 17.0 %collective-permute-start.34 = (bf16[4,256,2048]{2,1,0:T(8,128)(2,1)}, bf16[4,256,2048]{2,1,0:T(8,128)(2,1)S(1)}, u32[]{:S(2)}, u32[]{:S(2)}) collective-permute-start(bf16[4,256,2048]{2,1,0:T(8,128)(2,1)} %grad_w2_sent.1), channel_id=1, source_target_pairs={{0,4},{4,0},{8,12},{12,8},{16,20},{20,16},{24,28},{28,24},{1,5},{5... | collective-permute-start | bytes 12582920 | tf_op jit(solution)/shard_map/ppermute | solution.py:834
  414.3 68.9 %all-to-all-start.3 = ((bf16[4,256,2048]{2,1,0:T(8,128)(2,1)}), bf16[4,256,2048]{2,1,0:T(8,128)(2,1)}, u32[]{:S(2)}, u32[]{:S(2)}) async-start(bf16[4,256,2048]{2,1,0:T(8,128)(2,1)} %grad_w2_kept.1), calls=%async_computation.3 | async-start | bytes 8388608 | tf_op jit(solution)/shard_map/all_to_all | solution.py:868
  422.4 243.3 %reduce-scatter.6.cloned.1.call-start = ((), (), s32[]{:S(2)}) async-start(), calls=%async_computation.15 | async-start | bytes 5242880 | tf_op jit(solution)/shard_map/reduce_scatter | solution.py:768
  497.6 12.8 %collective-permute-start.35 = (bf16[4,256,2048]{2,1,0:T(8,128)(2,1)}, bf16[4,256,2048]{2,1,0:T(8,128)(2,1)}, u32[]{:S(2)}, u32[]{:S(2)}) collective-permute-start(bf16[4,256,2048]{2,1,0:T(8,128)(2,1)} %grad_w1_sent.1), channel_id=1, source_target_pairs={{0,4},{4,0},{8,12},{12,8},{16,20},{20,16},{24,28},{28,24},{1,5},{5... | collective-permute-start | bytes 12582920 | tf_op jit(solution)/shard_map/ppermute | solution.py:834
  497.9 12.5 %collective-permute-start.36 = (bf16[4,64,2048]{2,1,0:T(8,128)(2,1)}, bf16[4,64,2048]{2,1,0:T(8,128)(2,1)S(1)}, u32[]{:S(2)}, u32[]{:S(2)}) collective-permute-start(bf16[4,64,2048]{2,1,0:T(8,128)(2,1)} %bitcast.175), channel_id=1, source_target_pairs={{0,4},{4,0},{8,12},{12,8},{16,20},{20,16},{24,28},{28,24},{1,5},{5... | collective-permute-start | bytes 3145736 | tf_op jit(solution)/shard_map/ppermute | solution.py:859
  511.8 20.6 %all-to-all-start.4 = ((bf16[4,64,2048]{2,1,0:T(8,128)(2,1)}), bf16[4,64,2048]{2,1,0:T(8,128)(2,1)S(1)}, u32[]{:S(2)}, u32[]{:S(2)}) async-start(bf16[4,64,2048]{2,1,0:T(8,128)(2,1)} %add_convert_fusion), calls=%async_computation.4 | async-start | bytes 2097152 | tf_op jit(solution)/shard_map/all_to_all | solution.py:868
  533.4 53.2 %all-to-all-start.5 = ((bf16[4,256,2048]{2,1,0:T(8,128)(2,1)}), bf16[4,256,2048]{2,1,0:T(8,128)(2,1)}, u32[]{:S(2)}, u32[]{:S(2)}) async-start(bf16[4,256,2048]{2,1,0:T(8,128)(2,1)} %grad_w1_kept.1), calls=%async_computation.5 | async-start | bytes 8388608 | tf_op jit(solution)/shard_map/all_to_all | solution.py:868
  538.3 131.0 %reduce-scatter.8.cloned.1.call-start = ((), (), s32[]{:S(2)}) async-start(), calls=%async_computation.16 | async-start | bytes 5242880 | tf_op jit(solution)/shard_map/reduce_scatter | solution.py:768
  588.7 12.5 %collective-permute-start.37 = (bf16[4,256,1536]{2,1,0:T(8,128)(2,1)}, bf16[4,256,1536]{2,1,0:T(8,128)(2,1)}, u32[]{:S(2)}, u32[]{:S(2)}) collective-permute-start(bf16[4,256,1536]{2,1,0:T(8,128)(2,1)} %grad_wq_sent.1), channel_id=1, source_target_pairs={{0,4},{4,0},{8,12},{12,8},{16,20},{20,16},{24,28},{28,24},{1,5},{5... | collective-permute-start | bytes 9437192 | tf_op jit(solution)/shard_map/ppermute | solution.py:859
  592.5 30.4 %all-to-all-start.6 = ((bf16[2,8,32,2048]{3,2,0,1:T(8,128)(2,1)}), bf16[2,8,32,2048]{3,2,0,1:T(8,128)(2,1)S(1)}, u32[]{:S(2)}, u32[]{:S(2)}) async-start(bf16[2,8,32,2048]{3,2,0,1:T(8,128)(2,1)} %pad_maximum_fusion.1), calls=%async_computation.7 | async-start | bytes 4194304 | tf_op jit(solution)/shard_map/all_to_all | solution.py:611
  624.3 41.8 %all-to-all-start.7 = ((bf16[4,256,1536]{2,1,0:T(8,128)(2,1)}), bf16[4,256,1536]{2,1,0:T(8,128)(2,1)}, u32[]{:S(2)}, u32[]{:S(2)}) async-start(bf16[4,256,1536]{2,1,0:T(8,128)(2,1)} %grad_wq_kept.1), calls=%async_computation.8 | async-start | bytes 6291456 | tf_op jit(solution)/shard_map/all_to_all | solution.py:868
  630.7 30.6 %collective-permute-start.38 = (f32[1728]{0:T(1024)S(1)}, f32[1728]{0:T(1024)S(1)}, u32[]{:S(2)}, u32[]{:S(2)}) collective-permute-start(f32[1728]{0:T(1024)S(1)} %get-tuple-element.657), channel_id=1, source_target_pairs={{0,4},{4,8},{8,12},{12,16},{16,20},{20,24},{24,28},{28,0},{1,5},{5... | collective-permute-start | bytes 20744 | tf_op jit(solution)/shard_map/ppermute | solution.py:949
  630.8 34.0 %collective-permute-start.39 = (f32[1728]{0:T(1024)S(1)}, f32[1728]{0:T(1024)S(1)}, u32[]{:S(2)}, u32[]{:S(2)}) collective-permute-start(f32[1728]{0:T(1024)S(1)} %get-tuple-element.656), channel_id=1, source_target_pairs={{0,8},{4,12},{8,16},{12,20},{16,24},{20,28},{24,0},{28,4},{1,9},{5... | collective-permute-start | bytes 20744 | tf_op jit(solution)/shard_map/ppermute | solution.py:949
  637.3 28.4 %collective-permute-start.40 = (f32[1728]{0:T(1024)S(1)}, f32[1728]{0:T(1024)S(1)}, u32[]{:S(2)}, u32[]{:S(2)}) collective-permute-start(f32[1728]{0:T(1024)S(1)} %get-tuple-element.655), channel_id=1, source_target_pairs={{0,12},{4,16},{8,20},{12,24},{16,28},{20,0},{24,4},{28,8},{1,13},{... | collective-permute-start | bytes 20744 | tf_op jit(solution)/shard_map/ppermute | solution.py:949
  639.6 26.2 %collective-permute-start.41 = (f32[1728]{0:T(1024)S(1)}, f32[1728]{0:T(1024)S(1)}, u32[]{:S(2)}, u32[]{:S(2)}) collective-permute-start(f32[1728]{0:T(1024)S(1)} %get-tuple-element.654), channel_id=1, source_target_pairs={{0,16},{4,20},{8,24},{12,28},{16,0},{20,4},{24,8},{28,12},{1,17},{... | collective-permute-start | bytes 20744 | tf_op jit(solution)/shard_map/ppermute | solution.py:949
  640.1 25.6 %collective-permute-start.42 = (f32[1728]{0:T(1024)S(1)}, f32[1728]{0:T(1024)S(1)}, u32[]{:S(2)}, u32[]{:S(2)}) collective-permute-start(f32[1728]{0:T(1024)S(1)} %get-tuple-element.653), channel_id=1, source_target_pairs={{0,20},{4,24},{8,28},{12,0},{16,4},{20,8},{24,12},{28,16},{1,21},{... | collective-permute-start | bytes 20744 | tf_op jit(solution)/shard_map/ppermute | solution.py:949
  661.3 4.4 collective-permute-start.43
  664.7 1.4 collective-permute-start.44
  676.7 31.0 %all-to-all-start.8 = ((bf16[2,8,32,2048]{3,2,0,1:T(8,128)(2,1)}), bf16[2,8,32,2048]{3,2,0,1:T(8,128)(2,1)}, u32[]{:S(2)}, u32[]{:S(2)}) async-start(bf16[2,8,32,2048]{3,2,0,1:T(8,128)(2,1)} %pad_maximum_fusion.2), calls=%async_computation.11 | async-start | bytes 4194304 | tf_op jit(solution)/shard_map/all_to_all | solution.py:611
  681.2 17.0 %collective-permute-start.45 = (f32[320]{0:T(512)S(1)}, f32[320]{0:T(512)S(1)}, u32[]{:S(2)}, u32[]{:S(2)}) collective-permute-start(f32[320]{0:T(512)S(1)} %get-tuple-element.658), channel_id=1, source_target_pairs={{0,1},{1,2},{2,3},{3,0},{4,5},{5,6},{6,7},{7,4},{8,9},{9,10},{10,1... | collective-permute-start | bytes 3848 | tf_op jit(solution)/shard_map/ppermute | solution.py:67
  682.7 15.5 %collective-permute-start.46 = (f32[320]{0:T(512)S(1)}, f32[320]{0:T(512)S(1)}, u32[]{:S(2)}, u32[]{:S(2)}) collective-permute-start(f32[320]{0:T(512)S(1)} %get-tuple-element.660), channel_id=1, source_target_pairs={{0,2},{1,3},{2,0},{3,1},{4,6},{5,7},{6,4},{7,5},{8,10},{9,11},{10,... | collective-permute-start | bytes 3848 | tf_op jit(solution)/shard_map/ppermute | solution.py:67
  684.4 13.8 %collective-permute-start.47 = (f32[320]{0:T(512)S(1)}, f32[320]{0:T(512)S(1)}, u32[]{:S(2)}, u32[]{:S(2)}) collective-permute-start(f32[320]{0:T(512)S(1)} %get-tuple-element.659), channel_id=1, source_target_pairs={{0,3},{1,0},{2,1},{3,2},{4,7},{5,4},{6,5},{7,6},{8,11},{9,8},{10,9... | collective-permute-start | bytes 3848 | tf_op jit(solution)/shard_map/ppermute | solution.py:67
  (47 other events, 422.6 us)
Sparse Core Ops, SparseCore 0:
  31.2 103.0 all-gather.4
  136.2 26.9 all-gather.8
  165.1 64.4 all-gather.6
  360.1 149.9 reduce-scatter.3
  512.2 77.4 reduce-scatter.5
  592.0 77.2 reduce-scatter.7
